TPU v7x, 32 devices: a whole 2x2x4 slice. The times are simulated.
32 devices in a mesh: dp: 16 (over z, y, x), tensor: 2 (over core).
Axes of the slice: x: 2, y: 2, z: 4, core: 2. Of those that a mesh axis runs over, the one named last changes fastest.
Arguments:
- inputs: bfloat16 [8192, 768], P(('dp', 'tensor')), may hold values from -6 to 6
- gain_attn: bfloat16 [768], P('dp'), may hold values from 0.5 to 1.5
- w_qkv: bfloat16 [3, 768, 768], P(None, 'dp', 'tensor')
- w_out: bfloat16 [768, 768], P('tensor', 'dp'), may hold values from -1.75 to 1.75
- gain_ffn: bfloat16 [768], P('dp'), may hold values from 0.5 to 1.5
- w_in: bfloat16 [768, 2, 1152], P('dp', None, 'tensor'), may hold values from -0.21875 to 0.21875
- w_down: bfloat16 [1152, 768], P('tensor', 'dp'), may hold values from -0.1875 to 0.1875
- cotangent: bfloat16 [8192, 768], P(('dp', 'tensor')), may hold values from -6 to 6
- segments: int32 [32, 256], P('dp'), may hold values from 0 to 2, never falling along the last dimension, each value on 1 to 160 neighbouring positions
- lengths: int32 [32], P('dp'), may hold values from 192 to 256
- counts: int32 [16], P('dp'), may hold values from 1 to 2, as said below
Outputs:
- output: bfloat16 [8192, 768], P(('dp', 'tensor'))
- grad_inputs: float32 [8192, 768], P(('dp', 'tensor'))
- grad_gain_attn: float32 [768], P('dp')
- grad_qkv: float32 [3, 768, 768], P(None, 'dp', 'tensor')
- grad_out: float32 [768, 768], P('tensor', 'dp')
- grad_gain_ffn: float32 [768], P('dp')
- grad_in: float32 [768, 2, 1152], P('dp', None, 'tensor')
- grad_down: float32 [1152, 768], P('tensor', 'dp')
Inputs may be any that keep to these rules, and one draw needn't show every extreme that they name: `counts`: each group uses 1 to 2 of its block slots; some group uses all 2 and some exactly 1. `segments`: along each block the ids start at 0, never fall and end at 2 or below; a sequence holds at most 256 * 5 // 8 slots.
All inputs are finite; a program needn't handle non-finite values.
Results may differ from a plain program's by a relative error of at most 0.019.
Values may be sent and summed in bfloat16 or wider, within the bound.
No kernel may reach another device: no remote copies, remote signals or barrier semaphores. Data moves between devices by JAX's collectives and lax.ppermute only.
A program may use at most 128 MiB of HBM per device.

v0:
```python
import functools

import jax
import jax.numpy as jnp
from jax import lax
from jax.experimental import pallas as pl
from jax.experimental.pallas import tpu as pltpu
from jax.sharding import PartitionSpec as P


HD = 64
LANES = 128

THETA_BASE = 160000.0
EPSILON = 1e-05
SQRT_HALF = 0.7071067811865476
INV_ROOT_TWO_PI = 0.3989422804014327
MASKED_SCORE = -1e30

F32 = jnp.float32
BF16 = jnp.bfloat16


NN = (((1,), (0,)), ((), ()))
NT = (((1,), (1,)), ((), ()))
TN = (((0,), (0,)), ((), ()))

X, Y, Z, ZZ = 1, 2, 4, 8
Z_ALL = (0, Z, ZZ, Z | ZZ)
Z_HALVES = (0, ZZ, Z, Z | ZZ)
XY_ALL = (0, X, Y, X | Y)
XY_HALVES = (0, Y, X, X | Y)


def shift(distances, by):
    return tuple(d ^ by for d in distances)


PLANE_PIECES = (Z_ALL, shift(Z_ALL, X), shift(Z_ALL, Y), (3, 7), (11, 15))
LINE_PIECES = tuple(shift(XY_ALL, z) for z in Z_ALL)

GRAD_A = (tuple(y + z for y in (0, Y) for z in Z_HALVES), X)
GRAD_B = (tuple(x + z for x in (0, X) for z in Z_HALVES), Y)
GRAD_C = (tuple(z + xy for z in (0, ZZ) for xy in XY_HALVES), Z)


def mm(left, right, dims):
    return lax.dot_general(left, right, dims, preferred_element_type=F32)


def norm_parts(rows_in):
    centre = rows_in - jnp.mean(rows_in, axis=-1, keepdims=True)
    inv_std = lax.rsqrt(jnp.mean(centre * centre, axis=-1, keepdims=True) + EPSILON)
    return centre * inv_std, inv_std


def norm_back(grad_normed, normed, inv_std, gain_row):
    scaled = grad_normed * gain_row
    inner_mean = jnp.mean(scaled * normed, axis=-1, keepdims=True)
    grad_rows = inv_std * (scaled - jnp.mean(scaled, axis=-1, keepdims=True) - normed * inner_mean)
    return grad_rows, jnp.sum(grad_normed * normed, axis=0, keepdims=True)


def lane_index(shape):
    return lax.broadcasted_iota(jnp.int32, shape, 1)


def swap_halves(chunk):
    half = HD // 2
    return jnp.where(
        lane_index(chunk.shape) % HD < half,
        pltpu.roll(chunk, LANES - half, 1),
        pltpu.roll(chunk, half, 1),
    )


def column_to_row(columns, lane):
    pick = (lane_index((8, LANES)) == lane).astype(BF16)
    return mm(pick, columns, NT)[0:1]


def row_to_columns(row):
    return jnp.transpose(jnp.broadcast_to(row, (LANES, row.shape[1])), (1, 0))


class Pieces:
    def __init__(self, me, refs, rows, layout):
        self.me, self.refs, self.rows, self.layout = me, refs, rows, layout

    def copy(self, dst, dst_col, src_col, width):
        for ref, (distances, first, last) in zip(self.refs, self.layout):
            low, high = max(first, src_col), min(last, src_col + width)
            if low >= high:
                continue
            at = slice(dst_col + low - src_col, dst_col + high - src_col)
            cols = slice(low - first, high - first)
            if distances is None:
                dst[:, at] = ref[:, cols]
                continue
            for i, distance in enumerate(distances):
                base = pl.multiple_of((self.me ^ distance) * self.rows, self.rows)
                dst[pl.ds(base, self.rows), at] = ref[i, :, cols]


def attn_mask(seg_row, seg_col, live_row):
    same = seg_col == seg_row
    shape = same.shape
    diagonal = lax.broadcasted_iota(jnp.int32, shape, 0) == lane_index(shape)
    return (same & (live_row > 0)) | diagonal


def attn_forward_kernel(cfg, n_pieces, *refs):
    me_ref, x_ref = refs[:2]
    own = refs[2 : 2 + n_pieces]
    other = refs[2 + n_pieces : 2 + 2 * n_pieces]
    seg_row, seg_col, live_row, cos_ref, sin_ref = refs[2 + 2 * n_pieces : 7 + 2 * n_pieces]
    w_ref, qkv_ref, att_ref, logt_ref, n1_ref, gain_ref, gcol = refs[7 + 2 * n_pieces :]
    me = me_ref[0]
    half, width = cfg["half"], 2 * cfg["half"]
    for which, pieces in enumerate((own, other)):
        part = Pieces(me, pieces, cfg["rows"], cfg["layout"])
        for c in range(3):
            part.copy(w_ref, c * width + which * half, c * half, half)
        if which == 0:
            part.copy(gcol, 0, 3 * half, LANES)
    gain_row = column_to_row(gcol[...], 0)
    gain_ref[...] = jnp.broadcast_to(gain_row, gain_ref.shape)
    normed, _ = norm_parts(x_ref[...].astype(F32))
    n1 = (normed * gain_row).astype(BF16)
    n1_ref[...] = n1
    cosine, sine = cos_ref[...], sin_ref[...]
    step = 2 * LANES
    for at in range(0, 3 * width, step):
        product = mm(n1, w_ref[:, at : at + step], NN)
        for sub in range(0, step, LANES):
            chunk = product[:, sub : sub + LANES]
            if at < 2 * width:
                chunk = chunk * cosine + swap_halves(chunk) * sine
            qkv_ref[:, at + sub : at + sub + LANES] = chunk.astype(BF16)
    mask = attn_mask(seg_row[...], seg_col[...], live_row[...])
    scale = HD ** (-0.5)
    rows = x_ref.shape[0]
    low = lane_index((rows, LANES)) < HD
    lanes = lane_index((rows, LANES))
    totals = jnp.zeros((rows, LANES), F32)
    for pair in range(width // LANES):
        at = pair * LANES
        queries = qkv_ref[:, at : at + LANES]
        keys = qkv_ref[:, width + at : width + at + LANES]
        values = qkv_ref[:, 2 * width + at : 2 * width + at + LANES]
        outs = []
        for side in range(2):
            picked = jnp.where(low if side == 0 else ~low, queries, jnp.zeros_like(queries))
            scores = jnp.where(mask, mm(picked, keys, NT) * scale, MASKED_SCORE)
            row_max = jnp.max(scores, axis=-1, keepdims=True)
            weights = jnp.exp(scores - row_max)
            total = jnp.sum(weights, axis=-1, keepdims=True)
            prob = (weights * (1.0 / total)).astype(BF16)
            outs.append(mm(prob, values, NN))
            totals = jnp.where(lanes == 2 * pair + side, row_max + jnp.log(total), totals)
        att_ref[:, at : at + LANES] = jnp.where(low, outs[0], outs[1]).astype(BF16)
    logt_ref[...] = totals


def ffn_kernel(cfg, n_pieces, *refs):
    me_ref, x_ref, att_ref, cot_ref, live_ref = refs[:5]
    own = refs[5 : 5 + n_pieces]
    other = refs[5 + n_pieces : 5 + 2 * n_pieces]
    rest = refs[5 + 2 * n_pieces :]
    out_ref, gh_ref, wo_ref, swap_ref, keep_ref = rest[:5]
    win_ref, wgate_ref, wdown_ref, gcol = rest[5:]
    me = me_ref[0]
    half, units, main = cfg["half"], cfg["units"], cfg["main"]
    tail = units - main
    model = x_ref.shape[1]
    out_at = 2 * units
    for which, pieces in enumerate((own, other)):
        part = Pieces(me, pieces, cfg["rows"], cfg["layout"])
        part.copy(win_ref, which * main, 0, main)
        part.copy(wgate_ref, which * main, main, main)
        part.copy(win_ref, 2 * main + which * tail, 2 * main, tail)
        part.copy(wgate_ref, 2 * main + which * tail, 2 * main + tail, tail)
        part.copy(wo_ref, which * half, out_at, half)
        part.copy(wdown_ref, which * main, out_at + half, main)
        part.copy(wdown_ref, 2 * main + which * tail, out_at + half + main, tail)
        if which == 0:
            part.copy(gcol, 0, out_at + half + main, LANES)
    lanes8 = lane_index((8, LANES))
    pick = (lanes8 == tail).astype(BF16)
    gain_row = mm(pick, gcol[...], NT)[0:1]
    att = att_ref[...]
    hidden = x_ref[...].astype(F32) + mm(att, wo_ref[...], NT)
    normed, inv_std = norm_parts(hidden)
    n2 = (normed * gain_row).astype(BF16)
    live = live_ref[...]
    grad_mixed = live * cot_ref[...].astype(F32)
    grad_mixed_bf = grad_mixed.astype(BF16)
    rows = x_ref.shape[0]
    swap_ref[0:rows, 0:model] = n2
    swap_ref[0:rows, model : 2 * model] = grad_mixed_bf
    base = 3 * model
    step = 3 * LANES
    mixed = hidden
    grad_normed = jnp.zeros((rows, model), F32)
    for at in range(0, 2 * units, step):
        unit_in = mm(n2, win_ref[:, at : at + step], NN)
        unit_gate = mm(n2, wgate_ref[:, at : at + step], NN)
        grad_act = mm(grad_mixed_bf, wdown_ref[:, at : at + step], NN)
        cdf = 0.5 * (1.0 + lax.erf(unit_in * SQRT_HALF))
        gelu = unit_in * cdf
        slope = cdf + unit_in * INV_ROOT_TWO_PI * jnp.exp(-0.5 * unit_in * unit_in)
        activated = (gelu * unit_gate).astype(BF16)
        grad_in = (grad_act * unit_gate * slope).astype(BF16)
        grad_gate = (grad_act * gelu).astype(BF16)
        mixed = mixed + mm(activated, wdown_ref[:, at : at + step], NT)
        grad_normed = (
            grad_normed
            + mm(grad_in, win_ref[:, at : at + step], NT)
            + mm(grad_gate, wgate_ref[:, at : at + step], NT)
        )
        for sub in range(0, step, LANES):
            lo = at + sub
            a, gi, gg = (v[:, sub : sub + LANES] for v in (activated, grad_in, grad_gate))
            if lo < 2 * main:
                which, col = divmod(lo, main)
                ref, off = (keep_ref, 0) if which == 0 else (swap_ref, base)
                ref[0:rows, off + col : off + col + LANES] = gi
                ref[0:rows, off + main + col : off + main + col + LANES] = gg
                col = off + 2 * units + half + col
                ref[0:rows, col : col + LANES] = a
            else:
                low = lane_index((rows, LANES)) < tail
                gi, gg, a = gi.astype(F32), gg.astype(F32), a.astype(F32)
                mine = jnp.where(low, gi, pltpu.roll(gg, tail, 1)).astype(BF16)
                theirs = jnp.where(low, pltpu.roll(gi, tail, 1), gg).astype(BF16)
                at_tail = 2 * main
                keep_ref[0:rows, at_tail : at_tail + LANES] = mine
                swap_ref[0:rows, base + at_tail : base + at_tail + LANES] = theirs
                at_tail = 2 * units + half + main
                keep_ref[0:rows, at_tail : at_tail + LANES] = a.astype(BF16)
                swap_ref[0:rows, base + at_tail : base + at_tail + LANES] = pltpu.roll(
                    a, tail, 1
                ).astype(BF16)
    out_ref[...] = (live * mixed).astype(BF16)
    grad_rows, gain_term = norm_back(grad_normed, normed, inv_std, gain_row)
    grad_hidden = grad_mixed + grad_rows
    gh_ref[...] = grad_hidden
    swap_ref[0:rows, 2 * model : base] = grad_hidden.astype(BF16)
    keep_ref[0:rows, 2 * units : 2 * units + half] = att[:, 0:half]
    swap_ref[0:rows, base + 2 * units : base + 2 * units + half] = att[:, half:]
    put_gain(swap_ref, gain_term, rows)


def put_gain(ref, gain_term, rows):
    model = gain_term.shape[1]
    extra = ref.shape[0] - rows
    high = gain_term.astype(BF16).astype(F32)
    first = lax.broadcasted_iota(jnp.int32, (extra, model), 0)
    block = jnp.where(first == 0, high, jnp.where(first == 1, gain_term - high, 0.0))
    ref[rows:, 0:model] = block.astype(BF16)
    ref[rows:, model:] = jnp.zeros((extra, ref.shape[1] - model), BF16)


def attn_backward_kernel(cfg, *refs):
    (x_ref, gh_ref, wo_ref, w_ref, qkv_ref, att_ref, logt_ref, gain_ref) = refs[:8]
    seg_row, seg_col, live_row, cos_ref, sin_ref, n1_ref = refs[8:14]
    gin_ref, swap_ref, keep_ref, gatt_ref, gqkv_ref = refs[14:]
    half, width = cfg["half"], 2 * cfg["half"]
    rows, model = x_ref.shape
    gatt_ref[...] = mm(gh_ref[...].astype(BF16), wo_ref[...], NN).astype(BF16)
    mask = attn_mask(seg_row[...], seg_col[...], live_row[...])
    scale = HD ** (-0.5)
    low = lane_index((rows, LANES)) < HD
    cosine, sine = cos_ref[...], sin_ref[...]
    for pair in range(width // LANES):
        at = pair * LANES
        queries = qkv_ref[:, at : at + LANES]
        keys = qkv_ref[:, width + at : width + at + LANES]
        values = qkv_ref[:, 2 * width + at : 2 * width + at + LANES]
        grad_att = gatt_ref[:, at : at + LANES]
        products = grad_att.astype(F32) * att_ref[:, at : at + LANES].astype(F32)
        grads_q, grad_k, grad_v = [], 0.0, 0.0
        for side in range(2):
            on = low if side == 0 else ~low
            q_side = jnp.where(on, queries, jnp.zeros_like(queries))
            g_side = jnp.where(on, grad_att, jnp.zeros_like(grad_att))
            head = 2 * pair + side
            scores = jnp.where(mask, mm(q_side, keys, NT) * scale, MASKED_SCORE)
            prob = jnp.exp(scores - logt_ref[:, head : head + 1])
            row_inner = jnp.sum(jnp.where(on, products, 0.0), axis=-1, keepdims=True)
            grad_prob = mm(g_side, values, NT)
            grad_scores = (prob * (grad_prob - row_inner)).astype(BF16)
            grad_v = grad_v + mm(prob.astype(BF16), g_side, TN)
            grads_q.append(mm(grad_scores, keys, NN))
            grad_k = grad_k + mm(grad_scores, q_side, TN)
        grad_q = jnp.where(low, grads_q[0], grads_q[1]) * scale
        grad_k = grad_k * scale
        grad_q = grad_q * cosine - swap_halves(grad_q) * sine
        grad_k = grad_k * cosine - swap_halves(grad_k) * sine
        for c, value in enumerate((grad_q, grad_k, grad_v)):
            value = value.astype(BF16)
            gqkv_ref[:, c * width + at : c * width + at + LANES] = value
            if at < half:
                keep_ref[0:rows, c * half + at : c * half + at + LANES] = value
            else:
                col = model + c * half + at - half
                swap_ref[0:rows, col : col + LANES] = value
    swap_ref[0:rows, 0:model] = n1_ref[...]
    grad_normed = mm(gqkv_ref[...], w_ref[...], NT)
    normed, inv_std = norm_parts(x_ref[...].astype(F32))
    grad_rows, gain_term = norm_back(grad_normed, normed, inv_std, gain_ref[0:1])
    gin_ref[...] = gh_ref[...] + grad_rows
    put_gain(swap_ref, gain_term, rows)


def grads_kernel(cfg, sections, fast, me_ref, mine, keep, theirs, *refs):
    grad_ref = refs[-1]
    outs = refs[:-1]
    tokens = keep.shape[0]
    base = cfg["base"]
    for left, at, size in sections:
        l_mine = mine[0:tokens, left : left + cfg["model"]]
        l_theirs = theirs[0:tokens, left : left + cfg["model"]]
        grad_ref[:, at : at + size] = mm(l_mine, keep[:, at : at + size], TN) + mm(
            l_theirs, theirs[0:tokens, base + at : base + at + size], TN
        )
    gain = jnp.zeros((1, cfg["model"]), F32)
    for ref in (mine, theirs):
        block = ref[tokens:, 0 : cfg["model"]].astype(F32)
        gain = gain + block[0:1] + block[1:2]
    columns = row_to_columns(gain)
    total = grad_ref.shape[1]
    last = slice(total - LANES, total)
    if cfg["gain_lane"]:
        keep_low = lane_index(columns.shape) < cfg["gain_lane"]
        columns = jnp.where(keep_low, grad_ref[:, last], columns)
    grad_ref[:, last] = columns
    if not fast:
        outs[0][...] = grad_ref[...]
        return
    me, rows = me_ref[0], cfg["rows"]
    at = 0
    for (order, bit), (first, last) in cfg["emit"]:
        for which in (0, 1):
            for i, distance in enumerate(order):
                start = pl.multiple_of((me ^ distance ^ (bit * which)) * rows, rows)
                outs[at + which][i] = grad_ref[pl.ds(start, rows), first:last].astype(BF16)
        at += 2


def stack_kernel(*refs):
    for i, ref in enumerate(refs[:-1]):
        refs[-1][i] = ref[...]


def combine_kernel(joined, *refs):
    n = (len(refs) - 2) // 2 if joined else len(refs) // 4
    ins, outs = refs[: 2 * n], refs[2 * n :]
    at = 0
    for i in range(n):
        kept, came = ins[2 * i], ins[2 * i + 1]
        blocks, _, cols = kept.shape
        keep, send = (outs[0], outs[1]) if joined else (outs[2 * i], outs[2 * i + 1])
        for j in range(blocks):
            total = kept[j].astype(F32) + came[j].astype(F32)
            ref, k = (keep, j) if j < blocks // 2 else (send, j - blocks // 2)
            ref[k, :, at : at + cols] = total.astype(ref.dtype)
        at += cols if joined else 0


def final_ffn_kernel(kept_c, came_c, kept_ab, came_ab, share):
    cut = kept_c.shape[2]
    share[:, :cut] = kept_c[0] + came_c[0].astype(F32)
    share[:, cut:] = kept_ab[0] + came_ab[0].astype(F32)


def final_qkv_kernel(kept, came, grad, gain):
    half = grad.shape[2]
    for c in range(3):
        cols = slice(c * half, (c + 1) * half)
        grad[c] = kept[0, :, cols] + came[0, :, cols].astype(F32)
    gain[...] = kept[0, :, 3 * half :] + came[0, :, 3 * half :].astype(F32)


VMEM = pl.BlockSpec(memory_space=pltpu.VMEM)
SMEM = pl.BlockSpec(memory_space=pltpu.SMEM)


def call(kernel, operands, outs, scratch, scalars=1, flops=0):
    moved = sum(o.size * o.dtype.itemsize for o in operands)
    moved += sum(s.size * s.dtype.itemsize for s in outs)
    return pl.pallas_call(
        kernel,
        out_shape=outs,
        in_specs=[SMEM] * scalars + [VMEM] * (len(operands) - scalars),
        out_specs=[VMEM] * len(outs),
        scratch_shapes=scratch,
        cost_estimate=pl.CostEstimate(flops=flops, bytes_accessed=moved, transcendentals=0),
        compiler_params=pltpu.CompilerParams(vmem_limit_bytes=60 * 1024 * 1024),
    )(*operands)


def shape(*dims, dtype=BF16):
    return jax.ShapeDtypeStruct(dims, dtype)


def stack(planes):
    outs = [shape(len(planes), *planes[0].shape)]
    return call(stack_kernel, list(planes), outs, [], scalars=0)[0]


def combine(joined, *arrays):
    outs = []
    for kept in arrays[::2]:
        blocks, rows, cols = kept.shape
        outs += [shape(blocks // 2, rows, cols, dtype=F32), shape(blocks // 2, rows, cols)]
    if joined:
        blocks, rows = outs[0].shape[:2]
        cols = sum(o.shape[2] for o in outs[::2])
        outs = [shape(blocks, rows, cols, dtype=F32), shape(blocks, rows, cols)]
    kernel = functools.partial(combine_kernel, joined)
    return call(kernel, list(arrays), outs, [], scalars=0)


def shards(
    inputs, gain_attn, w_qkv, w_out, gain_ffn, w_in, w_down, cotangent, segments, lengths, counts
):
    dp, cores = lax.axis_size("dp"), lax.axis_size("tensor")
    me, core = lax.axis_index("dp"), lax.axis_index("tensor")
    seq = segments.shape[1]
    tokens, model = inputs.shape
    rows, half, units = gain_attn.shape[0], w_qkv.shape[2], w_in.shape[2]
    main = units // LANES * LANES
    tail = units - main
    if cores != 2 or tokens != seq or segments.shape[0] != cores or 2 * tail != LANES:
        raise ValueError("unsupported shapes")
    fast = fast_path(dp) and rows % 16 == 0

    def swap_cores(value):
        return lax.ppermute(value, "tensor", [(0, 1), (1, 0)])

    def exchange(value, distance):
        pairs = [(i, i ^ distance) for i in range(dp)]
        return lax.ppermute(value, "dp", pairs)

    def across_z(value):
        return [value] + [exchange(value, z) for z in Z_ALL[1:]]

    def plane(stacked):
        came_x = exchange(stacked, X)
        came_y = exchange(stacked, Y)
        far_a = exchange(came_y[:2], X)
        far_b = exchange(came_x[2:], Y)
        return [stacked, came_x, came_y, far_a, far_b]

    def both_cores(pieces):
        return [swap_cores(piece) for piece in pieces]

    pack_qkv = jnp.concatenate(
        [w_qkv[0], w_qkv[1], w_qkv[2], jnp.pad(gain_attn[:, None], ((0, 0), (0, LANES - 1)))],
        axis=1,
    )
    out_t, down_t = w_out.T, w_down.T
    pack_ffn = jnp.concatenate(
        [
            w_in[:, 0, :main],
            w_in[:, 1, :main],
            w_in[:, 0, main:],
            w_in[:, 1, main:],
            out_t,
            down_t,
            jnp.pad(gain_ffn[:, None], ((0, 0), (0, tail - 1))),
        ],
        axis=1,
    )
    total_qkv, total_ffn = pack_qkv.shape[1], pack_ffn.shape[1]
    cut = total_ffn * 3 // 10 // LANES * LANES
    if fast:
        own_qkv = plane(stack(across_z(pack_qkv)))
        other_qkv = both_cores(own_qkv)
        pack_c, pack_f = pack_ffn[:, :cut], pack_ffn[:, cut:]
        came_x, came_y = exchange(pack_c, X), exchange(pack_c, Y)
        stack_c = stack([pack_c, came_x, came_y, exchange(came_y, X)])
        own_c = across_z(stack_c)
        own_f = plane(stack(across_z(pack_f)))
        own_ffn = own_c + own_f
        other_ffn = both_cores(own_c) + both_cores(own_f)
        layout_qkv = [(d, 0, total_qkv) for d in PLANE_PIECES]
        layout_ffn = [(d, 0, cut) for d in LINE_PIECES]
        layout_ffn += [(d, cut, total_ffn) for d in PLANE_PIECES]
    else:
        own_qkv = [lax.all_gather(pack_qkv, "dp", axis=0, tiled=True)]
        own_ffn = [lax.all_gather(pack_ffn, "dp", axis=0, tiled=True)]
        other_qkv, other_ffn = both_cores(own_qkv), both_cores(own_ffn)
        layout_qkv, layout_ffn = [(None, 0, total_qkv)], [(None, 0, total_ffn)]

    seg = lax.dynamic_slice_in_dim(segments, core, 1, axis=0)
    length = lax.dynamic_slice_in_dim(lengths, core, 1, axis=0)
    live = ((jnp.arange(seq, dtype=jnp.int32) < length) & (core < counts[0])).astype(F32)
    seg_row, seg_col = seg, seg.reshape(seq, 1)
    live_row, live_col = live.reshape(1, seq), live.reshape(seq, 1)
    earlier = jnp.sum((seg_row < seg_col).astype(jnp.int32), axis=1)
    position = (jnp.arange(seq, dtype=jnp.int32) - earlier).astype(F32)
    frequency = jnp.power(F32(THETA_BASE), -(jnp.arange(HD // 2, dtype=F32) * (2.0 / HD)))
    angle = position[:, None] * frequency[None, :]
    cosine, sine = jnp.cos(angle), jnp.sin(angle)
    repeats = LANES // HD
    cosine = jnp.concatenate([cosine, cosine] * repeats, axis=1)
    sine = jnp.concatenate([-sine, sine] * repeats, axis=1)
    me_vec = me.astype(jnp.int32).reshape(1)

    cfg = dict(half=half, rows=rows, layout=layout_qkv, units=units, main=main, model=model)
    width = 2 * half
    w_full, qkv, att, logt, n1, gain1 = call(
        functools.partial(attn_forward_kernel, cfg, len(own_qkv)),
        [me_vec, inputs, *own_qkv, *other_qkv, seg_row, seg_col, live_row, cosine, sine],
        [
            shape(model, 3 * width),
            shape(tokens, 3 * width),
            shape(tokens, width),
            shape(tokens, LANES, dtype=F32),
            shape(tokens, model),
            shape(8, model, dtype=F32),
        ],
        [pltpu.VMEM((model, LANES), BF16)],
        flops=2 * tokens * model * 3 * width,
    )
    ffn_cfg = dict(cfg, layout=layout_ffn)
    side = 2 * units + half + main + LANES
    output, grad_hidden, wo_full, swap1, keep1 = call(
        functools.partial(ffn_kernel, ffn_cfg, len(own_ffn)),
        [me_vec, inputs, att, cotangent, live_col, *own_ffn, *other_ffn],
        [
            shape(tokens, model),
            shape(tokens, model, dtype=F32),
            shape(model, width),
            shape(tokens + 16, 3 * model + side),
            shape(tokens, side),
        ],
        [pltpu.VMEM((model, 2 * units), BF16)] * 3 + [pltpu.VMEM((model, LANES), BF16)],
        flops=2 * tokens * model * 12 * units,
    )

    def grads(sections, swap_mine, keep, cfg):
        total = cfg["total"]
        outs = [shape(model, total, dtype=F32)]
        if fast:
            outs = [shape(8, rows, last - first) for _, (first, last) in cfg["emit"] for _ in "ks"]
        theirs = swap_cores(swap_mine)
        return call(
            functools.partial(grads_kernel, cfg, sections, fast),
            [me_vec, swap_mine, keep, theirs],
            outs,
            [pltpu.VMEM((model, total), F32)],
            flops=4 * tokens * model * total,
        )

    sections1 = [
        (0, 0, 2 * units),
        (2 * model, 2 * units, half),
        (model, 2 * units + half, main + LANES),
    ]
    mid = cut + (side - cut) // 2 // LANES * LANES
    emit1 = [(GRAD_C, (0, cut)), (GRAD_A, (cut, mid)), (GRAD_B, (mid, side))]
    cfg1 = dict(ffn_cfg, base=3 * model, total=side, gain_lane=tail, emit=emit1)
    pieces1 = grads(sections1, swap1, keep1, cfg1)
    grad_inputs, swap2, keep2 = call(
        functools.partial(attn_backward_kernel, cfg),
        [
            inputs, grad_hidden, wo_full, w_full, qkv, att, logt, gain1,
            seg_row, seg_col, live_row, cosine, sine, n1,
        ],
        [
            shape(tokens, model, dtype=F32),
            shape(tokens + 16, model + 3 * half),
            shape(tokens, 3 * half),
        ],
        [pltpu.VMEM((tokens, width), BF16), pltpu.VMEM((tokens, 3 * width), BF16)],
        scalars=0,
        flops=2 * tokens * model * 5 * width,
    )
    total2 = 3 * half + LANES
    emit2 = [(GRAD_A, (0, total2 // 2)), (GRAD_B, (total2 // 2, total2))]
    cfg2 = dict(cfg, base=model, total=total2, gain_lane=0, emit=emit2)
    pieces2 = grads([(0, 0, 3 * half)], swap2, keep2, cfg2)

    if fast:
        keep_c, send_c, keep_a, send_a, keep_b, send_b = pieces1
        keep_a, send_a, keep_b, send_b = combine(
            False, keep_a, exchange(send_a, X), keep_b, exchange(send_b, Y)
        )
        keep_c, send_c = combine(False, keep_c, exchange(send_c, Z))
        keep_c, send_c = combine(False, keep_c, exchange(send_c, ZZ))
        keep, send = combine(True, keep_a, exchange(send_a, Y), keep_b, exchange(send_b, X))
        keep_c, send_c = combine(False, keep_c, exchange(send_c, X))
        keep, send = combine(False, keep, exchange(send, Z))
        came_c, came = exchange(send_c, Y), exchange(send, ZZ)
        share1 = call(
            final_ffn_kernel,
            [keep_c, came_c, keep, came],
            [shape(rows, side, dtype=F32)],
            [],
            scalars=0,
        )[0]
        keep_a, send_a, keep_b, send_b = pieces2
        keep_a, send_a, keep_b, send_b = combine(
            False, keep_a, exchange(send_a, X), keep_b, exchange(send_b, Y)
        )
        keep, send = combine(True, keep_a, exchange(send_a, Y), keep_b, exchange(send_b, X))
        keep, send = combine(False, keep, exchange(send, Z))
        grad_qkv, gain1_share = call(
            final_qkv_kernel,
            [keep, exchange(send, ZZ)],
            [shape(3, rows, half, dtype=F32), shape(rows, LANES, dtype=F32)],
            [],
            scalars=0,
        )
        grad_gain1 = gain1_share[:, 0]
    else:
        share1, share2 = (
            lax.psum_scatter(pieces[0], "dp", scatter_dimension=0, tiled=True)
            for pieces in (pieces1, pieces2)
        )
        grad_qkv = jnp.stack([share2[:, c * half : (c + 1) * half] for c in range(3)])
        grad_gain1 = share2[:, 3 * half]
    heads = share1[:, : 2 * main].reshape(rows, 2, main)
    tails = share1[:, 2 * main : 2 * units].reshape(rows, 2, tail)
    grad_in = jnp.concatenate([heads, tails], axis=2)
    grad_out = share1[:, 2 * units : 2 * units + half].T
    grad_down = share1[:, 2 * units + half : 2 * units + half + units].T
    grad_gain2 = share1[:, 2 * units + half + units]
    return (
        output,
        grad_inputs,
        grad_gain1,
        grad_qkv,
        grad_out,
        grad_gain2,
        grad_in,
        grad_down,
    )


def fast_path(dp):
    return dp == 16


def solution(mesh):
    in_specs = (
        P(("dp", "tensor"), None),
        P("dp"),
        P(None, "dp", "tensor"),
        P("tensor", "dp"),
        P("dp"),
        P("dp", None, "tensor"),
        P("tensor", "dp"),
        P(("dp", "tensor"), None),
        P("dp", None),
        P("dp"),
        P("dp"),
    )
    out_specs = (
        P(("dp", "tensor"), None),
        P(("dp", "tensor"), None),
        P("dp"),
        P(None, "dp", "tensor"),
        P("tensor", "dp"),
        P("dp"),
        P("dp", None, "tensor"),
        P("tensor", "dp"),
    )

    return jax.shard_map(shards, mesh=mesh, in_specs=in_specs, out_specs=out_specs, check_vma=False)
```

profile of v0, /device:TPU:0, one launch (start us, length us, event | category | flops | bytes accessed | tf_op | source)
XLA Modules:
  0.0 227.1 jit_solution(16398047034866111167)
XLA Ops:
  0.7 1.1 fusion.6
  1.9 3.1 %collective-permute-start.13 = (bf16[48,640]{1,0:T(8,128)(2,1)S(1)}, bf16[48,640]{1,0:T(8,128)(2,1)S(1)}, u32[]{:S(2)}, u32[]{:S(2)}) collective-permute-start(bf16[48,640]{1,0:T(8,128)(2,1)S(1)} %pad_maximum_fusion.3.refs_0_), channel_id=1, source_target_pairs={{0,4},{2,6},{4,0},{6,2},{8,12},{10,14},{12,8},{14,10},{16,20},{18,... | collective-permute-start | bytes 184328 | tf_op jit(solution)/shard_map/ppermute | solution.py:444
  4.9 1.5 collective-permute-start.12
  8.0 3.7 %collective-permute-start.2 = (bf16[48,1280]{1,0:T(8,128)(2,1)S(1)}, bf16[48,1280]{1,0:T(8,128)(2,1)S(1)}, u32[]{:S(2)}, u32[]{:S(2)}) collective-permute-start(bf16[48,1280]{1,0:T(8,128)(2,1)S(1)} %fusion.3.refs_0_), channel_id=1, source_target_pairs={{0,24},{2,26},{4,28},{6,30},{8,16},{10,18},{12,20},{14,22},{16,8},... | collective-permute-start | bytes 368648 | tf_op jit(solution)/shard_map/ppermute | solution.py:444
  15.4 2.1 collective-permute-start.1
  17.5 1.3 collective-permute-start
  19.4 3.7 %collective-permute-done.14.refs_3_ = bf16[48,640]{1,0:T(8,128)(2,1)S(1)} collective-permute-done((bf16[48,640]{1,0:T(8,128)(2,1)S(1)}, bf16[48,640]{1,0:T(8,128)(2,1)S(1)}, u32[]{:S(2)}, u32[]{:S(2)}) %collective-permute-start.14) | collective-permute-done | bytes 61472 | tf_op jit(solution)/shard_map/ppermute | solution.py:444
  23.1 7.0 %collective-permute-start.18 = (bf16[48,1536]{1,0:T(8,128)(2,1)S(1)}, bf16[48,1536]{1,0:T(8,128)(2,1)S(1)}, u32[]{:S(2)}, u32[]{:S(2)}) collective-permute-start(bf16[48,1536]{1,0:T(8,128)(2,1)S(1)} %slice.80.refs_0_), channel_id=1, source_target_pairs={{0,8},{2,10},{4,12},{6,14},{8,0},{10,2},{12,4},{14,6},{16,24},{18,... | collective-permute-start | bytes 442376 | tf_op jit(solution)/shard_map/ppermute | solution.py:444
  30.1 1.6 shard_map.172.refs_5_
  31.7 2.5 %collective-permute-done.1.refs_2_ = bf16[48,1280]{1,0:T(8,128)(2,1)S(1)} collective-permute-done((bf16[48,1280]{1,0:T(8,128)(2,1)S(1)}, bf16[48,1280]{1,0:T(8,128)(2,1)S(1)}, u32[]{:S(2)}, u32[]{:S(2)}) %collective-permute-start.1) | collective-permute-done | bytes 122912 | tf_op jit(solution)/shard_map/ppermute | solution.py:444
  34.2 3.0 %collective-permute-start.17 = (bf16[4,48,640]{2,1,0:T(8,128)(2,1)}, bf16[4,48,640]{2,1,0:T(8,128)(2,1)S(1)}, u32[]{:S(2)}, u32[]{:S(2)}) collective-permute-start(bf16[4,48,640]{2,1,0:T(8,128)(2,1)} %shard_map.172.refs_5_), channel_id=1, source_target_pairs={{0,24},{2,26},{4,28},{6,30},{8,16},{10,18},{12,20},{14,22},{16,8},... | collective-permute-start | bytes 737288 | tf_op jit(solution)/shard_map/ppermute | solution.py:444
  37.4 1.3 collective-permute-start.15
  38.7 1.9 shard_map.170.refs_2_
  41.2 4.0 %collective-permute-done.17.refs_8_ = bf16[4,48,640]{2,1,0:T(8,128)(2,1)S(1)} collective-permute-done((bf16[4,48,640]{2,1,0:T(8,128)(2,1)}, bf16[4,48,640]{2,1,0:T(8,128)(2,1)S(1)}, u32[]{:S(2)}, u32[]{:S(2)}) %collective-permute-start.17) | collective-permute-done | bytes 245792 | tf_op jit(solution)/shard_map/ppermute | solution.py:444
  45.8 2.0 shard_map.173.refs_9_
  47.7 8.9 %collective-permute-done.16.refs_7_ = bf16[4,48,640]{2,1,0:T(8,128)(2,1)S(1)} collective-permute-done((bf16[4,48,640]{2,1,0:T(8,128)(2,1)}, bf16[4,48,640]{2,1,0:T(8,128)(2,1)S(1)}, u32[]{:S(2)}, u32[]{:S(2)}) %collective-permute-start.16) | collective-permute-done | bytes 245792 | tf_op jit(solution)/shard_map/ppermute | solution.py:444
  59.7 1.5 collective-permute-start.5
  61.2 1.3 fusion.2.refs_4_
  62.5 7.6 %collective-permute-done.22.refs_11_ = bf16[4,48,1536]{2,1,0:T(8,128)(2,1)} collective-permute-done((bf16[4,48,1536]{2,1,0:T(8,128)(2,1)}, bf16[4,48,1536]{2,1,0:T(8,128)(2,1)}, u32[]{:S(2)}, u32[]{:S(2)}) %collective-permute-start.22) | collective-permute-done | bytes 589856 | tf_op jit(solution)/shard_map/ppermute | solution.py:444
  70.1 3.5 %collective-permute-done.21.refs_10_ = bf16[4,48,1536]{2,1,0:T(8,128)(2,1)} collective-permute-done((bf16[4,48,1536]{2,1,0:T(8,128)(2,1)}, bf16[4,48,1536]{2,1,0:T(8,128)(2,1)}, u32[]{:S(2)}, u32[]{:S(2)}) %collective-permute-start.21) | collective-permute-done | bytes 589856 | tf_op jit(solution)/shard_map/ppermute | solution.py:444
  75.9 1.3 collective-permute-start.6
  78.5 6.2 %collective-permute-done.6.refs_6_ = bf16[2,48,1280]{2,1,0:T(8,128)(2,1)S(1)} collective-permute-done((bf16[2,48,1280]{2,1,0:T(8,128)(2,1)S(1)}, bf16[2,48,1280]{2,1,0:T(8,128)(2,1)S(1)}, u32[]{:S(2)}, u32[]{:S(2)}) %collective-permute-start.6) | collective-permute-done | bytes 245792 | tf_op jit(solution)/shard_map/ppermute | solution.py:444
  84.8 1.6 collective-permute-done.23.refs_12_
  86.4 4.3 %collective-permute-done.24.refs_13_ = bf16[2,48,1536]{2,1,0:T(8,128)(2,1)} collective-permute-done((bf16[2,48,1536]{2,1,0:T(8,128)(2,1)S(1)}, bf16[2,48,1536]{2,1,0:T(8,128)(2,1)}, u32[]{:S(2)}, u32[]{:S(2)}) %collective-permute-start.24) | collective-permute-done | bytes 294944 | tf_op jit(solution)/shard_map/ppermute | solution.py:444
  93.8 1.2 and_convert_fusion.refs_14_.refs_10_
  95.0 1.0 pad_maximum_fusion.1
  96.1 7.5 %shard_map.171 = (bf16[768,2304]{1,0:T(8,128)(2,1)}, bf16[256,2304]{1,0:T(8,128)(2,1)}, bf16[256,768]{1,0:T(8,128)(2,1)}, f32[256,128]{1,0:T(8,128)}, bf16[256,768]{1,0:T(8,128)(2,1)}, /*index=5*/f32[8,768]{1,0:T(8,128)}) custom-call(s32[1]{0:T(128)} %bitcast.refs_0_.me_ref, bf16[256,768]{1,0:T(8,128)(2,1)} %refs_0_.1, ...), custom_call_target="tpu_custom_call" | custom-call | flops 905969664 | bytes 10251268 | tf_op jit(solution)/shard_map/pallas_call | solution.py:392
  104.3 11.3 %shard_map.174 = (bf16[256,768]{1,0:T(8,128)(2,1)}, f32[256,768]{1,0:T(8,128)}, bf16[768,768]{1,0:T(8,128)(2,1)}, bf16[272,4480]{1,0:T(8,128)(2,1)}, bf16[256,2176]{1,0:T(8,128)(2,1)}) custom-call(s32[1]{0:T(128)} %bitcast.refs_0_.me_ref, bf16[256,768]{1,0:T(8,128)(2,1)} %refs_0_.1, bf16[256,768]{1,0:T(8,128)(2,1)} %get-tuple-element.56.refs_2_.refs_5_, ...), custom_call_target="tpu_custom_call" | custom-call | flops 2717908992 | bytes 13775876 | tf_op jit(solution)/shard_map/pallas_call | solution.py:392
  116.0 11.5 %shard_map.175 = (f32[256,768]{1,0:T(8,128)}, bf16[272,1920]{1,0:T(8,128)(2,1)}, bf16[256,1152]{1,0:T(8,128)(2,1)}) custom-call(bf16[256,768]{1,0:T(8,128)(2,1)} %refs_0_.1, f32[256,768]{1,0:T(8,128)} %get-tuple-element.58.refs_1_, bf16[768,768]{1,0:T(8,128)(2,1)} %get-tuple-element.59.refs_2_, bf16[768,2304]{1,0:T(8,128)(2,1)} %get-tuple-element.60.refs_3_, ...), custom_call_target="tpu_custom_call" | custom-call | flops 1509949440 | bytes 10705920 | tf_op jit(solution)/shard_map/pallas_call | solution.py:392
  127.7 1.5 copy-done.39
  129.2 6.8 %shard_map.181 = (bf16[8,48,640]{2,1,0:T(8,128)(2,1)}, bf16[8,48,640]{2,1,0:T(8,128)(2,1)}, bf16[8,48,768]{2,1,0:T(8,128)(2,1)}, bf16[8,48,768]{2,1,0:T(8,128)(2...) custom-call(s32[1]{0:T(128)} %bitcast.refs_0_.me_ref, bf16[272,4480]{1,0:T(8,128)(2,1)} %get-tuple-element.82.mine, ...), custom_call_target="tpu_custom_call" | custom-call | flops 1711276032 | bytes 9330692 | tf_op jit(solution)/shard_map/pallas_call | solution.py:392
  136.5 1.2 collective-permute-start.47
  137.8 1.0 copy-done.40
  138.8 4.3 %shard_map.176 = (bf16[8,48,640]{2,1,0:T(8,128)(2,1)}, bf16[8,48,640]{2,1,0:T(8,128)(2,1)}, bf16[8,48,640]{2,1,0:T(8,128)(2,1)}, bf16[8,48,640]{2,1,0:T(8,128)(2,1)}) custom-call(s32[1]{0:T(128)} %bitcast.refs_0_.me_ref, bf16[272,1920]{1,0:T(8,128)(2,1)} %get-tuple-element.66.mine, bf16[256,1152]{1,0:T(8,128)(2,1)} %get-tuple-element.67.keep, ...), custom_call_target="tpu_custom_call" | custom-call | flops 1006632960 | bytes 4644868 | tf_op jit(solution)/shard_map/pallas_call | solution.py:392
  143.0 1.5 collective-permute-start.35
  145.3 7.5 %collective-permute-start.42 = (bf16[8,48,640]{2,1,0:T(8,128)(2,1)S(1)}, bf16[8,48,640]{2,1,0:T(8,128)(2,1)S(1)}, u32[]{:S(2)}, u32[]{:S(2)}) collective-permute-start(bf16[8,48,640]{2,1,0:T(8,128)(2,1)S(1)} %copy-done.41), channel_id=1, source_target_pairs={{0,8},{2,10},{4,12},{6,14},{8,0},{10,2},{12,4},{14,6},{16,24},{18,... | collective-permute-start | bytes 1474568 | tf_op jit(solution)/shard_map/ppermute | solution.py:444
  153.9 3.1 %shard_map.185 = (f32[4,48,768]{2,1,0:T(8,128)}, bf16[4,48,768]{2,1,0:T(8,128)(2,1)}, f32[4,48,768]{2,1,0:T(8,128)}, bf16[4,48,768]{2,1,0:T(8,128)(2,1)}) custom-call(bf16[8,48,768]{2,1,0:T(8,128)(2,1)} %get-tuple-element.92.refs_0_, bf16[8,48,768]{2,1,0:T(8,128)(2,1)} %copy-done.4, bf16[8,48,768]{2,1,0:T(8,128)(2,1)} %get-tuple-element.94.refs_2_, ...), custom_call_target="tpu_custom_call" | custom-call | bytes 4128768 | tf_op jit(solution)/shard_map/pallas_call | solution.py:392
  157.0 1.1 collective-permute-start.48
  158.1 1.5 collective-permute-start.49
  159.6 3.3 %collective-permute-done.35.refs_1_ = bf16[8,48,640]{2,1,0:T(8,128)(2,1)S(1)} collective-permute-done((bf16[8,48,640]{2,1,0:T(8,128)(2,1)}, bf16[8,48,640]{2,1,0:T(8,128)(2,1)S(1)}, u32[]{:S(2)}, u32[]{:S(2)}) %collective-permute-start.35) | collective-permute-done | bytes 491552 | tf_op jit(solution)/shard_map/ppermute | solution.py:444
  164.3 2.6 %shard_map.177 = (f32[4,48,640]{2,1,0:T(8,128)}, bf16[4,48,640]{2,1,0:T(8,128)(2,1)}, f32[4,48,640]{2,1,0:T(8,128)}, bf16[4,48,640]{2,1,0:T(8,128)(2,1)}) custom-call(bf16[8,48,640]{2,1,0:T(8,128)(2,1)} %get-tuple-element.68.refs_0_, bf16[8,48,640]{2,1,0:T(8,128)(2,1)} %copy-done.11, bf16[8,48,640]{2,1,0:T(8,128)(2,1)} %get-tuple-element.70.refs_2_, ...), custom_call_target="tpu_custom_call" | custom-call | bytes 3440640 | tf_op jit(solution)/shard_map/pallas_call | solution.py:392
  166.9 1.2 collective-permute-start.37
  168.1 1.5 collective-permute-start.38
  169.6 4.5 %collective-permute-done.37.refs_1_ = bf16[4,48,640]{2,1,0:T(8,128)(2,1)S(1)} collective-permute-done((bf16[4,48,640]{2,1,0:T(8,128)(2,1)}, bf16[4,48,640]{2,1,0:T(8,128)(2,1)S(1)}, u32[]{:S(2)}, u32[]{:S(2)}) %collective-permute-start.37) | collective-permute-done | bytes 245792 | tf_op jit(solution)/shard_map/ppermute | solution.py:444
  175.3 2.3 %shard_map.178 = (f32[2,48,1280]{2,1,0:T(8,128)}, bf16[2,48,1280]{2,1,0:T(8,128)(2,1)}) custom-call(f32[4,48,640]{2,1,0:T(8,128)} %get-tuple-element.72.refs_0_, bf16[4,48,640]{2,1,0:T(8,128)(2,1)} %copy-done.22, f32[4,48,640]{2,1,0:T(8,128)} %get-tuple-element.74.refs_2_, bf16[4,48,640]{2,1,0:T(8,128)(2,1)} %copy-done.23), custom_call_target="tpu_custom_call" | custom-call | bytes 2211840 | tf_op jit(solution)/shard_map/pallas_call | solution.py:392
  177.6 7.2 %collective-permute-start.39 = (bf16[2,48,1280]{2,1,0:T(8,128)(2,1)}, bf16[2,48,1280]{2,1,0:T(8,128)(2,1)S(1)}, u32[]{:S(2)}, u32[]{:S(2)}) collective-permute-start(bf16[2,48,1280]{2,1,0:T(8,128)(2,1)} %get-tuple-element.77), channel_id=1, source_target_pairs={{0,8},{2,10},{4,12},{6,14},{8,0},{10,2},{12,4},{14,6},{16,24},{18,... | collective-permute-start | bytes 737288 | tf_op jit(solution)/shard_map/ppermute | solution.py:444
  185.5 2.1 shard_map.182
  188.5 2.4 %shard_map.186 = (f32[2,48,1536]{2,1,0:T(8,128)}, bf16[2,48,1536]{2,1,0:T(8,128)(2,1)}) custom-call(f32[4,48,768]{2,1,0:T(8,128)} %get-tuple-element.96.refs_0_, bf16[4,48,768]{2,1,0:T(8,128)(2,1)} %copy-done.13, f32[4,48,768]{2,1,0:T(8,128)} %get-tuple-element.98.refs_2_, bf16[4,48,768]{2,1,0:T(8,128)(2,1)} %copy-done.14), custom_call_target="tpu_custom_call" | custom-call | bytes 2654208 | tf_op jit(solution)/shard_map/pallas_call | solution.py:392
  190.9 1.3 collective-permute-start.50
  192.9 1.8 shard_map.179
  194.8 1.6 collective-permute-start.40
  196.4 5.1 %collective-permute-done.43.refs_1_ = bf16[4,48,640]{2,1,0:T(8,128)(2,1)S(1)} collective-permute-done((bf16[4,48,640]{2,1,0:T(8,128)(2,1)}, bf16[4,48,640]{2,1,0:T(8,128)(2,1)S(1)}, u32[]{:S(2)}, u32[]{:S(2)}) %collective-permute-start.43) | collective-permute-done | bytes 245792 | tf_op jit(solution)/shard_map/ppermute | solution.py:444
  202.1 1.9 shard_map.183
  204.0 1.5 collective-permute-start.44
  206.2 1.9 shard_map.187
  208.8 1.7 shard_map.180
  211.2 1.7 shard_map.184
  212.9 1.1 collective-permute-start.45
  213.9 1.4 slice_reduce_fusion.1
  215.3 2.0 collective-permute-done.45.came_c
  218.0 1.9 shard_map.188
  219.9 1.4 slice_reduce_fusion
  222.0 1.5 slice_bitcast_fusion.1
  223.6 1.6 slice_bitcast_fusion
  (195 shorter events, 30.5 us)
Async XLA Ops:
  0.6 73.0 %copy-start = (s32[2,256]{1,0:T(2,128)S(1)}, s32[2,256]{1,0:T(2,128)}, u32[]{:S(2)}) copy-start(s32[2,256]{1,0:T(2,128)} %param.19) | copy-start | bytes 6148
  0.6 58.2 %copy-start.49 = (s32[2]{0:T(128)S(1)}, s32[2]{0:T(128)}, u32[]{:S(2)}) copy-start(s32[2]{0:T(128)} %param.20) | copy-start | bytes 28
  1.8 28.2 %copy-start.24 = (bf16[48,640]{1,0:T(8,128)(2,1)}, bf16[48,640]{1,0:T(8,128)(2,1)S(1)}, u32[]{:S(2)}) copy-start(bf16[48,640]{1,0:T(8,128)(2,1)S(1)} %pad_maximum_fusion.3.refs_0_) | copy-start | bytes 184324
  1.9 13.5 %collective-permute-start.13 = (bf16[48,640]{1,0:T(8,128)(2,1)S(1)}, bf16[48,640]{1,0:T(8,128)(2,1)S(1)}, u32[]{:S(2)}, u32[]{:S(2)}) collective-permute-start(bf16[48,640]{1,0:T(8,128)(2,1)S(1)} %pad_maximum_fusion.3.refs_0_), channel_id=1, source_target_pairs={{0,4},{2,6},{4,0},{6,2},{8,12},{10,14},{12,8},{14,10},{16,20},{18,... | collective-permute-start | bytes 184328 | tf_op jit(solution)/shard_map/ppermute | solution.py:444
  4.9 12.6 %collective-permute-start.12 = (bf16[48,640]{1,0:T(8,128)(2,1)S(1)}, bf16[48,640]{1,0:T(8,128)(2,1)S(1)}, u32[]{:S(2)}, u32[]{:S(2)}) collective-permute-start(bf16[48,640]{1,0:T(8,128)(2,1)S(1)} %pad_maximum_fusion.3.refs_0_), channel_id=1, source_target_pairs={{0,2},{2,0},{4,6},{6,4},{8,10},{10,8},{12,14},{14,12},{16,18},{18,... | collective-permute-start | bytes 184328 | tf_op jit(solution)/shard_map/ppermute | solution.py:444
  8.0 30.7 %copy-start.10 = (bf16[48,1280]{1,0:T(8,128)(2,1)}, bf16[48,1280]{1,0:T(8,128)(2,1)S(1)}, u32[]{:S(2)}) copy-start(bf16[48,1280]{1,0:T(8,128)(2,1)S(1)} %fusion.3.refs_0_) | copy-start | bytes 368644
  8.0 10.8 %collective-permute-start.2 = (bf16[48,1280]{1,0:T(8,128)(2,1)S(1)}, bf16[48,1280]{1,0:T(8,128)(2,1)S(1)}, u32[]{:S(2)}, u32[]{:S(2)}) collective-permute-start(bf16[48,1280]{1,0:T(8,128)(2,1)S(1)} %fusion.3.refs_0_), channel_id=1, source_target_pairs={{0,24},{2,26},{4,28},{6,30},{8,16},{10,18},{12,20},{14,22},{16,8},... | collective-permute-start | bytes 368648 | tf_op jit(solution)/shard_map/ppermute | solution.py:444
  14.3 31.4 %copy-start.3 = (bf16[48,1536]{1,0:T(8,128)(2,1)}, bf16[48,1536]{1,0:T(8,128)(2,1)S(1)}, u32[]{:S(2)}) copy-start(bf16[48,1536]{1,0:T(8,128)(2,1)S(1)} %slice.80.refs_0_) | copy-start | bytes 442372
  14.3 23.0 %collective-permute-start.20 = (bf16[48,1536]{1,0:T(8,128)(2,1)S(1)}, bf16[48,1536]{1,0:T(8,128)(2,1)S(1)}, u32[]{:S(2)}, u32[]{:S(2)}) collective-permute-start(bf16[48,1536]{1,0:T(8,128)(2,1)S(1)} %slice.80.refs_0_), channel_id=1, source_target_pairs={{0,24},{2,26},{4,28},{6,30},{8,16},{10,18},{12,20},{14,22},{16,8},... | collective-permute-start | bytes 442376 | tf_op jit(solution)/shard_map/ppermute | solution.py:444
  14.6 22.8 %collective-permute-start.19 = (bf16[48,1536]{1,0:T(8,128)(2,1)S(1)}, bf16[48,1536]{1,0:T(8,128)(2,1)S(1)}, u32[]{:S(2)}, u32[]{:S(2)}) collective-permute-start(bf16[48,1536]{1,0:T(8,128)(2,1)S(1)} %slice.80.refs_0_), channel_id=1, source_target_pairs={{0,16},{2,18},{4,20},{6,22},{8,24},{10,26},{12,28},{14,30},{16,0},... | collective-permute-start | bytes 442376 | tf_op jit(solution)/shard_map/ppermute | solution.py:444
  15.4 18.8 %collective-permute-start.1 = (bf16[48,1280]{1,0:T(8,128)(2,1)S(1)}, bf16[48,1280]{1,0:T(8,128)(2,1)S(1)}, u32[]{:S(2)}, u32[]{:S(2)}) collective-permute-start(bf16[48,1280]{1,0:T(8,128)(2,1)S(1)} %fusion.3.refs_0_), channel_id=1, source_target_pairs={{0,16},{2,18},{4,20},{6,22},{8,24},{10,26},{12,28},{14,30},{16,0},... | collective-permute-start | bytes 368648 | tf_op jit(solution)/shard_map/ppermute | solution.py:444
  17.5 19.7 %collective-permute-start = (bf16[48,1280]{1,0:T(8,128)(2,1)S(1)}, bf16[48,1280]{1,0:T(8,128)(2,1)S(1)}, u32[]{:S(2)}, u32[]{:S(2)}) collective-permute-start(bf16[48,1280]{1,0:T(8,128)(2,1)S(1)} %fusion.3.refs_0_), channel_id=1, source_target_pairs={{0,8},{2,10},{4,12},{6,14},{8,0},{10,2},{12,4},{14,6},{16,24},{18,... | collective-permute-start | bytes 368648 | tf_op jit(solution)/shard_map/ppermute | solution.py:444
  18.9 19.9 %copy-start.29 = (bf16[48,1280]{1,0:T(8,128)(2,1)}, bf16[48,1280]{1,0:T(8,128)(2,1)S(1)}, u32[]{:S(2)}) copy-start(bf16[48,1280]{1,0:T(8,128)(2,1)S(1)} %collective-permute-done.2.refs_3_) | copy-start | bytes 368644
  18.9 4.2 %collective-permute-start.14 = (bf16[48,640]{1,0:T(8,128)(2,1)S(1)}, bf16[48,640]{1,0:T(8,128)(2,1)S(1)}, u32[]{:S(2)}, u32[]{:S(2)}) collective-permute-start(bf16[48,640]{1,0:T(8,128)(2,1)S(1)} %collective-permute-done.13.refs_2_), channel_id=1, source_target_pairs={{0,2},{2,0},{4,6},{6,4},{8,10},{10,8},{12,14},{14,12},{16,18},{18,... | collective-permute-start | bytes 184328 | tf_op jit(solution)/shard_map/ppermute | solution.py:444
  23.1 17.6 %collective-permute-start.18 = (bf16[48,1536]{1,0:T(8,128)(2,1)S(1)}, bf16[48,1536]{1,0:T(8,128)(2,1)S(1)}, u32[]{:S(2)}, u32[]{:S(2)}) collective-permute-start(bf16[48,1536]{1,0:T(8,128)(2,1)S(1)} %slice.80.refs_0_), channel_id=1, source_target_pairs={{0,8},{2,10},{4,12},{6,14},{8,0},{10,2},{12,4},{14,6},{16,24},{18,... | collective-permute-start | bytes 442376 | tf_op jit(solution)/shard_map/ppermute | solution.py:444
  34.2 10.9 %collective-permute-start.17 = (bf16[4,48,640]{2,1,0:T(8,128)(2,1)}, bf16[4,48,640]{2,1,0:T(8,128)(2,1)S(1)}, u32[]{:S(2)}, u32[]{:S(2)}) collective-permute-start(bf16[4,48,640]{2,1,0:T(8,128)(2,1)} %shard_map.172.refs_5_), channel_id=1, source_target_pairs={{0,24},{2,26},{4,28},{6,30},{8,16},{10,18},{12,20},{14,22},{16,8},... | collective-permute-start | bytes 737288 | tf_op jit(solution)/shard_map/ppermute | solution.py:444
  37.3 7.9 %collective-permute-start.25 = (bf16[4,48,640]{2,1,0:T(8,128)(2,1)}, bf16[4,48,640]{2,1,0:T(8,128)(2,1)}, u32[]{:S(2)}, u32[]{:S(2)}) collective-permute-start(bf16[4,48,640]{2,1,0:T(8,128)(2,1)} %shard_map.172.refs_5_), channel_id=1, source_target_pairs={{0,1},{1,0},{2,3},{3,2},{4,5},{5,4},{6,7},{7,6},{8,9},{9,8},{10,11... | collective-permute-start | bytes 737288 | tf_op jit(solution)/shard_map/ppermute | solution.py:440
  37.3 19.3 %collective-permute-start.16 = (bf16[4,48,640]{2,1,0:T(8,128)(2,1)}, bf16[4,48,640]{2,1,0:T(8,128)(2,1)S(1)}, u32[]{:S(2)}, u32[]{:S(2)}) collective-permute-start(bf16[4,48,640]{2,1,0:T(8,128)(2,1)} %shard_map.172.refs_5_), channel_id=1, source_target_pairs={{0,16},{2,18},{4,20},{6,22},{8,24},{10,26},{12,28},{14,30},{16,0},... | collective-permute-start | bytes 737288 | tf_op jit(solution)/shard_map/ppermute | solution.py:444
  37.4 19.7 %collective-permute-start.15 = (bf16[4,48,640]{2,1,0:T(8,128)(2,1)}, bf16[4,48,640]{2,1,0:T(8,128)(2,1)S(1)}, u32[]{:S(2)}, u32[]{:S(2)}) collective-permute-start(bf16[4,48,640]{2,1,0:T(8,128)(2,1)} %shard_map.172.refs_5_), channel_id=1, source_target_pairs={{0,8},{2,10},{4,12},{6,14},{8,0},{10,2},{12,4},{14,6},{16,24},{18,... | collective-permute-start | bytes 737288 | tf_op jit(solution)/shard_map/ppermute | solution.py:444
  40.7 17.0 %collective-permute-start.4 = (bf16[4,48,1280]{2,1,0:T(8,128)(2,1)}, bf16[4,48,1280]{2,1,0:T(8,128)(2,1)S(1)}, u32[]{:S(2)}, u32[]{:S(2)}) collective-permute-start(bf16[4,48,1280]{2,1,0:T(8,128)(2,1)} %shard_map.170.refs_2_), channel_id=1, source_target_pairs={{0,4},{2,6},{4,0},{6,2},{8,12},{10,14},{12,8},{14,10},{16,20},{18,... | collective-permute-start | bytes 1474568 | tf_op jit(solution)/shard_map/ppermute | solution.py:444
  45.1 12.5 %collective-permute-start.28 = (bf16[4,48,640]{2,1,0:T(8,128)(2,1)S(1)}, bf16[4,48,640]{2,1,0:T(8,128)(2,1)S(1)}, u32[]{:S(2)}, u32[]{:S(2)}) collective-permute-start(bf16[4,48,640]{2,1,0:T(8,128)(2,1)S(1)} %collective-permute-done.17.refs_8_), channel_id=1, source_target_pairs={{0,1},{1,0},{2,3},{3,2},{4,5},{5,4},{6,7},{7,6},{8,9},{9,8},{10,11... | collective-permute-start | bytes 737288 | tf_op jit(solution)/shard_map/ppermute | solution.py:440
  45.1 14.5 %collective-permute-start.3 = (bf16[4,48,1280]{2,1,0:T(8,128)(2,1)}, bf16[4,48,1280]{2,1,0:T(8,128)(2,1)S(1)}, u32[]{:S(2)}, u32[]{:S(2)}) collective-permute-start(bf16[4,48,1280]{2,1,0:T(8,128)(2,1)} %shard_map.170.refs_2_), channel_id=1, source_target_pairs={{0,2},{2,0},{4,6},{6,4},{8,10},{10,8},{12,14},{14,12},{16,18},{18,... | collective-permute-start | bytes 1474568 | tf_op jit(solution)/shard_map/ppermute | solution.py:444
  56.6 13.5 %collective-permute-start.22 = (bf16[4,48,1536]{2,1,0:T(8,128)(2,1)}, bf16[4,48,1536]{2,1,0:T(8,128)(2,1)}, u32[]{:S(2)}, u32[]{:S(2)}) collective-permute-start(bf16[4,48,1536]{2,1,0:T(8,128)(2,1)} %shard_map.173.refs_9_), channel_id=1, source_target_pairs={{0,4},{2,6},{4,0},{6,2},{8,12},{10,14},{12,8},{14,10},{16,20},{18,... | collective-permute-start | bytes 1769480 | tf_op jit(solution)/shard_map/ppermute | solution.py:444
  57.1 18.7 %copy-start.45 = (bf16[4,48,640]{2,1,0:T(8,128)(2,1)}, bf16[4,48,640]{2,1,0:T(8,128)(2,1)S(1)}, u32[]{:S(2)}) copy-start(bf16[4,48,640]{2,1,0:T(8,128)(2,1)S(1)} %collective-permute-done.15.refs_6_) | copy-start | bytes 737284
  57.1 16.5 %collective-permute-start.21 = (bf16[4,48,1536]{2,1,0:T(8,128)(2,1)}, bf16[4,48,1536]{2,1,0:T(8,128)(2,1)}, u32[]{:S(2)}, u32[]{:S(2)}) collective-permute-start(bf16[4,48,1536]{2,1,0:T(8,128)(2,1)} %shard_map.173.refs_9_), channel_id=1, source_target_pairs={{0,2},{2,0},{4,6},{6,4},{8,10},{10,8},{12,14},{14,12},{16,18},{18,... | collective-permute-start | bytes 1769480 | tf_op jit(solution)/shard_map/ppermute | solution.py:444
  57.7 1.9 collective-permute-start.27
  57.7 38.3 %copy-start.1 = (bf16[4,48,1280]{2,1,0:T(8,128)(2,1)}, bf16[4,48,1280]{2,1,0:T(8,128)(2,1)S(1)}, u32[]{:S(2)}) copy-start(bf16[4,48,1280]{2,1,0:T(8,128)(2,1)S(1)} %collective-permute-done.4.refs_4_) | copy-start | bytes 1474564
  57.7 19.5 %collective-permute-start.7 = (bf16[4,48,1280]{2,1,0:T(8,128)(2,1)}, bf16[4,48,1280]{2,1,0:T(8,128)(2,1)S(1)}, u32[]{:S(2)}, u32[]{:S(2)}) collective-permute-start(bf16[4,48,1280]{2,1,0:T(8,128)(2,1)} %shard_map.170.refs_2_), channel_id=1, source_target_pairs={{0,1},{1,0},{2,3},{3,2},{4,5},{5,4},{6,7},{7,6},{8,9},{9,8},{10,11... | collective-permute-start | bytes 1474568 | tf_op jit(solution)/shard_map/ppermute | solution.py:440
  59.5 16.3 %collective-permute-start.26 = (bf16[4,48,640]{2,1,0:T(8,128)(2,1)S(1)}, bf16[4,48,640]{2,1,0:T(8,128)(2,1)S(1)}, u32[]{:S(2)}, u32[]{:S(2)}) collective-permute-start(bf16[4,48,640]{2,1,0:T(8,128)(2,1)S(1)} %collective-permute-done.15.refs_6_), channel_id=1, source_target_pairs={{0,1},{1,0},{2,3},{3,2},{4,5},{5,4},{6,7},{7,6},{8,9},{9,8},{10,11... | collective-permute-start | bytes 737288 | tf_op jit(solution)/shard_map/ppermute | solution.py:440
  59.7 36.4 %copy-start.2 = (bf16[4,48,1280]{2,1,0:T(8,128)(2,1)}, bf16[4,48,1280]{2,1,0:T(8,128)(2,1)S(1)}, u32[]{:S(2)}) copy-start(bf16[4,48,1280]{2,1,0:T(8,128)(2,1)S(1)} %collective-permute-done.3.refs_3_) | copy-start | bytes 1474564
  59.7 18.0 %collective-permute-start.5 = (bf16[2,48,1280]{2,1,0:T(8,128)(2,1)S(1)}, bf16[2,48,1280]{2,1,0:T(8,128)(2,1)S(1)}, u32[]{:S(2)}, u32[]{:S(2)}) collective-permute-start(bf16[2,48,1280]{2,1,0:T(8,128)(2,1)S(1)} %slice.78), channel_id=1, source_target_pairs={{0,2},{2,0},{4,6},{6,4},{8,10},{10,8},{12,14},{14,12},{16,18},{18,... | collective-permute-start | bytes 737288 | tf_op jit(solution)/shard_map/ppermute | solution.py:444
  70.1 20.6 %collective-permute-start.9 = (bf16[4,48,1280]{2,1,0:T(8,128)(2,1)S(1)}, bf16[4,48,1280]{2,1,0:T(8,128)(2,1)S(1)}, u32[]{:S(2)}, u32[]{:S(2)}) collective-permute-start(bf16[4,48,1280]{2,1,0:T(8,128)(2,1)S(1)} %collective-permute-done.4.refs_4_), channel_id=1, source_target_pairs={{0,1},{1,0},{2,3},{3,2},{4,5},{5,4},{6,7},{7,6},{8,9},{9,8},{10,11... | collective-permute-start | bytes 1474568 | tf_op jit(solution)/shard_map/ppermute | solution.py:440
  73.6 17.7 %collective-permute-start.8 = (bf16[4,48,1280]{2,1,0:T(8,128)(2,1)S(1)}, bf16[4,48,1280]{2,1,0:T(8,128)(2,1)S(1)}, u32[]{:S(2)}, u32[]{:S(2)}) collective-permute-start(bf16[4,48,1280]{2,1,0:T(8,128)(2,1)S(1)} %collective-permute-done.3.refs_3_), channel_id=1, source_target_pairs={{0,1},{1,0},{2,3},{3,2},{4,5},{5,4},{6,7},{7,6},{8,9},{9,8},{10,11... | collective-permute-start | bytes 1474568 | tf_op jit(solution)/shard_map/ppermute | solution.py:440
  73.6 22.4 %copy-start.38 = (s32[1,256]{1,0:T(1,128)}, s32[1,256]{1,0:T(1,128)S(1)}, u32[]{:S(2)}) copy-start(s32[1,256]{1,0:T(1,128)S(1)} %constant_dynamic-slice_fusion.refs_12_.refs_8_) | copy-start | bytes 3076
  75.9 8.9 %collective-permute-start.6 = (bf16[2,48,1280]{2,1,0:T(8,128)(2,1)S(1)}, bf16[2,48,1280]{2,1,0:T(8,128)(2,1)S(1)}, u32[]{:S(2)}, u32[]{:S(2)}) collective-permute-start(bf16[2,48,1280]{2,1,0:T(8,128)(2,1)S(1)} %slice.79), channel_id=1, source_target_pairs={{0,4},{2,6},{4,0},{6,2},{8,12},{10,14},{12,8},{14,10},{16,20},{18,... | collective-permute-start | bytes 737288 | tf_op jit(solution)/shard_map/ppermute | solution.py:444
  77.2 18.9 %copy-start.6 = (bf16[4,48,1280]{2,1,0:T(8,128)(2,1)}, bf16[4,48,1280]{2,1,0:T(8,128)(2,1)S(1)}, u32[]{:S(2)}) copy-start(bf16[4,48,1280]{2,1,0:T(8,128)(2,1)S(1)} %collective-permute-done.7.refs_7_) | copy-start | bytes 1474564
  77.2 9.2 %collective-permute-start.23 = (bf16[2,48,1536]{2,1,0:T(8,128)(2,1)S(1)}, bf16[2,48,1536]{2,1,0:T(8,128)(2,1)}, u32[]{:S(2)}, u32[]{:S(2)}) collective-permute-start(bf16[2,48,1536]{2,1,0:T(8,128)(2,1)S(1)} %slice.81), channel_id=1, source_target_pairs={{0,2},{2,0},{4,6},{6,4},{8,10},{10,8},{12,14},{14,12},{16,18},{18,... | collective-permute-start | bytes 884744 | tf_op jit(solution)/shard_map/ppermute | solution.py:444
  77.7 18.3 %copy-start.16 = (bf16[2,48,1280]{2,1,0:T(8,128)(2,1)}, bf16[2,48,1280]{2,1,0:T(8,128)(2,1)S(1)}, u32[]{:S(2)}) copy-start(bf16[2,48,1280]{2,1,0:T(8,128)(2,1)S(1)} %collective-permute-done.5.refs_5_) | copy-start | bytes 737284
  77.7 13.0 %collective-permute-start.24 = (bf16[2,48,1536]{2,1,0:T(8,128)(2,1)S(1)}, bf16[2,48,1536]{2,1,0:T(8,128)(2,1)}, u32[]{:S(2)}, u32[]{:S(2)}) collective-permute-start(bf16[2,48,1536]{2,1,0:T(8,128)(2,1)S(1)} %slice.82), channel_id=1, source_target_pairs={{0,4},{2,6},{4,0},{6,2},{8,12},{10,14},{12,8},{14,10},{16,20},{18,... | collective-permute-start | bytes 884744 | tf_op jit(solution)/shard_map/ppermute | solution.py:444
  84.8 18.8 %collective-permute-start.29 = (bf16[4,48,1536]{2,1,0:T(8,128)(2,1)}, bf16[4,48,1536]{2,1,0:T(8,128)(2,1)}, u32[]{:S(2)}, u32[]{:S(2)}) collective-permute-start(bf16[4,48,1536]{2,1,0:T(8,128)(2,1)} %shard_map.173.refs_9_), channel_id=1, source_target_pairs={{0,1},{1,0},{2,3},{3,2},{4,5},{5,4},{6,7},{7,6},{8,9},{9,8},{10,11... | collective-permute-start | bytes 1769480 | tf_op jit(solution)/shard_map/ppermute | solution.py:440
  86.4 17.2 %collective-permute-start.31 = (bf16[4,48,1536]{2,1,0:T(8,128)(2,1)}, bf16[4,48,1536]{2,1,0:T(8,128)(2,1)}, u32[]{:S(2)}, u32[]{:S(2)}) collective-permute-start(bf16[4,48,1536]{2,1,0:T(8,128)(2,1)} %collective-permute-done.22.refs_11_), channel_id=1, source_target_pairs={{0,1},{1,0},{2,3},{3,2},{4,5},{5,4},{6,7},{7,6},{8,9},{9,8},{10,11... | collective-permute-start | bytes 1769480 | tf_op jit(solution)/shard_map/ppermute | solution.py:440
  90.7 12.9 %collective-permute-start.30 = (bf16[4,48,1536]{2,1,0:T(8,128)(2,1)}, bf16[4,48,1536]{2,1,0:T(8,128)(2,1)}, u32[]{:S(2)}, u32[]{:S(2)}) collective-permute-start(bf16[4,48,1536]{2,1,0:T(8,128)(2,1)} %collective-permute-done.21.refs_10_), channel_id=1, source_target_pairs={{0,1},{1,0},{2,3},{3,2},{4,5},{5,4},{6,7},{7,6},{8,9},{9,8},{10,11... | collective-permute-start | bytes 1769480 | tf_op jit(solution)/shard_map/ppermute | solution.py:440
  90.7 2.5 %collective-permute-start.10 = (bf16[2,48,1280]{2,1,0:T(8,128)(2,1)S(1)}, bf16[2,48,1280]{2,1,0:T(8,128)(2,1)S(1)}, u32[]{:S(2)}, u32[]{:S(2)}) collective-permute-start(bf16[2,48,1280]{2,1,0:T(8,128)(2,1)S(1)} %collective-permute-done.5.refs_5_), channel_id=1, source_target_pairs={{0,1},{1,0},{2,3},{3,2},{4,5},{5,4},{6,7},{7,6},{8,9},{9,8},{10,11... | collective-permute-start | bytes 737288 | tf_op jit(solution)/shard_map/ppermute | solution.py:440
  91.3 2.3 %collective-permute-start.11 = (bf16[2,48,1280]{2,1,0:T(8,128)(2,1)S(1)}, bf16[2,48,1280]{2,1,0:T(8,128)(2,1)S(1)}, u32[]{:S(2)}, u32[]{:S(2)}) collective-permute-start(bf16[2,48,1280]{2,1,0:T(8,128)(2,1)S(1)} %collective-permute-done.6.refs_6_), channel_id=1, source_target_pairs={{0,1},{1,0},{2,3},{3,2},{4,5},{5,4},{6,7},{7,6},{8,9},{9,8},{10,11... | collective-permute-start | bytes 737288 | tf_op jit(solution)/shard_map/ppermute | solution.py:440
  93.3 10.3 %collective-permute-start.32 = (bf16[2,48,1536]{2,1,0:T(8,128)(2,1)}, bf16[2,48,1536]{2,1,0:T(8,128)(2,1)S(1)}, u32[]{:S(2)}, u32[]{:S(2)}) collective-permute-start(bf16[2,48,1536]{2,1,0:T(8,128)(2,1)} %collective-permute-done.23.refs_12_), channel_id=1, source_target_pairs={{0,1},{1,0},{2,3},{3,2},{4,5},{5,4},{6,7},{7,6},{8,9},{9,8},{10,11... | collective-permute-start | bytes 884744 | tf_op jit(solution)/shard_map/ppermute | solution.py:440
  93.6 10.0 %collective-permute-start.33 = (bf16[2,48,1536]{2,1,0:T(8,128)(2,1)}, bf16[2,48,1536]{2,1,0:T(8,128)(2,1)}, u32[]{:S(2)}, u32[]{:S(2)}) collective-permute-start(bf16[2,48,1536]{2,1,0:T(8,128)(2,1)} %collective-permute-done.24.refs_13_), channel_id=1, source_target_pairs={{0,1},{1,0},{2,3},{3,2},{4,5},{5,4},{6,7},{7,6},{8,9},{9,8},{10,11... | collective-permute-start | bytes 884744 | tf_op jit(solution)/shard_map/ppermute | solution.py:440
  115.7 12.0 %collective-permute-start.41 = (bf16[272,4480]{1,0:T(8,128)(2,1)}, bf16[272,4480]{1,0:T(8,128)(2,1)S(1)}, u32[]{:S(2)}, u32[]{:S(2)}) collective-permute-start(bf16[272,4480]{1,0:T(8,128)(2,1)} %get-tuple-element.82.mine), channel_id=1, source_target_pairs={{0,1},{1,0},{2,3},{3,2},{4,5},{5,4},{6,7},{7,6},{8,9},{9,8},{10,11... | collective-permute-start | bytes 7311368 | tf_op jit(solution)/shard_map/ppermute | solution.py:440
  127.5 10.3 %collective-permute-start.34 = (bf16[272,1920]{1,0:T(8,128)(2,1)}, bf16[272,1920]{1,0:T(8,128)(2,1)S(1)}, u32[]{:S(2)}, u32[]{:S(2)}) collective-permute-start(bf16[272,1920]{1,0:T(8,128)(2,1)} %get-tuple-element.66.mine), channel_id=1, source_target_pairs={{0,1},{1,0},{2,3},{3,2},{4,5},{5,4},{6,7},{7,6},{8,9},{9,8},{10,11... | collective-permute-start | bytes 3133448 | tf_op jit(solution)/shard_map/ppermute | solution.py:440
  136.0 16.9 %collective-permute-start.46 = (bf16[8,48,768]{2,1,0:T(8,128)(2,1)}, bf16[8,48,768]{2,1,0:T(8,128)(2,1)S(1)}, u32[]{:S(2)}, u32[]{:S(2)}) collective-permute-start(bf16[8,48,768]{2,1,0:T(8,128)(2,1)} %get-tuple-element.93), channel_id=1, source_target_pairs={{0,2},{2,0},{4,6},{6,4},{8,10},{10,8},{12,14},{14,12},{16,18},{18,... | collective-permute-start | bytes 1769480 | tf_op jit(solution)/shard_map/ppermute | solution.py:444
  136.5 16.4 %collective-permute-start.47 = (bf16[8,48,768]{2,1,0:T(8,128)(2,1)}, bf16[8,48,768]{2,1,0:T(8,128)(2,1)S(1)}, u32[]{:S(2)}, u32[]{:S(2)}) collective-permute-start(bf16[8,48,768]{2,1,0:T(8,128)(2,1)} %get-tuple-element.95), channel_id=1, source_target_pairs={{0,4},{2,6},{4,0},{6,2},{8,12},{10,14},{12,8},{14,10},{16,20},{18,... | collective-permute-start | bytes 1769480 | tf_op jit(solution)/shard_map/ppermute | solution.py:444
  143.0 19.9 %collective-permute-start.35 = (bf16[8,48,640]{2,1,0:T(8,128)(2,1)}, bf16[8,48,640]{2,1,0:T(8,128)(2,1)S(1)}, u32[]{:S(2)}, u32[]{:S(2)}) collective-permute-start(bf16[8,48,640]{2,1,0:T(8,128)(2,1)} %get-tuple-element.69), channel_id=1, source_target_pairs={{0,2},{2,0},{4,6},{6,4},{8,10},{10,8},{12,14},{14,12},{16,18},{18,... | collective-permute-start | bytes 1474568 | tf_op jit(solution)/shard_map/ppermute | solution.py:444
  144.5 18.9 %collective-permute-start.36 = (bf16[8,48,640]{2,1,0:T(8,128)(2,1)}, bf16[8,48,640]{2,1,0:T(8,128)(2,1)S(1)}, u32[]{:S(2)}, u32[]{:S(2)}) collective-permute-start(bf16[8,48,640]{2,1,0:T(8,128)(2,1)} %get-tuple-element.71), channel_id=1, source_target_pairs={{0,4},{2,6},{4,0},{6,2},{8,12},{10,14},{12,8},{14,10},{16,20},{18,... | collective-permute-start | bytes 1474568 | tf_op jit(solution)/shard_map/ppermute | solution.py:444
  145.3 39.4 %collective-permute-start.42 = (bf16[8,48,640]{2,1,0:T(8,128)(2,1)S(1)}, bf16[8,48,640]{2,1,0:T(8,128)(2,1)S(1)}, u32[]{:S(2)}, u32[]{:S(2)}) collective-permute-start(bf16[8,48,640]{2,1,0:T(8,128)(2,1)S(1)} %copy-done.41), channel_id=1, source_target_pairs={{0,8},{2,10},{4,12},{6,14},{8,0},{10,2},{12,4},{14,6},{16,24},{18,... | collective-permute-start | bytes 1474568 | tf_op jit(solution)/shard_map/ppermute | solution.py:444
  157.0 30.7 %collective-permute-start.48 = (bf16[4,48,768]{2,1,0:T(8,128)(2,1)}, bf16[4,48,768]{2,1,0:T(8,128)(2,1)S(1)}, u32[]{:S(2)}, u32[]{:S(2)}) collective-permute-start(bf16[4,48,768]{2,1,0:T(8,128)(2,1)} %get-tuple-element.97), channel_id=1, source_target_pairs={{0,4},{2,6},{4,0},{6,2},{8,12},{10,14},{12,8},{14,10},{16,20},{18,... | collective-permute-start | bytes 884744 | tf_op jit(solution)/shard_map/ppermute | solution.py:444
  158.1 29.6 %collective-permute-start.49 = (bf16[4,48,768]{2,1,0:T(8,128)(2,1)}, bf16[4,48,768]{2,1,0:T(8,128)(2,1)S(1)}, u32[]{:S(2)}, u32[]{:S(2)}) collective-permute-start(bf16[4,48,768]{2,1,0:T(8,128)(2,1)} %get-tuple-element.99), channel_id=1, source_target_pairs={{0,2},{2,0},{4,6},{6,4},{8,10},{10,8},{12,14},{14,12},{16,18},{18,... | collective-permute-start | bytes 884744 | tf_op jit(solution)/shard_map/ppermute | solution.py:444
  166.9 7.3 %collective-permute-start.37 = (bf16[4,48,640]{2,1,0:T(8,128)(2,1)}, bf16[4,48,640]{2,1,0:T(8,128)(2,1)S(1)}, u32[]{:S(2)}, u32[]{:S(2)}) collective-permute-start(bf16[4,48,640]{2,1,0:T(8,128)(2,1)} %get-tuple-element.73), channel_id=1, source_target_pairs={{0,4},{2,6},{4,0},{6,2},{8,12},{10,14},{12,8},{14,10},{16,20},{18,... | collective-permute-start | bytes 737288 | tf_op jit(solution)/shard_map/ppermute | solution.py:444
  168.1 6.4 %collective-permute-start.38 = (bf16[4,48,640]{2,1,0:T(8,128)(2,1)}, bf16[4,48,640]{2,1,0:T(8,128)(2,1)S(1)}, u32[]{:S(2)}, u32[]{:S(2)}) collective-permute-start(bf16[4,48,640]{2,1,0:T(8,128)(2,1)} %get-tuple-element.75), channel_id=1, source_target_pairs={{0,2},{2,0},{4,6},{6,4},{8,10},{10,8},{12,14},{14,12},{16,18},{18,... | collective-permute-start | bytes 737288 | tf_op jit(solution)/shard_map/ppermute | solution.py:444
  177.6 14.7 %collective-permute-start.39 = (bf16[2,48,1280]{2,1,0:T(8,128)(2,1)}, bf16[2,48,1280]{2,1,0:T(8,128)(2,1)S(1)}, u32[]{:S(2)}, u32[]{:S(2)}) collective-permute-start(bf16[2,48,1280]{2,1,0:T(8,128)(2,1)} %get-tuple-element.77), channel_id=1, source_target_pairs={{0,8},{2,10},{4,12},{6,14},{8,0},{10,2},{12,4},{14,6},{16,24},{18,... | collective-permute-start | bytes 737288 | tf_op jit(solution)/shard_map/ppermute | solution.py:444
  187.7 13.8 %collective-permute-start.43 = (bf16[4,48,640]{2,1,0:T(8,128)(2,1)}, bf16[4,48,640]{2,1,0:T(8,128)(2,1)S(1)}, u32[]{:S(2)}, u32[]{:S(2)}) collective-permute-start(bf16[4,48,640]{2,1,0:T(8,128)(2,1)} %get-tuple-element.87), channel_id=1, source_target_pairs={{0,16},{2,18},{4,20},{6,22},{8,24},{10,26},{12,28},{14,30},{16,0},... | collective-permute-start | bytes 737288 | tf_op jit(solution)/shard_map/ppermute | solution.py:444
  190.9 14.6 %collective-permute-start.50 = (bf16[2,48,1536]{2,1,0:T(8,128)(2,1)}, bf16[2,48,1536]{2,1,0:T(8,128)(2,1)S(1)}, u32[]{:S(2)}, u32[]{:S(2)}) collective-permute-start(bf16[2,48,1536]{2,1,0:T(8,128)(2,1)} %get-tuple-element.101), channel_id=1, source_target_pairs={{0,8},{2,10},{4,12},{6,14},{8,0},{10,2},{12,4},{14,6},{16,24},{18,... | collective-permute-start | bytes 884744 | tf_op jit(solution)/shard_map/ppermute | solution.py:444
  194.8 13.3 %collective-permute-start.40 = (bf16[1,48,1280]{2,1,0:T(8,128)(2,1)}, bf16[1,48,1280]{2,1,0:T(8,128)(2,1)S(1)}, u32[]{:S(2)}, u32[]{:S(2)}) collective-permute-start(bf16[1,48,1280]{2,1,0:T(8,128)(2,1)} %get-tuple-element.79), channel_id=1, source_target_pairs={{0,16},{2,18},{4,20},{6,22},{8,24},{10,26},{12,28},{14,30},{16,0},... | collective-permute-start | bytes 368648 | tf_op jit(solution)/shard_map/ppermute | solution.py:444
  204.0 6.5 %collective-permute-start.44 = (bf16[2,48,640]{2,1,0:T(8,128)(2,1)}, bf16[2,48,640]{2,1,0:T(8,128)(2,1)S(1)}, u32[]{:S(2)}, u32[]{:S(2)}) collective-permute-start(bf16[2,48,640]{2,1,0:T(8,128)(2,1)} %get-tuple-element.89), channel_id=1, source_target_pairs={{0,2},{2,0},{4,6},{6,4},{8,10},{10,8},{12,14},{14,12},{16,18},{18,... | collective-permute-start | bytes 368648 | tf_op jit(solution)/shard_map/ppermute | solution.py:444
  208.1 9.2 %collective-permute-start.51 = (bf16[1,48,1536]{2,1,0:T(8,128)(2,1)}, bf16[1,48,1536]{2,1,0:T(8,128)(2,1)S(1)}, u32[]{:S(2)}, u32[]{:S(2)}) collective-permute-start(bf16[1,48,1536]{2,1,0:T(8,128)(2,1)} %get-tuple-element.103), channel_id=1, source_target_pairs={{0,16},{2,18},{4,20},{6,22},{8,24},{10,26},{12,28},{14,30},{16,0},... | collective-permute-start | bytes 442376 | tf_op jit(solution)/shard_map/ppermute | solution.py:444
  212.9 4.4 %collective-permute-start.45 = (bf16[1,48,640]{2,1,0:T(8,128)(2,1)}, bf16[1,48,640]{2,1,0:T(8,128)(2,1)S(1)}, u32[]{:S(2)}, u32[]{:S(2)}) collective-permute-start(bf16[1,48,640]{2,1,0:T(8,128)(2,1)} %get-tuple-element.91), channel_id=1, source_target_pairs={{0,4},{2,6},{4,0},{6,2},{8,12},{10,14},{12,8},{14,10},{16,20},{18,... | collective-permute-start | bytes 184328 | tf_op jit(solution)/shard_map/ppermute | solution.py:444
  (38 other events, 161.9 us)
where the time goes:
time: 228 us; the launch traced here: 227 us
  Pallas kernels  70.4 us (31%)
  starting transfers between devices  62.8 us (28%)
  waiting for transfers between devices  59.1 us (26%)
  local copies, waits for them, and re-layouts  28 us (12%)
  other arithmetic  5.09 us (2%)
    pallas_call x19, Pallas kernels, call(): pl.pallas_call(kernel, out_shape=outs, in_specs=[SMEM] * scalars + [VMEM]...  70.4 us
    ppermute x36, starting transfers between devices, exchange(): return lax.ppermute(value, 'dp', pairs)  60.6 us
    ppermute x36, waiting for transfers between devices, exchange(): return lax.ppermute(value, 'dp', pairs)  58.3 us
    unnamed x100, local copies, waits for them, and re-layouts  11.4 us
  transfers between devices with their start and end apart: 52, of which 18 were waited for; matrix products, arithmetic and copies ran while one was open for 6% of the time, Pallas kernels for 25%

commit v1 on v0

--- a/solution.py
+++ b/solution.py
@@ -1,4 +1,5 @@
 import functools
+import math
 
 import jax
 import jax.numpy as jnp
@@ -386,9 +387,10 @@
 SMEM = pl.BlockSpec(memory_space=pltpu.SMEM)
 
 
-def call(kernel, operands, outs, scratch, scalars=1, flops=0):
+def call(kernel, operands, outs, scratch, scalars=1, flops=0, spare=1 << 20):
     moved = sum(o.size * o.dtype.itemsize for o in operands)
     moved += sum(s.size * s.dtype.itemsize for s in outs)
+    held = sum(math.prod(s.shape) * jnp.dtype(s.dtype).itemsize for s in scratch)
     return pl.pallas_call(
         kernel,
         out_shape=outs,
@@ -396,7 +398,7 @@
         out_specs=[VMEM] * len(outs),
         scratch_shapes=scratch,
         cost_estimate=pl.CostEstimate(flops=flops, bytes_accessed=moved, transcendentals=0),
-        compiler_params=pltpu.CompilerParams(vmem_limit_bytes=60 * 1024 * 1024),
+        compiler_params=pltpu.CompilerParams(vmem_limit_bytes=moved + held + spare),
     )(*operands)
 
 
@@ -524,6 +526,7 @@
         ],
         [pltpu.VMEM((model, LANES), BF16)],
         flops=2 * tokens * model * 3 * width,
+        spare=6 << 20,
     )
     ffn_cfg = dict(cfg, layout=layout_ffn)
     side = 2 * units + half + main + LANES
@@ -539,6 +542,7 @@
         ],
         [pltpu.VMEM((model, 2 * units), BF16)] * 3 + [pltpu.VMEM((model, LANES), BF16)],
         flops=2 * tokens * model * 12 * units,
+        spare=6 << 20,
     )
 
     def grads(sections, swap_mine, keep, cfg):
@@ -553,6 +557,7 @@
             outs,
             [pltpu.VMEM((model, total), F32)],
             flops=4 * tokens * model * total,
+            spare=6 << 20,
         )
 
     sections1 = [
@@ -578,6 +583,7 @@
         [pltpu.VMEM((tokens, width), BF16), pltpu.VMEM((tokens, 3 * width), BF16)],
         scalars=0,
         flops=2 * tokens * model * 5 * width,
+        spare=6 << 20,
     )
     total2 = 3 * half + LANES
     emit2 = [(GRAD_A, (0, total2 // 2)), (GRAD_B, (total2 // 2, total2))]

time: 228 us -> 200 us (0.88)
  Pallas kernels: 70.4 us -> 27.2 us
  waiting for transfers between devices: 59.1 us -> 85.8 us
  local copies, waits for them, and re-layouts: 28 us -> 16.8 us
    pallas_call x19, Pallas kernels: 70.4 us -> 27.2 us  [call(): pl.pallas_call(kernel, out_shape=outs, in_specs=[SMEM] * scalars + [VMEM]...]
    ppermute x36, waiting for transfers between devices: 58.3 us -> 85.2 us  [exchange(): return lax.ppermute(value, 'dp', pairs)]
    unnamed x100 -> x48, local copies, waits for them, and re-layouts: 11.4 us -> 5.82 us
  transfers between devices with their start and end apart: 52 -> 52, of which waited for: 18 -> 20; matrix products, arithmetic and copies ran while one was open for 6% -> 5% of each run, Pallas kernels for 25% -> 10%
where the time goes in v1:
time: 200 us
  waiting for transfers between devices  85.8 us (43%)
  starting transfers between devices  64.7 us (32%)
  Pallas kernels  27.2 us (14%)
  local copies, waits for them, and re-layouts  16.8 us (8%)
  other arithmetic  3.15 us (2%)
    ppermute x36, waiting for transfers between devices, exchange(): return lax.ppermute(value, 'dp', pairs)  85.2 us
    ppermute x36, starting transfers between devices, exchange(): return lax.ppermute(value, 'dp', pairs)  62.4 us
    pallas_call x19, Pallas kernels, call(): pl.pallas_call(kernel, out_shape=outs, in_specs=[SMEM] * scalars + [VMEM]...  27.2 us
    unnamed x48, local copies, waits for them, and re-layouts  5.82 us
  transfers between devices with their start and end apart: 52, of which 20 were waited for; matrix products, arithmetic and copies ran while one was open for 5% of the time, Pallas kernels for 10%

profile of v1, /device:TPU:0, one launch (start us, length us, event | category | flops | bytes accessed | tf_op | source)
XLA Modules:
  0.0 199.5 jit_solution(4226160556934439180)
XLA Ops:
  0.7 1.1 fusion.6
  1.8 3.1 %collective-permute-start.13 = (bf16[48,640]{1,0:T(8,128)(2,1)S(1)}, bf16[48,640]{1,0:T(8,128)(2,1)S(1)}, u32[]{:S(2)}, u32[]{:S(2)}) collective-permute-start(bf16[48,640]{1,0:T(8,128)(2,1)S(1)} %pad_maximum_fusion.3.refs_0_), channel_id=1, source_target_pairs={{0,4},{2,6},{4,0},{6,2},{8,12},{10,14},{12,8},{14,10},{16,20},{18,... | collective-permute-start | bytes 184328 | tf_op jit(solution)/shard_map/ppermute | solution.py:446
  4.9 1.5 collective-permute-start.12
  6.4 0.8 copy.41
  7.2 0.8 slice_bitcast_fusion.4
  8.0 3.7 %collective-permute-start.2 = (bf16[48,1280]{1,0:T(8,128)(2,1)S(1)}, bf16[48,1280]{1,0:T(8,128)(2,1)S(1)}, u32[]{:S(2)}, u32[]{:S(2)}) collective-permute-start(bf16[48,1280]{1,0:T(8,128)(2,1)S(1)} %fusion.3.refs_0_), channel_id=1, source_target_pairs={{0,24},{2,26},{4,28},{6,30},{8,16},{10,18},{12,20},{14,22},{16,8},... | collective-permute-start | bytes 368648 | tf_op jit(solution)/shard_map/ppermute | solution.py:446
  11.7 0.9 fusion.5
  12.5 0.8 copy.49
  13.3 0.9 concatenate.23
  14.6 0.8 collective-permute-start.19
  15.4 2.1 %collective-permute-start.1 = (bf16[48,1280]{1,0:T(8,128)(2,1)S(1)}, bf16[48,1280]{1,0:T(8,128)(2,1)S(1)}, u32[]{:S(2)}, u32[]{:S(2)}) collective-permute-start(bf16[48,1280]{1,0:T(8,128)(2,1)S(1)} %fusion.3.refs_0_), channel_id=1, source_target_pairs={{0,16},{2,18},{4,20},{6,22},{8,24},{10,26},{12,28},{14,30},{16,0},... | collective-permute-start | bytes 368648 | tf_op jit(solution)/shard_map/ppermute | solution.py:446
  17.5 1.3 collective-permute-start
  19.3 3.7 %collective-permute-done.14.refs_3_ = bf16[48,640]{1,0:T(8,128)(2,1)S(1)} collective-permute-done((bf16[48,640]{1,0:T(8,128)(2,1)S(1)}, bf16[48,640]{1,0:T(8,128)(2,1)S(1)}, u32[]{:S(2)}, u32[]{:S(2)}) %collective-permute-start.14) | collective-permute-done | bytes 61472 | tf_op jit(solution)/shard_map/ppermute | solution.py:446
  23.0 7.0 %collective-permute-start.18 = (bf16[48,1536]{1,0:T(8,128)(2,1)S(1)}, bf16[48,1536]{1,0:T(8,128)(2,1)S(1)}, u32[]{:S(2)}, u32[]{:S(2)}) collective-permute-start(bf16[48,1536]{1,0:T(8,128)(2,1)S(1)} %slice.80.refs_0_), channel_id=1, source_target_pairs={{0,8},{2,10},{4,12},{6,14},{8,0},{10,2},{12,4},{14,6},{16,24},{18,... | collective-permute-start | bytes 442376 | tf_op jit(solution)/shard_map/ppermute | solution.py:446
  30.1 4.1 %collective-permute-done.1.refs_2_ = bf16[48,1280]{1,0:T(8,128)(2,1)S(1)} collective-permute-done((bf16[48,1280]{1,0:T(8,128)(2,1)S(1)}, bf16[48,1280]{1,0:T(8,128)(2,1)S(1)}, u32[]{:S(2)}, u32[]{:S(2)}) %collective-permute-start.1) | collective-permute-done | bytes 122912 | tf_op jit(solution)/shard_map/ppermute | solution.py:446
  34.2 3.2 %collective-permute-start.17 = (bf16[4,48,640]{2,1,0:T(8,128)(2,1)S(1)}, bf16[4,48,640]{2,1,0:T(8,128)(2,1)S(1)}, u32[]{:S(2)}, u32[]{:S(2)}) collective-permute-start(bf16[4,48,640]{2,1,0:T(8,128)(2,1)S(1)} %shard_map.172.refs_5_), channel_id=1, source_target_pairs={{0,24},{2,26},{4,28},{6,30},{8,16},{10,18},{12,20},{14,22},{16,8},... | collective-permute-start | bytes 737288 | tf_op jit(solution)/shard_map/ppermute | solution.py:446
  37.6 1.1 collective-permute-start.15
  39.3 5.6 %collective-permute-done.17.refs_8_ = bf16[4,48,640]{2,1,0:T(8,128)(2,1)S(1)} collective-permute-done((bf16[4,48,640]{2,1,0:T(8,128)(2,1)S(1)}, bf16[4,48,640]{2,1,0:T(8,128)(2,1)S(1)}, u32[]{:S(2)}, u32[]{:S(2)}) %collective-permute-start.17) | collective-permute-done | bytes 245792 | tf_op jit(solution)/shard_map/ppermute | solution.py:446
  44.9 0.7 copy-done.13
  46.2 10.1 %collective-permute-done.16.refs_7_ = bf16[4,48,640]{2,1,0:T(8,128)(2,1)S(1)} collective-permute-done((bf16[4,48,640]{2,1,0:T(8,128)(2,1)S(1)}, bf16[4,48,640]{2,1,0:T(8,128)(2,1)S(1)}, u32[]{:S(2)}, u32[]{:S(2)}) %collective-permute-start.16) | collective-permute-done | bytes 245792 | tf_op jit(solution)/shard_map/ppermute | solution.py:446
  57.4 0.7 copy-done.19
  60.1 1.5 collective-permute-start.5
  61.6 0.7 fusion.2.refs_4_
  62.2 7.2 %collective-permute-done.22.refs_11_ = bf16[4,48,1536]{2,1,0:T(8,128)(2,1)} collective-permute-done((bf16[4,48,1536]{2,1,0:T(8,128)(2,1)S(1)}, bf16[4,48,1536]{2,1,0:T(8,128)(2,1)}, u32[]{:S(2)}, u32[]{:S(2)}) %collective-permute-start.22) | collective-permute-done | bytes 589856 | tf_op jit(solution)/shard_map/ppermute | solution.py:446
  69.5 3.7 %collective-permute-done.21.refs_10_ = bf16[4,48,1536]{2,1,0:T(8,128)(2,1)} collective-permute-done((bf16[4,48,1536]{2,1,0:T(8,128)(2,1)S(1)}, bf16[4,48,1536]{2,1,0:T(8,128)(2,1)}, u32[]{:S(2)}, u32[]{:S(2)}) %collective-permute-start.21) | collective-permute-done | bytes 589856 | tf_op jit(solution)/shard_map/ppermute | solution.py:446
  73.4 1.0 slice.81
  74.4 1.0 slice.82
  75.4 0.7 copy-done.21
  76.1 1.5 collective-permute-start.6
  78.7 6.4 %collective-permute-done.6.refs_6_ = bf16[2,48,1280]{2,1,0:T(8,128)(2,1)} collective-permute-done((bf16[2,48,1280]{2,1,0:T(8,128)(2,1)S(1)}, bf16[2,48,1280]{2,1,0:T(8,128)(2,1)}, u32[]{:S(2)}, u32[]{:S(2)}) %collective-permute-start.6) | collective-permute-done | bytes 245792 | tf_op jit(solution)/shard_map/ppermute | solution.py:446
  85.0 1.7 collective-permute-done.23.refs_12_
  86.7 4.0 %collective-permute-done.24.refs_13_ = bf16[2,48,1536]{2,1,0:T(8,128)(2,1)S(1)} collective-permute-done((bf16[2,48,1536]{2,1,0:T(8,128)(2,1)S(1)}, bf16[2,48,1536]{2,1,0:T(8,128)(2,1)S(1)}, u32[]{:S(2)}, u32[]{:S(2)}) %collective-permute-start.24) | collective-permute-done | bytes 294944 | tf_op jit(solution)/shard_map/ppermute | solution.py:446
  90.8 0.8 copy-done.2
  92.1 0.8 copy-done.4
  94.8 0.7 and_convert_fusion.refs_14_.refs_10_
  95.8 1.0 copy-done.3
  96.8 1.0 copy-done.5
  97.9 5.9 %shard_map.171 = (bf16[768,2304]{1,0:T(8,128)(2,1)S(1)}, bf16[256,2304]{1,0:T(8,128)(2,1)S(1)}, bf16[256,768]{1,0:T(8,128)(2,1)S(1)}, f32[256,128]{1,0:T(8,128)S...) custom-call(s32[1]{0:T(128)} %bitcast.refs_0_.me_ref, bf16[256,768]{1,0:T(8,128)(2,1)S(1)} %copy-done.1, ...), custom_call_target="tpu_custom_call" | custom-call | flops 905969664 | bytes 10251268 | tf_op jit(solution)/shard_map/pallas_call | solution.py:394
  104.0 7.8 %shard_map.174 = (bf16[256,768]{1,0:T(8,128)(2,1)}, f32[256,768]{1,0:T(8,128)S(1)}, bf16[768,768]{1,0:T(8,128)(2,1)S(1)}, bf16[272,4480]{1,0:T(8,128)(2,1)S(1)}, bf16[256,2176]{1,0:T(8,128)(2,1)S(1)}) custom-call(s32[1]{0:T(128)} %bitcast.refs_0_.me_ref, bf16[256,768]{1,0:T(8,128)(2,1)S(1)} %copy-done.1, ...), custom_call_target="tpu_custom_call" | custom-call | flops 2717908992 | bytes 13775876 | tf_op jit(solution)/shard_map/pallas_call | solution.py:394
  112.2 7.7 %shard_map.175 = (f32[256,768]{1,0:T(8,128)}, bf16[272,1920]{1,0:T(8,128)(2,1)S(1)}, bf16[256,1152]{1,0:T(8,128)(2,1)S(1)}) custom-call(bf16[256,768]{1,0:T(8,128)(2,1)S(1)} %copy-done.1, f32[256,768]{1,0:T(8,128)S(1)} %get-tuple-element.58.refs_1_, bf16[768,768]{1,0:T(8,128)(2,1)S(1)} %get-tuple-element.59.refs_2_, ...), custom_call_target="tpu_custom_call" | custom-call | flops 1509949440 | bytes 10705920 | tf_op jit(solution)/shard_map/pallas_call | solution.py:394
  120.0 2.6 %shard_map.181 = (bf16[8,48,640]{2,1,0:T(8,128)(2,1)S(1)}, bf16[8,48,640]{2,1,0:T(8,128)(2,1)S(1)}, bf16[8,48,768]{2,1,0:T(8,128)(2,1)S(1)}, bf16[8,48,768]{2,1,...) custom-call(s32[1]{0:T(128)} %bitcast.refs_0_.me_ref, ...), custom_call_target="tpu_custom_call" | custom-call | flops 1711276032 | bytes 9330692 | tf_op jit(solution)/shard_map/pallas_call | solution.py:394
  123.2 1.5 collective-permute-start.47
  124.7 1.4 shard_map.176
  126.1 1.6 collective-permute-start.35
  128.2 8.4 %collective-permute-start.42 = (bf16[8,48,640]{2,1,0:T(8,128)(2,1)S(1)}, bf16[8,48,640]{2,1,0:T(8,128)(2,1)S(1)}, u32[]{:S(2)}, u32[]{:S(2)}) collective-permute-start(bf16[8,48,640]{2,1,0:T(8,128)(2,1)S(1)} %get-tuple-element.85), channel_id=1, source_target_pairs={{0,8},{2,10},{4,12},{6,14},{8,0},{10,2},{12,4},{14,6},{16,24},{18,... | collective-permute-start | bytes 1474568 | tf_op jit(solution)/shard_map/ppermute | solution.py:446
  136.6 2.2 %collective-permute-done.46.refs_1_ = bf16[8,48,768]{2,1,0:T(8,128)(2,1)S(1)} collective-permute-done((bf16[8,48,768]{2,1,0:T(8,128)(2,1)S(1)}, bf16[8,48,768]{2,1,0:T(8,128)(2,1)S(1)}, u32[]{:S(2)}, u32[]{:S(2)}) %collective-permute-start.46) | collective-permute-done | bytes 589856 | tf_op jit(solution)/shard_map/ppermute | solution.py:446
  139.6 1.6 collective-permute-start.48
  141.2 1.5 collective-permute-start.49
  142.7 6.7 %collective-permute-done.35.refs_1_ = bf16[8,48,640]{2,1,0:T(8,128)(2,1)S(1)} collective-permute-done((bf16[8,48,640]{2,1,0:T(8,128)(2,1)S(1)}, bf16[8,48,640]{2,1,0:T(8,128)(2,1)S(1)}, u32[]{:S(2)}, u32[]{:S(2)}) %collective-permute-start.35) | collective-permute-done | bytes 491552 | tf_op jit(solution)/shard_map/ppermute | solution.py:446
  150.1 1.6 collective-permute-start.37
  151.7 1.5 collective-permute-start.38
  153.2 7.4 %collective-permute-done.37.refs_1_ = bf16[4,48,640]{2,1,0:T(8,128)(2,1)S(1)} collective-permute-done((bf16[4,48,640]{2,1,0:T(8,128)(2,1)S(1)}, bf16[4,48,640]{2,1,0:T(8,128)(2,1)S(1)}, u32[]{:S(2)}, u32[]{:S(2)}) %collective-permute-start.37) | collective-permute-done | bytes 245792 | tf_op jit(solution)/shard_map/ppermute | solution.py:446
  160.7 8.5 %collective-permute-start.39 = (bf16[2,48,1280]{2,1,0:T(8,128)(2,1)S(1)}, bf16[2,48,1280]{2,1,0:T(8,128)(2,1)S(1)}, u32[]{:S(2)}, u32[]{:S(2)}) collective-permute-start(bf16[2,48,1280]{2,1,0:T(8,128)(2,1)S(1)} %get-tuple-element.77), channel_id=1, source_target_pairs={{0,8},{2,10},{4,12},{6,14},{8,0},{10,2},{12,4},{14,6},{16,24},{18,... | collective-permute-start | bytes 737288 | tf_op jit(solution)/shard_map/ppermute | solution.py:446
  169.6 1.5 collective-permute-start.50
  171.0 8.9 %collective-permute-done.39.refs_1_ = bf16[2,48,1280]{2,1,0:T(8,128)(2,1)S(1)} collective-permute-done((bf16[2,48,1280]{2,1,0:T(8,128)(2,1)S(1)}, bf16[2,48,1280]{2,1,0:T(8,128)(2,1)S(1)}, u32[]{:S(2)}, u32[]{:S(2)}) %collective-permute-start.39) | collective-permute-done | bytes 245792 | tf_op jit(solution)/shard_map/ppermute | solution.py:446
  180.4 3.5 %collective-permute-done.43.refs_1_ = bf16[4,48,640]{2,1,0:T(8,128)(2,1)S(1)} collective-permute-done((bf16[4,48,640]{2,1,0:T(8,128)(2,1)S(1)}, bf16[4,48,640]{2,1,0:T(8,128)(2,1)S(1)}, u32[]{:S(2)}, u32[]{:S(2)}) %collective-permute-start.43) | collective-permute-done | bytes 245792 | tf_op jit(solution)/shard_map/ppermute | solution.py:446
  183.9 1.5 collective-permute-start.44
  185.4 3.3 %collective-permute-done.50.refs_1_ = bf16[2,48,1536]{2,1,0:T(8,128)(2,1)S(1)} collective-permute-done((bf16[2,48,1536]{2,1,0:T(8,128)(2,1)S(1)}, bf16[2,48,1536]{2,1,0:T(8,128)(2,1)S(1)}, u32[]{:S(2)}, u32[]{:S(2)}) %collective-permute-start.50) | collective-permute-done | bytes 294944 | tf_op jit(solution)/shard_map/ppermute | solution.py:446
  188.9 0.7 shard_map.180
  190.9 3.1 %collective-permute-done.45.came_c = bf16[1,48,640]{2,1,0:T(8,128)(2,1)S(1)} collective-permute-done((bf16[1,48,640]{2,1,0:T(8,128)(2,1)S(1)}, bf16[1,48,640]{2,1,0:T(8,128)(2,1)S(1)}, u32[]{:S(2)}, u32[]{:S(2)}) %collective-permute-start.45) | collective-permute-done | bytes 61472 | tf_op jit(solution)/shard_map/ppermute | solution.py:446
  194.0 2.4 %collective-permute-done.51.came_ab = bf16[1,48,1536]{2,1,0:T(8,128)(2,1)S(1)} collective-permute-done((bf16[1,48,1536]{2,1,0:T(8,128)(2,1)S(1)}, bf16[1,48,1536]{2,1,0:T(8,128)(2,1)S(1)}, u32[]{:S(2)}, u32[]{:S(2)}) %collective-permute-start.51) | collective-permute-done | bytes 147488 | tf_op jit(solution)/shard_map/ppermute | solution.py:446
  196.4 0.7 slice_reduce_fusion
  197.8 0.7 slice_bitcast_fusion
  198.7 0.8 pad_maximum_fusion
  (143 shorter events, 15.0 us)
Async XLA Ops:
  0.6 72.6 %copy-start = (s32[2,256]{1,0:T(2,128)S(1)}, s32[2,256]{1,0:T(2,128)}, u32[]{:S(2)}) copy-start(s32[2,256]{1,0:T(2,128)} %param.19) | copy-start | bytes 6148
  0.6 58.6 %copy-start.23 = (s32[2]{0:T(128)S(1)}, s32[2]{0:T(128)}, u32[]{:S(2)}) copy-start(s32[2]{0:T(128)} %param.20) | copy-start | bytes 28
  1.8 13.5 %collective-permute-start.13 = (bf16[48,640]{1,0:T(8,128)(2,1)S(1)}, bf16[48,640]{1,0:T(8,128)(2,1)S(1)}, u32[]{:S(2)}, u32[]{:S(2)}) collective-permute-start(bf16[48,640]{1,0:T(8,128)(2,1)S(1)} %pad_maximum_fusion.3.refs_0_), channel_id=1, source_target_pairs={{0,4},{2,6},{4,0},{6,2},{8,12},{10,14},{12,8},{14,10},{16,20},{18,... | collective-permute-start | bytes 184328 | tf_op jit(solution)/shard_map/ppermute | solution.py:446
  4.9 12.6 %collective-permute-start.12 = (bf16[48,640]{1,0:T(8,128)(2,1)S(1)}, bf16[48,640]{1,0:T(8,128)(2,1)S(1)}, u32[]{:S(2)}, u32[]{:S(2)}) collective-permute-start(bf16[48,640]{1,0:T(8,128)(2,1)S(1)} %pad_maximum_fusion.3.refs_0_), channel_id=1, source_target_pairs={{0,2},{2,0},{4,6},{6,4},{8,10},{10,8},{12,14},{14,12},{16,18},{18,... | collective-permute-start | bytes 184328 | tf_op jit(solution)/shard_map/ppermute | solution.py:446
  8.0 10.8 %collective-permute-start.2 = (bf16[48,1280]{1,0:T(8,128)(2,1)S(1)}, bf16[48,1280]{1,0:T(8,128)(2,1)S(1)}, u32[]{:S(2)}, u32[]{:S(2)}) collective-permute-start(bf16[48,1280]{1,0:T(8,128)(2,1)S(1)} %fusion.3.refs_0_), channel_id=1, source_target_pairs={{0,24},{2,26},{4,28},{6,30},{8,16},{10,18},{12,20},{14,22},{16,8},... | collective-permute-start | bytes 368648 | tf_op jit(solution)/shard_map/ppermute | solution.py:446
  14.3 23.2 %collective-permute-start.20 = (bf16[48,1536]{1,0:T(8,128)(2,1)S(1)}, bf16[48,1536]{1,0:T(8,128)(2,1)S(1)}, u32[]{:S(2)}, u32[]{:S(2)}) collective-permute-start(bf16[48,1536]{1,0:T(8,128)(2,1)S(1)} %slice.80.refs_0_), channel_id=1, source_target_pairs={{0,24},{2,26},{4,28},{6,30},{8,16},{10,18},{12,20},{14,22},{16,8},... | collective-permute-start | bytes 442376 | tf_op jit(solution)/shard_map/ppermute | solution.py:446
  14.6 23.0 %collective-permute-start.19 = (bf16[48,1536]{1,0:T(8,128)(2,1)S(1)}, bf16[48,1536]{1,0:T(8,128)(2,1)S(1)}, u32[]{:S(2)}, u32[]{:S(2)}) collective-permute-start(bf16[48,1536]{1,0:T(8,128)(2,1)S(1)} %slice.80.refs_0_), channel_id=1, source_target_pairs={{0,16},{2,18},{4,20},{6,22},{8,24},{10,26},{12,28},{14,30},{16,0},... | collective-permute-start | bytes 442376 | tf_op jit(solution)/shard_map/ppermute | solution.py:446
  15.4 18.9 %collective-permute-start.1 = (bf16[48,1280]{1,0:T(8,128)(2,1)S(1)}, bf16[48,1280]{1,0:T(8,128)(2,1)S(1)}, u32[]{:S(2)}, u32[]{:S(2)}) collective-permute-start(bf16[48,1280]{1,0:T(8,128)(2,1)S(1)} %fusion.3.refs_0_), channel_id=1, source_target_pairs={{0,16},{2,18},{4,20},{6,22},{8,24},{10,26},{12,28},{14,30},{16,0},... | collective-permute-start | bytes 368648 | tf_op jit(solution)/shard_map/ppermute | solution.py:446
  17.5 20.0 %collective-permute-start = (bf16[48,1280]{1,0:T(8,128)(2,1)S(1)}, bf16[48,1280]{1,0:T(8,128)(2,1)S(1)}, u32[]{:S(2)}, u32[]{:S(2)}) collective-permute-start(bf16[48,1280]{1,0:T(8,128)(2,1)S(1)} %fusion.3.refs_0_), channel_id=1, source_target_pairs={{0,8},{2,10},{4,12},{6,14},{8,0},{10,2},{12,4},{14,6},{16,24},{18,... | collective-permute-start | bytes 368648 | tf_op jit(solution)/shard_map/ppermute | solution.py:446
  18.8 4.2 %collective-permute-start.14 = (bf16[48,640]{1,0:T(8,128)(2,1)S(1)}, bf16[48,640]{1,0:T(8,128)(2,1)S(1)}, u32[]{:S(2)}, u32[]{:S(2)}) collective-permute-start(bf16[48,640]{1,0:T(8,128)(2,1)S(1)} %collective-permute-done.13.refs_2_), channel_id=1, source_target_pairs={{0,2},{2,0},{4,6},{6,4},{8,10},{10,8},{12,14},{14,12},{16,18},{18,... | collective-permute-start | bytes 184328 | tf_op jit(solution)/shard_map/ppermute | solution.py:446
  23.0 15.7 %collective-permute-start.18 = (bf16[48,1536]{1,0:T(8,128)(2,1)S(1)}, bf16[48,1536]{1,0:T(8,128)(2,1)S(1)}, u32[]{:S(2)}, u32[]{:S(2)}) collective-permute-start(bf16[48,1536]{1,0:T(8,128)(2,1)S(1)} %slice.80.refs_0_), channel_id=1, source_target_pairs={{0,8},{2,10},{4,12},{6,14},{8,0},{10,2},{12,4},{14,6},{16,24},{18,... | collective-permute-start | bytes 442376 | tf_op jit(solution)/shard_map/ppermute | solution.py:446
  34.2 10.7 %collective-permute-start.17 = (bf16[4,48,640]{2,1,0:T(8,128)(2,1)S(1)}, bf16[4,48,640]{2,1,0:T(8,128)(2,1)S(1)}, u32[]{:S(2)}, u32[]{:S(2)}) collective-permute-start(bf16[4,48,640]{2,1,0:T(8,128)(2,1)S(1)} %shard_map.172.refs_5_), channel_id=1, source_target_pairs={{0,24},{2,26},{4,28},{6,30},{8,16},{10,18},{12,20},{14,22},{16,8},... | collective-permute-start | bytes 737288 | tf_op jit(solution)/shard_map/ppermute | solution.py:446
  37.5 7.4 %collective-permute-start.25 = (bf16[4,48,640]{2,1,0:T(8,128)(2,1)S(1)}, bf16[4,48,640]{2,1,0:T(8,128)(2,1)S(1)}, u32[]{:S(2)}, u32[]{:S(2)}) collective-permute-start(bf16[4,48,640]{2,1,0:T(8,128)(2,1)S(1)} %shard_map.172.refs_5_), channel_id=1, source_target_pairs={{0,1},{1,0},{2,3},{3,2},{4,5},{5,4},{6,7},{7,6},{8,9},{9,8},{10,11... | collective-permute-start | bytes 737288 | tf_op jit(solution)/shard_map/ppermute | solution.py:442
  37.5 18.9 %collective-permute-start.16 = (bf16[4,48,640]{2,1,0:T(8,128)(2,1)S(1)}, bf16[4,48,640]{2,1,0:T(8,128)(2,1)S(1)}, u32[]{:S(2)}, u32[]{:S(2)}) collective-permute-start(bf16[4,48,640]{2,1,0:T(8,128)(2,1)S(1)} %shard_map.172.refs_5_), channel_id=1, source_target_pairs={{0,16},{2,18},{4,20},{6,22},{8,24},{10,26},{12,28},{14,30},{16,0},... | collective-permute-start | bytes 737288 | tf_op jit(solution)/shard_map/ppermute | solution.py:446
  37.6 19.3 %collective-permute-start.15 = (bf16[4,48,640]{2,1,0:T(8,128)(2,1)S(1)}, bf16[4,48,640]{2,1,0:T(8,128)(2,1)S(1)}, u32[]{:S(2)}, u32[]{:S(2)}) collective-permute-start(bf16[4,48,640]{2,1,0:T(8,128)(2,1)S(1)} %shard_map.172.refs_5_), channel_id=1, source_target_pairs={{0,8},{2,10},{4,12},{6,14},{8,0},{10,2},{12,4},{14,6},{16,24},{18,... | collective-permute-start | bytes 737288 | tf_op jit(solution)/shard_map/ppermute | solution.py:446
  38.7 57.1 %copy-start.1 = (bf16[256,768]{1,0:T(8,128)(2,1)S(1)}, bf16[256,768]{1,0:T(8,128)(2,1)}, u32[]{:S(2)}) copy-start(bf16[256,768]{1,0:T(8,128)(2,1)} %refs_0_.1) | copy-start | bytes 1179652
  38.7 19.4 %collective-permute-start.4 = (bf16[4,48,1280]{2,1,0:T(8,128)(2,1)S(1)}, bf16[4,48,1280]{2,1,0:T(8,128)(2,1)S(1)}, u32[]{:S(2)}, u32[]{:S(2)}) collective-permute-start(bf16[4,48,1280]{2,1,0:T(8,128)(2,1)S(1)} %shard_map.170.refs_2_), channel_id=1, source_target_pairs={{0,4},{2,6},{4,0},{6,2},{8,12},{10,14},{12,8},{14,10},{16,20},{18,... | collective-permute-start | bytes 1474568 | tf_op jit(solution)/shard_map/ppermute | solution.py:446
  44.9 13.2 %copy-start.11 = (bf16[4,48,640]{2,1,0:T(8,128)(2,1)}, bf16[4,48,640]{2,1,0:T(8,128)(2,1)S(1)}, u32[]{:S(2)}) copy-start(bf16[4,48,640]{2,1,0:T(8,128)(2,1)S(1)} %collective-permute-done.17.refs_8_) | copy-start | bytes 737284
  44.9 12.5 %collective-permute-start.28 = (bf16[4,48,640]{2,1,0:T(8,128)(2,1)S(1)}, bf16[4,48,640]{2,1,0:T(8,128)(2,1)S(1)}, u32[]{:S(2)}, u32[]{:S(2)}) collective-permute-start(bf16[4,48,640]{2,1,0:T(8,128)(2,1)S(1)} %collective-permute-done.17.refs_8_), channel_id=1, source_target_pairs={{0,1},{1,0},{2,3},{3,2},{4,5},{5,4},{6,7},{7,6},{8,9},{9,8},{10,11... | collective-permute-start | bytes 737288 | tf_op jit(solution)/shard_map/ppermute | solution.py:442
  45.6 14.4 %collective-permute-start.3 = (bf16[4,48,1280]{2,1,0:T(8,128)(2,1)S(1)}, bf16[4,48,1280]{2,1,0:T(8,128)(2,1)S(1)}, u32[]{:S(2)}, u32[]{:S(2)}) collective-permute-start(bf16[4,48,1280]{2,1,0:T(8,128)(2,1)S(1)} %shard_map.170.refs_2_), channel_id=1, source_target_pairs={{0,2},{2,0},{4,6},{6,4},{8,10},{10,8},{12,14},{14,12},{16,18},{18,... | collective-permute-start | bytes 1474568 | tf_op jit(solution)/shard_map/ppermute | solution.py:446
  56.4 13.1 %collective-permute-start.22 = (bf16[4,48,1536]{2,1,0:T(8,128)(2,1)S(1)}, bf16[4,48,1536]{2,1,0:T(8,128)(2,1)}, u32[]{:S(2)}, u32[]{:S(2)}) collective-permute-start(bf16[4,48,1536]{2,1,0:T(8,128)(2,1)S(1)} %shard_map.173.refs_9_), channel_id=1, source_target_pairs={{0,4},{2,6},{4,0},{6,2},{8,12},{10,14},{12,8},{14,10},{16,20},{18,... | collective-permute-start | bytes 1769480 | tf_op jit(solution)/shard_map/ppermute | solution.py:446
  56.9 16.3 %collective-permute-start.21 = (bf16[4,48,1536]{2,1,0:T(8,128)(2,1)S(1)}, bf16[4,48,1536]{2,1,0:T(8,128)(2,1)}, u32[]{:S(2)}, u32[]{:S(2)}) collective-permute-start(bf16[4,48,1536]{2,1,0:T(8,128)(2,1)S(1)} %shard_map.173.refs_9_), channel_id=1, source_target_pairs={{0,2},{2,0},{4,6},{6,4},{8,10},{10,8},{12,14},{14,12},{16,18},{18,... | collective-permute-start | bytes 1769480 | tf_op jit(solution)/shard_map/ppermute | solution.py:446
  58.1 1.8 collective-permute-start.27
  58.1 19.5 %collective-permute-start.7 = (bf16[4,48,1280]{2,1,0:T(8,128)(2,1)S(1)}, bf16[4,48,1280]{2,1,0:T(8,128)(2,1)S(1)}, u32[]{:S(2)}, u32[]{:S(2)}) collective-permute-start(bf16[4,48,1280]{2,1,0:T(8,128)(2,1)S(1)} %shard_map.170.refs_2_), channel_id=1, source_target_pairs={{0,1},{1,0},{2,3},{3,2},{4,5},{5,4},{6,7},{7,6},{8,9},{9,8},{10,11... | collective-permute-start | bytes 1474568 | tf_op jit(solution)/shard_map/ppermute | solution.py:442
  59.9 15.5 %collective-permute-start.26 = (bf16[4,48,640]{2,1,0:T(8,128)(2,1)}, bf16[4,48,640]{2,1,0:T(8,128)(2,1)S(1)}, u32[]{:S(2)}, u32[]{:S(2)}) collective-permute-start(bf16[4,48,640]{2,1,0:T(8,128)(2,1)} %copy-done.17), channel_id=1, source_target_pairs={{0,1},{1,0},{2,3},{3,2},{4,5},{5,4},{6,7},{7,6},{8,9},{9,8},{10,11... | collective-permute-start | bytes 737288 | tf_op jit(solution)/shard_map/ppermute | solution.py:442
  60.1 18.1 %collective-permute-start.5 = (bf16[2,48,1280]{2,1,0:T(8,128)(2,1)S(1)}, bf16[2,48,1280]{2,1,0:T(8,128)(2,1)}, u32[]{:S(2)}, u32[]{:S(2)}) collective-permute-start(bf16[2,48,1280]{2,1,0:T(8,128)(2,1)S(1)} %slice.78), channel_id=1, source_target_pairs={{0,2},{2,0},{4,6},{6,4},{8,10},{10,8},{12,14},{14,12},{16,18},{18,... | collective-permute-start | bytes 737288 | tf_op jit(solution)/shard_map/ppermute | solution.py:446
  69.5 21.3 %collective-permute-start.9 = (bf16[4,48,1280]{2,1,0:T(8,128)(2,1)S(1)}, bf16[4,48,1280]{2,1,0:T(8,128)(2,1)S(1)}, u32[]{:S(2)}, u32[]{:S(2)}) collective-permute-start(bf16[4,48,1280]{2,1,0:T(8,128)(2,1)S(1)} %collective-permute-done.4.refs_4_), channel_id=1, source_target_pairs={{0,1},{1,0},{2,3},{3,2},{4,5},{5,4},{6,7},{7,6},{8,9},{9,8},{10,11... | collective-permute-start | bytes 1474568 | tf_op jit(solution)/shard_map/ppermute | solution.py:442
  73.2 18.9 %collective-permute-start.8 = (bf16[4,48,1280]{2,1,0:T(8,128)(2,1)S(1)}, bf16[4,48,1280]{2,1,0:T(8,128)(2,1)S(1)}, u32[]{:S(2)}, u32[]{:S(2)}) collective-permute-start(bf16[4,48,1280]{2,1,0:T(8,128)(2,1)S(1)} %collective-permute-done.3.refs_3_), channel_id=1, source_target_pairs={{0,1},{1,0},{2,3},{3,2},{4,5},{5,4},{6,7},{7,6},{8,9},{9,8},{10,11... | collective-permute-start | bytes 1474568 | tf_op jit(solution)/shard_map/ppermute | solution.py:442
  76.1 8.9 %collective-permute-start.6 = (bf16[2,48,1280]{2,1,0:T(8,128)(2,1)S(1)}, bf16[2,48,1280]{2,1,0:T(8,128)(2,1)}, u32[]{:S(2)}, u32[]{:S(2)}) collective-permute-start(bf16[2,48,1280]{2,1,0:T(8,128)(2,1)S(1)} %slice.79), channel_id=1, source_target_pairs={{0,4},{2,6},{4,0},{6,2},{8,12},{10,14},{12,8},{14,10},{16,20},{18,... | collective-permute-start | bytes 737288 | tf_op jit(solution)/shard_map/ppermute | solution.py:446
  77.6 9.1 %collective-permute-start.23 = (bf16[2,48,1536]{2,1,0:T(8,128)(2,1)S(1)}, bf16[2,48,1536]{2,1,0:T(8,128)(2,1)S(1)}, u32[]{:S(2)}, u32[]{:S(2)}) collective-permute-start(bf16[2,48,1536]{2,1,0:T(8,128)(2,1)S(1)} %slice.81), channel_id=1, source_target_pairs={{0,2},{2,0},{4,6},{6,4},{8,10},{10,8},{12,14},{14,12},{16,18},{18,... | collective-permute-start | bytes 884744 | tf_op jit(solution)/shard_map/ppermute | solution.py:446
  78.1 12.6 %collective-permute-start.24 = (bf16[2,48,1536]{2,1,0:T(8,128)(2,1)S(1)}, bf16[2,48,1536]{2,1,0:T(8,128)(2,1)S(1)}, u32[]{:S(2)}, u32[]{:S(2)}) collective-permute-start(bf16[2,48,1536]{2,1,0:T(8,128)(2,1)S(1)} %slice.82), channel_id=1, source_target_pairs={{0,4},{2,6},{4,0},{6,2},{8,12},{10,14},{12,8},{14,10},{16,20},{18,... | collective-permute-start | bytes 884744 | tf_op jit(solution)/shard_map/ppermute | solution.py:446
  85.0 18.8 %collective-permute-start.29 = (bf16[4,48,1536]{2,1,0:T(8,128)(2,1)S(1)}, bf16[4,48,1536]{2,1,0:T(8,128)(2,1)}, u32[]{:S(2)}, u32[]{:S(2)}) collective-permute-start(bf16[4,48,1536]{2,1,0:T(8,128)(2,1)S(1)} %shard_map.173.refs_9_), channel_id=1, source_target_pairs={{0,1},{1,0},{2,3},{3,2},{4,5},{5,4},{6,7},{7,6},{8,9},{9,8},{10,11... | collective-permute-start | bytes 1769480 | tf_op jit(solution)/shard_map/ppermute | solution.py:442
  86.7 17.1 %collective-permute-start.31 = (bf16[4,48,1536]{2,1,0:T(8,128)(2,1)}, bf16[4,48,1536]{2,1,0:T(8,128)(2,1)}, u32[]{:S(2)}, u32[]{:S(2)}) collective-permute-start(bf16[4,48,1536]{2,1,0:T(8,128)(2,1)} %collective-permute-done.22.refs_11_), channel_id=1, source_target_pairs={{0,1},{1,0},{2,3},{3,2},{4,5},{5,4},{6,7},{7,6},{8,9},{9,8},{10,11... | collective-permute-start | bytes 1769480 | tf_op jit(solution)/shard_map/ppermute | solution.py:442
  90.8 13.1 %collective-permute-start.30 = (bf16[4,48,1536]{2,1,0:T(8,128)(2,1)}, bf16[4,48,1536]{2,1,0:T(8,128)(2,1)}, u32[]{:S(2)}, u32[]{:S(2)}) collective-permute-start(bf16[4,48,1536]{2,1,0:T(8,128)(2,1)} %collective-permute-done.21.refs_10_), channel_id=1, source_target_pairs={{0,1},{1,0},{2,3},{3,2},{4,5},{5,4},{6,7},{7,6},{8,9},{9,8},{10,11... | collective-permute-start | bytes 1769480 | tf_op jit(solution)/shard_map/ppermute | solution.py:442
  91.6 2.0 %collective-permute-start.10 = (bf16[2,48,1280]{2,1,0:T(8,128)(2,1)}, bf16[2,48,1280]{2,1,0:T(8,128)(2,1)}, u32[]{:S(2)}, u32[]{:S(2)}) collective-permute-start(bf16[2,48,1280]{2,1,0:T(8,128)(2,1)} %collective-permute-done.5.refs_5_), channel_id=1, source_target_pairs={{0,1},{1,0},{2,3},{3,2},{4,5},{5,4},{6,7},{7,6},{8,9},{9,8},{10,11... | collective-permute-start | bytes 737288 | tf_op jit(solution)/shard_map/ppermute | solution.py:442
  92.9 1.9 collective-permute-start.11
  93.6 10.3 %collective-permute-start.32 = (bf16[2,48,1536]{2,1,0:T(8,128)(2,1)}, bf16[2,48,1536]{2,1,0:T(8,128)(2,1)S(1)}, u32[]{:S(2)}, u32[]{:S(2)}) collective-permute-start(bf16[2,48,1536]{2,1,0:T(8,128)(2,1)} %copy-done.7), channel_id=1, source_target_pairs={{0,1},{1,0},{2,3},{3,2},{4,5},{5,4},{6,7},{7,6},{8,9},{9,8},{10,11... | collective-permute-start | bytes 884744 | tf_op jit(solution)/shard_map/ppermute | solution.py:442
  94.7 9.2 %collective-permute-start.33 = (bf16[2,48,1536]{2,1,0:T(8,128)(2,1)}, bf16[2,48,1536]{2,1,0:T(8,128)(2,1)S(1)}, u32[]{:S(2)}, u32[]{:S(2)}) collective-permute-start(bf16[2,48,1536]{2,1,0:T(8,128)(2,1)} %copy-done.9), channel_id=1, source_target_pairs={{0,1},{1,0},{2,3},{3,2},{4,5},{5,4},{6,7},{7,6},{8,9},{9,8},{10,11... | collective-permute-start | bytes 884744 | tf_op jit(solution)/shard_map/ppermute | solution.py:442
  95.5 8.4 %copy-start.6 = (bf16[256,768]{1,0:T(8,128)(2,1)S(1)}, bf16[256,768]{1,0:T(8,128)(2,1)}, u32[]{:S(2)}) copy-start(bf16[256,768]{1,0:T(8,128)(2,1)} %refs_3_.1) | copy-start | bytes 1179652
  95.5 8.4 %copy-start.12 = (bf16[4,48,640]{2,1,0:T(8,128)(2,1)S(1)}, bf16[4,48,640]{2,1,0:T(8,128)(2,1)}, u32[]{:S(2)}) copy-start(bf16[4,48,640]{2,1,0:T(8,128)(2,1)} %copy-done.11) | copy-start | bytes 737284
  97.9 6.1 %copy-start.10 = (bf16[2,48,1536]{2,1,0:T(8,128)(2,1)S(1)}, bf16[2,48,1536]{2,1,0:T(8,128)(2,1)}, u32[]{:S(2)}) copy-start(bf16[2,48,1536]{2,1,0:T(8,128)(2,1)} %copy-done.9) | copy-start | bytes 884740
  97.9 6.1 %copy-start.14 = (bf16[4,48,640]{2,1,0:T(8,128)(2,1)S(1)}, bf16[4,48,640]{2,1,0:T(8,128)(2,1)}, u32[]{:S(2)}) copy-start(bf16[4,48,640]{2,1,0:T(8,128)(2,1)} %copy-done.13) | copy-start | bytes 737284
  97.9 6.1 %copy-start.16 = (bf16[4,48,640]{2,1,0:T(8,128)(2,1)S(1)}, bf16[4,48,640]{2,1,0:T(8,128)(2,1)}, u32[]{:S(2)}) copy-start(bf16[4,48,640]{2,1,0:T(8,128)(2,1)} %copy-done.15) | copy-start | bytes 737284
  97.9 6.1 %copy-start.18 = (bf16[4,48,640]{2,1,0:T(8,128)(2,1)S(1)}, bf16[4,48,640]{2,1,0:T(8,128)(2,1)}, u32[]{:S(2)}) copy-start(bf16[4,48,640]{2,1,0:T(8,128)(2,1)} %copy-done.17) | copy-start | bytes 737284
  97.9 6.1 %copy-start.20 = (bf16[4,48,640]{2,1,0:T(8,128)(2,1)S(1)}, bf16[4,48,640]{2,1,0:T(8,128)(2,1)}, u32[]{:S(2)}) copy-start(bf16[4,48,640]{2,1,0:T(8,128)(2,1)} %copy-done.19) | copy-start | bytes 737284
  97.9 6.1 %copy-start.22 = (bf16[4,48,640]{2,1,0:T(8,128)(2,1)S(1)}, bf16[4,48,640]{2,1,0:T(8,128)(2,1)}, u32[]{:S(2)}) copy-start(bf16[4,48,640]{2,1,0:T(8,128)(2,1)} %copy-done.21) | copy-start | bytes 737284
  111.8 8.2 %collective-permute-start.41 = (bf16[272,4480]{1,0:T(8,128)(2,1)S(1)}, bf16[272,4480]{1,0:T(8,128)(2,1)S(1)}, u32[]{:S(2)}, u32[]{:S(2)}) collective-permute-start(bf16[272,4480]{1,0:T(8,128)(2,1)S(1)} %get-tuple-element.82.mine), channel_id=1, source_target_pairs={{0,1},{1,0},{2,3},{3,2},{4,5},{5,4},{6,7},{7,6},{8,9},{9,8},{10,11... | collective-permute-start | bytes 7311368 | tf_op jit(solution)/shard_map/ppermute | solution.py:442
  119.8 4.9 %collective-permute-start.34 = (bf16[272,1920]{1,0:T(8,128)(2,1)S(1)}, bf16[272,1920]{1,0:T(8,128)(2,1)S(1)}, u32[]{:S(2)}, u32[]{:S(2)}) collective-permute-start(bf16[272,1920]{1,0:T(8,128)(2,1)S(1)} %get-tuple-element.66.mine), channel_id=1, source_target_pairs={{0,1},{1,0},{2,3},{3,2},{4,5},{5,4},{6,7},{7,6},{8,9},{9,8},{10,11... | collective-permute-start | bytes 3133448 | tf_op jit(solution)/shard_map/ppermute | solution.py:442
  122.6 16.3 %collective-permute-start.46 = (bf16[8,48,768]{2,1,0:T(8,128)(2,1)S(1)}, bf16[8,48,768]{2,1,0:T(8,128)(2,1)S(1)}, u32[]{:S(2)}, u32[]{:S(2)}) collective-permute-start(bf16[8,48,768]{2,1,0:T(8,128)(2,1)S(1)} %get-tuple-element.93), channel_id=1, source_target_pairs={{0,2},{2,0},{4,6},{6,4},{8,10},{10,8},{12,14},{14,12},{16,18},{18,... | collective-permute-start | bytes 1769480 | tf_op jit(solution)/shard_map/ppermute | solution.py:446
  123.2 16.2 %collective-permute-start.47 = (bf16[8,48,768]{2,1,0:T(8,128)(2,1)S(1)}, bf16[8,48,768]{2,1,0:T(8,128)(2,1)S(1)}, u32[]{:S(2)}, u32[]{:S(2)}) collective-permute-start(bf16[8,48,768]{2,1,0:T(8,128)(2,1)S(1)} %get-tuple-element.95), channel_id=1, source_target_pairs={{0,4},{2,6},{4,0},{6,2},{8,12},{10,14},{12,8},{14,10},{16,20},{18,... | collective-permute-start | bytes 1769480 | tf_op jit(solution)/shard_map/ppermute | solution.py:446
  126.1 23.3 %collective-permute-start.35 = (bf16[8,48,640]{2,1,0:T(8,128)(2,1)S(1)}, bf16[8,48,640]{2,1,0:T(8,128)(2,1)S(1)}, u32[]{:S(2)}, u32[]{:S(2)}) collective-permute-start(bf16[8,48,640]{2,1,0:T(8,128)(2,1)S(1)} %get-tuple-element.69), channel_id=1, source_target_pairs={{0,2},{2,0},{4,6},{6,4},{8,10},{10,8},{12,14},{14,12},{16,18},{18,... | collective-permute-start | bytes 1474568 | tf_op jit(solution)/shard_map/ppermute | solution.py:446
  127.7 22.2 %collective-permute-start.36 = (bf16[8,48,640]{2,1,0:T(8,128)(2,1)S(1)}, bf16[8,48,640]{2,1,0:T(8,128)(2,1)S(1)}, u32[]{:S(2)}, u32[]{:S(2)}) collective-permute-start(bf16[8,48,640]{2,1,0:T(8,128)(2,1)S(1)} %get-tuple-element.71), channel_id=1, source_target_pairs={{0,4},{2,6},{4,0},{6,2},{8,12},{10,14},{12,8},{14,10},{16,20},{18,... | collective-permute-start | bytes 1474568 | tf_op jit(solution)/shard_map/ppermute | solution.py:446
  128.2 41.0 %collective-permute-start.42 = (bf16[8,48,640]{2,1,0:T(8,128)(2,1)S(1)}, bf16[8,48,640]{2,1,0:T(8,128)(2,1)S(1)}, u32[]{:S(2)}, u32[]{:S(2)}) collective-permute-start(bf16[8,48,640]{2,1,0:T(8,128)(2,1)S(1)} %get-tuple-element.85), channel_id=1, source_target_pairs={{0,8},{2,10},{4,12},{6,14},{8,0},{10,2},{12,4},{14,6},{16,24},{18,... | collective-permute-start | bytes 1474568 | tf_op jit(solution)/shard_map/ppermute | solution.py:446
  139.6 29.8 %collective-permute-start.48 = (bf16[4,48,768]{2,1,0:T(8,128)(2,1)S(1)}, bf16[4,48,768]{2,1,0:T(8,128)(2,1)S(1)}, u32[]{:S(2)}, u32[]{:S(2)}) collective-permute-start(bf16[4,48,768]{2,1,0:T(8,128)(2,1)S(1)} %get-tuple-element.97), channel_id=1, source_target_pairs={{0,4},{2,6},{4,0},{6,2},{8,12},{10,14},{12,8},{14,10},{16,20},{18,... | collective-permute-start | bytes 884744 | tf_op jit(solution)/shard_map/ppermute | solution.py:446
  141.2 28.2 %collective-permute-start.49 = (bf16[4,48,768]{2,1,0:T(8,128)(2,1)S(1)}, bf16[4,48,768]{2,1,0:T(8,128)(2,1)S(1)}, u32[]{:S(2)}, u32[]{:S(2)}) collective-permute-start(bf16[4,48,768]{2,1,0:T(8,128)(2,1)S(1)} %get-tuple-element.99), channel_id=1, source_target_pairs={{0,2},{2,0},{4,6},{6,4},{8,10},{10,8},{12,14},{14,12},{16,18},{18,... | collective-permute-start | bytes 884744 | tf_op jit(solution)/shard_map/ppermute | solution.py:446
  150.1 10.5 %collective-permute-start.37 = (bf16[4,48,640]{2,1,0:T(8,128)(2,1)S(1)}, bf16[4,48,640]{2,1,0:T(8,128)(2,1)S(1)}, u32[]{:S(2)}, u32[]{:S(2)}) collective-permute-start(bf16[4,48,640]{2,1,0:T(8,128)(2,1)S(1)} %get-tuple-element.73), channel_id=1, source_target_pairs={{0,4},{2,6},{4,0},{6,2},{8,12},{10,14},{12,8},{14,10},{16,20},{18,... | collective-permute-start | bytes 737288 | tf_op jit(solution)/shard_map/ppermute | solution.py:446
  151.7 8.9 %collective-permute-start.38 = (bf16[4,48,640]{2,1,0:T(8,128)(2,1)S(1)}, bf16[4,48,640]{2,1,0:T(8,128)(2,1)S(1)}, u32[]{:S(2)}, u32[]{:S(2)}) collective-permute-start(bf16[4,48,640]{2,1,0:T(8,128)(2,1)S(1)} %get-tuple-element.75), channel_id=1, source_target_pairs={{0,2},{2,0},{4,6},{6,4},{8,10},{10,8},{12,14},{14,12},{16,18},{18,... | collective-permute-start | bytes 737288 | tf_op jit(solution)/shard_map/ppermute | solution.py:446
  160.7 19.2 %collective-permute-start.39 = (bf16[2,48,1280]{2,1,0:T(8,128)(2,1)S(1)}, bf16[2,48,1280]{2,1,0:T(8,128)(2,1)S(1)}, u32[]{:S(2)}, u32[]{:S(2)}) collective-permute-start(bf16[2,48,1280]{2,1,0:T(8,128)(2,1)S(1)} %get-tuple-element.77), channel_id=1, source_target_pairs={{0,8},{2,10},{4,12},{6,14},{8,0},{10,2},{12,4},{14,6},{16,24},{18,... | collective-permute-start | bytes 737288 | tf_op jit(solution)/shard_map/ppermute | solution.py:446
  169.4 14.5 %collective-permute-start.43 = (bf16[4,48,640]{2,1,0:T(8,128)(2,1)S(1)}, bf16[4,48,640]{2,1,0:T(8,128)(2,1)S(1)}, u32[]{:S(2)}, u32[]{:S(2)}) collective-permute-start(bf16[4,48,640]{2,1,0:T(8,128)(2,1)S(1)} %get-tuple-element.87), channel_id=1, source_target_pairs={{0,16},{2,18},{4,20},{6,22},{8,24},{10,26},{12,28},{14,30},{16,0},... | collective-permute-start | bytes 737288 | tf_op jit(solution)/shard_map/ppermute | solution.py:446
  169.6 19.2 %collective-permute-start.50 = (bf16[2,48,1536]{2,1,0:T(8,128)(2,1)S(1)}, bf16[2,48,1536]{2,1,0:T(8,128)(2,1)S(1)}, u32[]{:S(2)}, u32[]{:S(2)}) collective-permute-start(bf16[2,48,1536]{2,1,0:T(8,128)(2,1)S(1)} %get-tuple-element.101), channel_id=1, source_target_pairs={{0,8},{2,10},{4,12},{6,14},{8,0},{10,2},{12,4},{14,6},{16,24},{18,... | collective-permute-start | bytes 884744 | tf_op jit(solution)/shard_map/ppermute | solution.py:446
  180.0 9.0 %collective-permute-start.40 = (bf16[1,48,1280]{2,1,0:T(8,128)(2,1)S(1)}, bf16[1,48,1280]{2,1,0:T(8,128)(2,1)S(1)}, u32[]{:S(2)}, u32[]{:S(2)}) collective-permute-start(bf16[1,48,1280]{2,1,0:T(8,128)(2,1)S(1)} %get-tuple-element.79), channel_id=1, source_target_pairs={{0,16},{2,18},{4,20},{6,22},{8,24},{10,26},{12,28},{14,30},{16,0},... | collective-permute-start | bytes 368648 | tf_op jit(solution)/shard_map/ppermute | solution.py:446
  183.9 5.7 %collective-permute-start.44 = (bf16[2,48,640]{2,1,0:T(8,128)(2,1)S(1)}, bf16[2,48,640]{2,1,0:T(8,128)(2,1)S(1)}, u32[]{:S(2)}, u32[]{:S(2)}) collective-permute-start(bf16[2,48,640]{2,1,0:T(8,128)(2,1)S(1)} %get-tuple-element.89), channel_id=1, source_target_pairs={{0,2},{2,0},{4,6},{6,4},{8,10},{10,8},{12,14},{14,12},{16,18},{18,... | collective-permute-start | bytes 368648 | tf_op jit(solution)/shard_map/ppermute | solution.py:446
  188.8 7.5 %collective-permute-start.51 = (bf16[1,48,1536]{2,1,0:T(8,128)(2,1)S(1)}, bf16[1,48,1536]{2,1,0:T(8,128)(2,1)S(1)}, u32[]{:S(2)}, u32[]{:S(2)}) collective-permute-start(bf16[1,48,1536]{2,1,0:T(8,128)(2,1)S(1)} %get-tuple-element.103), channel_id=1, source_target_pairs={{0,16},{2,18},{4,20},{6,22},{8,24},{10,26},{12,28},{14,30},{16,0},... | collective-permute-start | bytes 442376 | tf_op jit(solution)/shard_map/ppermute | solution.py:446
  189.7 4.3 %collective-permute-start.45 = (bf16[1,48,640]{2,1,0:T(8,128)(2,1)S(1)}, bf16[1,48,640]{2,1,0:T(8,128)(2,1)S(1)}, u32[]{:S(2)}, u32[]{:S(2)}) collective-permute-start(bf16[1,48,640]{2,1,0:T(8,128)(2,1)S(1)} %get-tuple-element.91), channel_id=1, source_target_pairs={{0,4},{2,6},{4,0},{6,2},{8,12},{10,14},{12,8},{14,10},{16,20},{18,... | collective-permute-start | bytes 184328 | tf_op jit(solution)/shard_map/ppermute | solution.py:446
  (12 other events, 26.2 us)

commit v2 on v1

--- a/solution.py
+++ b/solution.py
@@ -115,7 +115,7 @@
     own = refs[2 : 2 + n_pieces]
     other = refs[2 + n_pieces : 2 + 2 * n_pieces]
     seg_row, seg_col, live_row, cos_ref, sin_ref = refs[2 + 2 * n_pieces : 7 + 2 * n_pieces]
-    w_ref, qkv_ref, att_ref, logt_ref, n1_ref, gain_ref, gcol = refs[7 + 2 * n_pieces :]
+    w_ref, qkv_ref, att_ref, far_ref, logt_ref, n1_ref, gain_ref, gcol = refs[7 + 2 * n_pieces :]
     me = me_ref[0]
     half, width = cfg["half"], 2 * cfg["half"]
     for which, pieces in enumerate((own, other)):
@@ -159,21 +159,24 @@
             prob = (weights * (1.0 / total)).astype(BF16)
             outs.append(mm(prob, values, NN))
             totals = jnp.where(lanes == 2 * pair + side, row_max + jnp.log(total), totals)
-        att_ref[:, at : at + LANES] = jnp.where(low, outs[0], outs[1]).astype(BF16)
+        attended = jnp.where(low, outs[0], outs[1]).astype(BF16)
+        att_ref[:, at : at + LANES] = attended
+        if at >= half:
+            far_ref[:, at - half : at - half + LANES] = attended
     logt_ref[...] = totals
 
 
 def ffn_kernel(cfg, n_pieces, *refs):
-    me_ref, x_ref, att_ref, cot_ref, live_ref = refs[:5]
+    me_ref, x_ref, att_ref, gm_ref, live_ref = refs[:5]
     own = refs[5 : 5 + n_pieces]
     other = refs[5 + n_pieces : 5 + 2 * n_pieces]
     rest = refs[5 + 2 * n_pieces :]
-    out_ref, gh_ref, wo_ref, swap_ref, keep_ref = rest[:5]
-    win_ref, wgate_ref, wdown_ref, gcol = rest[5:]
+    out_ref, hidden_ref, gain_ref, wo_ref, win_ref, wgate_ref, gi_ref, gg_ref = rest[:8]
+    swap_ref, keep_ref, wdown_ref, gcol = rest[8:]
     me = me_ref[0]
     half, units, main = cfg["half"], cfg["units"], cfg["main"]
     tail = units - main
-    model = x_ref.shape[1]
+    rows, model = x_ref.shape
     out_at = 2 * units
     for which, pieces in enumerate((own, other)):
         part = Pieces(me, pieces, cfg["rows"], cfg["layout"])
@@ -186,69 +189,60 @@
         part.copy(wdown_ref, 2 * main + which * tail, out_at + half + main, tail)
         if which == 0:
             part.copy(gcol, 0, out_at + half + main, LANES)
-    lanes8 = lane_index((8, LANES))
-    pick = (lanes8 == tail).astype(BF16)
-    gain_row = mm(pick, gcol[...], NT)[0:1]
-    att = att_ref[...]
-    hidden = x_ref[...].astype(F32) + mm(att, wo_ref[...], NT)
-    normed, inv_std = norm_parts(hidden)
-    n2 = (normed * gain_row).astype(BF16)
-    live = live_ref[...]
-    grad_mixed = live * cot_ref[...].astype(F32)
-    grad_mixed_bf = grad_mixed.astype(BF16)
-    rows = x_ref.shape[0]
-    swap_ref[0:rows, 0:model] = n2
-    swap_ref[0:rows, model : 2 * model] = grad_mixed_bf
-    base = 3 * model
+    gain_row = column_to_row(gcol[...], tail)
+    gain_ref[...] = jnp.broadcast_to(gain_row, gain_ref.shape)
+    hidden = x_ref[...].astype(F32) + mm(att_ref[...], wo_ref[...], NT)
+    hidden_ref[...] = hidden
+    n2 = (norm_parts(hidden)[0] * gain_row).astype(BF16)
+    swap_ref[:, 0:model] = n2
+    grad_mixed = gm_ref[...]
     step = 3 * LANES
     mixed = hidden
-    grad_normed = jnp.zeros((rows, model), F32)
     for at in range(0, 2 * units, step):
         unit_in = mm(n2, win_ref[:, at : at + step], NN)
         unit_gate = mm(n2, wgate_ref[:, at : at + step], NN)
-        grad_act = mm(grad_mixed_bf, wdown_ref[:, at : at + step], NN)
+        grad_act = mm(grad_mixed, wdown_ref[:, at : at + step], NN)
         cdf = 0.5 * (1.0 + lax.erf(unit_in * SQRT_HALF))
         gelu = unit_in * cdf
         slope = cdf + unit_in * INV_ROOT_TWO_PI * jnp.exp(-0.5 * unit_in * unit_in)
         activated = (gelu * unit_gate).astype(BF16)
         grad_in = (grad_act * unit_gate * slope).astype(BF16)
         grad_gate = (grad_act * gelu).astype(BF16)
+        gi_ref[:, at : at + step] = grad_in
+        gg_ref[:, at : at + step] = grad_gate
         mixed = mixed + mm(activated, wdown_ref[:, at : at + step], NT)
-        grad_normed = (
-            grad_normed
-            + mm(grad_in, win_ref[:, at : at + step], NT)
-            + mm(grad_gate, wgate_ref[:, at : at + step], NT)
-        )
         for sub in range(0, step, LANES):
             lo = at + sub
             a, gi, gg = (v[:, sub : sub + LANES] for v in (activated, grad_in, grad_gate))
             if lo < 2 * main:
                 which, col = divmod(lo, main)
-                ref, off = (keep_ref, 0) if which == 0 else (swap_ref, base)
-                ref[0:rows, off + col : off + col + LANES] = gi
-                ref[0:rows, off + main + col : off + main + col + LANES] = gg
-                col = off + 2 * units + half + col
-                ref[0:rows, col : col + LANES] = a
+                ref, off = (keep_ref, 0) if which == 0 else (swap_ref, model)
+                for value, start in ((gi, 0), (gg, main), (a, 2 * units)):
+                    ref[:, off + start + col : off + start + col + LANES] = value
             else:
                 low = lane_index((rows, LANES)) < tail
                 gi, gg, a = gi.astype(F32), gg.astype(F32), a.astype(F32)
-                mine = jnp.where(low, gi, pltpu.roll(gg, tail, 1)).astype(BF16)
-                theirs = jnp.where(low, pltpu.roll(gi, tail, 1), gg).astype(BF16)
-                at_tail = 2 * main
-                keep_ref[0:rows, at_tail : at_tail + LANES] = mine
-                swap_ref[0:rows, base + at_tail : base + at_tail + LANES] = theirs
-                at_tail = 2 * units + half + main
-                keep_ref[0:rows, at_tail : at_tail + LANES] = a.astype(BF16)
-                swap_ref[0:rows, base + at_tail : base + at_tail + LANES] = pltpu.roll(
-                    a, tail, 1
-                ).astype(BF16)
-    out_ref[...] = (live * mixed).astype(BF16)
-    grad_rows, gain_term = norm_back(grad_normed, normed, inv_std, gain_row)
-    grad_hidden = grad_mixed + grad_rows
+                mine = jnp.where(low, gi, pltpu.roll(gg, tail, 1))
+                theirs = jnp.where(low, pltpu.roll(gi, tail, 1), gg)
+                for start, here, there in (
+                    (2 * main, mine, theirs),
+                    (2 * units + main, a, pltpu.roll(a, tail, 1)),
+                ):
+                    keep_ref[:, start : start + LANES] = here.astype(BF16)
+                    start += model
+                    swap_ref[:, start : start + LANES] = there.astype(BF16)
+    out_ref[...] = (live_ref[...] * mixed).astype(BF16)
+
+
+def ffn_backward_kernel(hidden_ref, gm_ref, gain_ref, win_ref, wgate_ref, gi_ref, gg_ref, *outs):
+    gh_ref, swap_ref = outs
+    rows, _ = hidden_ref.shape
+    grad_normed = mm(gi_ref[...], win_ref[...], NT) + mm(gg_ref[...], wgate_ref[...], NT)
+    normed, inv_std = norm_parts(hidden_ref[...])
+    grad_rows, gain_term = norm_back(grad_normed, normed, inv_std, gain_ref[0:1])
+    grad_hidden = gm_ref[...].astype(F32) + grad_rows
     gh_ref[...] = grad_hidden
-    swap_ref[0:rows, 2 * model : base] = grad_hidden.astype(BF16)
-    keep_ref[0:rows, 2 * units : 2 * units + half] = att[:, 0:half]
-    swap_ref[0:rows, base + 2 * units : base + 2 * units + half] = att[:, half:]
+    swap_ref[0:rows, :] = grad_hidden.astype(BF16)
     put_gain(swap_ref, gain_term, rows)
 
 
@@ -259,7 +253,8 @@
     first = lax.broadcasted_iota(jnp.int32, (extra, model), 0)
     block = jnp.where(first == 0, high, jnp.where(first == 1, gain_term - high, 0.0))
     ref[rows:, 0:model] = block.astype(BF16)
-    ref[rows:, model:] = jnp.zeros((extra, ref.shape[1] - model), BF16)
+    if ref.shape[1] > model:
+        ref[rows:, model:] = jnp.zeros((extra, ref.shape[1] - model), BF16)
 
 
 def attn_backward_kernel(cfg, *refs):
@@ -314,20 +309,22 @@
     put_gain(swap_ref, gain_term, rows)
 
 
-def grads_kernel(cfg, sections, fast, me_ref, mine, keep, theirs, *refs):
-    grad_ref = refs[-1]
-    outs = refs[:-1]
-    tokens = keep.shape[0]
-    base = cfg["base"]
-    for left, at, size in sections:
-        l_mine = mine[0:tokens, left : left + cfg["model"]]
-        l_theirs = theirs[0:tokens, left : left + cfg["model"]]
-        grad_ref[:, at : at + size] = mm(l_mine, keep[:, at : at + size], TN) + mm(
-            l_theirs, theirs[0:tokens, base + at : base + at + size], TN
-        )
-    gain = jnp.zeros((1, cfg["model"]), F32)
-    for ref in (mine, theirs):
-        block = ref[tokens:, 0 : cfg["model"]].astype(F32)
+def grads_kernel(cfg, sections, n_in, fast, me_ref, *refs):
+    ins, outs, grad_ref = refs[:n_in], refs[n_in:-1], refs[-1]
+    model = cfg["model"]
+    tokens = cfg["tokens"]
+    for pairs, at, size in sections:
+        total = 0.0
+        for (left, left_at), (right, right_at) in pairs:
+            total = total + mm(
+                ins[left][0:tokens, left_at : left_at + model],
+                ins[right][0:tokens, right_at : right_at + size],
+                TN,
+            )
+        grad_ref[:, at : at + size] = total
+    gain = jnp.zeros((1, model), F32)
+    for which in cfg["gain_from"]:
+        block = ins[which][tokens:, 0:model].astype(F32)
         gain = gain + block[0:1] + block[1:2]
     columns = row_to_columns(gain)
     total = grad_ref.shape[1]
@@ -476,7 +473,7 @@
         axis=1,
     )
     total_qkv, total_ffn = pack_qkv.shape[1], pack_ffn.shape[1]
-    cut = total_ffn * 3 // 10 // LANES * LANES
+    cut = total_ffn * 9 // 25 // LANES * LANES
     if fast:
         own_qkv = plane(stack(across_z(pack_qkv)))
         other_qkv = both_cores(own_qkv)
@@ -509,17 +506,20 @@
     repeats = LANES // HD
     cosine = jnp.concatenate([cosine, cosine] * repeats, axis=1)
     sine = jnp.concatenate([-sine, sine] * repeats, axis=1)
+    grad_mixed = (live_col * cotangent.astype(F32)).astype(BF16)
+    their_mixed = swap_cores(grad_mixed)
     me_vec = me.astype(jnp.int32).reshape(1)
 
     cfg = dict(half=half, rows=rows, layout=layout_qkv, units=units, main=main, model=model)
     width = 2 * half
-    w_full, qkv, att, logt, n1, gain1 = call(
+    w_full, qkv, att, far, logt, n1, gain1 = call(
         functools.partial(attn_forward_kernel, cfg, len(own_qkv)),
         [me_vec, inputs, *own_qkv, *other_qkv, seg_row, seg_col, live_row, cosine, sine],
         [
             shape(model, 3 * width),
             shape(tokens, 3 * width),
             shape(tokens, width),
+            shape(tokens, half),
             shape(tokens, LANES, dtype=F32),
             shape(tokens, model),
             shape(8, model, dtype=F32),
@@ -528,47 +528,74 @@
         flops=2 * tokens * model * 3 * width,
         spare=6 << 20,
     )
+    their_far = swap_cores(far)
     ffn_cfg = dict(cfg, layout=layout_ffn)
-    side = 2 * units + half + main + LANES
-    output, grad_hidden, wo_full, swap1, keep1 = call(
+    side = 2 * units + main + LANES
+    output, hidden, gain2, wo_full, win_full, wgate_full, gi, gg, swap_b, keep1 = call(
         functools.partial(ffn_kernel, ffn_cfg, len(own_ffn)),
-        [me_vec, inputs, att, cotangent, live_col, *own_ffn, *other_ffn],
+        [me_vec, inputs, att, grad_mixed, live_col, *own_ffn, *other_ffn],
         [
             shape(tokens, model),
             shape(tokens, model, dtype=F32),
+            shape(8, model, dtype=F32),
             shape(model, width),
-            shape(tokens + 16, 3 * model + side),
+            shape(model, 2 * units),
+            shape(model, 2 * units),
+            shape(tokens, 2 * units),
+            shape(tokens, 2 * units),
+            shape(tokens, model + side),
             shape(tokens, side),
         ],
-        [pltpu.VMEM((model, 2 * units), BF16)] * 3 + [pltpu.VMEM((model, LANES), BF16)],
-        flops=2 * tokens * model * 12 * units,
+        [pltpu.VMEM((model, 2 * units), BF16), pltpu.VMEM((model, LANES), BF16)],
+        flops=2 * tokens * model * 8 * units,
         spare=6 << 20,
     )
-
-    def grads(sections, swap_mine, keep, cfg):
+    their_b = swap_cores(swap_b)
+    grad_hidden, swap_h = call(
+        ffn_backward_kernel,
+        [hidden, grad_mixed, gain2, win_full, wgate_full, gi, gg],
+        [shape(tokens, model, dtype=F32), shape(tokens + 16, model)],
+        [],
+        scalars=0,
+        flops=2 * tokens * model * 4 * units,
+        spare=6 << 20,
+    )
+    their_h = swap_cores(swap_h)
+
+    def grads(sections, operands, cfg):
         total = cfg["total"]
         outs = [shape(model, total, dtype=F32)]
         if fast:
             outs = [shape(8, rows, last - first) for _, (first, last) in cfg["emit"] for _ in "ks"]
-        theirs = swap_cores(swap_mine)
         return call(
-            functools.partial(grads_kernel, cfg, sections, fast),
-            [me_vec, swap_mine, keep, theirs],
+            functools.partial(grads_kernel, cfg, sections, len(operands), fast),
+            [me_vec, *operands],
             outs,
             [pltpu.VMEM((model, total), F32)],
             flops=4 * tokens * model * total,
             spare=6 << 20,
         )
 
+    total1 = 2 * units + half + main + LANES
     sections1 = [
-        (0, 0, 2 * units),
-        (2 * model, 2 * units, half),
-        (model, 2 * units + half, main + LANES),
+        ((((0, 0), (1, 0)), ((2, 0), (2, model))), 0, 2 * units),
+        ((((3, 0), (4, 0)), ((5, 0), (6, 0))), 2 * units, half),
+        (
+            (((7, 0), (1, 2 * units)), ((8, 0), (2, model + 2 * units))),
+            2 * units + half,
+            main + LANES,
+        ),
     ]
-    mid = cut + (side - cut) // 2 // LANES * LANES
-    emit1 = [(GRAD_C, (0, cut)), (GRAD_A, (cut, mid)), (GRAD_B, (mid, side))]
-    cfg1 = dict(ffn_cfg, base=3 * model, total=side, gain_lane=tail, emit=emit1)
-    pieces1 = grads(sections1, swap1, keep1, cfg1)
+    operands1 = [
+        swap_b, keep1, their_b, swap_h, att, their_h, their_far, grad_mixed, their_mixed,
+    ]
+    cut1 = total1 * 9 // 25 // LANES * LANES
+    mid = cut1 + (total1 - cut1) // 2 // LANES * LANES
+    emit1 = [(GRAD_C, (0, cut1)), (GRAD_A, (cut1, mid)), (GRAD_B, (mid, total1))]
+    cfg1 = dict(
+        ffn_cfg, tokens=tokens, total=total1, gain_lane=tail, emit=emit1, gain_from=(3, 5)
+    )
+    pieces1 = grads(sections1, operands1, cfg1)
     grad_inputs, swap2, keep2 = call(
         functools.partial(attn_backward_kernel, cfg),
         [
@@ -587,8 +614,10 @@
     )
     total2 = 3 * half + LANES
     emit2 = [(GRAD_A, (0, total2 // 2)), (GRAD_B, (total2 // 2, total2))]
-    cfg2 = dict(cfg, base=model, total=total2, gain_lane=0, emit=emit2)
-    pieces2 = grads([(0, 0, 3 * half)], swap2, keep2, cfg2)
+    cfg2 = dict(cfg, tokens=tokens, total=total2, gain_lane=0, emit=emit2, gain_from=(0, 2))
+    sections2 = [((((0, 0), (1, 0)), ((2, 0), (2, model))), 0, 3 * half)]
+    operands2 = [swap2, keep2, swap_cores(swap2)]
+    pieces2 = grads(sections2, operands2, cfg2)
 
     if fast:
         keep_c, send_c, keep_a, send_a, keep_b, send_b = pieces1
@@ -604,7 +633,7 @@
         share1 = call(
             final_ffn_kernel,
             [keep_c, came_c, keep, came],
-            [shape(rows, side, dtype=F32)],
+            [shape(rows, total1, dtype=F32)],
             [],
             scalars=0,
         )[0]

time: 200 us -> 194 us (0.970)
  waiting for transfers between devices: 85.8 us -> 80 us
  other arithmetic: 3.15 us -> 7.67 us
  local copies, waits for them, and re-layouts: 16.8 us -> 13.6 us
  starting transfers between devices: 64.7 us -> 62.7 us
    ppermute x36, waiting for transfers between devices: 85.2 us -> 76.9 us  [exchange(): return lax.ppermute(value, 'dp', pairs)]
    ppermute x36, starting transfers between devices: 62.4 us -> 58.6 us  [exchange(): return lax.ppermute(value, 'dp', pairs)]
    unnamed x48 -> x30, local copies, waits for them, and re-layouts: 5.82 us -> 3 us
    ppermute x16 -> x19, waiting for transfers between devices: 0.6 us -> 3.12 us  [swap_cores(): return lax.ppermute(value, 'tensor', [(0, 1), (1, 0)])]
    ppermute x16 -> x19, starting transfers between devices: 2.35 us -> 4.09 us  [swap_cores(): return lax.ppermute(value, 'tensor', [(0, 1), (1, 0)])]
    pallas_call x19 -> x20, Pallas kernels: 27.2 us -> 27.6 us  [call(): pl.pallas_call(kernel, out_shape=outs, in_specs=[SMEM] * scalars + [VMEM]...]
  transfers between devices with their start and end apart: 52 -> 55, of which waited for: 20 -> 20; matrix products, arithmetic and copies ran while one was open for 5% -> 7% of each run, Pallas kernels for 10% -> 11%
where the time goes in v2:
time: 194 us; the launch traced here: 193 us
  waiting for transfers between devices  80 us (41%)
  starting transfers between devices  62.7 us (32%)
  Pallas kernels  27.6 us (14%)
  local copies, waits for them, and re-layouts  13.6 us (7%)
  other arithmetic  7.67 us (4%)
    ppermute x36, waiting for transfers between devices, exchange(): return lax.ppermute(value, 'dp', pairs)  76.9 us
    ppermute x36, starting transfers between devices, exchange(): return lax.ppermute(value, 'dp', pairs)  58.6 us
    pallas_call x20, Pallas kernels, call(): pl.pallas_call(kernel, out_shape=outs, in_specs=[SMEM] * scalars + [VMEM]...  27.6 us
    ppermute x19, starting transfers between devices, swap_cores(): return lax.ppermute(value, 'tensor', [(0, 1), (1, 0)])  4.09 us
  transfers between devices with their start and end apart: 55, of which 20 were waited for; matrix products, arithmetic and copies ran while one was open for 7% of the time, Pallas kernels for 11%

profile of v2, /device:TPU:0, one launch (start us, length us, event | category | flops | bytes accessed | tf_op | source)
XLA Modules:
  0.0 193.4 jit_solution(14389070167002268488)
XLA Ops:
  0.7 1.2 fusion.6
  1.9 3.1 %collective-permute-start.13 = (bf16[48,768]{1,0:T(8,128)(2,1)S(1)}, bf16[48,768]{1,0:T(8,128)(2,1)S(1)}, u32[]{:S(2)}, u32[]{:S(2)}) collective-permute-start(bf16[48,768]{1,0:T(8,128)(2,1)S(1)} %pad_maximum_fusion.3.refs_0_), channel_id=1, source_target_pairs={{0,4},{2,6},{4,0},{6,2},{8,12},{10,14},{12,8},{14,10},{16,20},{18,... | collective-permute-start | bytes 221192 | tf_op jit(solution)/shard_map/ppermute | solution.py:443
  4.9 0.8 slice_bitcast_fusion.4
  5.8 0.8 copy.41
  6.5 1.6 collective-permute-start
  8.2 2.6 %collective-permute-start.1 = (bf16[48,1280]{1,0:T(8,128)(2,1)S(1)}, bf16[48,1280]{1,0:T(8,128)(2,1)S(1)}, u32[]{:S(2)}, u32[]{:S(2)}) collective-permute-start(bf16[48,1280]{1,0:T(8,128)(2,1)S(1)} %fusion.3.refs_0_), channel_id=1, source_target_pairs={{0,16},{2,18},{4,20},{6,22},{8,24},{10,26},{12,28},{14,30},{16,0},... | collective-permute-start | bytes 368648 | tf_op jit(solution)/shard_map/ppermute | solution.py:443
  11.0 1.5 collective-permute-start.12
  13.0 0.9 fusion.5
  13.9 1.5 collective-permute-done.12.refs_1_
  15.3 1.5 collective-permute-done.14.refs_3_
  16.9 0.7 collective-permute-start.15
  17.9 1.4 collective-permute-start.18
  19.3 0.9 collective-permute-done.1.refs_2_
  20.8 2.9 %collective-permute-start.19 = (bf16[48,1408]{1,0:T(8,128)(2,1)S(1)}, bf16[48,1408]{1,0:T(8,128)(2,1)S(1)}, u32[]{:S(2)}, u32[]{:S(2)}) collective-permute-start(bf16[48,1408]{1,0:T(8,128)(2,1)S(1)} %slice.80.refs_0_), channel_id=1, source_target_pairs={{0,16},{2,18},{4,20},{6,22},{8,24},{10,26},{12,28},{14,30},{16,0},... | collective-permute-start | bytes 405512 | tf_op jit(solution)/shard_map/ppermute | solution.py:443
  23.7 1.4 collective-permute-start.20
  25.1 9.2 %collective-permute-done.18.refs_1_ = bf16[48,1408]{1,0:T(8,128)(2,1)S(1)} collective-permute-done((bf16[48,1408]{1,0:T(8,128)(2,1)S(1)}, bf16[48,1408]{1,0:T(8,128)(2,1)S(1)}, u32[]{:S(2)}, u32[]{:S(2)}) %collective-permute-start.18) | collective-permute-done | bytes 135200 | tf_op jit(solution)/shard_map/ppermute | solution.py:443
  34.9 1.9 collective-permute-start.17
  36.8 1.5 collective-permute-start.3
  38.4 15.9 %collective-permute-done.16.refs_7_ = bf16[4,48,768]{2,1,0:T(8,128)(2,1)} collective-permute-done((bf16[4,48,768]{2,1,0:T(8,128)(2,1)S(1)}, bf16[4,48,768]{2,1,0:T(8,128)(2,1)}, u32[]{:S(2)}, u32[]{:S(2)}) %collective-permute-start.16) | collective-permute-done | bytes 294944 | tf_op jit(solution)/shard_map/ppermute | solution.py:443
  54.3 2.6 %collective-permute-start.22 = (bf16[4,48,1408]{2,1,0:T(8,128)(2,1)S(1)}, bf16[4,48,1408]{2,1,0:T(8,128)(2,1)S(1)}, u32[]{:S(2)}, u32[]{:S(2)}) collective-permute-start(bf16[4,48,1408]{2,1,0:T(8,128)(2,1)S(1)} %shard_map.173.refs_9_), channel_id=1, source_target_pairs={{0,4},{2,6},{4,0},{6,2},{8,12},{10,14},{12,8},{14,10},{16,20},{18,... | collective-permute-start | bytes 1622024 | tf_op jit(solution)/shard_map/ppermute | solution.py:443
  56.9 0.7 copy-done.5
  57.6 0.7 copy-done.7
  58.3 1.5 collective-permute-start.21
  61.0 6.6 %collective-permute-done.22.refs_11_ = bf16[4,48,1408]{2,1,0:T(8,128)(2,1)S(1)} collective-permute-done((bf16[4,48,1408]{2,1,0:T(8,128)(2,1)S(1)}, bf16[4,48,1408]{2,1,0:T(8,128)(2,1)S(1)}, u32[]{:S(2)}, u32[]{:S(2)}) %collective-permute-start.22) | collective-permute-done | bytes 540704 | tf_op jit(solution)/shard_map/ppermute | solution.py:443
  67.6 1.9 collective-permute-start.5
  69.5 1.7 slice.79
  71.2 0.7 slice.81
  71.9 1.5 collective-permute-done.21.refs_10_
  73.5 0.8 copy-done.2
  74.3 0.7 copy-done.9
  75.0 1.5 collective-permute-start.23
  76.6 1.3 fusion.4
  79.1 0.7 slice.82
  80.1 2.0 %collective-permute-start.24 = (bf16[2,48,1408]{2,1,0:T(8,128)(2,1)}, bf16[2,48,1408]{2,1,0:T(8,128)(2,1)}, u32[]{:S(2)}, u32[]{:S(2)}) collective-permute-start(bf16[2,48,1408]{2,1,0:T(8,128)(2,1)} %slice.82), channel_id=1, source_target_pairs={{0,4},{2,6},{4,0},{6,2},{8,12},{10,14},{12,8},{14,10},{16,20},{18,... | collective-permute-start | bytes 811016 | tf_op jit(solution)/shard_map/ppermute | solution.py:443
  82.7 1.3 fusion.2.refs_4_
  84.7 4.6 %collective-permute-done.24.refs_13_ = bf16[2,48,1408]{2,1,0:T(8,128)(2,1)} collective-permute-done((bf16[2,48,1408]{2,1,0:T(8,128)(2,1)}, bf16[2,48,1408]{2,1,0:T(8,128)(2,1)}, u32[]{:S(2)}, u32[]{:S(2)}) %collective-permute-start.24) | collective-permute-done | bytes 270368 | tf_op jit(solution)/shard_map/ppermute | solution.py:443
  90.5 1.6 pad_maximum_fusion.1
  92.8 1.1 multiply_convert_fusion.refs_3_.gm_ref.refs_7_
  94.0 6.3 %shard_map.171 = (bf16[768,2304]{1,0:T(8,128)(2,1)S(1)}, bf16[256,2304]{1,0:T(8,128)(2,1)S(1)}, bf16[256,768]{1,0:T(8,128)(2,1)S(1)}, bf16[256,384]{1,0:T(8,128)...) custom-call(s32[1]{0:T(128)} %bitcast.refs_0_.me_ref, ...), custom_call_target="tpu_custom_call" | custom-call | flops 905969664 | bytes 10447876 | tf_op jit(solution)/shard_map/pallas_call | solution.py:391
  100.4 6.5 %shard_map.174 = (bf16[256,768]{1,0:T(8,128)(2,1)}, f32[256,768]{1,0:T(8,128)S(1)}, f32[8,768]{1,0:T(8,128)S(1)}, bf16[768,768]{1,0:T(8,128)(2,1)S(1)}, bf16[768...) custom-call(s32[1]{0:T(128)} %bitcast.refs_0_.me_ref, ...), custom_call_target="tpu_custom_call" | custom-call | flops 1811939328 | bytes 17196036 | tf_op jit(solution)/shard_map/pallas_call | solution.py:391
  107.3 1.4 shard_map.175
  108.7 7.6 %shard_map.176 = (f32[256,768]{1,0:T(8,128)}, bf16[272,1920]{1,0:T(8,128)(2,1)S(1)}, bf16[256,1152]{1,0:T(8,128)(2,1)S(1)}) custom-call(bf16[256,768]{1,0:T(8,128)(2,1)S(1)} %copy-done.1, f32[256,768]{1,0:T(8,128)S(1)} %get-tuple-element.72.refs_1_, bf16[768,768]{1,0:T(8,128)(2,1)S(1)} %get-tuple-element.73.refs_2_, ...), custom_call_target="tpu_custom_call" | custom-call | flops 1509949440 | bytes 10705920 | tf_op jit(solution)/shard_map/pallas_call | solution.py:391
  117.4 2.8 %collective-permute-done.44.refs_8_ = bf16[256,768]{1,0:T(8,128)(2,1)S(1)} collective-permute-done((bf16[256,768]{1,0:T(8,128)(2,1)S(1)}, bf16[256,768]{1,0:T(8,128)(2,1)S(1)}, u32[]{:S(2)}, u32[]{:S(2)}) %collective-permute-start.44) | collective-permute-done | bytes 393248 | tf_op jit(solution)/shard_map/ppermute | solution.py:439
  120.5 2.6 %shard_map.182 = (bf16[8,48,768]{2,1,0:T(8,128)(2,1)S(1)}, bf16[8,48,768]{2,1,0:T(8,128)(2,1)S(1)}, bf16[8,48,640]{2,1,0:T(8,128)(2,1)S(1)}, bf16[8,48,640]{2,1,...) custom-call(s32[1]{0:T(128)} %bitcast.refs_0_.me_ref, ...), custom_call_target="tpu_custom_call" | custom-call | flops 1711276032 | bytes 9093124 | tf_op jit(solution)/shard_map/pallas_call | solution.py:391
  123.0 1.8 collective-permute-start.50
  124.9 1.4 shard_map.177
  127.1 1.5 collective-permute-start.49
  128.7 4.9 %collective-permute-start.45 = (bf16[8,48,768]{2,1,0:T(8,128)(2,1)S(1)}, bf16[8,48,768]{2,1,0:T(8,128)(2,1)S(1)}, u32[]{:S(2)}, u32[]{:S(2)}) collective-permute-start(bf16[8,48,768]{2,1,0:T(8,128)(2,1)S(1)} %get-tuple-element.101), channel_id=1, source_target_pairs={{0,8},{2,10},{4,12},{6,14},{8,0},{10,2},{12,4},{14,6},{16,24},{18,... | collective-permute-start | bytes 1769480 | tf_op jit(solution)/shard_map/ppermute | solution.py:443
  133.5 6.9 %collective-permute-done.35.refs_1_ = bf16[8,48,640]{2,1,0:T(8,128)(2,1)S(1)} collective-permute-done((bf16[8,48,640]{2,1,0:T(8,128)(2,1)S(1)}, bf16[8,48,640]{2,1,0:T(8,128)(2,1)S(1)}, u32[]{:S(2)}, u32[]{:S(2)}) %collective-permute-start.35) | collective-permute-done | bytes 491552 | tf_op jit(solution)/shard_map/ppermute | solution.py:443
  140.5 8.6 %collective-permute-done.36.refs_3_ = bf16[8,48,640]{2,1,0:T(8,128)(2,1)S(1)} collective-permute-done((bf16[8,48,640]{2,1,0:T(8,128)(2,1)S(1)}, bf16[8,48,640]{2,1,0:T(8,128)(2,1)S(1)}, u32[]{:S(2)}, u32[]{:S(2)}) %collective-permute-start.36) | collective-permute-done | bytes 491552 | tf_op jit(solution)/shard_map/ppermute | solution.py:443
  149.2 1.8 collective-permute-start.37
  151.8 1.6 collective-permute-start.52
  153.8 4.9 %collective-permute-start.46 = (bf16[4,48,768]{2,1,0:T(8,128)(2,1)S(1)}, bf16[4,48,768]{2,1,0:T(8,128)(2,1)S(1)}, u32[]{:S(2)}, u32[]{:S(2)}) collective-permute-start(bf16[4,48,768]{2,1,0:T(8,128)(2,1)S(1)} %get-tuple-element.103), channel_id=1, source_target_pairs={{0,16},{2,18},{4,20},{6,22},{8,24},{10,26},{12,28},{14,30},{16,0},... | collective-permute-start | bytes 884744 | tf_op jit(solution)/shard_map/ppermute | solution.py:443
  158.7 1.2 collective-permute-done.38.refs_3_
  160.0 3.8 %collective-permute-start.39 = (bf16[2,48,1280]{2,1,0:T(8,128)(2,1)S(1)}, bf16[2,48,1280]{2,1,0:T(8,128)(2,1)S(1)}, u32[]{:S(2)}, u32[]{:S(2)}) collective-permute-start(bf16[2,48,1280]{2,1,0:T(8,128)(2,1)S(1)} %get-tuple-element.91), channel_id=1, source_target_pairs={{0,8},{2,10},{4,12},{6,14},{8,0},{10,2},{12,4},{14,6},{16,24},{18,... | collective-permute-start | bytes 737288 | tf_op jit(solution)/shard_map/ppermute | solution.py:443
  164.3 3.8 %collective-permute-start.53 = (bf16[2,48,1408]{2,1,0:T(8,128)(2,1)S(1)}, bf16[2,48,1408]{2,1,0:T(8,128)(2,1)S(1)}, u32[]{:S(2)}, u32[]{:S(2)}) collective-permute-start(bf16[2,48,1408]{2,1,0:T(8,128)(2,1)S(1)} %get-tuple-element.117), channel_id=1, source_target_pairs={{0,8},{2,10},{4,12},{6,14},{8,0},{10,2},{12,4},{14,6},{16,24},{18,... | collective-permute-start | bytes 811016 | tf_op jit(solution)/shard_map/ppermute | solution.py:443
  168.2 2.3 %collective-permute-done.46.refs_1_ = bf16[4,48,768]{2,1,0:T(8,128)(2,1)S(1)} collective-permute-done((bf16[4,48,768]{2,1,0:T(8,128)(2,1)S(1)}, bf16[4,48,768]{2,1,0:T(8,128)(2,1)S(1)}, u32[]{:S(2)}, u32[]{:S(2)}) %collective-permute-start.46) | collective-permute-done | bytes 294944 | tf_op jit(solution)/shard_map/ppermute | solution.py:443
  171.0 3.3 %collective-permute-done.39.refs_1_ = bf16[2,48,1280]{2,1,0:T(8,128)(2,1)S(1)} collective-permute-done((bf16[2,48,1280]{2,1,0:T(8,128)(2,1)S(1)}, bf16[2,48,1280]{2,1,0:T(8,128)(2,1)S(1)}, u32[]{:S(2)}, u32[]{:S(2)}) %collective-permute-start.39) | collective-permute-done | bytes 245792 | tf_op jit(solution)/shard_map/ppermute | solution.py:443
  174.9 3.4 %collective-permute-done.53.refs_1_ = bf16[2,48,1408]{2,1,0:T(8,128)(2,1)S(1)} collective-permute-done((bf16[2,48,1408]{2,1,0:T(8,128)(2,1)S(1)}, bf16[2,48,1408]{2,1,0:T(8,128)(2,1)S(1)}, u32[]{:S(2)}, u32[]{:S(2)}) %collective-permute-start.53) | collective-permute-done | bytes 270368 | tf_op jit(solution)/shard_map/ppermute | solution.py:443
  178.4 1.0 collective-permute-start.54
  179.4 5.8 %collective-permute-done.40.came = bf16[1,48,1280]{2,1,0:T(8,128)(2,1)S(1)} collective-permute-done((bf16[1,48,1280]{2,1,0:T(8,128)(2,1)S(1)}, bf16[1,48,1280]{2,1,0:T(8,128)(2,1)S(1)}, u32[]{:S(2)}, u32[]{:S(2)}) %collective-permute-start.40) | collective-permute-done | bytes 122912 | tf_op jit(solution)/shard_map/ppermute | solution.py:443
  185.1 0.7 shard_map.181
  187.1 3.2 %collective-permute-done.48.came_c = bf16[1,48,768]{2,1,0:T(8,128)(2,1)S(1)} collective-permute-done((bf16[1,48,768]{2,1,0:T(8,128)(2,1)S(1)}, bf16[1,48,768]{2,1,0:T(8,128)(2,1)S(1)}, u32[]{:S(2)}, u32[]{:S(2)}) %collective-permute-start.48) | collective-permute-done | bytes 73760 | tf_op jit(solution)/shard_map/ppermute | solution.py:443
  192.6 0.8 pad_maximum_fusion
  (134 shorter events, 16.7 us)
Async XLA Ops:
  0.6 59.5 %copy-start = (s32[2,256]{1,0:T(2,128)S(1)}, s32[2,256]{1,0:T(2,128)}, u32[]{:S(2)}) copy-start(s32[2,256]{1,0:T(2,128)} %param.19) | copy-start | bytes 6148
  0.6 17.0 %copy-start.13 = (bf16[48]{0:T(256)(128)(2,1)S(1)}, bf16[48]{0:T(256)(128)(2,1)}, u32[]{:S(2)}) copy-start(bf16[48]{0:T(256)(128)(2,1)} %param.15) | copy-start | bytes 292
  0.7 17.1 %copy-start.12 = (bf16[384,48]{0,1:T(8,128)(2,1)S(1)}, bf16[384,48]{0,1:T(8,128)(2,1)}, u32[]{:S(2)}) copy-start(bf16[384,48]{0,1:T(8,128)(2,1)} %param.14) | copy-start | bytes 110596
  0.7 17.1 %copy-start.11 = (bf16[576,48]{0,1:T(8,128)(2,1)S(1)}, bf16[576,48]{0,1:T(8,128)(2,1)}, u32[]{:S(2)}) copy-start(bf16[576,48]{0,1:T(8,128)(2,1)} %param.17) | copy-start | bytes 165892
  1.9 10.6 %collective-permute-start.13 = (bf16[48,768]{1,0:T(8,128)(2,1)S(1)}, bf16[48,768]{1,0:T(8,128)(2,1)S(1)}, u32[]{:S(2)}, u32[]{:S(2)}) collective-permute-start(bf16[48,768]{1,0:T(8,128)(2,1)S(1)} %pad_maximum_fusion.3.refs_0_), channel_id=1, source_target_pairs={{0,4},{2,6},{4,0},{6,2},{8,12},{10,14},{12,8},{14,10},{16,20},{18,... | collective-permute-start | bytes 221192 | tf_op jit(solution)/shard_map/ppermute | solution.py:443
  6.5 12.8 %collective-permute-start = (bf16[48,1280]{1,0:T(8,128)(2,1)S(1)}, bf16[48,1280]{1,0:T(8,128)(2,1)S(1)}, u32[]{:S(2)}, u32[]{:S(2)}) collective-permute-start(bf16[48,1280]{1,0:T(8,128)(2,1)S(1)} %fusion.3.refs_0_), channel_id=1, source_target_pairs={{0,8},{2,10},{4,12},{6,14},{8,0},{10,2},{12,4},{14,6},{16,24},{18,... | collective-permute-start | bytes 368648 | tf_op jit(solution)/shard_map/ppermute | solution.py:443
  8.2 12.0 %collective-permute-start.1 = (bf16[48,1280]{1,0:T(8,128)(2,1)S(1)}, bf16[48,1280]{1,0:T(8,128)(2,1)S(1)}, u32[]{:S(2)}, u32[]{:S(2)}) collective-permute-start(bf16[48,1280]{1,0:T(8,128)(2,1)S(1)} %fusion.3.refs_0_), channel_id=1, source_target_pairs={{0,16},{2,18},{4,20},{6,22},{8,24},{10,26},{12,28},{14,30},{16,0},... | collective-permute-start | bytes 368648 | tf_op jit(solution)/shard_map/ppermute | solution.py:443
  10.8 9.4 %collective-permute-start.2 = (bf16[48,1280]{1,0:T(8,128)(2,1)S(1)}, bf16[48,1280]{1,0:T(8,128)(2,1)S(1)}, u32[]{:S(2)}, u32[]{:S(2)}) collective-permute-start(bf16[48,1280]{1,0:T(8,128)(2,1)S(1)} %fusion.3.refs_0_), channel_id=1, source_target_pairs={{0,24},{2,26},{4,28},{6,30},{8,16},{10,18},{12,20},{14,22},{16,8},... | collective-permute-start | bytes 368648 | tf_op jit(solution)/shard_map/ppermute | solution.py:443
  11.0 4.4 %collective-permute-start.12 = (bf16[48,768]{1,0:T(8,128)(2,1)S(1)}, bf16[48,768]{1,0:T(8,128)(2,1)S(1)}, u32[]{:S(2)}, u32[]{:S(2)}) collective-permute-start(bf16[48,768]{1,0:T(8,128)(2,1)S(1)} %pad_maximum_fusion.3.refs_0_), channel_id=1, source_target_pairs={{0,2},{2,0},{4,6},{6,4},{8,10},{10,8},{12,14},{14,12},{16,18},{18,... | collective-permute-start | bytes 221192 | tf_op jit(solution)/shard_map/ppermute | solution.py:443
  12.5 4.4 %collective-permute-start.14 = (bf16[48,768]{1,0:T(8,128)(2,1)S(1)}, bf16[48,768]{1,0:T(8,128)(2,1)S(1)}, u32[]{:S(2)}, u32[]{:S(2)}) collective-permute-start(bf16[48,768]{1,0:T(8,128)(2,1)S(1)} %collective-permute-done.13.refs_2_), channel_id=1, source_target_pairs={{0,2},{2,0},{4,6},{6,4},{8,10},{10,8},{12,14},{14,12},{16,18},{18,... | collective-permute-start | bytes 221192 | tf_op jit(solution)/shard_map/ppermute | solution.py:443
  16.9 19.9 %collective-permute-start.15 = (bf16[4,48,768]{2,1,0:T(8,128)(2,1)S(1)}, bf16[4,48,768]{2,1,0:T(8,128)(2,1)}, u32[]{:S(2)}, u32[]{:S(2)}) collective-permute-start(bf16[4,48,768]{2,1,0:T(8,128)(2,1)S(1)} %shard_map.172.refs_5_), channel_id=1, source_target_pairs={{0,8},{2,10},{4,12},{6,14},{8,0},{10,2},{12,4},{14,6},{16,24},{18,... | collective-permute-start | bytes 884744 | tf_op jit(solution)/shard_map/ppermute | solution.py:443
  17.9 16.4 %collective-permute-start.18 = (bf16[48,1408]{1,0:T(8,128)(2,1)S(1)}, bf16[48,1408]{1,0:T(8,128)(2,1)S(1)}, u32[]{:S(2)}, u32[]{:S(2)}) collective-permute-start(bf16[48,1408]{1,0:T(8,128)(2,1)S(1)} %slice.80.refs_0_), channel_id=1, source_target_pairs={{0,8},{2,10},{4,12},{6,14},{8,0},{10,2},{12,4},{14,6},{16,24},{18,... | collective-permute-start | bytes 405512 | tf_op jit(solution)/shard_map/ppermute | solution.py:443
  20.2 57.6 %copy-start.14 = (s32[2]{0:T(128)S(1)}, s32[2]{0:T(128)}, u32[]{:S(2)}) copy-start(s32[2]{0:T(128)} %param.20) | copy-start | bytes 28
  20.3 39.6 %collective-permute-start.4 = (bf16[4,48,1280]{2,1,0:T(8,128)(2,1)S(1)}, bf16[4,48,1280]{2,1,0:T(8,128)(2,1)S(1)}, u32[]{:S(2)}, u32[]{:S(2)}) collective-permute-start(bf16[4,48,1280]{2,1,0:T(8,128)(2,1)S(1)} %shard_map.170.refs_2_), channel_id=1, source_target_pairs={{0,4},{2,6},{4,0},{6,2},{8,12},{10,14},{12,8},{14,10},{16,20},{18,... | collective-permute-start | bytes 1474568 | tf_op jit(solution)/shard_map/ppermute | solution.py:443
  20.8 14.0 %collective-permute-start.19 = (bf16[48,1408]{1,0:T(8,128)(2,1)S(1)}, bf16[48,1408]{1,0:T(8,128)(2,1)S(1)}, u32[]{:S(2)}, u32[]{:S(2)}) collective-permute-start(bf16[48,1408]{1,0:T(8,128)(2,1)S(1)} %slice.80.refs_0_), channel_id=1, source_target_pairs={{0,16},{2,18},{4,20},{6,22},{8,24},{10,26},{12,28},{14,30},{16,0},... | collective-permute-start | bytes 405512 | tf_op jit(solution)/shard_map/ppermute | solution.py:443
  23.7 13.1 %collective-permute-start.20 = (bf16[48,1408]{1,0:T(8,128)(2,1)S(1)}, bf16[48,1408]{1,0:T(8,128)(2,1)S(1)}, u32[]{:S(2)}, u32[]{:S(2)}) collective-permute-start(bf16[48,1408]{1,0:T(8,128)(2,1)S(1)} %slice.80.refs_0_), channel_id=1, source_target_pairs={{0,24},{2,26},{4,28},{6,30},{8,16},{10,18},{12,20},{14,22},{16,8},... | collective-permute-start | bytes 405512 | tf_op jit(solution)/shard_map/ppermute | solution.py:443
  34.3 19.9 %collective-permute-start.16 = (bf16[4,48,768]{2,1,0:T(8,128)(2,1)S(1)}, bf16[4,48,768]{2,1,0:T(8,128)(2,1)}, u32[]{:S(2)}, u32[]{:S(2)}) collective-permute-start(bf16[4,48,768]{2,1,0:T(8,128)(2,1)S(1)} %shard_map.172.refs_5_), channel_id=1, source_target_pairs={{0,16},{2,18},{4,20},{6,22},{8,24},{10,26},{12,28},{14,30},{16,0},... | collective-permute-start | bytes 884744 | tf_op jit(solution)/shard_map/ppermute | solution.py:443
  34.9 22.0 %collective-permute-start.17 = (bf16[4,48,768]{2,1,0:T(8,128)(2,1)S(1)}, bf16[4,48,768]{2,1,0:T(8,128)(2,1)S(1)}, u32[]{:S(2)}, u32[]{:S(2)}) collective-permute-start(bf16[4,48,768]{2,1,0:T(8,128)(2,1)S(1)} %shard_map.172.refs_5_), channel_id=1, source_target_pairs={{0,24},{2,26},{4,28},{6,30},{8,16},{10,18},{12,20},{14,22},{16,8},... | collective-permute-start | bytes 884744 | tf_op jit(solution)/shard_map/ppermute | solution.py:443
  36.8 20.8 %collective-permute-start.25 = (bf16[4,48,768]{2,1,0:T(8,128)(2,1)S(1)}, bf16[4,48,768]{2,1,0:T(8,128)(2,1)S(1)}, u32[]{:S(2)}, u32[]{:S(2)}) collective-permute-start(bf16[4,48,768]{2,1,0:T(8,128)(2,1)S(1)} %shard_map.172.refs_5_), channel_id=1, source_target_pairs={{0,1},{1,0},{2,3},{3,2},{4,5},{5,4},{6,7},{7,6},{8,9},{9,8},{10,11... | collective-permute-start | bytes 884744 | tf_op jit(solution)/shard_map/ppermute | solution.py:439
  36.8 23.5 %collective-permute-start.3 = (bf16[4,48,1280]{2,1,0:T(8,128)(2,1)S(1)}, bf16[4,48,1280]{2,1,0:T(8,128)(2,1)}, u32[]{:S(2)}, u32[]{:S(2)}) collective-permute-start(bf16[4,48,1280]{2,1,0:T(8,128)(2,1)S(1)} %shard_map.170.refs_2_), channel_id=1, source_target_pairs={{0,2},{2,0},{4,6},{6,4},{8,10},{10,8},{12,14},{14,12},{16,18},{18,... | collective-permute-start | bytes 1474568 | tf_op jit(solution)/shard_map/ppermute | solution.py:443
  54.3 13.4 %collective-permute-start.22 = (bf16[4,48,1408]{2,1,0:T(8,128)(2,1)S(1)}, bf16[4,48,1408]{2,1,0:T(8,128)(2,1)S(1)}, u32[]{:S(2)}, u32[]{:S(2)}) collective-permute-start(bf16[4,48,1408]{2,1,0:T(8,128)(2,1)S(1)} %shard_map.173.refs_9_), channel_id=1, source_target_pairs={{0,4},{2,6},{4,0},{6,2},{8,12},{10,14},{12,8},{14,10},{16,20},{18,... | collective-permute-start | bytes 1622024 | tf_op jit(solution)/shard_map/ppermute | solution.py:443
  57.6 3.1 %collective-permute-start.7 = (bf16[4,48,1280]{2,1,0:T(8,128)(2,1)S(1)}, bf16[4,48,1280]{2,1,0:T(8,128)(2,1)}, u32[]{:S(2)}, u32[]{:S(2)}) collective-permute-start(bf16[4,48,1280]{2,1,0:T(8,128)(2,1)S(1)} %shard_map.170.refs_2_), channel_id=1, source_target_pairs={{0,1},{1,0},{2,3},{3,2},{4,5},{5,4},{6,7},{7,6},{8,9},{9,8},{10,11... | collective-permute-start | bytes 1474568 | tf_op jit(solution)/shard_map/ppermute | solution.py:439
  58.3 15.1 %collective-permute-start.21 = (bf16[4,48,1408]{2,1,0:T(8,128)(2,1)S(1)}, bf16[4,48,1408]{2,1,0:T(8,128)(2,1)S(1)}, u32[]{:S(2)}, u32[]{:S(2)}) collective-permute-start(bf16[4,48,1408]{2,1,0:T(8,128)(2,1)S(1)} %shard_map.173.refs_9_), channel_id=1, source_target_pairs={{0,2},{2,0},{4,6},{6,4},{8,10},{10,8},{12,14},{14,12},{16,18},{18,... | collective-permute-start | bytes 1622024 | tf_op jit(solution)/shard_map/ppermute | solution.py:443
  59.9 13.6 %collective-permute-start.29 = (bf16[4,48,1408]{2,1,0:T(8,128)(2,1)S(1)}, bf16[4,48,1408]{2,1,0:T(8,128)(2,1)S(1)}, u32[]{:S(2)}, u32[]{:S(2)}) collective-permute-start(bf16[4,48,1408]{2,1,0:T(8,128)(2,1)S(1)} %shard_map.173.refs_9_), channel_id=1, source_target_pairs={{0,1},{1,0},{2,3},{3,2},{4,5},{5,4},{6,7},{7,6},{8,9},{9,8},{10,11... | collective-permute-start | bytes 1622024 | tf_op jit(solution)/shard_map/ppermute | solution.py:439
  60.3 14.0 %collective-permute-start.26 = (bf16[4,48,768]{2,1,0:T(8,128)(2,1)}, bf16[4,48,768]{2,1,0:T(8,128)(2,1)S(1)}, u32[]{:S(2)}, u32[]{:S(2)}) collective-permute-start(bf16[4,48,768]{2,1,0:T(8,128)(2,1)} %collective-permute-done.15.refs_6_), channel_id=1, source_target_pairs={{0,1},{1,0},{2,3},{3,2},{4,5},{5,4},{6,7},{7,6},{8,9},{9,8},{10,11... | collective-permute-start | bytes 884744 | tf_op jit(solution)/shard_map/ppermute | solution.py:439
  60.7 19.1 %collective-permute-start.27 = (bf16[4,48,768]{2,1,0:T(8,128)(2,1)}, bf16[4,48,768]{2,1,0:T(8,128)(2,1)}, u32[]{:S(2)}, u32[]{:S(2)}) collective-permute-start(bf16[4,48,768]{2,1,0:T(8,128)(2,1)} %collective-permute-done.16.refs_7_), channel_id=1, source_target_pairs={{0,1},{1,0},{2,3},{3,2},{4,5},{5,4},{6,7},{7,6},{8,9},{9,8},{10,11... | collective-permute-start | bytes 884744 | tf_op jit(solution)/shard_map/ppermute | solution.py:439
  67.6 12.4 %collective-permute-start.5 = (bf16[2,48,1280]{2,1,0:T(8,128)(2,1)S(1)}, bf16[2,48,1280]{2,1,0:T(8,128)(2,1)}, u32[]{:S(2)}, u32[]{:S(2)}) collective-permute-start(bf16[2,48,1280]{2,1,0:T(8,128)(2,1)S(1)} %slice.78), channel_id=1, source_target_pairs={{0,2},{2,0},{4,6},{6,4},{8,10},{10,8},{12,14},{14,12},{16,18},{18,... | collective-permute-start | bytes 737288 | tf_op jit(solution)/shard_map/ppermute | solution.py:443
  71.9 22.0 %copy-start.1 = (bf16[256,768]{1,0:T(8,128)(2,1)S(1)}, bf16[256,768]{1,0:T(8,128)(2,1)}, u32[]{:S(2)}) copy-start(bf16[256,768]{1,0:T(8,128)(2,1)} %refs_0_.1) | copy-start | bytes 1179652
  73.5 10.6 %collective-permute-start.6 = (bf16[2,48,1280]{2,1,0:T(8,128)(2,1)}, bf16[2,48,1280]{2,1,0:T(8,128)(2,1)}, u32[]{:S(2)}, u32[]{:S(2)}) collective-permute-start(bf16[2,48,1280]{2,1,0:T(8,128)(2,1)} %slice.79), channel_id=1, source_target_pairs={{0,4},{2,6},{4,0},{6,2},{8,12},{10,14},{12,8},{14,10},{16,20},{18,... | collective-permute-start | bytes 737288 | tf_op jit(solution)/shard_map/ppermute | solution.py:443
  74.3 15.1 %collective-permute-start.8 = (bf16[4,48,1280]{2,1,0:T(8,128)(2,1)}, bf16[4,48,1280]{2,1,0:T(8,128)(2,1)}, u32[]{:S(2)}, u32[]{:S(2)}) collective-permute-start(bf16[4,48,1280]{2,1,0:T(8,128)(2,1)} %collective-permute-done.3.refs_3_), channel_id=1, source_target_pairs={{0,1},{1,0},{2,3},{3,2},{4,5},{5,4},{6,7},{7,6},{8,9},{9,8},{10,11... | collective-permute-start | bytes 1474568 | tf_op jit(solution)/shard_map/ppermute | solution.py:439
  75.0 9.2 %collective-permute-start.23 = (bf16[2,48,1408]{2,1,0:T(8,128)(2,1)}, bf16[2,48,1408]{2,1,0:T(8,128)(2,1)}, u32[]{:S(2)}, u32[]{:S(2)}) collective-permute-start(bf16[2,48,1408]{2,1,0:T(8,128)(2,1)} %slice.81), channel_id=1, source_target_pairs={{0,2},{2,0},{4,6},{6,4},{8,10},{10,8},{12,14},{14,12},{16,18},{18,... | collective-permute-start | bytes 811016 | tf_op jit(solution)/shard_map/ppermute | solution.py:443
  79.8 12.3 %collective-permute-start.9 = (bf16[4,48,1280]{2,1,0:T(8,128)(2,1)S(1)}, bf16[4,48,1280]{2,1,0:T(8,128)(2,1)}, u32[]{:S(2)}, u32[]{:S(2)}) collective-permute-start(bf16[4,48,1280]{2,1,0:T(8,128)(2,1)S(1)} %collective-permute-done.4.refs_4_), channel_id=1, source_target_pairs={{0,1},{1,0},{2,3},{3,2},{4,5},{5,4},{6,7},{7,6},{8,9},{9,8},{10,11... | collective-permute-start | bytes 1474568 | tf_op jit(solution)/shard_map/ppermute | solution.py:439
  80.1 9.3 %collective-permute-start.24 = (bf16[2,48,1408]{2,1,0:T(8,128)(2,1)}, bf16[2,48,1408]{2,1,0:T(8,128)(2,1)}, u32[]{:S(2)}, u32[]{:S(2)}) collective-permute-start(bf16[2,48,1408]{2,1,0:T(8,128)(2,1)} %slice.82), channel_id=1, source_target_pairs={{0,4},{2,6},{4,0},{6,2},{8,12},{10,14},{12,8},{14,10},{16,20},{18,... | collective-permute-start | bytes 811016 | tf_op jit(solution)/shard_map/ppermute | solution.py:443
  84.1 8.1 %collective-permute-start.10 = (bf16[2,48,1280]{2,1,0:T(8,128)(2,1)}, bf16[2,48,1280]{2,1,0:T(8,128)(2,1)}, u32[]{:S(2)}, u32[]{:S(2)}) collective-permute-start(bf16[2,48,1280]{2,1,0:T(8,128)(2,1)} %collective-permute-done.5.refs_5_), channel_id=1, source_target_pairs={{0,1},{1,0},{2,3},{3,2},{4,5},{5,4},{6,7},{7,6},{8,9},{9,8},{10,11... | collective-permute-start | bytes 737288 | tf_op jit(solution)/shard_map/ppermute | solution.py:439
  84.2 8.5 %collective-permute-start.11 = (bf16[2,48,1280]{2,1,0:T(8,128)(2,1)}, bf16[2,48,1280]{2,1,0:T(8,128)(2,1)}, u32[]{:S(2)}, u32[]{:S(2)}) collective-permute-start(bf16[2,48,1280]{2,1,0:T(8,128)(2,1)} %collective-permute-done.6.refs_6_), channel_id=1, source_target_pairs={{0,1},{1,0},{2,3},{3,2},{4,5},{5,4},{6,7},{7,6},{8,9},{9,8},{10,11... | collective-permute-start | bytes 737288 | tf_op jit(solution)/shard_map/ppermute | solution.py:439
  89.3 11.0 %collective-permute-start.30 = (bf16[4,48,1408]{2,1,0:T(8,128)(2,1)S(1)}, bf16[4,48,1408]{2,1,0:T(8,128)(2,1)S(1)}, u32[]{:S(2)}, u32[]{:S(2)}) collective-permute-start(bf16[4,48,1408]{2,1,0:T(8,128)(2,1)S(1)} %collective-permute-done.21.refs_10_), channel_id=1, source_target_pairs={{0,1},{1,0},{2,3},{3,2},{4,5},{5,4},{6,7},{7,6},{8,9},{9,8},{10,11... | collective-permute-start | bytes 1622024 | tf_op jit(solution)/shard_map/ppermute | solution.py:439
  89.3 11.0 %collective-permute-start.31 = (bf16[4,48,1408]{2,1,0:T(8,128)(2,1)S(1)}, bf16[4,48,1408]{2,1,0:T(8,128)(2,1)S(1)}, u32[]{:S(2)}, u32[]{:S(2)}) collective-permute-start(bf16[4,48,1408]{2,1,0:T(8,128)(2,1)S(1)} %collective-permute-done.22.refs_11_), channel_id=1, source_target_pairs={{0,1},{1,0},{2,3},{3,2},{4,5},{5,4},{6,7},{7,6},{8,9},{9,8},{10,11... | collective-permute-start | bytes 1622024 | tf_op jit(solution)/shard_map/ppermute | solution.py:439
  92.1 8.2 %collective-permute-start.28 = (bf16[4,48,768]{2,1,0:T(8,128)(2,1)}, bf16[4,48,768]{2,1,0:T(8,128)(2,1)S(1)}, u32[]{:S(2)}, u32[]{:S(2)}) collective-permute-start(bf16[4,48,768]{2,1,0:T(8,128)(2,1)} %copy-done.5), channel_id=1, source_target_pairs={{0,1},{1,0},{2,3},{3,2},{4,5},{5,4},{6,7},{7,6},{8,9},{9,8},{10,11... | collective-permute-start | bytes 884744 | tf_op jit(solution)/shard_map/ppermute | solution.py:439
  92.2 8.1 %collective-permute-start.32 = (bf16[2,48,1408]{2,1,0:T(8,128)(2,1)}, bf16[2,48,1408]{2,1,0:T(8,128)(2,1)S(1)}, u32[]{:S(2)}, u32[]{:S(2)}) collective-permute-start(bf16[2,48,1408]{2,1,0:T(8,128)(2,1)} %collective-permute-done.23.refs_12_), channel_id=1, source_target_pairs={{0,1},{1,0},{2,3},{3,2},{4,5},{5,4},{6,7},{7,6},{8,9},{9,8},{10,11... | collective-permute-start | bytes 811016 | tf_op jit(solution)/shard_map/ppermute | solution.py:439
  92.7 7.6 %collective-permute-start.33 = (bf16[2,48,1408]{2,1,0:T(8,128)(2,1)}, bf16[2,48,1408]{2,1,0:T(8,128)(2,1)S(1)}, u32[]{:S(2)}, u32[]{:S(2)}) collective-permute-start(bf16[2,48,1408]{2,1,0:T(8,128)(2,1)} %collective-permute-done.24.refs_13_), channel_id=1, source_target_pairs={{0,1},{1,0},{2,3},{3,2},{4,5},{5,4},{6,7},{7,6},{8,9},{9,8},{10,11... | collective-permute-start | bytes 811016 | tf_op jit(solution)/shard_map/ppermute | solution.py:439
  93.9 6.4 %copy-start.3 = (bf16[4,48,1408]{2,1,0:T(8,128)(2,1)S(1)}, bf16[4,48,1408]{2,1,0:T(8,128)(2,1)}, u32[]{:S(2)}) copy-start(bf16[4,48,1408]{2,1,0:T(8,128)(2,1)} %copy-done.2) | copy-start | bytes 1622020
  93.9 6.4 %copy-start.4 = (f32[256,1]{1,0:T(8,128)S(1)}, f32[256,1]{1,0:T(8,128)}, u32[]{:S(2)}) copy-start(f32[256,1]{1,0:T(8,128)} %fusion.2.refs_4_) | copy-start | bytes 3076
  93.9 6.4 %copy-start.6 = (bf16[4,48,768]{2,1,0:T(8,128)(2,1)S(1)}, bf16[4,48,768]{2,1,0:T(8,128)(2,1)}, u32[]{:S(2)}) copy-start(bf16[4,48,768]{2,1,0:T(8,128)(2,1)} %copy-done.5) | copy-start | bytes 884740
  106.9 13.6 %collective-permute-start.41 = (bf16[256,2560]{1,0:T(8,128)(2,1)S(1)}, bf16[256,2560]{1,0:T(8,128)(2,1)S(1)}, u32[]{:S(2)}, u32[]{:S(2)}) collective-permute-start(bf16[256,2560]{1,0:T(8,128)(2,1)S(1)} %get-tuple-element.96.refs_0_), channel_id=1, source_target_pairs={{0,1},{1,0},{2,3},{3,2},{4,5},{5,4},{6,7},{7,6},{8,9},{9,8},{10,11... | collective-permute-start | bytes 3932168 | tf_op jit(solution)/shard_map/ppermute | solution.py:439
  116.4 8.5 %collective-permute-start.34 = (bf16[272,1920]{1,0:T(8,128)(2,1)S(1)}, bf16[272,1920]{1,0:T(8,128)(2,1)S(1)}, u32[]{:S(2)}, u32[]{:S(2)}) collective-permute-start(bf16[272,1920]{1,0:T(8,128)(2,1)S(1)} %get-tuple-element.80.refs_0_), channel_id=1, source_target_pairs={{0,1},{1,0},{2,3},{3,2},{4,5},{5,4},{6,7},{7,6},{8,9},{9,8},{10,11... | collective-permute-start | bytes 3133448 | tf_op jit(solution)/shard_map/ppermute | solution.py:439
  116.5 4.0 %collective-permute-start.42 = (bf16[272,768]{1,0:T(8,128)(2,1)S(1)}, bf16[272,768]{1,0:T(8,128)(2,1)S(1)}, u32[]{:S(2)}, u32[]{:S(2)}) collective-permute-start(bf16[272,768]{1,0:T(8,128)(2,1)S(1)} %get-tuple-element.98.refs_3_), channel_id=1, source_target_pairs={{0,1},{1,0},{2,3},{3,2},{4,5},{5,4},{6,7},{7,6},{8,9},{9,8},{10,11... | collective-permute-start | bytes 1253384 | tf_op jit(solution)/shard_map/ppermute | solution.py:439
  116.9 3.3 %collective-permute-start.44 = (bf16[256,768]{1,0:T(8,128)(2,1)S(1)}, bf16[256,768]{1,0:T(8,128)(2,1)S(1)}, u32[]{:S(2)}, u32[]{:S(2)}) collective-permute-start(bf16[256,768]{1,0:T(8,128)(2,1)S(1)} %multiply_convert_fusion.refs_3_.gm_ref.refs_7_), channel_id=1, source_target_pairs={{0,1},{1,0},{2,3},{3,2},{4,5},{5,4},{6,7},{7,6},{8,9},{9,8},{10,11... | collective-permute-start | bytes 1179656 | tf_op jit(solution)/shard_map/ppermute | solution.py:439
  117.0 3.5 %collective-permute-start.43 = (bf16[256,384]{1,0:T(8,128)(2,1)S(1)}, bf16[256,384]{1,0:T(8,128)(2,1)S(1)}, u32[]{:S(2)}, u32[]{:S(2)}) collective-permute-start(bf16[256,384]{1,0:T(8,128)(2,1)S(1)} %get-tuple-element.99), channel_id=1, source_target_pairs={{0,1},{1,0},{2,3},{3,2},{4,5},{5,4},{6,7},{7,6},{8,9},{9,8},{10,11... | collective-permute-start | bytes 589832 | tf_op jit(solution)/shard_map/ppermute | solution.py:439
  123.0 28.5 %collective-permute-start.50 = (bf16[8,48,768]{2,1,0:T(8,128)(2,1)S(1)}, bf16[8,48,768]{2,1,0:T(8,128)(2,1)S(1)}, u32[]{:S(2)}, u32[]{:S(2)}) collective-permute-start(bf16[8,48,768]{2,1,0:T(8,128)(2,1)S(1)} %get-tuple-element.111), channel_id=1, source_target_pairs={{0,4},{2,6},{4,0},{6,2},{8,12},{10,14},{12,8},{14,10},{16,20},{18,... | collective-permute-start | bytes 1769480 | tf_op jit(solution)/shard_map/ppermute | solution.py:443
  126.3 14.2 %collective-permute-start.35 = (bf16[8,48,640]{2,1,0:T(8,128)(2,1)S(1)}, bf16[8,48,640]{2,1,0:T(8,128)(2,1)S(1)}, u32[]{:S(2)}, u32[]{:S(2)}) collective-permute-start(bf16[8,48,640]{2,1,0:T(8,128)(2,1)S(1)} %get-tuple-element.83), channel_id=1, source_target_pairs={{0,2},{2,0},{4,6},{6,4},{8,10},{10,8},{12,14},{14,12},{16,18},{18,... | collective-permute-start | bytes 1474568 | tf_op jit(solution)/shard_map/ppermute | solution.py:443
  126.8 22.2 %collective-permute-start.36 = (bf16[8,48,640]{2,1,0:T(8,128)(2,1)S(1)}, bf16[8,48,640]{2,1,0:T(8,128)(2,1)S(1)}, u32[]{:S(2)}, u32[]{:S(2)}) collective-permute-start(bf16[8,48,640]{2,1,0:T(8,128)(2,1)S(1)} %get-tuple-element.85), channel_id=1, source_target_pairs={{0,4},{2,6},{4,0},{6,2},{8,12},{10,14},{12,8},{14,10},{16,20},{18,... | collective-permute-start | bytes 1474568 | tf_op jit(solution)/shard_map/ppermute | solution.py:443
  127.1 24.4 %collective-permute-start.49 = (bf16[8,48,640]{2,1,0:T(8,128)(2,1)S(1)}, bf16[8,48,640]{2,1,0:T(8,128)(2,1)S(1)}, u32[]{:S(2)}, u32[]{:S(2)}) collective-permute-start(bf16[8,48,640]{2,1,0:T(8,128)(2,1)S(1)} %get-tuple-element.109), channel_id=1, source_target_pairs={{0,2},{2,0},{4,6},{6,4},{8,10},{10,8},{12,14},{14,12},{16,18},{18,... | collective-permute-start | bytes 1474568 | tf_op jit(solution)/shard_map/ppermute | solution.py:443
  128.7 25.0 %collective-permute-start.45 = (bf16[8,48,768]{2,1,0:T(8,128)(2,1)S(1)}, bf16[8,48,768]{2,1,0:T(8,128)(2,1)S(1)}, u32[]{:S(2)}, u32[]{:S(2)}) collective-permute-start(bf16[8,48,768]{2,1,0:T(8,128)(2,1)S(1)} %get-tuple-element.101), channel_id=1, source_target_pairs={{0,8},{2,10},{4,12},{6,14},{8,0},{10,2},{12,4},{14,6},{16,24},{18,... | collective-permute-start | bytes 1769480 | tf_op jit(solution)/shard_map/ppermute | solution.py:443
  149.2 9.5 %collective-permute-start.37 = (bf16[4,48,640]{2,1,0:T(8,128)(2,1)S(1)}, bf16[4,48,640]{2,1,0:T(8,128)(2,1)S(1)}, u32[]{:S(2)}, u32[]{:S(2)}) collective-permute-start(bf16[4,48,640]{2,1,0:T(8,128)(2,1)S(1)} %get-tuple-element.87), channel_id=1, source_target_pairs={{0,4},{2,6},{4,0},{6,2},{8,12},{10,14},{12,8},{14,10},{16,20},{18,... | collective-permute-start | bytes 737288 | tf_op jit(solution)/shard_map/ppermute | solution.py:443
  151.1 8.8 %collective-permute-start.38 = (bf16[4,48,640]{2,1,0:T(8,128)(2,1)S(1)}, bf16[4,48,640]{2,1,0:T(8,128)(2,1)S(1)}, u32[]{:S(2)}, u32[]{:S(2)}) collective-permute-start(bf16[4,48,640]{2,1,0:T(8,128)(2,1)S(1)} %get-tuple-element.89), channel_id=1, source_target_pairs={{0,2},{2,0},{4,6},{6,4},{8,10},{10,8},{12,14},{14,12},{16,18},{18,... | collective-permute-start | bytes 737288 | tf_op jit(solution)/shard_map/ppermute | solution.py:443
  151.8 12.4 %collective-permute-start.52 = (bf16[4,48,768]{2,1,0:T(8,128)(2,1)S(1)}, bf16[4,48,768]{2,1,0:T(8,128)(2,1)S(1)}, u32[]{:S(2)}, u32[]{:S(2)}) collective-permute-start(bf16[4,48,768]{2,1,0:T(8,128)(2,1)S(1)} %get-tuple-element.115), channel_id=1, source_target_pairs={{0,2},{2,0},{4,6},{6,4},{8,10},{10,8},{12,14},{14,12},{16,18},{18,... | collective-permute-start | bytes 884744 | tf_op jit(solution)/shard_map/ppermute | solution.py:443
  153.4 10.4 %collective-permute-start.51 = (bf16[4,48,640]{2,1,0:T(8,128)(2,1)S(1)}, bf16[4,48,640]{2,1,0:T(8,128)(2,1)S(1)}, u32[]{:S(2)}, u32[]{:S(2)}) collective-permute-start(bf16[4,48,640]{2,1,0:T(8,128)(2,1)S(1)} %get-tuple-element.113), channel_id=1, source_target_pairs={{0,4},{2,6},{4,0},{6,2},{8,12},{10,14},{12,8},{14,10},{16,20},{18,... | collective-permute-start | bytes 737288 | tf_op jit(solution)/shard_map/ppermute | solution.py:443
  153.8 16.6 %collective-permute-start.46 = (bf16[4,48,768]{2,1,0:T(8,128)(2,1)S(1)}, bf16[4,48,768]{2,1,0:T(8,128)(2,1)S(1)}, u32[]{:S(2)}, u32[]{:S(2)}) collective-permute-start(bf16[4,48,768]{2,1,0:T(8,128)(2,1)S(1)} %get-tuple-element.103), channel_id=1, source_target_pairs={{0,16},{2,18},{4,20},{6,22},{8,24},{10,26},{12,28},{14,30},{16,0},... | collective-permute-start | bytes 884744 | tf_op jit(solution)/shard_map/ppermute | solution.py:443
  160.0 14.3 %collective-permute-start.39 = (bf16[2,48,1280]{2,1,0:T(8,128)(2,1)S(1)}, bf16[2,48,1280]{2,1,0:T(8,128)(2,1)S(1)}, u32[]{:S(2)}, u32[]{:S(2)}) collective-permute-start(bf16[2,48,1280]{2,1,0:T(8,128)(2,1)S(1)} %get-tuple-element.91), channel_id=1, source_target_pairs={{0,8},{2,10},{4,12},{6,14},{8,0},{10,2},{12,4},{14,6},{16,24},{18,... | collective-permute-start | bytes 737288 | tf_op jit(solution)/shard_map/ppermute | solution.py:443
  164.3 14.0 %collective-permute-start.53 = (bf16[2,48,1408]{2,1,0:T(8,128)(2,1)S(1)}, bf16[2,48,1408]{2,1,0:T(8,128)(2,1)S(1)}, u32[]{:S(2)}, u32[]{:S(2)}) collective-permute-start(bf16[2,48,1408]{2,1,0:T(8,128)(2,1)S(1)} %get-tuple-element.117), channel_id=1, source_target_pairs={{0,8},{2,10},{4,12},{6,14},{8,0},{10,2},{12,4},{14,6},{16,24},{18,... | collective-permute-start | bytes 811016 | tf_op jit(solution)/shard_map/ppermute | solution.py:443
  170.5 15.3 %collective-permute-start.47 = (bf16[2,48,768]{2,1,0:T(8,128)(2,1)S(1)}, bf16[2,48,768]{2,1,0:T(8,128)(2,1)S(1)}, u32[]{:S(2)}, u32[]{:S(2)}) collective-permute-start(bf16[2,48,768]{2,1,0:T(8,128)(2,1)S(1)} %get-tuple-element.105), channel_id=1, source_target_pairs={{0,2},{2,0},{4,6},{6,4},{8,10},{10,8},{12,14},{14,12},{16,18},{18,... | collective-permute-start | bytes 442376 | tf_op jit(solution)/shard_map/ppermute | solution.py:443
  174.3 10.8 %collective-permute-start.40 = (bf16[1,48,1280]{2,1,0:T(8,128)(2,1)S(1)}, bf16[1,48,1280]{2,1,0:T(8,128)(2,1)S(1)}, u32[]{:S(2)}, u32[]{:S(2)}) collective-permute-start(bf16[1,48,1280]{2,1,0:T(8,128)(2,1)S(1)} %get-tuple-element.93), channel_id=1, source_target_pairs={{0,16},{2,18},{4,20},{6,22},{8,24},{10,26},{12,28},{14,30},{16,0},... | collective-permute-start | bytes 368648 | tf_op jit(solution)/shard_map/ppermute | solution.py:443
  178.4 11.9 %collective-permute-start.54 = (bf16[1,48,1408]{2,1,0:T(8,128)(2,1)S(1)}, bf16[1,48,1408]{2,1,0:T(8,128)(2,1)S(1)}, u32[]{:S(2)}, u32[]{:S(2)}) collective-permute-start(bf16[1,48,1408]{2,1,0:T(8,128)(2,1)S(1)} %get-tuple-element.119), channel_id=1, source_target_pairs={{0,16},{2,18},{4,20},{6,22},{8,24},{10,26},{12,28},{14,30},{16,0},... | collective-permute-start | bytes 405512 | tf_op jit(solution)/shard_map/ppermute | solution.py:443
  185.9 4.4 %collective-permute-start.48 = (bf16[1,48,768]{2,1,0:T(8,128)(2,1)S(1)}, bf16[1,48,768]{2,1,0:T(8,128)(2,1)S(1)}, u32[]{:S(2)}, u32[]{:S(2)}) collective-permute-start(bf16[1,48,768]{2,1,0:T(8,128)(2,1)S(1)} %get-tuple-element.107), channel_id=1, source_target_pairs={{0,4},{2,6},{4,0},{6,2},{8,12},{10,14},{12,8},{14,10},{16,20},{18,... | collective-permute-start | bytes 221192 | tf_op jit(solution)/shard_map/ppermute | solution.py:443
  (6 other events, 15.7 us)

commit v3 on v2

--- a/solution.py
+++ b/solution.py
@@ -115,19 +115,15 @@
     own = refs[2 : 2 + n_pieces]
     other = refs[2 + n_pieces : 2 + 2 * n_pieces]
     seg_row, seg_col, live_row, cos_ref, sin_ref = refs[2 + 2 * n_pieces : 7 + 2 * n_pieces]
-    w_ref, qkv_ref, att_ref, far_ref, logt_ref, n1_ref, gain_ref, gcol = refs[7 + 2 * n_pieces :]
+    w_ref, qkv_ref, att_ref, far_ref, logt_ref, n1_ref = refs[7 + 2 * n_pieces :]
     me = me_ref[0]
     half, width = cfg["half"], 2 * cfg["half"]
     for which, pieces in enumerate((own, other)):
         part = Pieces(me, pieces, cfg["rows"], cfg["layout"])
         for c in range(3):
             part.copy(w_ref, c * width + which * half, c * half, half)
-        if which == 0:
-            part.copy(gcol, 0, 3 * half, LANES)
-    gain_row = column_to_row(gcol[...], 0)
-    gain_ref[...] = jnp.broadcast_to(gain_row, gain_ref.shape)
     normed, _ = norm_parts(x_ref[...].astype(F32))
-    n1 = (normed * gain_row).astype(BF16)
+    n1 = normed.astype(BF16)
     n1_ref[...] = n1
     cosine, sine = cos_ref[...], sin_ref[...]
     step = 2 * LANES
@@ -258,9 +254,9 @@
 
 
 def attn_backward_kernel(cfg, *refs):
-    (x_ref, gh_ref, wo_ref, w_ref, qkv_ref, att_ref, logt_ref, gain_ref) = refs[:8]
-    seg_row, seg_col, live_row, cos_ref, sin_ref, n1_ref = refs[8:14]
-    gin_ref, swap_ref, keep_ref, gatt_ref, gqkv_ref = refs[14:]
+    (x_ref, gh_ref, wo_ref, w_ref, qkv_ref, att_ref, logt_ref) = refs[:7]
+    seg_row, seg_col, live_row, cos_ref, sin_ref, n1_ref = refs[7:13]
+    gin_ref, swap_ref, keep_ref, gatt_ref, gqkv_ref = refs[13:]
     half, width = cfg["half"], 2 * cfg["half"]
     rows, model = x_ref.shape
     gatt_ref[...] = mm(gh_ref[...].astype(BF16), wo_ref[...], NN).astype(BF16)
@@ -302,9 +298,9 @@
                 col = model + c * half + at - half
                 swap_ref[0:rows, col : col + LANES] = value
     swap_ref[0:rows, 0:model] = n1_ref[...]
-    grad_normed = mm(gqkv_ref[...], w_ref[...], NT)
+    scaled = mm(gqkv_ref[...], w_ref[...], NT)
     normed, inv_std = norm_parts(x_ref[...].astype(F32))
-    grad_rows, gain_term = norm_back(grad_normed, normed, inv_std, gain_ref[0:1])
+    grad_rows, gain_term = norm_back(scaled, normed, inv_std, 1.0)
     gin_ref[...] = gh_ref[...] + grad_rows
     put_gain(swap_ref, gain_term, rows)
 
@@ -351,6 +347,11 @@
         refs[-1][i] = ref[...]
 
 
+def take_kernel(first, source, taken):
+    for i in range(taken.shape[0]):
+        taken[i] = source[first + i]
+
+
 def combine_kernel(joined, *refs):
     n = (len(refs) - 2) // 2 if joined else len(refs) // 4
     ins, outs = refs[: 2 * n], refs[2 * n :]
@@ -372,12 +373,13 @@
     share[:, cut:] = kept_ab[0] + came_ab[0].astype(F32)
 
 
-def final_qkv_kernel(kept, came, grad, gain):
+def final_qkv_kernel(kept, came, gain_ref, grad, gain_grad):
     half = grad.shape[2]
+    gain = gain_ref[...]
     for c in range(3):
         cols = slice(c * half, (c + 1) * half)
-        grad[c] = kept[0, :, cols] + came[0, :, cols].astype(F32)
-    gain[...] = kept[0, :, 3 * half :] + came[0, :, 3 * half :].astype(F32)
+        grad[c] = (kept[0, :, cols] + came[0, :, cols].astype(F32)) * gain
+    gain_grad[...] = (kept[0, :, 3 * half :] + came[0, :, 3 * half :].astype(F32)) / gain
 
 
 VMEM = pl.BlockSpec(memory_space=pltpu.VMEM)
@@ -408,6 +410,12 @@
     return call(stack_kernel, list(planes), outs, [], scalars=0)[0]
 
 
+def take(source, first, count):
+    kernel = functools.partial(take_kernel, first)
+    outs = [shape(count, *source.shape[1:])]
+    return call(kernel, [source], outs, [], scalars=0)[0]
+
+
 def combine(joined, *arrays):
     outs = []
     for kept in arrays[::2]:
@@ -448,16 +456,16 @@
     def plane(stacked):
         came_x = exchange(stacked, X)
         came_y = exchange(stacked, Y)
-        far_a = exchange(came_y[:2], X)
-        far_b = exchange(came_x[2:], Y)
+        far_a = exchange(take(came_y, 0, 2), X)
+        far_b = exchange(take(came_x, 2, 2), Y)
         return [stacked, came_x, came_y, far_a, far_b]
 
     def both_cores(pieces):
         return [swap_cores(piece) for piece in pieces]
 
+    gain_col = gain_attn.astype(F32)[:, None]
     pack_qkv = jnp.concatenate(
-        [w_qkv[0], w_qkv[1], w_qkv[2], jnp.pad(gain_attn[:, None], ((0, 0), (0, LANES - 1)))],
-        axis=1,
+        [(w_qkv[c].astype(F32) * gain_col).astype(BF16) for c in range(3)], axis=1
     )
     out_t, down_t = w_out.T, w_down.T
     pack_ffn = jnp.concatenate(
@@ -473,7 +481,7 @@
         axis=1,
     )
     total_qkv, total_ffn = pack_qkv.shape[1], pack_ffn.shape[1]
-    cut = total_ffn * 9 // 25 // LANES * LANES
+    cut = total_ffn * 3 // 10 // LANES * LANES
     if fast:
         own_qkv = plane(stack(across_z(pack_qkv)))
         other_qkv = both_cores(own_qkv)
@@ -512,7 +520,7 @@
 
     cfg = dict(half=half, rows=rows, layout=layout_qkv, units=units, main=main, model=model)
     width = 2 * half
-    w_full, qkv, att, far, logt, n1, gain1 = call(
+    w_full, qkv, att, far, logt, n1 = call(
         functools.partial(attn_forward_kernel, cfg, len(own_qkv)),
         [me_vec, inputs, *own_qkv, *other_qkv, seg_row, seg_col, live_row, cosine, sine],
         [
@@ -522,9 +530,8 @@
             shape(tokens, half),
             shape(tokens, LANES, dtype=F32),
             shape(tokens, model),
-            shape(8, model, dtype=F32),
         ],
-        [pltpu.VMEM((model, LANES), BF16)],
+        [],
         flops=2 * tokens * model * 3 * width,
         spare=6 << 20,
     )
@@ -589,7 +596,7 @@
     operands1 = [
         swap_b, keep1, their_b, swap_h, att, their_h, their_far, grad_mixed, their_mixed,
     ]
-    cut1 = total1 * 9 // 25 // LANES * LANES
+    cut1 = total1 * 21 // 50 // LANES * LANES
     mid = cut1 + (total1 - cut1) // 2 // LANES * LANES
     emit1 = [(GRAD_C, (0, cut1)), (GRAD_A, (cut1, mid)), (GRAD_B, (mid, total1))]
     cfg1 = dict(
@@ -599,7 +606,7 @@
     grad_inputs, swap2, keep2 = call(
         functools.partial(attn_backward_kernel, cfg),
         [
-            inputs, grad_hidden, wo_full, w_full, qkv, att, logt, gain1,
+            inputs, grad_hidden, wo_full, w_full, qkv, att, logt,
             seg_row, seg_col, live_row, cosine, sine, n1,
         ],
         [
@@ -645,7 +652,7 @@
         keep, send = combine(False, keep, exchange(send, Z))
         grad_qkv, gain1_share = call(
             final_qkv_kernel,
-            [keep, exchange(send, ZZ)],
+            [keep, exchange(send, ZZ), gain_col],
             [shape(3, rows, half, dtype=F32), shape(rows, LANES, dtype=F32)],
             [],
             scalars=0,
@@ -656,8 +663,8 @@
             lax.psum_scatter(pieces[0], "dp", scatter_dimension=0, tiled=True)
             for pieces in (pieces1, pieces2)
         )
-        grad_qkv = jnp.stack([share2[:, c * half : (c + 1) * half] for c in range(3)])
-        grad_gain1 = share2[:, 3 * half]
+        grad_qkv = jnp.stack([share2[:, c * half : (c + 1) * half] * gain_col for c in range(3)])
+        grad_gain1 = share2[:, 3 * half] / gain_col[:, 0]
     heads = share1[:, : 2 * main].reshape(rows, 2, main)
     tails = share1[:, 2 * main : 2 * units].reshape(rows, 2, tail)
     grad_in = jnp.concatenate([heads, tails], axis=2)

time: 194 us -> 181 us (0.933)
  starting transfers between devices: 62.7 us -> 46.1 us
    ppermute x36, starting transfers between devices: 58.6 us -> 42.7 us  [exchange(): return lax.ppermute(value, 'dp', pairs)]
    unnamed x30 -> x54, local copies, waits for them, and re-layouts: 3 us -> 6.28 us
    slice x4 -> x0, local copies, waits for them, and re-layouts: 3.15 us -> none  [the longest x2 2.4 us: plane(): far_b = exchange(came_x[2:], Y)]
    pallas_call x20 -> x24, Pallas kernels: 27.6 us -> 29.2 us  [call(): pl.pallas_call(kernel, out_shape=outs, in_specs=[SMEM] * scalars + [VMEM]...]
  transfers between devices with their start and end apart: 55 -> 55, of which waited for: 20 -> 25; matrix products, arithmetic and copies ran while one was open for 7% -> 6% of each run, Pallas kernels for 11% -> 12%
where the time goes in v3:
time: 181 us; the launch traced here: 180 us
  waiting for transfers between devices  81.8 us (45%)
  starting transfers between devices  46.1 us (25%)
  Pallas kernels  29.2 us (16%)
  local copies, waits for them, and re-layouts  12.9 us (7%)
  other arithmetic  8.64 us (5%)
  between operations  1.85 us (1%)
    ppermute x36, waiting for transfers between devices, exchange(): return lax.ppermute(value, 'dp', pairs)  78.6 us
    ppermute x36, starting transfers between devices, exchange(): return lax.ppermute(value, 'dp', pairs)  42.7 us
    pallas_call x24, Pallas kernels, call(): pl.pallas_call(kernel, out_shape=outs, in_specs=[SMEM] * scalars + [VMEM]...  29.2 us
    unnamed x54, local copies, waits for them, and re-layouts  6.28 us
  transfers between devices with their start and end apart: 55, of which 25 were waited for; matrix products, arithmetic and copies ran while one was open for 6% of the time, Pallas kernels for 12%

profile of v3, /device:TPU:0, one launch (start us, length us, event | category | flops | bytes accessed | tf_op | source)
XLA Modules:
  0.0 180.5 jit_solution(2988016943839726965)
XLA Ops:
  1.4 0.9 fusion.4
  2.3 3.1 %collective-permute-start = (bf16[48,1152]{1,0:T(8,128)(2,1)S(1)}, bf16[48,1152]{1,0:T(8,128)(2,1)S(1)}, u32[]{:S(2)}, u32[]{:S(2)}) collective-permute-start(bf16[48,1152]{1,0:T(8,128)(2,1)S(1)} %pad_maximum_fusion.3.refs_0_), channel_id=1, source_target_pairs={{0,8},{2,10},{4,12},{6,14},{8,0},{10,2},{12,4},{14,6},{16,24},{18,... | collective-permute-start | bytes 331784 | tf_op jit(solution)/shard_map/ppermute | solution.py:451
  5.4 2.6 %collective-permute-start.1 = (bf16[48,1152]{1,0:T(8,128)(2,1)S(1)}, bf16[48,1152]{1,0:T(8,128)(2,1)S(1)}, u32[]{:S(2)}, u32[]{:S(2)}) collective-permute-start(bf16[48,1152]{1,0:T(8,128)(2,1)S(1)} %pad_maximum_fusion.3.refs_0_), channel_id=1, source_target_pairs={{0,16},{2,18},{4,20},{6,22},{8,24},{10,26},{12,28},{14,30},{16,0},... | collective-permute-start | bytes 331784 | tf_op jit(solution)/shard_map/ppermute | solution.py:451
  8.0 1.1 fusion.7
  9.2 1.6 collective-permute-start.13
  10.8 1.5 collective-permute-start.12
  12.3 0.9 fusion.6
  13.5 1.5 collective-permute-start.14
  15.8 1.3 collective-permute-start.2
  18.2 2.0 %collective-permute-start.19 = (bf16[48,1536]{1,0:T(8,128)(2,1)S(1)}, bf16[48,1536]{1,0:T(8,128)(2,1)S(1)}, u32[]{:S(2)}, u32[]{:S(2)}) collective-permute-start(bf16[48,1536]{1,0:T(8,128)(2,1)S(1)} %slice.62.refs_0_), channel_id=1, source_target_pairs={{0,16},{2,18},{4,20},{6,22},{8,24},{10,26},{12,28},{14,30},{16,0},... | collective-permute-start | bytes 442376 | tf_op jit(solution)/shard_map/ppermute | solution.py:451
  20.3 1.9 %collective-permute-start.20 = (bf16[48,1536]{1,0:T(8,128)(2,1)S(1)}, bf16[48,1536]{1,0:T(8,128)(2,1)S(1)}, u32[]{:S(2)}, u32[]{:S(2)}) collective-permute-start(bf16[48,1536]{1,0:T(8,128)(2,1)S(1)} %slice.62.refs_0_), channel_id=1, source_target_pairs={{0,24},{2,26},{4,28},{6,30},{8,16},{10,18},{12,20},{14,22},{16,8},... | collective-permute-start | bytes 442376 | tf_op jit(solution)/shard_map/ppermute | solution.py:451
  22.2 2.0 %collective-permute-done.2.refs_3_ = bf16[48,1152]{1,0:T(8,128)(2,1)S(1)} collective-permute-done((bf16[48,1152]{1,0:T(8,128)(2,1)S(1)}, bf16[48,1152]{1,0:T(8,128)(2,1)S(1)}, u32[]{:S(2)}, u32[]{:S(2)}) %collective-permute-start.2) | collective-permute-done | bytes 110624 | tf_op jit(solution)/shard_map/ppermute | solution.py:451
  24.2 1.8 collective-permute-done.18.refs_1_
  25.9 0.8 collective-permute-start.17
  26.8 4.0 %collective-permute-done.19.refs_2_ = bf16[48,1536]{1,0:T(8,128)(2,1)S(1)} collective-permute-done((bf16[48,1536]{1,0:T(8,128)(2,1)S(1)}, bf16[48,1536]{1,0:T(8,128)(2,1)S(1)}, u32[]{:S(2)}, u32[]{:S(2)}) %collective-permute-start.19) | collective-permute-done | bytes 147488 | tf_op jit(solution)/shard_map/ppermute | solution.py:451
  30.8 1.5 collective-permute-start.4
  32.3 3.5 %collective-permute-done.20.refs_3_ = bf16[48,1536]{1,0:T(8,128)(2,1)S(1)} collective-permute-done((bf16[48,1536]{1,0:T(8,128)(2,1)S(1)}, bf16[48,1536]{1,0:T(8,128)(2,1)S(1)}, u32[]{:S(2)}, u32[]{:S(2)}) %collective-permute-start.20) | collective-permute-done | bytes 147488 | tf_op jit(solution)/shard_map/ppermute | solution.py:451
  37.1 15.2 %collective-permute-done.16.refs_7_ = bf16[4,48,640]{2,1,0:T(8,128)(2,1)S(1)} collective-permute-done((bf16[4,48,640]{2,1,0:T(8,128)(2,1)S(1)}, bf16[4,48,640]{2,1,0:T(8,128)(2,1)S(1)}, u32[]{:S(2)}, u32[]{:S(2)}) %collective-permute-start.16) | collective-permute-done | bytes 245792 | tf_op jit(solution)/shard_map/ppermute | solution.py:451
  52.3 1.5 collective-permute-start.22
  56.7 1.5 collective-permute-start.5
  58.9 7.3 %collective-permute-done.22.source.refs_11_ = bf16[4,48,1536]{2,1,0:T(8,128)(2,1)S(1)} collective-permute-done((bf16[4,48,1536]{2,1,0:T(8,128)(2,1)S(1)}, bf16[4,48,1536]{2,1,0:T(8,128)(2,1)S(1)}, u32[]{:S(2)}, u32[]{:S(2)}) %collective-permute-start.22) | collective-permute-done | bytes 589856 | tf_op jit(solution)/shard_map/ppermute | solution.py:451
  67.5 2.4 %collective-permute-done.5.refs_5_ = bf16[2,48,1152]{2,1,0:T(8,128)(2,1)S(1)} collective-permute-done((bf16[2,48,1152]{2,1,0:T(8,128)(2,1)S(1)}, bf16[2,48,1152]{2,1,0:T(8,128)(2,1)S(1)}, u32[]{:S(2)}, u32[]{:S(2)}) %collective-permute-start.5) | collective-permute-done | bytes 221216 | tf_op jit(solution)/shard_map/ppermute | solution.py:451
  70.3 1.3 fusion.5
  71.6 0.7 shard_map.176
  72.3 0.7 shard_map.177
  73.9 0.7 copy-done.19
  74.6 1.6 collective-permute-start.23
  76.9 1.0 collective-permute-start.24
  77.9 0.8 copy-done.5
  78.7 0.8 copy-done.7
  80.6 0.8 copy.42.refs_13_.refs_8_
  81.4 0.8 fusion.1.refs_4_
  82.2 1.6 pad_maximum_fusion.1
  84.3 2.0 %collective-permute-done.24.refs_13_ = bf16[2,48,1536]{2,1,0:T(8,128)(2,1)} collective-permute-done((bf16[2,48,1536]{2,1,0:T(8,128)(2,1)}, bf16[2,48,1536]{2,1,0:T(8,128)(2,1)}, u32[]{:S(2)}, u32[]{:S(2)}) %collective-permute-start.24) | collective-permute-done | bytes 294944 | tf_op jit(solution)/shard_map/ppermute | solution.py:451
  86.2 1.1 multiply_convert_fusion.refs_3_.gm_ref.refs_7_
  87.4 0.9 copy-done.20
  88.4 0.9 copy-done.22
  89.3 5.4 %shard_map.173 = (bf16[768,2304]{1,0:T(8,128)(2,1)S(1)}, bf16[256,2304]{1,0:T(8,128)(2,1)S(1)}, bf16[256,768]{1,0:T(8,128)(2,1)S(1)}, bf16[256,384]{1,0:T(8,128)...) custom-call(s32[1]{0:T(128)} %bitcast.refs_0_.me_ref, bf16[256,768]{1,0:T(8,128)(2,1)S(1)} %copy-done.1, ...), custom_call_target="tpu_custom_call" | custom-call | flops 905969664 | bytes 10030084 | tf_op jit(solution)/shard_map/pallas_call | solution.py:393
  94.8 7.1 %shard_map.178 = (bf16[256,768]{1,0:T(8,128)(2,1)}, f32[256,768]{1,0:T(8,128)S(1)}, f32[8,768]{1,0:T(8,128)S(1)}, bf16[768,768]{1,0:T(8,128)(2,1)S(1)}, bf16[768...) custom-call(s32[1]{0:T(128)} %bitcast.refs_0_.me_ref, ...), custom_call_target="tpu_custom_call" | custom-call | flops 1811939328 | bytes 17196036 | tf_op jit(solution)/shard_map/pallas_call | solution.py:393
  102.4 1.5 shard_map.179
  103.9 7.6 %shard_map.180 = (f32[256,768]{1,0:T(8,128)}, bf16[272,1920]{1,0:T(8,128)(2,1)S(1)}, bf16[256,1152]{1,0:T(8,128)(2,1)S(1)}) custom-call(bf16[256,768]{1,0:T(8,128)(2,1)S(1)} %copy-done.1, f32[256,768]{1,0:T(8,128)S(1)} %get-tuple-element.71.refs_1_, bf16[768,768]{1,0:T(8,128)(2,1)S(1)} %get-tuple-element.72.refs_2_, ...), custom_call_target="tpu_custom_call" | custom-call | flops 1509949440 | bytes 10681344 | tf_op jit(solution)/shard_map/pallas_call | solution.py:393
  112.5 2.8 %collective-permute-done.44.refs_8_ = bf16[256,768]{1,0:T(8,128)(2,1)S(1)} collective-permute-done((bf16[256,768]{1,0:T(8,128)(2,1)S(1)}, bf16[256,768]{1,0:T(8,128)(2,1)S(1)}, u32[]{:S(2)}, u32[]{:S(2)}) %collective-permute-start.44) | collective-permute-done | bytes 393248 | tf_op jit(solution)/shard_map/ppermute | solution.py:447
  115.6 2.6 %shard_map.186 = (bf16[8,48,896]{2,1,0:T(8,128)(2,1)S(1)}, bf16[8,48,896]{2,1,0:T(8,128)(2,1)S(1)}, bf16[8,48,640]{2,1,0:T(8,128)(2,1)S(1)}, bf16[8,48,640]{2,1,...) custom-call(s32[1]{0:T(128)} %bitcast.refs_0_.me_ref, ...), custom_call_target="tpu_custom_call" | custom-call | flops 1711276032 | bytes 9093124 | tf_op jit(solution)/shard_map/pallas_call | solution.py:393
  118.2 5.3 %collective-permute-start.45 = (bf16[8,48,896]{2,1,0:T(8,128)(2,1)S(1)}, bf16[8,48,896]{2,1,0:T(8,128)(2,1)S(1)}, u32[]{:S(2)}, u32[]{:S(2)}) collective-permute-start(bf16[8,48,896]{2,1,0:T(8,128)(2,1)S(1)} %get-tuple-element.99), channel_id=1, source_target_pairs={{0,8},{2,10},{4,12},{6,14},{8,0},{10,2},{12,4},{14,6},{16,24},{18,... | collective-permute-start | bytes 2064392 | tf_op jit(solution)/shard_map/ppermute | solution.py:451
  123.5 1.4 shard_map.181
  125.3 1.2 collective-permute-start.36
  126.4 0.9 collective-permute-start.49
  127.3 1.7 collective-permute-start.50
  129.0 10.0 %collective-permute-done.35.refs_1_ = bf16[8,48,640]{2,1,0:T(8,128)(2,1)S(1)} collective-permute-done((bf16[8,48,640]{2,1,0:T(8,128)(2,1)S(1)}, bf16[8,48,640]{2,1,0:T(8,128)(2,1)S(1)}, u32[]{:S(2)}, u32[]{:S(2)}) %collective-permute-start.35) | collective-permute-done | bytes 491552 | tf_op jit(solution)/shard_map/ppermute | solution.py:451
  139.8 1.2 collective-permute-start.37
  141.0 0.9 collective-permute-start.38
  142.1 7.5 %collective-permute-done.49.refs_1_ = bf16[8,48,640]{2,1,0:T(8,128)(2,1)S(1)} collective-permute-done((bf16[8,48,640]{2,1,0:T(8,128)(2,1)S(1)}, bf16[8,48,640]{2,1,0:T(8,128)(2,1)S(1)}, u32[]{:S(2)}, u32[]{:S(2)}) %collective-permute-start.49) | collective-permute-done | bytes 491552 | tf_op jit(solution)/shard_map/ppermute | solution.py:451
  150.1 1.2 collective-permute-start.51
  151.4 0.9 collective-permute-start.52
  152.2 2.9 %collective-permute-done.37.refs_1_ = bf16[4,48,640]{2,1,0:T(8,128)(2,1)S(1)} collective-permute-done((bf16[4,48,640]{2,1,0:T(8,128)(2,1)S(1)}, bf16[4,48,640]{2,1,0:T(8,128)(2,1)S(1)}, u32[]{:S(2)}, u32[]{:S(2)}) %collective-permute-start.37) | collective-permute-done | bytes 245792 | tf_op jit(solution)/shard_map/ppermute | solution.py:451
  155.3 3.8 %collective-permute-done.51.refs_1_ = bf16[4,48,640]{2,1,0:T(8,128)(2,1)S(1)} collective-permute-done((bf16[4,48,640]{2,1,0:T(8,128)(2,1)S(1)}, bf16[4,48,640]{2,1,0:T(8,128)(2,1)S(1)}, u32[]{:S(2)}, u32[]{:S(2)}) %collective-permute-start.51) | collective-permute-done | bytes 245792 | tf_op jit(solution)/shard_map/ppermute | solution.py:451
  159.7 1.7 collective-permute-start.47
  161.4 2.8 %collective-permute-done.39.refs_1_ = bf16[2,48,1280]{2,1,0:T(8,128)(2,1)S(1)} collective-permute-done((bf16[2,48,1280]{2,1,0:T(8,128)(2,1)S(1)}, bf16[2,48,1280]{2,1,0:T(8,128)(2,1)S(1)}, u32[]{:S(2)}, u32[]{:S(2)}) %collective-permute-start.39) | collective-permute-done | bytes 245792 | tf_op jit(solution)/shard_map/ppermute | solution.py:451
  164.3 4.8 %collective-permute-done.53.refs_1_ = bf16[2,48,1280]{2,1,0:T(8,128)(2,1)S(1)} collective-permute-done((bf16[2,48,1280]{2,1,0:T(8,128)(2,1)S(1)}, bf16[2,48,1280]{2,1,0:T(8,128)(2,1)S(1)}, u32[]{:S(2)}, u32[]{:S(2)}) %collective-permute-start.53) | collective-permute-done | bytes 245792 | tf_op jit(solution)/shard_map/ppermute | solution.py:451
  169.3 2.6 %collective-permute-done.40.came = bf16[1,48,1280]{2,1,0:T(8,128)(2,1)S(1)} collective-permute-done((bf16[1,48,1280]{2,1,0:T(8,128)(2,1)S(1)}, bf16[1,48,1280]{2,1,0:T(8,128)(2,1)S(1)}, u32[]{:S(2)}, u32[]{:S(2)}) %collective-permute-start.40) | collective-permute-done | bytes 122912 | tf_op jit(solution)/shard_map/ppermute | solution.py:451
  172.0 0.8 shard_map.185
  173.8 1.9 %collective-permute-done.54.came_ab = bf16[1,48,1280]{2,1,0:T(8,128)(2,1)S(1)} collective-permute-done((bf16[1,48,1280]{2,1,0:T(8,128)(2,1)S(1)}, bf16[1,48,1280]{2,1,0:T(8,128)(2,1)S(1)}, u32[]{:S(2)}, u32[]{:S(2)}) %collective-permute-start.54) | collective-permute-done | bytes 122912 | tf_op jit(solution)/shard_map/ppermute | solution.py:451
  175.6 1.7 collective-permute-done.48.came_c
  179.7 0.8 pad_maximum_fusion
  (159 shorter events, 20.1 us)
Async XLA Ops:
  0.6 53.8 %copy-start = (s32[2,256]{1,0:T(2,128)S(1)}, s32[2,256]{1,0:T(2,128)}, u32[]{:S(2)}) copy-start(s32[2,256]{1,0:T(2,128)} %param.19) | copy-start | bytes 6148
  0.6 14.3 %copy-start.25 = (bf16[48]{0:T(256)(128)(2,1)S(1)}, bf16[48]{0:T(256)(128)(2,1)}, u32[]{:S(2)}) copy-start(bf16[48]{0:T(256)(128)(2,1)} %param.15) | copy-start | bytes 292
  0.7 14.4 %copy-start.24 = (bf16[384,48]{0,1:T(8,128)(2,1)S(1)}, bf16[384,48]{0,1:T(8,128)(2,1)}, u32[]{:S(2)}) copy-start(bf16[384,48]{0,1:T(8,128)(2,1)} %param.14) | copy-start | bytes 110596
  0.7 14.4 %copy-start.23 = (bf16[576,48]{0,1:T(8,128)(2,1)S(1)}, bf16[576,48]{0,1:T(8,128)(2,1)}, u32[]{:S(2)}) copy-start(bf16[576,48]{0,1:T(8,128)(2,1)} %param.17) | copy-start | bytes 165892
  2.3 16.0 %collective-permute-start = (bf16[48,1152]{1,0:T(8,128)(2,1)S(1)}, bf16[48,1152]{1,0:T(8,128)(2,1)S(1)}, u32[]{:S(2)}, u32[]{:S(2)}) collective-permute-start(bf16[48,1152]{1,0:T(8,128)(2,1)S(1)} %pad_maximum_fusion.3.refs_0_), channel_id=1, source_target_pairs={{0,8},{2,10},{4,12},{6,14},{8,0},{10,2},{12,4},{14,6},{16,24},{18,... | collective-permute-start | bytes 331784 | tf_op jit(solution)/shard_map/ppermute | solution.py:451
  5.4 14.9 %collective-permute-start.1 = (bf16[48,1152]{1,0:T(8,128)(2,1)S(1)}, bf16[48,1152]{1,0:T(8,128)(2,1)S(1)}, u32[]{:S(2)}, u32[]{:S(2)}) collective-permute-start(bf16[48,1152]{1,0:T(8,128)(2,1)S(1)} %pad_maximum_fusion.3.refs_0_), channel_id=1, source_target_pairs={{0,16},{2,18},{4,20},{6,22},{8,24},{10,26},{12,28},{14,30},{16,0},... | collective-permute-start | bytes 331784 | tf_op jit(solution)/shard_map/ppermute | solution.py:451
  9.2 4.3 %collective-permute-start.13 = (bf16[48,640]{1,0:T(8,128)(2,1)S(1)}, bf16[48,640]{1,0:T(8,128)(2,1)S(1)}, u32[]{:S(2)}, u32[]{:S(2)}) collective-permute-start(bf16[48,640]{1,0:T(8,128)(2,1)S(1)} %pad_maximum_fusion.4.refs_0_), channel_id=1, source_target_pairs={{0,4},{2,6},{4,0},{6,2},{8,12},{10,14},{12,8},{14,10},{16,20},{18,... | collective-permute-start | bytes 184328 | tf_op jit(solution)/shard_map/ppermute | solution.py:451
  10.8 5.0 %collective-permute-start.12 = (bf16[48,640]{1,0:T(8,128)(2,1)S(1)}, bf16[48,640]{1,0:T(8,128)(2,1)S(1)}, u32[]{:S(2)}, u32[]{:S(2)}) collective-permute-start(bf16[48,640]{1,0:T(8,128)(2,1)S(1)} %pad_maximum_fusion.4.refs_0_), channel_id=1, source_target_pairs={{0,2},{2,0},{4,6},{6,4},{8,10},{10,8},{12,14},{14,12},{16,18},{18,... | collective-permute-start | bytes 184328 | tf_op jit(solution)/shard_map/ppermute | solution.py:451
  13.5 4.2 %collective-permute-start.14 = (bf16[48,640]{1,0:T(8,128)(2,1)S(1)}, bf16[48,640]{1,0:T(8,128)(2,1)S(1)}, u32[]{:S(2)}, u32[]{:S(2)}) collective-permute-start(bf16[48,640]{1,0:T(8,128)(2,1)S(1)} %collective-permute-done.13.refs_2_), channel_id=1, source_target_pairs={{0,2},{2,0},{4,6},{6,4},{8,10},{10,8},{12,14},{14,12},{16,18},{18,... | collective-permute-start | bytes 184328 | tf_op jit(solution)/shard_map/ppermute | solution.py:451
  15.2 40.1 %copy-start.26 = (s32[2]{0:T(128)S(1)}, s32[2]{0:T(128)}, u32[]{:S(2)}) copy-start(s32[2]{0:T(128)} %param.20) | copy-start | bytes 28
  15.2 10.7 %collective-permute-start.18 = (bf16[48,1536]{1,0:T(8,128)(2,1)S(1)}, bf16[48,1536]{1,0:T(8,128)(2,1)S(1)}, u32[]{:S(2)}, u32[]{:S(2)}) collective-permute-start(bf16[48,1536]{1,0:T(8,128)(2,1)S(1)} %slice.62.refs_0_), channel_id=1, source_target_pairs={{0,8},{2,10},{4,12},{6,14},{8,0},{10,2},{12,4},{14,6},{16,24},{18,... | collective-permute-start | bytes 442376 | tf_op jit(solution)/shard_map/ppermute | solution.py:451
  15.8 8.4 %collective-permute-start.2 = (bf16[48,1152]{1,0:T(8,128)(2,1)S(1)}, bf16[48,1152]{1,0:T(8,128)(2,1)S(1)}, u32[]{:S(2)}, u32[]{:S(2)}) collective-permute-start(bf16[48,1152]{1,0:T(8,128)(2,1)S(1)} %pad_maximum_fusion.3.refs_0_), channel_id=1, source_target_pairs={{0,24},{2,26},{4,28},{6,30},{8,16},{10,18},{12,20},{14,22},{16,8},... | collective-permute-start | bytes 331784 | tf_op jit(solution)/shard_map/ppermute | solution.py:451
  17.7 38.9 %copy-start.3 = (bf16[4,48,640]{2,1,0:T(8,128)(2,1)}, bf16[4,48,640]{2,1,0:T(8,128)(2,1)S(1)}, u32[]{:S(2)}) copy-start(bf16[4,48,640]{2,1,0:T(8,128)(2,1)S(1)} %shard_map.174.refs_5_) | copy-start | bytes 737284
  17.7 18.7 %collective-permute-start.15 = (bf16[4,48,640]{2,1,0:T(8,128)(2,1)S(1)}, bf16[4,48,640]{2,1,0:T(8,128)(2,1)S(1)}, u32[]{:S(2)}, u32[]{:S(2)}) collective-permute-start(bf16[4,48,640]{2,1,0:T(8,128)(2,1)S(1)} %shard_map.174.refs_5_), channel_id=1, source_target_pairs={{0,8},{2,10},{4,12},{6,14},{8,0},{10,2},{12,4},{14,6},{16,24},{18,... | collective-permute-start | bytes 737288 | tf_op jit(solution)/shard_map/ppermute | solution.py:451
  18.2 12.5 %collective-permute-start.19 = (bf16[48,1536]{1,0:T(8,128)(2,1)S(1)}, bf16[48,1536]{1,0:T(8,128)(2,1)S(1)}, u32[]{:S(2)}, u32[]{:S(2)}) collective-permute-start(bf16[48,1536]{1,0:T(8,128)(2,1)S(1)} %slice.62.refs_0_), channel_id=1, source_target_pairs={{0,16},{2,18},{4,20},{6,22},{8,24},{10,26},{12,28},{14,30},{16,0},... | collective-permute-start | bytes 442376 | tf_op jit(solution)/shard_map/ppermute | solution.py:451
  20.3 15.6 %collective-permute-start.20 = (bf16[48,1536]{1,0:T(8,128)(2,1)S(1)}, bf16[48,1536]{1,0:T(8,128)(2,1)S(1)}, u32[]{:S(2)}, u32[]{:S(2)}) collective-permute-start(bf16[48,1536]{1,0:T(8,128)(2,1)S(1)} %slice.62.refs_0_), channel_id=1, source_target_pairs={{0,24},{2,26},{4,28},{6,30},{8,16},{10,18},{12,20},{14,22},{16,8},... | collective-permute-start | bytes 442376 | tf_op jit(solution)/shard_map/ppermute | solution.py:451
  24.2 28.2 %collective-permute-start.16 = (bf16[4,48,640]{2,1,0:T(8,128)(2,1)S(1)}, bf16[4,48,640]{2,1,0:T(8,128)(2,1)S(1)}, u32[]{:S(2)}, u32[]{:S(2)}) collective-permute-start(bf16[4,48,640]{2,1,0:T(8,128)(2,1)S(1)} %shard_map.174.refs_5_), channel_id=1, source_target_pairs={{0,16},{2,18},{4,20},{6,22},{8,24},{10,26},{12,28},{14,30},{16,0},... | collective-permute-start | bytes 737288 | tf_op jit(solution)/shard_map/ppermute | solution.py:451
  25.9 27.9 %collective-permute-start.17 = (bf16[4,48,640]{2,1,0:T(8,128)(2,1)S(1)}, bf16[4,48,640]{2,1,0:T(8,128)(2,1)}, u32[]{:S(2)}, u32[]{:S(2)}) collective-permute-start(bf16[4,48,640]{2,1,0:T(8,128)(2,1)S(1)} %shard_map.174.refs_5_), channel_id=1, source_target_pairs={{0,24},{2,26},{4,28},{6,30},{8,16},{10,18},{12,20},{14,22},{16,8},... | collective-permute-start | bytes 737288 | tf_op jit(solution)/shard_map/ppermute | solution.py:451
  30.8 23.9 %collective-permute-start.4 = (bf16[4,48,1152]{2,1,0:T(8,128)(2,1)S(1)}, bf16[4,48,1152]{2,1,0:T(8,128)(2,1)S(1)}, u32[]{:S(2)}, u32[]{:S(2)}) collective-permute-start(bf16[4,48,1152]{2,1,0:T(8,128)(2,1)S(1)} %shard_map.170.refs_2_), channel_id=1, source_target_pairs={{0,4},{2,6},{4,0},{6,2},{8,12},{10,14},{12,8},{14,10},{16,20},{18,... | collective-permute-start | bytes 1327112 | tf_op jit(solution)/shard_map/ppermute | solution.py:451
  35.9 19.4 %collective-permute-start.3 = (bf16[4,48,1152]{2,1,0:T(8,128)(2,1)S(1)}, bf16[4,48,1152]{2,1,0:T(8,128)(2,1)S(1)}, u32[]{:S(2)}, u32[]{:S(2)}) collective-permute-start(bf16[4,48,1152]{2,1,0:T(8,128)(2,1)S(1)} %shard_map.170.refs_2_), channel_id=1, source_target_pairs={{0,2},{2,0},{4,6},{6,4},{8,10},{10,8},{12,14},{14,12},{16,18},{18,... | collective-permute-start | bytes 1327112 | tf_op jit(solution)/shard_map/ppermute | solution.py:451
  37.1 17.3 %collective-permute-start.25 = (bf16[4,48,640]{2,1,0:T(8,128)(2,1)S(1)}, bf16[4,48,640]{2,1,0:T(8,128)(2,1)}, u32[]{:S(2)}, u32[]{:S(2)}) collective-permute-start(bf16[4,48,640]{2,1,0:T(8,128)(2,1)S(1)} %shard_map.174.refs_5_), channel_id=1, source_target_pairs={{0,1},{1,0},{2,3},{3,2},{4,5},{5,4},{6,7},{7,6},{8,9},{9,8},{10,11... | collective-permute-start | bytes 737288 | tf_op jit(solution)/shard_map/ppermute | solution.py:447
  52.3 13.9 %collective-permute-start.22 = (bf16[4,48,1536]{2,1,0:T(8,128)(2,1)S(1)}, bf16[4,48,1536]{2,1,0:T(8,128)(2,1)S(1)}, u32[]{:S(2)}, u32[]{:S(2)}) collective-permute-start(bf16[4,48,1536]{2,1,0:T(8,128)(2,1)S(1)} %shard_map.175.refs_9_), channel_id=1, source_target_pairs={{0,4},{2,6},{4,0},{6,2},{8,12},{10,14},{12,8},{14,10},{16,20},{18,... | collective-permute-start | bytes 1769480 | tf_op jit(solution)/shard_map/ppermute | solution.py:451
  53.8 13.6 %collective-permute-start.21 = (bf16[4,48,1536]{2,1,0:T(8,128)(2,1)S(1)}, bf16[4,48,1536]{2,1,0:T(8,128)(2,1)S(1)}, u32[]{:S(2)}, u32[]{:S(2)}) collective-permute-start(bf16[4,48,1536]{2,1,0:T(8,128)(2,1)S(1)} %shard_map.175.refs_9_), channel_id=1, source_target_pairs={{0,2},{2,0},{4,6},{6,4},{8,10},{10,8},{12,14},{14,12},{16,18},{18,... | collective-permute-start | bytes 1769480 | tf_op jit(solution)/shard_map/ppermute | solution.py:451
  54.4 2.2 %collective-permute-start.7 = (bf16[4,48,1152]{2,1,0:T(8,128)(2,1)S(1)}, bf16[4,48,1152]{2,1,0:T(8,128)(2,1)}, u32[]{:S(2)}, u32[]{:S(2)}) collective-permute-start(bf16[4,48,1152]{2,1,0:T(8,128)(2,1)S(1)} %shard_map.170.refs_2_), channel_id=1, source_target_pairs={{0,1},{1,0},{2,3},{3,2},{4,5},{5,4},{6,7},{7,6},{8,9},{9,8},{10,11... | collective-permute-start | bytes 1327112 | tf_op jit(solution)/shard_map/ppermute | solution.py:447
  54.7 3.5 %collective-permute-start.26 = (bf16[4,48,640]{2,1,0:T(8,128)(2,1)}, bf16[4,48,640]{2,1,0:T(8,128)(2,1)}, u32[]{:S(2)}, u32[]{:S(2)}) collective-permute-start(bf16[4,48,640]{2,1,0:T(8,128)(2,1)} %copy-done.9), channel_id=1, source_target_pairs={{0,1},{1,0},{2,3},{3,2},{4,5},{5,4},{6,7},{7,6},{8,9},{9,8},{10,11... | collective-permute-start | bytes 737288 | tf_op jit(solution)/shard_map/ppermute | solution.py:447
  55.3 3.7 %collective-permute-start.27 = (bf16[4,48,640]{2,1,0:T(8,128)(2,1)}, bf16[4,48,640]{2,1,0:T(8,128)(2,1)}, u32[]{:S(2)}, u32[]{:S(2)}) collective-permute-start(bf16[4,48,640]{2,1,0:T(8,128)(2,1)} %copy-done.11), channel_id=1, source_target_pairs={{0,1},{1,0},{2,3},{3,2},{4,5},{5,4},{6,7},{7,6},{8,9},{9,8},{10,11... | collective-permute-start | bytes 737288 | tf_op jit(solution)/shard_map/ppermute | solution.py:447
  56.7 13.1 %collective-permute-start.5 = (bf16[2,48,1152]{2,1,0:T(8,128)(2,1)S(1)}, bf16[2,48,1152]{2,1,0:T(8,128)(2,1)S(1)}, u32[]{:S(2)}, u32[]{:S(2)}) collective-permute-start(bf16[2,48,1152]{2,1,0:T(8,128)(2,1)S(1)} %shard_map.171), channel_id=1, source_target_pairs={{0,2},{2,0},{4,6},{6,4},{8,10},{10,8},{12,14},{14,12},{16,18},{18,... | collective-permute-start | bytes 663560 | tf_op jit(solution)/shard_map/ppermute | solution.py:451
  58.2 11.6 %collective-permute-start.6 = (bf16[2,48,1152]{2,1,0:T(8,128)(2,1)S(1)}, bf16[2,48,1152]{2,1,0:T(8,128)(2,1)S(1)}, u32[]{:S(2)}, u32[]{:S(2)}) collective-permute-start(bf16[2,48,1152]{2,1,0:T(8,128)(2,1)S(1)} %shard_map.172), channel_id=1, source_target_pairs={{0,4},{2,6},{4,0},{6,2},{8,12},{10,14},{12,8},{14,10},{16,20},{18,... | collective-permute-start | bytes 663560 | tf_op jit(solution)/shard_map/ppermute | solution.py:451
  58.9 19.0 %collective-permute-start.8 = (bf16[4,48,1152]{2,1,0:T(8,128)(2,1)S(1)}, bf16[4,48,1152]{2,1,0:T(8,128)(2,1)S(1)}, u32[]{:S(2)}, u32[]{:S(2)}) collective-permute-start(bf16[4,48,1152]{2,1,0:T(8,128)(2,1)S(1)} %collective-permute-done.3.source.refs_3_), channel_id=1, source_target_pairs={{0,1},{1,0},{2,3},{3,2},{4,5},{5,4},{6,7},{7,6},{8,9},{9,8},{10,11... | collective-permute-start | bytes 1327112 | tf_op jit(solution)/shard_map/ppermute | solution.py:447
  66.2 12.5 %collective-permute-start.9 = (bf16[4,48,1152]{2,1,0:T(8,128)(2,1)S(1)}, bf16[4,48,1152]{2,1,0:T(8,128)(2,1)S(1)}, u32[]{:S(2)}, u32[]{:S(2)}) collective-permute-start(bf16[4,48,1152]{2,1,0:T(8,128)(2,1)S(1)} %collective-permute-done.4.source.refs_4_), channel_id=1, source_target_pairs={{0,1},{1,0},{2,3},{3,2},{4,5},{5,4},{6,7},{7,6},{8,9},{9,8},{10,11... | collective-permute-start | bytes 1327112 | tf_op jit(solution)/shard_map/ppermute | solution.py:447
  67.4 5.6 %collective-permute-start.28 = (bf16[4,48,640]{2,1,0:T(8,128)(2,1)}, bf16[4,48,640]{2,1,0:T(8,128)(2,1)S(1)}, u32[]{:S(2)}, u32[]{:S(2)}) collective-permute-start(bf16[4,48,640]{2,1,0:T(8,128)(2,1)} %collective-permute-done.17.refs_8_), channel_id=1, source_target_pairs={{0,1},{1,0},{2,3},{3,2},{4,5},{5,4},{6,7},{7,6},{8,9},{9,8},{10,11... | collective-permute-start | bytes 737288 | tf_op jit(solution)/shard_map/ppermute | solution.py:447
  69.8 8.9 %copy-start.15 = (bf16[2,48,1152]{2,1,0:T(8,128)(2,1)}, bf16[2,48,1152]{2,1,0:T(8,128)(2,1)S(1)}, u32[]{:S(2)}) copy-start(bf16[2,48,1152]{2,1,0:T(8,128)(2,1)S(1)} %collective-permute-done.5.refs_5_) | copy-start | bytes 663556
  69.8 4.1 %collective-permute-start.10 = (bf16[2,48,1152]{2,1,0:T(8,128)(2,1)S(1)}, bf16[2,48,1152]{2,1,0:T(8,128)(2,1)S(1)}, u32[]{:S(2)}, u32[]{:S(2)}) collective-permute-start(bf16[2,48,1152]{2,1,0:T(8,128)(2,1)S(1)} %collective-permute-done.5.refs_5_), channel_id=1, source_target_pairs={{0,1},{1,0},{2,3},{3,2},{4,5},{5,4},{6,7},{7,6},{8,9},{9,8},{10,11... | collective-permute-start | bytes 663560 | tf_op jit(solution)/shard_map/ppermute | solution.py:447
  69.8 10.1 %copy-start.17 = (bf16[2,48,1152]{2,1,0:T(8,128)(2,1)}, bf16[2,48,1152]{2,1,0:T(8,128)(2,1)S(1)}, u32[]{:S(2)}) copy-start(bf16[2,48,1152]{2,1,0:T(8,128)(2,1)S(1)} %collective-permute-done.6.refs_6_) | copy-start | bytes 663556
  69.8 6.3 %collective-permute-start.11 = (bf16[2,48,1152]{2,1,0:T(8,128)(2,1)S(1)}, bf16[2,48,1152]{2,1,0:T(8,128)(2,1)S(1)}, u32[]{:S(2)}, u32[]{:S(2)}) collective-permute-start(bf16[2,48,1152]{2,1,0:T(8,128)(2,1)S(1)} %collective-permute-done.6.refs_6_), channel_id=1, source_target_pairs={{0,1},{1,0},{2,3},{3,2},{4,5},{5,4},{6,7},{7,6},{8,9},{9,8},{10,11... | collective-permute-start | bytes 663560 | tf_op jit(solution)/shard_map/ppermute | solution.py:447
  72.3 15.0 %copy-start.1 = (bf16[256,768]{1,0:T(8,128)(2,1)S(1)}, bf16[256,768]{1,0:T(8,128)(2,1)}, u32[]{:S(2)}) copy-start(bf16[256,768]{1,0:T(8,128)(2,1)} %refs_0_.1) | copy-start | bytes 1179652
  73.8 20.9 %collective-permute-start.29 = (bf16[4,48,1536]{2,1,0:T(8,128)(2,1)S(1)}, bf16[4,48,1536]{2,1,0:T(8,128)(2,1)}, u32[]{:S(2)}, u32[]{:S(2)}) collective-permute-start(bf16[4,48,1536]{2,1,0:T(8,128)(2,1)S(1)} %shard_map.175.refs_9_), channel_id=1, source_target_pairs={{0,1},{1,0},{2,3},{3,2},{4,5},{5,4},{6,7},{7,6},{8,9},{9,8},{10,11... | collective-permute-start | bytes 1769480 | tf_op jit(solution)/shard_map/ppermute | solution.py:447
  74.6 9.7 %collective-permute-start.23 = (bf16[2,48,1536]{2,1,0:T(8,128)(2,1)}, bf16[2,48,1536]{2,1,0:T(8,128)(2,1)}, u32[]{:S(2)}, u32[]{:S(2)}) collective-permute-start(bf16[2,48,1536]{2,1,0:T(8,128)(2,1)} %shard_map.176), channel_id=1, source_target_pairs={{0,2},{2,0},{4,6},{6,4},{8,10},{10,8},{12,14},{14,12},{16,18},{18,... | collective-permute-start | bytes 884744 | tf_op jit(solution)/shard_map/ppermute | solution.py:451
  76.9 9.4 %collective-permute-start.24 = (bf16[2,48,1536]{2,1,0:T(8,128)(2,1)}, bf16[2,48,1536]{2,1,0:T(8,128)(2,1)}, u32[]{:S(2)}, u32[]{:S(2)}) collective-permute-start(bf16[2,48,1536]{2,1,0:T(8,128)(2,1)} %shard_map.177), channel_id=1, source_target_pairs={{0,4},{2,6},{4,0},{6,2},{8,12},{10,14},{12,8},{14,10},{16,20},{18,... | collective-permute-start | bytes 884744 | tf_op jit(solution)/shard_map/ppermute | solution.py:451
  78.7 16.0 %collective-permute-start.30 = (bf16[4,48,1536]{2,1,0:T(8,128)(2,1)S(1)}, bf16[4,48,1536]{2,1,0:T(8,128)(2,1)}, u32[]{:S(2)}, u32[]{:S(2)}) collective-permute-start(bf16[4,48,1536]{2,1,0:T(8,128)(2,1)S(1)} %collective-permute-done.21.source.refs_10_), channel_id=1, source_target_pairs={{0,1},{1,0},{2,3},{3,2},{4,5},{5,4},{6,7},{7,6},{8,9},{9,8},{10,11... | collective-permute-start | bytes 1769480 | tf_op jit(solution)/shard_map/ppermute | solution.py:447
  79.4 15.3 %collective-permute-start.31 = (bf16[4,48,1536]{2,1,0:T(8,128)(2,1)S(1)}, bf16[4,48,1536]{2,1,0:T(8,128)(2,1)}, u32[]{:S(2)}, u32[]{:S(2)}) collective-permute-start(bf16[4,48,1536]{2,1,0:T(8,128)(2,1)S(1)} %collective-permute-done.22.source.refs_11_), channel_id=1, source_target_pairs={{0,1},{1,0},{2,3},{3,2},{4,5},{5,4},{6,7},{7,6},{8,9},{9,8},{10,11... | collective-permute-start | bytes 1769480 | tf_op jit(solution)/shard_map/ppermute | solution.py:447
  84.3 10.5 %collective-permute-start.32 = (bf16[2,48,1536]{2,1,0:T(8,128)(2,1)}, bf16[2,48,1536]{2,1,0:T(8,128)(2,1)S(1)}, u32[]{:S(2)}, u32[]{:S(2)}) collective-permute-start(bf16[2,48,1536]{2,1,0:T(8,128)(2,1)} %collective-permute-done.23.refs_12_), channel_id=1, source_target_pairs={{0,1},{1,0},{2,3},{3,2},{4,5},{5,4},{6,7},{7,6},{8,9},{9,8},{10,11... | collective-permute-start | bytes 884744 | tf_op jit(solution)/shard_map/ppermute | solution.py:447
  86.2 8.5 %collective-permute-start.33 = (bf16[2,48,1536]{2,1,0:T(8,128)(2,1)}, bf16[2,48,1536]{2,1,0:T(8,128)(2,1)S(1)}, u32[]{:S(2)}, u32[]{:S(2)}) collective-permute-start(bf16[2,48,1536]{2,1,0:T(8,128)(2,1)} %collective-permute-done.24.refs_13_), channel_id=1, source_target_pairs={{0,1},{1,0},{2,3},{3,2},{4,5},{5,4},{6,7},{7,6},{8,9},{9,8},{10,11... | collective-permute-start | bytes 884744 | tf_op jit(solution)/shard_map/ppermute | solution.py:447
  101.9 13.7 %collective-permute-start.41 = (bf16[256,2560]{1,0:T(8,128)(2,1)S(1)}, bf16[256,2560]{1,0:T(8,128)(2,1)S(1)}, u32[]{:S(2)}, u32[]{:S(2)}) collective-permute-start(bf16[256,2560]{1,0:T(8,128)(2,1)S(1)} %get-tuple-element.94.refs_0_), channel_id=1, source_target_pairs={{0,1},{1,0},{2,3},{3,2},{4,5},{5,4},{6,7},{7,6},{8,9},{9,8},{10,11... | collective-permute-start | bytes 3932168 | tf_op jit(solution)/shard_map/ppermute | solution.py:447
  111.5 12.0 %collective-permute-start.34 = (bf16[272,1920]{1,0:T(8,128)(2,1)S(1)}, bf16[272,1920]{1,0:T(8,128)(2,1)S(1)}, u32[]{:S(2)}, u32[]{:S(2)}) collective-permute-start(bf16[272,1920]{1,0:T(8,128)(2,1)S(1)} %get-tuple-element.78.refs_0_), channel_id=1, source_target_pairs={{0,1},{1,0},{2,3},{3,2},{4,5},{5,4},{6,7},{7,6},{8,9},{9,8},{10,11... | collective-permute-start | bytes 3133448 | tf_op jit(solution)/shard_map/ppermute | solution.py:447
  111.5 4.1 %collective-permute-start.42 = (bf16[272,768]{1,0:T(8,128)(2,1)S(1)}, bf16[272,768]{1,0:T(8,128)(2,1)S(1)}, u32[]{:S(2)}, u32[]{:S(2)}) collective-permute-start(bf16[272,768]{1,0:T(8,128)(2,1)S(1)} %get-tuple-element.96.refs_3_), channel_id=1, source_target_pairs={{0,1},{1,0},{2,3},{3,2},{4,5},{5,4},{6,7},{7,6},{8,9},{9,8},{10,11... | collective-permute-start | bytes 1253384 | tf_op jit(solution)/shard_map/ppermute | solution.py:447
  112.0 3.3 %collective-permute-start.44 = (bf16[256,768]{1,0:T(8,128)(2,1)S(1)}, bf16[256,768]{1,0:T(8,128)(2,1)S(1)}, u32[]{:S(2)}, u32[]{:S(2)}) collective-permute-start(bf16[256,768]{1,0:T(8,128)(2,1)S(1)} %multiply_convert_fusion.refs_3_.gm_ref.refs_7_), channel_id=1, source_target_pairs={{0,1},{1,0},{2,3},{3,2},{4,5},{5,4},{6,7},{7,6},{8,9},{9,8},{10,11... | collective-permute-start | bytes 1179656 | tf_op jit(solution)/shard_map/ppermute | solution.py:447
  112.0 3.6 %collective-permute-start.43 = (bf16[256,384]{1,0:T(8,128)(2,1)S(1)}, bf16[256,384]{1,0:T(8,128)(2,1)S(1)}, u32[]{:S(2)}, u32[]{:S(2)}) collective-permute-start(bf16[256,384]{1,0:T(8,128)(2,1)S(1)} %get-tuple-element.97), channel_id=1, source_target_pairs={{0,1},{1,0},{2,3},{3,2},{4,5},{5,4},{6,7},{7,6},{8,9},{9,8},{10,11... | collective-permute-start | bytes 589832 | tf_op jit(solution)/shard_map/ppermute | solution.py:447
  118.2 23.7 %collective-permute-start.45 = (bf16[8,48,896]{2,1,0:T(8,128)(2,1)S(1)}, bf16[8,48,896]{2,1,0:T(8,128)(2,1)S(1)}, u32[]{:S(2)}, u32[]{:S(2)}) collective-permute-start(bf16[8,48,896]{2,1,0:T(8,128)(2,1)S(1)} %get-tuple-element.99), channel_id=1, source_target_pairs={{0,8},{2,10},{4,12},{6,14},{8,0},{10,2},{12,4},{14,6},{16,24},{18,... | collective-permute-start | bytes 2064392 | tf_op jit(solution)/shard_map/ppermute | solution.py:451
  124.9 14.2 %collective-permute-start.35 = (bf16[8,48,640]{2,1,0:T(8,128)(2,1)S(1)}, bf16[8,48,640]{2,1,0:T(8,128)(2,1)S(1)}, u32[]{:S(2)}, u32[]{:S(2)}) collective-permute-start(bf16[8,48,640]{2,1,0:T(8,128)(2,1)S(1)} %get-tuple-element.81), channel_id=1, source_target_pairs={{0,2},{2,0},{4,6},{6,4},{8,10},{10,8},{12,14},{14,12},{16,18},{18,... | collective-permute-start | bytes 1474568 | tf_op jit(solution)/shard_map/ppermute | solution.py:451
  125.3 14.1 %collective-permute-start.36 = (bf16[8,48,640]{2,1,0:T(8,128)(2,1)S(1)}, bf16[8,48,640]{2,1,0:T(8,128)(2,1)S(1)}, u32[]{:S(2)}, u32[]{:S(2)}) collective-permute-start(bf16[8,48,640]{2,1,0:T(8,128)(2,1)S(1)} %get-tuple-element.83), channel_id=1, source_target_pairs={{0,4},{2,6},{4,0},{6,2},{8,12},{10,14},{12,8},{14,10},{16,20},{18,... | collective-permute-start | bytes 1474568 | tf_op jit(solution)/shard_map/ppermute | solution.py:451
  126.4 23.2 %collective-permute-start.49 = (bf16[8,48,640]{2,1,0:T(8,128)(2,1)S(1)}, bf16[8,48,640]{2,1,0:T(8,128)(2,1)S(1)}, u32[]{:S(2)}, u32[]{:S(2)}) collective-permute-start(bf16[8,48,640]{2,1,0:T(8,128)(2,1)S(1)} %get-tuple-element.107), channel_id=1, source_target_pairs={{0,2},{2,0},{4,6},{6,4},{8,10},{10,8},{12,14},{14,12},{16,18},{18,... | collective-permute-start | bytes 1474568 | tf_op jit(solution)/shard_map/ppermute | solution.py:451
  127.3 22.6 %collective-permute-start.50 = (bf16[8,48,640]{2,1,0:T(8,128)(2,1)S(1)}, bf16[8,48,640]{2,1,0:T(8,128)(2,1)S(1)}, u32[]{:S(2)}, u32[]{:S(2)}) collective-permute-start(bf16[8,48,640]{2,1,0:T(8,128)(2,1)S(1)} %get-tuple-element.109), channel_id=1, source_target_pairs={{0,4},{2,6},{4,0},{6,2},{8,12},{10,14},{12,8},{14,10},{16,20},{18,... | collective-permute-start | bytes 1474568 | tf_op jit(solution)/shard_map/ppermute | solution.py:451
  139.8 15.4 %collective-permute-start.37 = (bf16[4,48,640]{2,1,0:T(8,128)(2,1)S(1)}, bf16[4,48,640]{2,1,0:T(8,128)(2,1)S(1)}, u32[]{:S(2)}, u32[]{:S(2)}) collective-permute-start(bf16[4,48,640]{2,1,0:T(8,128)(2,1)S(1)} %get-tuple-element.85), channel_id=1, source_target_pairs={{0,4},{2,6},{4,0},{6,2},{8,12},{10,14},{12,8},{14,10},{16,20},{18,... | collective-permute-start | bytes 737288 | tf_op jit(solution)/shard_map/ppermute | solution.py:451
  141.0 14.1 %collective-permute-start.38 = (bf16[4,48,640]{2,1,0:T(8,128)(2,1)S(1)}, bf16[4,48,640]{2,1,0:T(8,128)(2,1)S(1)}, u32[]{:S(2)}, u32[]{:S(2)}) collective-permute-start(bf16[4,48,640]{2,1,0:T(8,128)(2,1)S(1)} %get-tuple-element.87), channel_id=1, source_target_pairs={{0,2},{2,0},{4,6},{6,4},{8,10},{10,8},{12,14},{14,12},{16,18},{18,... | collective-permute-start | bytes 737288 | tf_op jit(solution)/shard_map/ppermute | solution.py:451
  142.1 17.5 %collective-permute-start.46 = (bf16[4,48,896]{2,1,0:T(8,128)(2,1)S(1)}, bf16[4,48,896]{2,1,0:T(8,128)(2,1)S(1)}, u32[]{:S(2)}, u32[]{:S(2)}) collective-permute-start(bf16[4,48,896]{2,1,0:T(8,128)(2,1)S(1)} %get-tuple-element.101), channel_id=1, source_target_pairs={{0,16},{2,18},{4,20},{6,22},{8,24},{10,26},{12,28},{14,30},{16,0},... | collective-permute-start | bytes 1032200 | tf_op jit(solution)/shard_map/ppermute | solution.py:451
  150.1 9.0 %collective-permute-start.51 = (bf16[4,48,640]{2,1,0:T(8,128)(2,1)S(1)}, bf16[4,48,640]{2,1,0:T(8,128)(2,1)S(1)}, u32[]{:S(2)}, u32[]{:S(2)}) collective-permute-start(bf16[4,48,640]{2,1,0:T(8,128)(2,1)S(1)} %get-tuple-element.111), channel_id=1, source_target_pairs={{0,4},{2,6},{4,0},{6,2},{8,12},{10,14},{12,8},{14,10},{16,20},{18,... | collective-permute-start | bytes 737288 | tf_op jit(solution)/shard_map/ppermute | solution.py:451
  151.4 7.8 %collective-permute-start.52 = (bf16[4,48,640]{2,1,0:T(8,128)(2,1)S(1)}, bf16[4,48,640]{2,1,0:T(8,128)(2,1)S(1)}, u32[]{:S(2)}, u32[]{:S(2)}) collective-permute-start(bf16[4,48,640]{2,1,0:T(8,128)(2,1)S(1)} %get-tuple-element.113), channel_id=1, source_target_pairs={{0,2},{2,0},{4,6},{6,4},{8,10},{10,8},{12,14},{14,12},{16,18},{18,... | collective-permute-start | bytes 737288 | tf_op jit(solution)/shard_map/ppermute | solution.py:451
  155.3 8.9 %collective-permute-start.39 = (bf16[2,48,1280]{2,1,0:T(8,128)(2,1)S(1)}, bf16[2,48,1280]{2,1,0:T(8,128)(2,1)S(1)}, u32[]{:S(2)}, u32[]{:S(2)}) collective-permute-start(bf16[2,48,1280]{2,1,0:T(8,128)(2,1)S(1)} %get-tuple-element.89), channel_id=1, source_target_pairs={{0,8},{2,10},{4,12},{6,14},{8,0},{10,2},{12,4},{14,6},{16,24},{18,... | collective-permute-start | bytes 737288 | tf_op jit(solution)/shard_map/ppermute | solution.py:451
  159.2 9.9 %collective-permute-start.53 = (bf16[2,48,1280]{2,1,0:T(8,128)(2,1)S(1)}, bf16[2,48,1280]{2,1,0:T(8,128)(2,1)S(1)}, u32[]{:S(2)}, u32[]{:S(2)}) collective-permute-start(bf16[2,48,1280]{2,1,0:T(8,128)(2,1)S(1)} %get-tuple-element.115), channel_id=1, source_target_pairs={{0,8},{2,10},{4,12},{6,14},{8,0},{10,2},{12,4},{14,6},{16,24},{18,... | collective-permute-start | bytes 737288 | tf_op jit(solution)/shard_map/ppermute | solution.py:451
  159.7 13.1 %collective-permute-start.47 = (bf16[2,48,896]{2,1,0:T(8,128)(2,1)S(1)}, bf16[2,48,896]{2,1,0:T(8,128)(2,1)S(1)}, u32[]{:S(2)}, u32[]{:S(2)}) collective-permute-start(bf16[2,48,896]{2,1,0:T(8,128)(2,1)S(1)} %get-tuple-element.103), channel_id=1, source_target_pairs={{0,2},{2,0},{4,6},{6,4},{8,10},{10,8},{12,14},{14,12},{16,18},{18,... | collective-permute-start | bytes 516104 | tf_op jit(solution)/shard_map/ppermute | solution.py:451
  164.2 7.8 %collective-permute-start.40 = (bf16[1,48,1280]{2,1,0:T(8,128)(2,1)S(1)}, bf16[1,48,1280]{2,1,0:T(8,128)(2,1)S(1)}, u32[]{:S(2)}, u32[]{:S(2)}) collective-permute-start(bf16[1,48,1280]{2,1,0:T(8,128)(2,1)S(1)} %get-tuple-element.91), channel_id=1, source_target_pairs={{0,16},{2,18},{4,20},{6,22},{8,24},{10,26},{12,28},{14,30},{16,0},... | collective-permute-start | bytes 368648 | tf_op jit(solution)/shard_map/ppermute | solution.py:451
  169.2 6.4 %collective-permute-start.54 = (bf16[1,48,1280]{2,1,0:T(8,128)(2,1)S(1)}, bf16[1,48,1280]{2,1,0:T(8,128)(2,1)S(1)}, u32[]{:S(2)}, u32[]{:S(2)}) collective-permute-start(bf16[1,48,1280]{2,1,0:T(8,128)(2,1)S(1)} %get-tuple-element.117), channel_id=1, source_target_pairs={{0,16},{2,18},{4,20},{6,22},{8,24},{10,26},{12,28},{14,30},{16,0},... | collective-permute-start | bytes 368648 | tf_op jit(solution)/shard_map/ppermute | solution.py:451
  172.8 4.6 %collective-permute-start.48 = (bf16[1,48,896]{2,1,0:T(8,128)(2,1)S(1)}, bf16[1,48,896]{2,1,0:T(8,128)(2,1)S(1)}, u32[]{:S(2)}, u32[]{:S(2)}) collective-permute-start(bf16[1,48,896]{2,1,0:T(8,128)(2,1)S(1)} %get-tuple-element.105), channel_id=1, source_target_pairs={{0,4},{2,6},{4,0},{6,2},{8,12},{10,14},{12,8},{14,10},{16,20},{18,... | collective-permute-start | bytes 258056 | tf_op jit(solution)/shard_map/ppermute | solution.py:451
  (18 other events, 59.5 us)

commit v4 on v3

--- a/solution.py
+++ b/solution.py
@@ -347,11 +347,6 @@
         refs[-1][i] = ref[...]
 
 
-def take_kernel(first, source, taken):
-    for i in range(taken.shape[0]):
-        taken[i] = source[first + i]
-
-
 def combine_kernel(joined, *refs):
     n = (len(refs) - 2) // 2 if joined else len(refs) // 4
     ins, outs = refs[: 2 * n], refs[2 * n :]
@@ -410,12 +405,6 @@
     return call(stack_kernel, list(planes), outs, [], scalars=0)[0]
 
 
-def take(source, first, count):
-    kernel = functools.partial(take_kernel, first)
-    outs = [shape(count, *source.shape[1:])]
-    return call(kernel, [source], outs, [], scalars=0)[0]
-
-
 def combine(joined, *arrays):
     outs = []
     for kept in arrays[::2]:
@@ -456,8 +445,8 @@
     def plane(stacked):
         came_x = exchange(stacked, X)
         came_y = exchange(stacked, Y)
-        far_a = exchange(take(came_y, 0, 2), X)
-        far_b = exchange(take(came_x, 2, 2), Y)
+        far_a = exchange(came_y[:2], X)
+        far_b = exchange(came_x[2:], Y)
         return [stacked, came_x, came_y, far_a, far_b]
 
     def both_cores(pieces):
@@ -596,7 +585,7 @@
     operands1 = [
         swap_b, keep1, their_b, swap_h, att, their_h, their_far, grad_mixed, their_mixed,
     ]
-    cut1 = total1 * 21 // 50 // LANES * LANES
+    cut1 = total1 * 9 // 25 // LANES * LANES
     mid = cut1 + (total1 - cut1) // 2 // LANES * LANES
     emit1 = [(GRAD_C, (0, cut1)), (GRAD_A, (cut1, mid)), (GRAD_B, (mid, total1))]
     cfg1 = dict(

time: 181 us -> 187 us (1.033)
  starting transfers between devices: 46.1 us -> 67.9 us
  waiting for transfers between devices: 81.8 us -> 67.4 us
    ppermute x36, starting transfers between devices: 42.7 us -> 64.6 us  [exchange(): return lax.ppermute(value, 'dp', pairs)]
    ppermute x36, waiting for transfers between devices: 78.6 us -> 64.3 us  [exchange(): return lax.ppermute(value, 'dp', pairs)]
    slice x0 -> x4, local copies, waits for them, and re-layouts: none -> 2.45 us  [the longest x2 1.7 us: plane(): far_b = exchange(came_x[2:], Y)]
    pallas_call x24 -> x20, Pallas kernels: 29.2 us -> 27.6 us  [call(): pl.pallas_call(kernel, out_shape=outs, in_specs=[SMEM] * scalars + [VMEM]...]
    unnamed x54 -> x48, local copies, waits for them, and re-layouts: 6.28 us -> 4.62 us
  transfers between devices with their start and end apart: 55 -> 55, of which waited for: 25 -> 22; matrix products, arithmetic and copies ran while one was open for 6% -> 7% of each run, Pallas kernels for 12% -> 11%
where the time goes in v4:
time: 187 us; the launch traced here: 186 us
  starting transfers between devices  67.9 us (36%)
  waiting for transfers between devices  67.4 us (36%)
  Pallas kernels  27.6 us (15%)
  local copies, waits for them, and re-layouts  13 us (7%)
  other arithmetic  8.66 us (5%)
    ppermute x36, starting transfers between devices, exchange(): return lax.ppermute(value, 'dp', pairs)  64.6 us
    ppermute x36, waiting for transfers between devices, exchange(): return lax.ppermute(value, 'dp', pairs)  64.3 us
    pallas_call x20, Pallas kernels, call(): pl.pallas_call(kernel, out_shape=outs, in_specs=[SMEM] * scalars + [VMEM]...  27.6 us
    unnamed x48, local copies, waits for them, and re-layouts  4.62 us
  transfers between devices with their start and end apart: 55, of which 22 were waited for; matrix products, arithmetic and copies ran while one was open for 7% of the time, Pallas kernels for 11%

profile of v4, /device:TPU:0, one launch (start us, length us, event | category | flops | bytes accessed | tf_op | source)
XLA Modules:
  0.0 186.5 jit_solution(14530832092522531119)
XLA Ops:
  1.4 0.9 fusion.4
  2.3 3.1 %collective-permute-start = (bf16[48,1152]{1,0:T(8,128)(2,1)S(1)}, bf16[48,1152]{1,0:T(8,128)(2,1)S(1)}, u32[]{:S(2)}, u32[]{:S(2)}) collective-permute-start(bf16[48,1152]{1,0:T(8,128)(2,1)S(1)} %pad_maximum_fusion.3.refs_0_), channel_id=1, source_target_pairs={{0,8},{2,10},{4,12},{6,14},{8,0},{10,2},{12,4},{14,6},{16,24},{18,... | collective-permute-start | bytes 331784 | tf_op jit(solution)/shard_map/ppermute | solution.py:440
  5.4 2.6 %collective-permute-start.1 = (bf16[48,1152]{1,0:T(8,128)(2,1)S(1)}, bf16[48,1152]{1,0:T(8,128)(2,1)S(1)}, u32[]{:S(2)}, u32[]{:S(2)}) collective-permute-start(bf16[48,1152]{1,0:T(8,128)(2,1)S(1)} %pad_maximum_fusion.3.refs_0_), channel_id=1, source_target_pairs={{0,16},{2,18},{4,20},{6,22},{8,24},{10,26},{12,28},{14,30},{16,0},... | collective-permute-start | bytes 331784 | tf_op jit(solution)/shard_map/ppermute | solution.py:440
  8.0 1.1 fusion.7
  9.2 1.6 collective-permute-start.13
  10.8 1.5 collective-permute-start.12
  12.3 0.9 fusion.6
  13.5 1.5 collective-permute-start.14
  15.8 1.3 collective-permute-start.2
  18.2 2.0 %collective-permute-start.19 = (bf16[48,1536]{1,0:T(8,128)(2,1)S(1)}, bf16[48,1536]{1,0:T(8,128)(2,1)S(1)}, u32[]{:S(2)}, u32[]{:S(2)}) collective-permute-start(bf16[48,1536]{1,0:T(8,128)(2,1)S(1)} %slice.80.refs_0_), channel_id=1, source_target_pairs={{0,16},{2,18},{4,20},{6,22},{8,24},{10,26},{12,28},{14,30},{16,0},... | collective-permute-start | bytes 442376 | tf_op jit(solution)/shard_map/ppermute | solution.py:440
  20.2 1.9 %collective-permute-start.20 = (bf16[48,1536]{1,0:T(8,128)(2,1)S(1)}, bf16[48,1536]{1,0:T(8,128)(2,1)S(1)}, u32[]{:S(2)}, u32[]{:S(2)}) collective-permute-start(bf16[48,1536]{1,0:T(8,128)(2,1)S(1)} %slice.80.refs_0_), channel_id=1, source_target_pairs={{0,24},{2,26},{4,28},{6,30},{8,16},{10,18},{12,20},{14,22},{16,8},... | collective-permute-start | bytes 442376 | tf_op jit(solution)/shard_map/ppermute | solution.py:440
  22.2 2.0 %collective-permute-done.2.refs_3_ = bf16[48,1152]{1,0:T(8,128)(2,1)S(1)} collective-permute-done((bf16[48,1152]{1,0:T(8,128)(2,1)S(1)}, bf16[48,1152]{1,0:T(8,128)(2,1)S(1)}, u32[]{:S(2)}, u32[]{:S(2)}) %collective-permute-start.2) | collective-permute-done | bytes 110624 | tf_op jit(solution)/shard_map/ppermute | solution.py:440
  24.2 1.8 collective-permute-done.18.refs_1_
  25.9 0.8 collective-permute-start.17
  26.8 4.0 %collective-permute-done.19.refs_2_ = bf16[48,1536]{1,0:T(8,128)(2,1)S(1)} collective-permute-done((bf16[48,1536]{1,0:T(8,128)(2,1)S(1)}, bf16[48,1536]{1,0:T(8,128)(2,1)S(1)}, u32[]{:S(2)}, u32[]{:S(2)}) %collective-permute-start.19) | collective-permute-done | bytes 147488 | tf_op jit(solution)/shard_map/ppermute | solution.py:440
  30.8 1.5 collective-permute-start.4
  32.3 3.5 %collective-permute-done.20.refs_3_ = bf16[48,1536]{1,0:T(8,128)(2,1)S(1)} collective-permute-done((bf16[48,1536]{1,0:T(8,128)(2,1)S(1)}, bf16[48,1536]{1,0:T(8,128)(2,1)S(1)}, u32[]{:S(2)}, u32[]{:S(2)}) %collective-permute-start.20) | collective-permute-done | bytes 147488 | tf_op jit(solution)/shard_map/ppermute | solution.py:440
  36.5 15.9 %collective-permute-done.16.refs_7_ = bf16[4,48,640]{2,1,0:T(8,128)(2,1)S(1)} collective-permute-done((bf16[4,48,640]{2,1,0:T(8,128)(2,1)S(1)}, bf16[4,48,640]{2,1,0:T(8,128)(2,1)S(1)}, u32[]{:S(2)}, u32[]{:S(2)}) %collective-permute-start.16) | collective-permute-done | bytes 245792 | tf_op jit(solution)/shard_map/ppermute | solution.py:440
  52.3 1.5 collective-permute-start.22
  56.6 1.0 slice.79
  57.6 1.5 collective-permute-start.5
  59.6 6.1 %collective-permute-done.22.refs_11_ = bf16[4,48,1536]{2,1,0:T(8,128)(2,1)S(1)} collective-permute-done((bf16[4,48,1536]{2,1,0:T(8,128)(2,1)S(1)}, bf16[4,48,1536]{2,1,0:T(8,128)(2,1)S(1)}, u32[]{:S(2)}, u32[]{:S(2)}) %collective-permute-start.22) | collective-permute-done | bytes 589856 | tf_op jit(solution)/shard_map/ppermute | solution.py:440
  66.4 1.0 collective-permute-done.21.refs_10_
  67.5 2.4 %collective-permute-done.5.refs_5_ = bf16[2,48,1152]{2,1,0:T(8,128)(2,1)S(1)} collective-permute-done((bf16[2,48,1152]{2,1,0:T(8,128)(2,1)S(1)}, bf16[2,48,1152]{2,1,0:T(8,128)(2,1)S(1)}, u32[]{:S(2)}, u32[]{:S(2)}) %collective-permute-start.5) | collective-permute-done | bytes 221216 | tf_op jit(solution)/shard_map/ppermute | solution.py:440
  70.3 1.3 fusion.5
  74.6 0.9 collective-permute-start.23
  76.2 1.7 collective-permute-start.24
  77.9 0.8 copy-done.2
  78.7 0.8 copy-done.4
  80.8 0.8 fusion.1.refs_4_
  81.6 1.6 pad_maximum_fusion.1
  83.1 1.1 collective-permute-done.23.refs_12_
  84.3 1.3 collective-permute-done.24.refs_13_
  85.6 1.1 multiply_convert_fusion.refs_3_.gm_ref.refs_7_
  86.8 0.9 copy-done.19
  87.7 5.5 %shard_map.171 = (bf16[768,2304]{1,0:T(8,128)(2,1)S(1)}, bf16[256,2304]{1,0:T(8,128)(2,1)S(1)}, bf16[256,768]{1,0:T(8,128)(2,1)S(1)}, bf16[256,384]{1,0:T(8,128)...) custom-call(s32[1]{0:T(128)} %bitcast.refs_0_.me_ref, bf16[256,768]{1,0:T(8,128)(2,1)S(1)} %copy-done.1, ...), custom_call_target="tpu_custom_call" | custom-call | flops 905969664 | bytes 10030084 | tf_op jit(solution)/shard_map/pallas_call | solution.py:388
  93.3 7.1 %shard_map.174 = (bf16[256,768]{1,0:T(8,128)(2,1)}, f32[256,768]{1,0:T(8,128)S(1)}, f32[8,768]{1,0:T(8,128)S(1)}, bf16[768,768]{1,0:T(8,128)(2,1)S(1)}, bf16[768...) custom-call(s32[1]{0:T(128)} %bitcast.refs_0_.me_ref, ...), custom_call_target="tpu_custom_call" | custom-call | flops 1811939328 | bytes 17196036 | tf_op jit(solution)/shard_map/pallas_call | solution.py:388
  100.9 1.4 shard_map.175
  102.4 7.6 %shard_map.176 = (f32[256,768]{1,0:T(8,128)}, bf16[272,1920]{1,0:T(8,128)(2,1)S(1)}, bf16[256,1152]{1,0:T(8,128)(2,1)S(1)}) custom-call(bf16[256,768]{1,0:T(8,128)(2,1)S(1)} %copy-done.1, f32[256,768]{1,0:T(8,128)S(1)} %get-tuple-element.71.refs_1_, bf16[768,768]{1,0:T(8,128)(2,1)S(1)} %get-tuple-element.72.refs_2_, ...), custom_call_target="tpu_custom_call" | custom-call | flops 1509949440 | bytes 10681344 | tf_op jit(solution)/shard_map/pallas_call | solution.py:388
  111.0 2.8 %collective-permute-done.44.refs_8_ = bf16[256,768]{1,0:T(8,128)(2,1)S(1)} collective-permute-done((bf16[256,768]{1,0:T(8,128)(2,1)S(1)}, bf16[256,768]{1,0:T(8,128)(2,1)S(1)}, u32[]{:S(2)}, u32[]{:S(2)}) %collective-permute-start.44) | collective-permute-done | bytes 393248 | tf_op jit(solution)/shard_map/ppermute | solution.py:436
  114.1 2.6 %shard_map.182 = (bf16[8,48,768]{2,1,0:T(8,128)(2,1)S(1)}, bf16[8,48,768]{2,1,0:T(8,128)(2,1)S(1)}, bf16[8,48,640]{2,1,0:T(8,128)(2,1)S(1)}, bf16[8,48,640]{2,1,...) custom-call(s32[1]{0:T(128)} %bitcast.refs_0_.me_ref, ...), custom_call_target="tpu_custom_call" | custom-call | flops 1711276032 | bytes 9093124 | tf_op jit(solution)/shard_map/pallas_call | solution.py:388
  116.7 1.7 collective-permute-start.50
  118.4 1.4 shard_map.177
  120.2 1.2 collective-permute-start.36
  121.4 0.9 collective-permute-start.49
  122.3 5.8 %collective-permute-start.45 = (bf16[8,48,768]{2,1,0:T(8,128)(2,1)S(1)}, bf16[8,48,768]{2,1,0:T(8,128)(2,1)S(1)}, u32[]{:S(2)}, u32[]{:S(2)}) collective-permute-start(bf16[8,48,768]{2,1,0:T(8,128)(2,1)S(1)} %get-tuple-element.99), channel_id=1, source_target_pairs={{0,8},{2,10},{4,12},{6,14},{8,0},{10,2},{12,4},{14,6},{16,24},{18,... | collective-permute-start | bytes 1769480 | tf_op jit(solution)/shard_map/ppermute | solution.py:440
  128.2 5.9 %collective-permute-done.35.refs_1_ = bf16[8,48,640]{2,1,0:T(8,128)(2,1)S(1)} collective-permute-done((bf16[8,48,640]{2,1,0:T(8,128)(2,1)S(1)}, bf16[8,48,640]{2,1,0:T(8,128)(2,1)S(1)}, u32[]{:S(2)}, u32[]{:S(2)}) %collective-permute-start.35) | collective-permute-done | bytes 491552 | tf_op jit(solution)/shard_map/ppermute | solution.py:440
  134.0 8.7 %collective-permute-done.36.refs_3_ = bf16[8,48,640]{2,1,0:T(8,128)(2,1)S(1)} collective-permute-done((bf16[8,48,640]{2,1,0:T(8,128)(2,1)S(1)}, bf16[8,48,640]{2,1,0:T(8,128)(2,1)S(1)}, u32[]{:S(2)}, u32[]{:S(2)}) %collective-permute-start.36) | collective-permute-done | bytes 491552 | tf_op jit(solution)/shard_map/ppermute | solution.py:440
  142.9 1.7 collective-permute-start.37
  145.2 1.8 collective-permute-start.52
  147.5 4.8 %collective-permute-start.46 = (bf16[4,48,768]{2,1,0:T(8,128)(2,1)S(1)}, bf16[4,48,768]{2,1,0:T(8,128)(2,1)S(1)}, u32[]{:S(2)}, u32[]{:S(2)}) collective-permute-start(bf16[4,48,768]{2,1,0:T(8,128)(2,1)S(1)} %get-tuple-element.101), channel_id=1, source_target_pairs={{0,16},{2,18},{4,20},{6,22},{8,24},{10,26},{12,28},{14,30},{16,0},... | collective-permute-start | bytes 884744 | tf_op jit(solution)/shard_map/ppermute | solution.py:440
  152.3 1.2 collective-permute-done.38.refs_3_
  153.5 4.5 %collective-permute-start.39 = (bf16[2,48,1280]{2,1,0:T(8,128)(2,1)S(1)}, bf16[2,48,1280]{2,1,0:T(8,128)(2,1)S(1)}, u32[]{:S(2)}, u32[]{:S(2)}) collective-permute-start(bf16[2,48,1280]{2,1,0:T(8,128)(2,1)S(1)} %get-tuple-element.89), channel_id=1, source_target_pairs={{0,8},{2,10},{4,12},{6,14},{8,0},{10,2},{12,4},{14,6},{16,24},{18,... | collective-permute-start | bytes 737288 | tf_op jit(solution)/shard_map/ppermute | solution.py:440
  158.2 4.3 %collective-permute-start.53 = (bf16[2,48,1408]{2,1,0:T(8,128)(2,1)S(1)}, bf16[2,48,1408]{2,1,0:T(8,128)(2,1)S(1)}, u32[]{:S(2)}, u32[]{:S(2)}) collective-permute-start(bf16[2,48,1408]{2,1,0:T(8,128)(2,1)S(1)} %get-tuple-element.115), channel_id=1, source_target_pairs={{0,8},{2,10},{4,12},{6,14},{8,0},{10,2},{12,4},{14,6},{16,24},{18,... | collective-permute-start | bytes 811016 | tf_op jit(solution)/shard_map/ppermute | solution.py:440
  162.5 1.5 collective-permute-done.46.refs_1_
  164.1 0.9 collective-permute-start.47
  165.0 2.5 %collective-permute-done.39.refs_1_ = bf16[2,48,1280]{2,1,0:T(8,128)(2,1)S(1)} collective-permute-done((bf16[2,48,1280]{2,1,0:T(8,128)(2,1)S(1)}, bf16[2,48,1280]{2,1,0:T(8,128)(2,1)S(1)}, u32[]{:S(2)}, u32[]{:S(2)}) %collective-permute-start.39) | collective-permute-done | bytes 245792 | tf_op jit(solution)/shard_map/ppermute | solution.py:440
  167.6 2.0 %collective-permute-start.40 = (bf16[1,48,1280]{2,1,0:T(8,128)(2,1)S(1)}, bf16[1,48,1280]{2,1,0:T(8,128)(2,1)S(1)}, u32[]{:S(2)}, u32[]{:S(2)}) collective-permute-start(bf16[1,48,1280]{2,1,0:T(8,128)(2,1)S(1)} %get-tuple-element.91), channel_id=1, source_target_pairs={{0,16},{2,18},{4,20},{6,22},{8,24},{10,26},{12,28},{14,30},{16,0},... | collective-permute-start | bytes 368648 | tf_op jit(solution)/shard_map/ppermute | solution.py:440
  169.6 2.1 %collective-permute-done.53.refs_1_ = bf16[2,48,1408]{2,1,0:T(8,128)(2,1)S(1)} collective-permute-done((bf16[2,48,1408]{2,1,0:T(8,128)(2,1)S(1)}, bf16[2,48,1408]{2,1,0:T(8,128)(2,1)S(1)}, u32[]{:S(2)}, u32[]{:S(2)}) %collective-permute-start.53) | collective-permute-done | bytes 270368 | tf_op jit(solution)/shard_map/ppermute | solution.py:440
  171.7 2.3 %collective-permute-start.54 = (bf16[1,48,1408]{2,1,0:T(8,128)(2,1)S(1)}, bf16[1,48,1408]{2,1,0:T(8,128)(2,1)S(1)}, u32[]{:S(2)}, u32[]{:S(2)}) collective-permute-start(bf16[1,48,1408]{2,1,0:T(8,128)(2,1)S(1)} %get-tuple-element.117), channel_id=1, source_target_pairs={{0,16},{2,18},{4,20},{6,22},{8,24},{10,26},{12,28},{14,30},{16,0},... | collective-permute-start | bytes 405512 | tf_op jit(solution)/shard_map/ppermute | solution.py:440
  174.8 0.8 shard_map.181
  175.7 5.3 %collective-permute-start.48 = (bf16[1,48,768]{2,1,0:T(8,128)(2,1)S(1)}, bf16[1,48,768]{2,1,0:T(8,128)(2,1)S(1)}, u32[]{:S(2)}, u32[]{:S(2)}) collective-permute-start(bf16[1,48,768]{2,1,0:T(8,128)(2,1)S(1)} %get-tuple-element.105), channel_id=1, source_target_pairs={{0,4},{2,6},{4,0},{6,2},{8,12},{10,14},{12,8},{14,10},{16,20},{18,... | collective-permute-start | bytes 221192 | tf_op jit(solution)/shard_map/ppermute | solution.py:440
  181.6 1.7 collective-permute-done.48.came_c
  185.7 0.8 pad_maximum_fusion
  (153 shorter events, 20.0 us)
Async XLA Ops:
  0.6 53.8 %copy-start = (s32[2,256]{1,0:T(2,128)S(1)}, s32[2,256]{1,0:T(2,128)}, u32[]{:S(2)}) copy-start(s32[2,256]{1,0:T(2,128)} %param.19) | copy-start | bytes 6148
  0.6 14.3 %copy-start.22 = (bf16[48]{0:T(256)(128)(2,1)S(1)}, bf16[48]{0:T(256)(128)(2,1)}, u32[]{:S(2)}) copy-start(bf16[48]{0:T(256)(128)(2,1)} %param.15) | copy-start | bytes 292
  0.7 14.4 %copy-start.21 = (bf16[384,48]{0,1:T(8,128)(2,1)S(1)}, bf16[384,48]{0,1:T(8,128)(2,1)}, u32[]{:S(2)}) copy-start(bf16[384,48]{0,1:T(8,128)(2,1)} %param.14) | copy-start | bytes 110596
  0.7 14.4 %copy-start.20 = (bf16[576,48]{0,1:T(8,128)(2,1)S(1)}, bf16[576,48]{0,1:T(8,128)(2,1)}, u32[]{:S(2)}) copy-start(bf16[576,48]{0,1:T(8,128)(2,1)} %param.17) | copy-start | bytes 165892
  2.3 15.9 %collective-permute-start = (bf16[48,1152]{1,0:T(8,128)(2,1)S(1)}, bf16[48,1152]{1,0:T(8,128)(2,1)S(1)}, u32[]{:S(2)}, u32[]{:S(2)}) collective-permute-start(bf16[48,1152]{1,0:T(8,128)(2,1)S(1)} %pad_maximum_fusion.3.refs_0_), channel_id=1, source_target_pairs={{0,8},{2,10},{4,12},{6,14},{8,0},{10,2},{12,4},{14,6},{16,24},{18,... | collective-permute-start | bytes 331784 | tf_op jit(solution)/shard_map/ppermute | solution.py:440
  5.4 14.8 %collective-permute-start.1 = (bf16[48,1152]{1,0:T(8,128)(2,1)S(1)}, bf16[48,1152]{1,0:T(8,128)(2,1)S(1)}, u32[]{:S(2)}, u32[]{:S(2)}) collective-permute-start(bf16[48,1152]{1,0:T(8,128)(2,1)S(1)} %pad_maximum_fusion.3.refs_0_), channel_id=1, source_target_pairs={{0,16},{2,18},{4,20},{6,22},{8,24},{10,26},{12,28},{14,30},{16,0},... | collective-permute-start | bytes 331784 | tf_op jit(solution)/shard_map/ppermute | solution.py:440
  9.2 4.3 %collective-permute-start.13 = (bf16[48,640]{1,0:T(8,128)(2,1)S(1)}, bf16[48,640]{1,0:T(8,128)(2,1)S(1)}, u32[]{:S(2)}, u32[]{:S(2)}) collective-permute-start(bf16[48,640]{1,0:T(8,128)(2,1)S(1)} %pad_maximum_fusion.4.refs_0_), channel_id=1, source_target_pairs={{0,4},{2,6},{4,0},{6,2},{8,12},{10,14},{12,8},{14,10},{16,20},{18,... | collective-permute-start | bytes 184328 | tf_op jit(solution)/shard_map/ppermute | solution.py:440
  10.8 5.0 %collective-permute-start.12 = (bf16[48,640]{1,0:T(8,128)(2,1)S(1)}, bf16[48,640]{1,0:T(8,128)(2,1)S(1)}, u32[]{:S(2)}, u32[]{:S(2)}) collective-permute-start(bf16[48,640]{1,0:T(8,128)(2,1)S(1)} %pad_maximum_fusion.4.refs_0_), channel_id=1, source_target_pairs={{0,2},{2,0},{4,6},{6,4},{8,10},{10,8},{12,14},{14,12},{16,18},{18,... | collective-permute-start | bytes 184328 | tf_op jit(solution)/shard_map/ppermute | solution.py:440
  13.5 4.2 %collective-permute-start.14 = (bf16[48,640]{1,0:T(8,128)(2,1)S(1)}, bf16[48,640]{1,0:T(8,128)(2,1)S(1)}, u32[]{:S(2)}, u32[]{:S(2)}) collective-permute-start(bf16[48,640]{1,0:T(8,128)(2,1)S(1)} %collective-permute-done.13.refs_2_), channel_id=1, source_target_pairs={{0,2},{2,0},{4,6},{6,4},{8,10},{10,8},{12,14},{14,12},{16,18},{18,... | collective-permute-start | bytes 184328 | tf_op jit(solution)/shard_map/ppermute | solution.py:440
  15.2 40.1 %copy-start.23 = (s32[2]{0:T(128)S(1)}, s32[2]{0:T(128)}, u32[]{:S(2)}) copy-start(s32[2]{0:T(128)} %param.20) | copy-start | bytes 28
  15.2 10.7 %collective-permute-start.18 = (bf16[48,1536]{1,0:T(8,128)(2,1)S(1)}, bf16[48,1536]{1,0:T(8,128)(2,1)S(1)}, u32[]{:S(2)}, u32[]{:S(2)}) collective-permute-start(bf16[48,1536]{1,0:T(8,128)(2,1)S(1)} %slice.80.refs_0_), channel_id=1, source_target_pairs={{0,8},{2,10},{4,12},{6,14},{8,0},{10,2},{12,4},{14,6},{16,24},{18,... | collective-permute-start | bytes 442376 | tf_op jit(solution)/shard_map/ppermute | solution.py:440
  15.8 8.4 %collective-permute-start.2 = (bf16[48,1152]{1,0:T(8,128)(2,1)S(1)}, bf16[48,1152]{1,0:T(8,128)(2,1)S(1)}, u32[]{:S(2)}, u32[]{:S(2)}) collective-permute-start(bf16[48,1152]{1,0:T(8,128)(2,1)S(1)} %pad_maximum_fusion.3.refs_0_), channel_id=1, source_target_pairs={{0,24},{2,26},{4,28},{6,30},{8,16},{10,18},{12,20},{14,22},{16,8},... | collective-permute-start | bytes 331784 | tf_op jit(solution)/shard_map/ppermute | solution.py:440
  17.7 18.7 %collective-permute-start.15 = (bf16[4,48,640]{2,1,0:T(8,128)(2,1)S(1)}, bf16[4,48,640]{2,1,0:T(8,128)(2,1)S(1)}, u32[]{:S(2)}, u32[]{:S(2)}) collective-permute-start(bf16[4,48,640]{2,1,0:T(8,128)(2,1)S(1)} %shard_map.172.refs_5_), channel_id=1, source_target_pairs={{0,8},{2,10},{4,12},{6,14},{8,0},{10,2},{12,4},{14,6},{16,24},{18,... | collective-permute-start | bytes 737288 | tf_op jit(solution)/shard_map/ppermute | solution.py:440
  18.2 12.6 %collective-permute-start.19 = (bf16[48,1536]{1,0:T(8,128)(2,1)S(1)}, bf16[48,1536]{1,0:T(8,128)(2,1)S(1)}, u32[]{:S(2)}, u32[]{:S(2)}) collective-permute-start(bf16[48,1536]{1,0:T(8,128)(2,1)S(1)} %slice.80.refs_0_), channel_id=1, source_target_pairs={{0,16},{2,18},{4,20},{6,22},{8,24},{10,26},{12,28},{14,30},{16,0},... | collective-permute-start | bytes 442376 | tf_op jit(solution)/shard_map/ppermute | solution.py:440
  20.2 15.6 %collective-permute-start.20 = (bf16[48,1536]{1,0:T(8,128)(2,1)S(1)}, bf16[48,1536]{1,0:T(8,128)(2,1)S(1)}, u32[]{:S(2)}, u32[]{:S(2)}) collective-permute-start(bf16[48,1536]{1,0:T(8,128)(2,1)S(1)} %slice.80.refs_0_), channel_id=1, source_target_pairs={{0,24},{2,26},{4,28},{6,30},{8,16},{10,18},{12,20},{14,22},{16,8},... | collective-permute-start | bytes 442376 | tf_op jit(solution)/shard_map/ppermute | solution.py:440
  24.2 28.2 %collective-permute-start.16 = (bf16[4,48,640]{2,1,0:T(8,128)(2,1)S(1)}, bf16[4,48,640]{2,1,0:T(8,128)(2,1)S(1)}, u32[]{:S(2)}, u32[]{:S(2)}) collective-permute-start(bf16[4,48,640]{2,1,0:T(8,128)(2,1)S(1)} %shard_map.172.refs_5_), channel_id=1, source_target_pairs={{0,16},{2,18},{4,20},{6,22},{8,24},{10,26},{12,28},{14,30},{16,0},... | collective-permute-start | bytes 737288 | tf_op jit(solution)/shard_map/ppermute | solution.py:440
  25.9 27.9 %collective-permute-start.17 = (bf16[4,48,640]{2,1,0:T(8,128)(2,1)S(1)}, bf16[4,48,640]{2,1,0:T(8,128)(2,1)}, u32[]{:S(2)}, u32[]{:S(2)}) collective-permute-start(bf16[4,48,640]{2,1,0:T(8,128)(2,1)S(1)} %shard_map.172.refs_5_), channel_id=1, source_target_pairs={{0,24},{2,26},{4,28},{6,30},{8,16},{10,18},{12,20},{14,22},{16,8},... | collective-permute-start | bytes 737288 | tf_op jit(solution)/shard_map/ppermute | solution.py:440
  30.8 23.9 %collective-permute-start.4 = (bf16[4,48,1152]{2,1,0:T(8,128)(2,1)S(1)}, bf16[4,48,1152]{2,1,0:T(8,128)(2,1)S(1)}, u32[]{:S(2)}, u32[]{:S(2)}) collective-permute-start(bf16[4,48,1152]{2,1,0:T(8,128)(2,1)S(1)} %shard_map.170.refs_2_), channel_id=1, source_target_pairs={{0,4},{2,6},{4,0},{6,2},{8,12},{10,14},{12,8},{14,10},{16,20},{18,... | collective-permute-start | bytes 1327112 | tf_op jit(solution)/shard_map/ppermute | solution.py:440
  35.9 19.4 %collective-permute-start.3 = (bf16[4,48,1152]{2,1,0:T(8,128)(2,1)S(1)}, bf16[4,48,1152]{2,1,0:T(8,128)(2,1)}, u32[]{:S(2)}, u32[]{:S(2)}) collective-permute-start(bf16[4,48,1152]{2,1,0:T(8,128)(2,1)S(1)} %shard_map.170.refs_2_), channel_id=1, source_target_pairs={{0,2},{2,0},{4,6},{6,4},{8,10},{10,8},{12,14},{14,12},{16,18},{18,... | collective-permute-start | bytes 1327112 | tf_op jit(solution)/shard_map/ppermute | solution.py:440
  36.4 33.9 %copy-start.6 = (bf16[4,48,640]{2,1,0:T(8,128)(2,1)}, bf16[4,48,640]{2,1,0:T(8,128)(2,1)S(1)}, u32[]{:S(2)}) copy-start(bf16[4,48,640]{2,1,0:T(8,128)(2,1)S(1)} %collective-permute-done.15.refs_6_) | copy-start | bytes 737284
  36.4 18.0 %collective-permute-start.25 = (bf16[4,48,640]{2,1,0:T(8,128)(2,1)S(1)}, bf16[4,48,640]{2,1,0:T(8,128)(2,1)}, u32[]{:S(2)}, u32[]{:S(2)}) collective-permute-start(bf16[4,48,640]{2,1,0:T(8,128)(2,1)S(1)} %shard_map.172.refs_5_), channel_id=1, source_target_pairs={{0,1},{1,0},{2,3},{3,2},{4,5},{5,4},{6,7},{7,6},{8,9},{9,8},{10,11... | collective-permute-start | bytes 737288 | tf_op jit(solution)/shard_map/ppermute | solution.py:436
  52.3 18.0 %copy-start.8 = (bf16[4,48,640]{2,1,0:T(8,128)(2,1)}, bf16[4,48,640]{2,1,0:T(8,128)(2,1)S(1)}, u32[]{:S(2)}) copy-start(bf16[4,48,640]{2,1,0:T(8,128)(2,1)S(1)} %collective-permute-done.16.refs_7_) | copy-start | bytes 737284
  52.3 13.5 %collective-permute-start.22 = (bf16[4,48,1536]{2,1,0:T(8,128)(2,1)S(1)}, bf16[4,48,1536]{2,1,0:T(8,128)(2,1)S(1)}, u32[]{:S(2)}, u32[]{:S(2)}) collective-permute-start(bf16[4,48,1536]{2,1,0:T(8,128)(2,1)S(1)} %shard_map.173.refs_9_), channel_id=1, source_target_pairs={{0,4},{2,6},{4,0},{6,2},{8,12},{10,14},{12,8},{14,10},{16,20},{18,... | collective-permute-start | bytes 1769480 | tf_op jit(solution)/shard_map/ppermute | solution.py:440
  53.8 13.6 %collective-permute-start.21 = (bf16[4,48,1536]{2,1,0:T(8,128)(2,1)S(1)}, bf16[4,48,1536]{2,1,0:T(8,128)(2,1)S(1)}, u32[]{:S(2)}, u32[]{:S(2)}) collective-permute-start(bf16[4,48,1536]{2,1,0:T(8,128)(2,1)S(1)} %shard_map.173.refs_9_), channel_id=1, source_target_pairs={{0,2},{2,0},{4,6},{6,4},{8,10},{10,8},{12,14},{14,12},{16,18},{18,... | collective-permute-start | bytes 1769480 | tf_op jit(solution)/shard_map/ppermute | solution.py:440
  54.4 3.2 %collective-permute-start.7 = (bf16[4,48,1152]{2,1,0:T(8,128)(2,1)S(1)}, bf16[4,48,1152]{2,1,0:T(8,128)(2,1)}, u32[]{:S(2)}, u32[]{:S(2)}) collective-permute-start(bf16[4,48,1152]{2,1,0:T(8,128)(2,1)S(1)} %shard_map.170.refs_2_), channel_id=1, source_target_pairs={{0,1},{1,0},{2,3},{3,2},{4,5},{5,4},{6,7},{7,6},{8,9},{9,8},{10,11... | collective-permute-start | bytes 1327112 | tf_op jit(solution)/shard_map/ppermute | solution.py:436
  54.7 4.4 %collective-permute-start.26 = (bf16[4,48,640]{2,1,0:T(8,128)(2,1)S(1)}, bf16[4,48,640]{2,1,0:T(8,128)(2,1)}, u32[]{:S(2)}, u32[]{:S(2)}) collective-permute-start(bf16[4,48,640]{2,1,0:T(8,128)(2,1)S(1)} %collective-permute-done.15.refs_6_), channel_id=1, source_target_pairs={{0,1},{1,0},{2,3},{3,2},{4,5},{5,4},{6,7},{7,6},{8,9},{9,8},{10,11... | collective-permute-start | bytes 737288 | tf_op jit(solution)/shard_map/ppermute | solution.py:436
  55.2 4.4 %collective-permute-start.27 = (bf16[4,48,640]{2,1,0:T(8,128)(2,1)S(1)}, bf16[4,48,640]{2,1,0:T(8,128)(2,1)}, u32[]{:S(2)}, u32[]{:S(2)}) collective-permute-start(bf16[4,48,640]{2,1,0:T(8,128)(2,1)S(1)} %collective-permute-done.16.refs_7_), channel_id=1, source_target_pairs={{0,1},{1,0},{2,3},{3,2},{4,5},{5,4},{6,7},{7,6},{8,9},{9,8},{10,11... | collective-permute-start | bytes 737288 | tf_op jit(solution)/shard_map/ppermute | solution.py:436
  57.6 12.2 %collective-permute-start.5 = (bf16[2,48,1152]{2,1,0:T(8,128)(2,1)S(1)}, bf16[2,48,1152]{2,1,0:T(8,128)(2,1)S(1)}, u32[]{:S(2)}, u32[]{:S(2)}) collective-permute-start(bf16[2,48,1152]{2,1,0:T(8,128)(2,1)S(1)} %slice.78), channel_id=1, source_target_pairs={{0,2},{2,0},{4,6},{6,4},{8,10},{10,8},{12,14},{14,12},{16,18},{18,... | collective-permute-start | bytes 663560 | tf_op jit(solution)/shard_map/ppermute | solution.py:440
  59.1 10.7 %collective-permute-start.6 = (bf16[2,48,1152]{2,1,0:T(8,128)(2,1)S(1)}, bf16[2,48,1152]{2,1,0:T(8,128)(2,1)S(1)}, u32[]{:S(2)}, u32[]{:S(2)}) collective-permute-start(bf16[2,48,1152]{2,1,0:T(8,128)(2,1)S(1)} %slice.79), channel_id=1, source_target_pairs={{0,4},{2,6},{4,0},{6,2},{8,12},{10,14},{12,8},{14,10},{16,20},{18,... | collective-permute-start | bytes 663560 | tf_op jit(solution)/shard_map/ppermute | solution.py:440
  59.6 18.2 %collective-permute-start.8 = (bf16[4,48,1152]{2,1,0:T(8,128)(2,1)}, bf16[4,48,1152]{2,1,0:T(8,128)(2,1)S(1)}, u32[]{:S(2)}, u32[]{:S(2)}) collective-permute-start(bf16[4,48,1152]{2,1,0:T(8,128)(2,1)} %collective-permute-done.3.refs_3_), channel_id=1, source_target_pairs={{0,1},{1,0},{2,3},{3,2},{4,5},{5,4},{6,7},{7,6},{8,9},{9,8},{10,11... | collective-permute-start | bytes 1327112 | tf_op jit(solution)/shard_map/ppermute | solution.py:436
  65.8 12.9 %collective-permute-start.9 = (bf16[4,48,1152]{2,1,0:T(8,128)(2,1)S(1)}, bf16[4,48,1152]{2,1,0:T(8,128)(2,1)S(1)}, u32[]{:S(2)}, u32[]{:S(2)}) collective-permute-start(bf16[4,48,1152]{2,1,0:T(8,128)(2,1)S(1)} %collective-permute-done.4.refs_4_), channel_id=1, source_target_pairs={{0,1},{1,0},{2,3},{3,2},{4,5},{5,4},{6,7},{7,6},{8,9},{9,8},{10,11... | collective-permute-start | bytes 1327112 | tf_op jit(solution)/shard_map/ppermute | solution.py:436
  67.4 5.7 %collective-permute-start.28 = (bf16[4,48,640]{2,1,0:T(8,128)(2,1)}, bf16[4,48,640]{2,1,0:T(8,128)(2,1)S(1)}, u32[]{:S(2)}, u32[]{:S(2)}) collective-permute-start(bf16[4,48,640]{2,1,0:T(8,128)(2,1)} %collective-permute-done.17.refs_8_), channel_id=1, source_target_pairs={{0,1},{1,0},{2,3},{3,2},{4,5},{5,4},{6,7},{7,6},{8,9},{9,8},{10,11... | collective-permute-start | bytes 737288 | tf_op jit(solution)/shard_map/ppermute | solution.py:436
  69.8 4.1 %collective-permute-start.10 = (bf16[2,48,1152]{2,1,0:T(8,128)(2,1)S(1)}, bf16[2,48,1152]{2,1,0:T(8,128)(2,1)S(1)}, u32[]{:S(2)}, u32[]{:S(2)}) collective-permute-start(bf16[2,48,1152]{2,1,0:T(8,128)(2,1)S(1)} %collective-permute-done.5.refs_5_), channel_id=1, source_target_pairs={{0,1},{1,0},{2,3},{3,2},{4,5},{5,4},{6,7},{7,6},{8,9},{9,8},{10,11... | collective-permute-start | bytes 663560 | tf_op jit(solution)/shard_map/ppermute | solution.py:436
  69.8 10.1 %copy-start.14 = (bf16[2,48,1152]{2,1,0:T(8,128)(2,1)}, bf16[2,48,1152]{2,1,0:T(8,128)(2,1)S(1)}, u32[]{:S(2)}) copy-start(bf16[2,48,1152]{2,1,0:T(8,128)(2,1)S(1)} %collective-permute-done.6.refs_6_) | copy-start | bytes 663556
  69.8 5.7 %collective-permute-start.11 = (bf16[2,48,1152]{2,1,0:T(8,128)(2,1)S(1)}, bf16[2,48,1152]{2,1,0:T(8,128)(2,1)S(1)}, u32[]{:S(2)}, u32[]{:S(2)}) collective-permute-start(bf16[2,48,1152]{2,1,0:T(8,128)(2,1)S(1)} %collective-permute-done.6.refs_6_), channel_id=1, source_target_pairs={{0,1},{1,0},{2,3},{3,2},{4,5},{5,4},{6,7},{7,6},{8,9},{9,8},{10,11... | collective-permute-start | bytes 663560 | tf_op jit(solution)/shard_map/ppermute | solution.py:436
  71.6 15.1 %copy-start.1 = (bf16[256,768]{1,0:T(8,128)(2,1)S(1)}, bf16[256,768]{1,0:T(8,128)(2,1)}, u32[]{:S(2)}) copy-start(bf16[256,768]{1,0:T(8,128)(2,1)} %refs_0_.1) | copy-start | bytes 1179652
  73.8 19.4 %collective-permute-start.29 = (bf16[4,48,1536]{2,1,0:T(8,128)(2,1)S(1)}, bf16[4,48,1536]{2,1,0:T(8,128)(2,1)}, u32[]{:S(2)}, u32[]{:S(2)}) collective-permute-start(bf16[4,48,1536]{2,1,0:T(8,128)(2,1)S(1)} %shard_map.173.refs_9_), channel_id=1, source_target_pairs={{0,1},{1,0},{2,3},{3,2},{4,5},{5,4},{6,7},{7,6},{8,9},{9,8},{10,11... | collective-permute-start | bytes 1769480 | tf_op jit(solution)/shard_map/ppermute | solution.py:436
  74.6 9.7 %collective-permute-start.23 = (bf16[2,48,1536]{2,1,0:T(8,128)(2,1)}, bf16[2,48,1536]{2,1,0:T(8,128)(2,1)}, u32[]{:S(2)}, u32[]{:S(2)}) collective-permute-start(bf16[2,48,1536]{2,1,0:T(8,128)(2,1)} %slice.81), channel_id=1, source_target_pairs={{0,2},{2,0},{4,6},{6,4},{8,10},{10,8},{12,14},{14,12},{16,18},{18,... | collective-permute-start | bytes 884744 | tf_op jit(solution)/shard_map/ppermute | solution.py:440
  76.2 9.4 %collective-permute-start.24 = (bf16[2,48,1536]{2,1,0:T(8,128)(2,1)}, bf16[2,48,1536]{2,1,0:T(8,128)(2,1)}, u32[]{:S(2)}, u32[]{:S(2)}) collective-permute-start(bf16[2,48,1536]{2,1,0:T(8,128)(2,1)} %slice.82), channel_id=1, source_target_pairs={{0,4},{2,6},{4,0},{6,2},{8,12},{10,14},{12,8},{14,10},{16,20},{18,... | collective-permute-start | bytes 884744 | tf_op jit(solution)/shard_map/ppermute | solution.py:440
  78.6 14.6 %collective-permute-start.30 = (bf16[4,48,1536]{2,1,0:T(8,128)(2,1)S(1)}, bf16[4,48,1536]{2,1,0:T(8,128)(2,1)}, u32[]{:S(2)}, u32[]{:S(2)}) collective-permute-start(bf16[4,48,1536]{2,1,0:T(8,128)(2,1)S(1)} %collective-permute-done.21.refs_10_), channel_id=1, source_target_pairs={{0,1},{1,0},{2,3},{3,2},{4,5},{5,4},{6,7},{7,6},{8,9},{9,8},{10,11... | collective-permute-start | bytes 1769480 | tf_op jit(solution)/shard_map/ppermute | solution.py:436
  79.4 13.8 %collective-permute-start.31 = (bf16[4,48,1536]{2,1,0:T(8,128)(2,1)S(1)}, bf16[4,48,1536]{2,1,0:T(8,128)(2,1)}, u32[]{:S(2)}, u32[]{:S(2)}) collective-permute-start(bf16[4,48,1536]{2,1,0:T(8,128)(2,1)S(1)} %collective-permute-done.22.refs_11_), channel_id=1, source_target_pairs={{0,1},{1,0},{2,3},{3,2},{4,5},{5,4},{6,7},{7,6},{8,9},{9,8},{10,11... | collective-permute-start | bytes 1769480 | tf_op jit(solution)/shard_map/ppermute | solution.py:436
  84.3 9.0 %collective-permute-start.32 = (bf16[2,48,1536]{2,1,0:T(8,128)(2,1)}, bf16[2,48,1536]{2,1,0:T(8,128)(2,1)S(1)}, u32[]{:S(2)}, u32[]{:S(2)}) collective-permute-start(bf16[2,48,1536]{2,1,0:T(8,128)(2,1)} %collective-permute-done.23.refs_12_), channel_id=1, source_target_pairs={{0,1},{1,0},{2,3},{3,2},{4,5},{5,4},{6,7},{7,6},{8,9},{9,8},{10,11... | collective-permute-start | bytes 884744 | tf_op jit(solution)/shard_map/ppermute | solution.py:436
  85.6 7.7 %collective-permute-start.33 = (bf16[2,48,1536]{2,1,0:T(8,128)(2,1)}, bf16[2,48,1536]{2,1,0:T(8,128)(2,1)S(1)}, u32[]{:S(2)}, u32[]{:S(2)}) collective-permute-start(bf16[2,48,1536]{2,1,0:T(8,128)(2,1)} %collective-permute-done.24.refs_13_), channel_id=1, source_target_pairs={{0,1},{1,0},{2,3},{3,2},{4,5},{5,4},{6,7},{7,6},{8,9},{9,8},{10,11... | collective-permute-start | bytes 884744 | tf_op jit(solution)/shard_map/ppermute | solution.py:436
  100.4 13.7 %collective-permute-start.41 = (bf16[256,2560]{1,0:T(8,128)(2,1)S(1)}, bf16[256,2560]{1,0:T(8,128)(2,1)S(1)}, u32[]{:S(2)}, u32[]{:S(2)}) collective-permute-start(bf16[256,2560]{1,0:T(8,128)(2,1)S(1)} %get-tuple-element.94.refs_0_), channel_id=1, source_target_pairs={{0,1},{1,0},{2,3},{3,2},{4,5},{5,4},{6,7},{7,6},{8,9},{9,8},{10,11... | collective-permute-start | bytes 3932168 | tf_op jit(solution)/shard_map/ppermute | solution.py:436
  110.0 8.4 %collective-permute-start.34 = (bf16[272,1920]{1,0:T(8,128)(2,1)S(1)}, bf16[272,1920]{1,0:T(8,128)(2,1)S(1)}, u32[]{:S(2)}, u32[]{:S(2)}) collective-permute-start(bf16[272,1920]{1,0:T(8,128)(2,1)S(1)} %get-tuple-element.78.refs_0_), channel_id=1, source_target_pairs={{0,1},{1,0},{2,3},{3,2},{4,5},{5,4},{6,7},{7,6},{8,9},{9,8},{10,11... | collective-permute-start | bytes 3133448 | tf_op jit(solution)/shard_map/ppermute | solution.py:436
  110.0 4.1 %collective-permute-start.42 = (bf16[272,768]{1,0:T(8,128)(2,1)S(1)}, bf16[272,768]{1,0:T(8,128)(2,1)S(1)}, u32[]{:S(2)}, u32[]{:S(2)}) collective-permute-start(bf16[272,768]{1,0:T(8,128)(2,1)S(1)} %get-tuple-element.96.refs_3_), channel_id=1, source_target_pairs={{0,1},{1,0},{2,3},{3,2},{4,5},{5,4},{6,7},{7,6},{8,9},{9,8},{10,11... | collective-permute-start | bytes 1253384 | tf_op jit(solution)/shard_map/ppermute | solution.py:436
  110.5 3.3 %collective-permute-start.44 = (bf16[256,768]{1,0:T(8,128)(2,1)S(1)}, bf16[256,768]{1,0:T(8,128)(2,1)S(1)}, u32[]{:S(2)}, u32[]{:S(2)}) collective-permute-start(bf16[256,768]{1,0:T(8,128)(2,1)S(1)} %multiply_convert_fusion.refs_3_.gm_ref.refs_7_), channel_id=1, source_target_pairs={{0,1},{1,0},{2,3},{3,2},{4,5},{5,4},{6,7},{7,6},{8,9},{9,8},{10,11... | collective-permute-start | bytes 1179656 | tf_op jit(solution)/shard_map/ppermute | solution.py:436
  110.5 3.6 %collective-permute-start.43 = (bf16[256,384]{1,0:T(8,128)(2,1)S(1)}, bf16[256,384]{1,0:T(8,128)(2,1)S(1)}, u32[]{:S(2)}, u32[]{:S(2)}) collective-permute-start(bf16[256,384]{1,0:T(8,128)(2,1)S(1)} %get-tuple-element.97), channel_id=1, source_target_pairs={{0,1},{1,0},{2,3},{3,2},{4,5},{5,4},{6,7},{7,6},{8,9},{9,8},{10,11... | collective-permute-start | bytes 589832 | tf_op jit(solution)/shard_map/ppermute | solution.py:436
  116.7 28.2 %collective-permute-start.50 = (bf16[8,48,768]{2,1,0:T(8,128)(2,1)S(1)}, bf16[8,48,768]{2,1,0:T(8,128)(2,1)S(1)}, u32[]{:S(2)}, u32[]{:S(2)}) collective-permute-start(bf16[8,48,768]{2,1,0:T(8,128)(2,1)S(1)} %get-tuple-element.109), channel_id=1, source_target_pairs={{0,4},{2,6},{4,0},{6,2},{8,12},{10,14},{12,8},{14,10},{16,20},{18,... | collective-permute-start | bytes 1769480 | tf_op jit(solution)/shard_map/ppermute | solution.py:440
  119.9 14.2 %collective-permute-start.35 = (bf16[8,48,640]{2,1,0:T(8,128)(2,1)S(1)}, bf16[8,48,640]{2,1,0:T(8,128)(2,1)S(1)}, u32[]{:S(2)}, u32[]{:S(2)}) collective-permute-start(bf16[8,48,640]{2,1,0:T(8,128)(2,1)S(1)} %get-tuple-element.81), channel_id=1, source_target_pairs={{0,2},{2,0},{4,6},{6,4},{8,10},{10,8},{12,14},{14,12},{16,18},{18,... | collective-permute-start | bytes 1474568 | tf_op jit(solution)/shard_map/ppermute | solution.py:440
  120.2 22.5 %collective-permute-start.36 = (bf16[8,48,640]{2,1,0:T(8,128)(2,1)S(1)}, bf16[8,48,640]{2,1,0:T(8,128)(2,1)S(1)}, u32[]{:S(2)}, u32[]{:S(2)}) collective-permute-start(bf16[8,48,640]{2,1,0:T(8,128)(2,1)S(1)} %get-tuple-element.83), channel_id=1, source_target_pairs={{0,4},{2,6},{4,0},{6,2},{8,12},{10,14},{12,8},{14,10},{16,20},{18,... | collective-permute-start | bytes 1474568 | tf_op jit(solution)/shard_map/ppermute | solution.py:440
  121.4 23.5 %collective-permute-start.49 = (bf16[8,48,640]{2,1,0:T(8,128)(2,1)S(1)}, bf16[8,48,640]{2,1,0:T(8,128)(2,1)S(1)}, u32[]{:S(2)}, u32[]{:S(2)}) collective-permute-start(bf16[8,48,640]{2,1,0:T(8,128)(2,1)S(1)} %get-tuple-element.107), channel_id=1, source_target_pairs={{0,2},{2,0},{4,6},{6,4},{8,10},{10,8},{12,14},{14,12},{16,18},{18,... | collective-permute-start | bytes 1474568 | tf_op jit(solution)/shard_map/ppermute | solution.py:440
  122.3 25.0 %collective-permute-start.45 = (bf16[8,48,768]{2,1,0:T(8,128)(2,1)S(1)}, bf16[8,48,768]{2,1,0:T(8,128)(2,1)S(1)}, u32[]{:S(2)}, u32[]{:S(2)}) collective-permute-start(bf16[8,48,768]{2,1,0:T(8,128)(2,1)S(1)} %get-tuple-element.99), channel_id=1, source_target_pairs={{0,8},{2,10},{4,12},{6,14},{8,0},{10,2},{12,4},{14,6},{16,24},{18,... | collective-permute-start | bytes 1769480 | tf_op jit(solution)/shard_map/ppermute | solution.py:440
  142.9 9.4 %collective-permute-start.37 = (bf16[4,48,640]{2,1,0:T(8,128)(2,1)S(1)}, bf16[4,48,640]{2,1,0:T(8,128)(2,1)S(1)}, u32[]{:S(2)}, u32[]{:S(2)}) collective-permute-start(bf16[4,48,640]{2,1,0:T(8,128)(2,1)S(1)} %get-tuple-element.85), channel_id=1, source_target_pairs={{0,4},{2,6},{4,0},{6,2},{8,12},{10,14},{12,8},{14,10},{16,20},{18,... | collective-permute-start | bytes 737288 | tf_op jit(solution)/shard_map/ppermute | solution.py:440
  144.6 8.8 %collective-permute-start.38 = (bf16[4,48,640]{2,1,0:T(8,128)(2,1)S(1)}, bf16[4,48,640]{2,1,0:T(8,128)(2,1)S(1)}, u32[]{:S(2)}, u32[]{:S(2)}) collective-permute-start(bf16[4,48,640]{2,1,0:T(8,128)(2,1)S(1)} %get-tuple-element.87), channel_id=1, source_target_pairs={{0,2},{2,0},{4,6},{6,4},{8,10},{10,8},{12,14},{14,12},{16,18},{18,... | collective-permute-start | bytes 737288 | tf_op jit(solution)/shard_map/ppermute | solution.py:440
  145.2 12.9 %collective-permute-start.52 = (bf16[4,48,768]{2,1,0:T(8,128)(2,1)S(1)}, bf16[4,48,768]{2,1,0:T(8,128)(2,1)S(1)}, u32[]{:S(2)}, u32[]{:S(2)}) collective-permute-start(bf16[4,48,768]{2,1,0:T(8,128)(2,1)S(1)} %get-tuple-element.113), channel_id=1, source_target_pairs={{0,2},{2,0},{4,6},{6,4},{8,10},{10,8},{12,14},{14,12},{16,18},{18,... | collective-permute-start | bytes 884744 | tf_op jit(solution)/shard_map/ppermute | solution.py:440
  147.0 11.1 %collective-permute-start.51 = (bf16[4,48,640]{2,1,0:T(8,128)(2,1)S(1)}, bf16[4,48,640]{2,1,0:T(8,128)(2,1)S(1)}, u32[]{:S(2)}, u32[]{:S(2)}) collective-permute-start(bf16[4,48,640]{2,1,0:T(8,128)(2,1)S(1)} %get-tuple-element.111), channel_id=1, source_target_pairs={{0,4},{2,6},{4,0},{6,2},{8,12},{10,14},{12,8},{14,10},{16,20},{18,... | collective-permute-start | bytes 737288 | tf_op jit(solution)/shard_map/ppermute | solution.py:440
  147.5 16.5 %collective-permute-start.46 = (bf16[4,48,768]{2,1,0:T(8,128)(2,1)S(1)}, bf16[4,48,768]{2,1,0:T(8,128)(2,1)S(1)}, u32[]{:S(2)}, u32[]{:S(2)}) collective-permute-start(bf16[4,48,768]{2,1,0:T(8,128)(2,1)S(1)} %get-tuple-element.101), channel_id=1, source_target_pairs={{0,16},{2,18},{4,20},{6,22},{8,24},{10,26},{12,28},{14,30},{16,0},... | collective-permute-start | bytes 884744 | tf_op jit(solution)/shard_map/ppermute | solution.py:440
  153.5 14.0 %collective-permute-start.39 = (bf16[2,48,1280]{2,1,0:T(8,128)(2,1)S(1)}, bf16[2,48,1280]{2,1,0:T(8,128)(2,1)S(1)}, u32[]{:S(2)}, u32[]{:S(2)}) collective-permute-start(bf16[2,48,1280]{2,1,0:T(8,128)(2,1)S(1)} %get-tuple-element.89), channel_id=1, source_target_pairs={{0,8},{2,10},{4,12},{6,14},{8,0},{10,2},{12,4},{14,6},{16,24},{18,... | collective-permute-start | bytes 737288 | tf_op jit(solution)/shard_map/ppermute | solution.py:440
  158.2 13.5 %collective-permute-start.53 = (bf16[2,48,1408]{2,1,0:T(8,128)(2,1)S(1)}, bf16[2,48,1408]{2,1,0:T(8,128)(2,1)S(1)}, u32[]{:S(2)}, u32[]{:S(2)}) collective-permute-start(bf16[2,48,1408]{2,1,0:T(8,128)(2,1)S(1)} %get-tuple-element.115), channel_id=1, source_target_pairs={{0,8},{2,10},{4,12},{6,14},{8,0},{10,2},{12,4},{14,6},{16,24},{18,... | collective-permute-start | bytes 811016 | tf_op jit(solution)/shard_map/ppermute | solution.py:440
  164.1 11.5 %collective-permute-start.47 = (bf16[2,48,768]{2,1,0:T(8,128)(2,1)S(1)}, bf16[2,48,768]{2,1,0:T(8,128)(2,1)S(1)}, u32[]{:S(2)}, u32[]{:S(2)}) collective-permute-start(bf16[2,48,768]{2,1,0:T(8,128)(2,1)S(1)} %get-tuple-element.103), channel_id=1, source_target_pairs={{0,2},{2,0},{4,6},{6,4},{8,10},{10,8},{12,14},{14,12},{16,18},{18,... | collective-permute-start | bytes 442376 | tf_op jit(solution)/shard_map/ppermute | solution.py:440
  167.6 7.3 %collective-permute-start.40 = (bf16[1,48,1280]{2,1,0:T(8,128)(2,1)S(1)}, bf16[1,48,1280]{2,1,0:T(8,128)(2,1)S(1)}, u32[]{:S(2)}, u32[]{:S(2)}) collective-permute-start(bf16[1,48,1280]{2,1,0:T(8,128)(2,1)S(1)} %get-tuple-element.91), channel_id=1, source_target_pairs={{0,16},{2,18},{4,20},{6,22},{8,24},{10,26},{12,28},{14,30},{16,0},... | collective-permute-start | bytes 368648 | tf_op jit(solution)/shard_map/ppermute | solution.py:440
  171.7 11.6 %collective-permute-start.54 = (bf16[1,48,1408]{2,1,0:T(8,128)(2,1)S(1)}, bf16[1,48,1408]{2,1,0:T(8,128)(2,1)S(1)}, u32[]{:S(2)}, u32[]{:S(2)}) collective-permute-start(bf16[1,48,1408]{2,1,0:T(8,128)(2,1)S(1)} %get-tuple-element.117), channel_id=1, source_target_pairs={{0,16},{2,18},{4,20},{6,22},{8,24},{10,26},{12,28},{14,30},{16,0},... | collective-permute-start | bytes 405512 | tf_op jit(solution)/shard_map/ppermute | solution.py:440
  175.7 7.7 %collective-permute-start.48 = (bf16[1,48,768]{2,1,0:T(8,128)(2,1)S(1)}, bf16[1,48,768]{2,1,0:T(8,128)(2,1)S(1)}, u32[]{:S(2)}, u32[]{:S(2)}) collective-permute-start(bf16[1,48,768]{2,1,0:T(8,128)(2,1)S(1)} %get-tuple-element.105), channel_id=1, source_target_pairs={{0,4},{2,6},{4,0},{6,2},{8,12},{10,14},{12,8},{14,10},{16,20},{18,... | collective-permute-start | bytes 221192 | tf_op jit(solution)/shard_map/ppermute | solution.py:440
  (15 other events, 60.0 us)

commit v5 on v4

--- a/solution.py
+++ b/solution.py
@@ -133,9 +133,11 @@
             chunk = product[:, sub : sub + LANES]
             if at < 2 * width:
                 chunk = chunk * cosine + swap_halves(chunk) * sine
-            qkv_ref[:, at + sub : at + sub + LANES] = chunk.astype(BF16)
+            chunk = chunk.astype(BF16)
+            if at + sub < width:
+                chunk = chunk * BF16(HD ** (-0.5))
+            qkv_ref[:, at + sub : at + sub + LANES] = chunk
     mask = attn_mask(seg_row[...], seg_col[...], live_row[...])
-    scale = HD ** (-0.5)
     rows = x_ref.shape[0]
     low = lane_index((rows, LANES)) < HD
     lanes = lane_index((rows, LANES))
@@ -148,7 +150,7 @@
         outs = []
         for side in range(2):
             picked = jnp.where(low if side == 0 else ~low, queries, jnp.zeros_like(queries))
-            scores = jnp.where(mask, mm(picked, keys, NT) * scale, MASKED_SCORE)
+            scores = jnp.where(mask, mm(picked, keys, NT), MASKED_SCORE)
             row_max = jnp.max(scores, axis=-1, keepdims=True)
             weights = jnp.exp(scores - row_max)
             total = jnp.sum(weights, axis=-1, keepdims=True)
@@ -277,7 +279,7 @@
             q_side = jnp.where(on, queries, jnp.zeros_like(queries))
             g_side = jnp.where(on, grad_att, jnp.zeros_like(grad_att))
             head = 2 * pair + side
-            scores = jnp.where(mask, mm(q_side, keys, NT) * scale, MASKED_SCORE)
+            scores = jnp.where(mask, mm(q_side, keys, NT), MASKED_SCORE)
             prob = jnp.exp(scores - logt_ref[:, head : head + 1])
             row_inner = jnp.sum(jnp.where(on, products, 0.0), axis=-1, keepdims=True)
             grad_prob = mm(g_side, values, NT)
@@ -286,7 +288,6 @@
             grads_q.append(mm(grad_scores, keys, NN))
             grad_k = grad_k + mm(grad_scores, q_side, TN)
         grad_q = jnp.where(low, grads_q[0], grads_q[1]) * scale
-        grad_k = grad_k * scale
         grad_q = grad_q * cosine - swap_halves(grad_q) * sine
         grad_k = grad_k * cosine - swap_halves(grad_k) * sine
         for c, value in enumerate((grad_q, grad_k, grad_v)):
@@ -374,7 +375,10 @@
     for c in range(3):
         cols = slice(c * half, (c + 1) * half)
         grad[c] = (kept[0, :, cols] + came[0, :, cols].astype(F32)) * gain
-    gain_grad[...] = (kept[0, :, 3 * half :] + came[0, :, 3 * half :].astype(F32)) / gain
+    columns = (kept[0, :, 3 * half :] + came[0, :, 3 * half :].astype(F32)) / gain
+    row = lax.broadcasted_iota(jnp.int32, columns.shape, 0)
+    picked = jnp.where(row == lane_index(columns.shape), columns, 0.0)
+    gain_grad[...] = jnp.sum(picked, axis=0)[: gain_grad.shape[0]]
 
 
 VMEM = pl.BlockSpec(memory_space=pltpu.VMEM)
@@ -470,7 +474,7 @@
         axis=1,
     )
     total_qkv, total_ffn = pack_qkv.shape[1], pack_ffn.shape[1]
-    cut = total_ffn * 3 // 10 // LANES * LANES
+    cut = total_ffn // 4 // LANES * LANES
     if fast:
         own_qkv = plane(stack(across_z(pack_qkv)))
         other_qkv = both_cores(own_qkv)
@@ -639,14 +643,13 @@
         )
         keep, send = combine(True, keep_a, exchange(send_a, Y), keep_b, exchange(send_b, X))
         keep, send = combine(False, keep, exchange(send, Z))
-        grad_qkv, gain1_share = call(
+        grad_qkv, grad_gain1 = call(
             final_qkv_kernel,
             [keep, exchange(send, ZZ), gain_col],
-            [shape(3, rows, half, dtype=F32), shape(rows, LANES, dtype=F32)],
+            [shape(3, rows, half, dtype=F32), shape(rows, dtype=F32)],
             [],
             scalars=0,
         )
-        grad_gain1 = gain1_share[:, 0]
     else:
         share1, share2 = (
             lax.psum_scatter(pieces[0], "dp", scatter_dimension=0, tiled=True)

time: 187 us -> 176 us (0.941)
  waiting for transfers between devices: 67.4 us -> 77.3 us
  local copies, waits for them, and re-layouts: 13 us -> 5.45 us
  starting transfers between devices: 67.9 us -> 60.4 us
  other arithmetic: 8.66 us -> 5.5 us
  Pallas kernels: 27.6 us -> 24.7 us
    ppermute x36, waiting for transfers between devices: 64.3 us -> 72.9 us  [exchange(): return lax.ppermute(value, 'dp', pairs)]
    ppermute x36, starting transfers between devices: 64.6 us -> 56.4 us  [exchange(): return lax.ppermute(value, 'dp', pairs)]
    unnamed x48 -> x16, local copies, waits for them, and re-layouts: 4.62 us -> 0.06 us
    pallas_call x20, Pallas kernels: 27.6 us -> 24.7 us  [call(): pl.pallas_call(kernel, out_shape=outs, in_specs=[SMEM] * scalars + [VMEM]...]
  transfers between devices with their start and end apart: 55 -> 55, of which waited for: 22 -> 20; matrix products, arithmetic and copies ran while one was open for 7% -> 4% of each run, Pallas kernels for 11% -> 11%
where the time goes in v5:
time: 176 us; the launch traced here: 175 us
  waiting for transfers between devices  77.3 us (44%)
  starting transfers between devices  60.4 us (34%)
  Pallas kernels  24.7 us (14%)
  other arithmetic  5.5 us (3%)
  local copies, waits for them, and re-layouts  5.45 us (3%)
  between operations  1.8 us (1%)
    ppermute x36, waiting for transfers between devices, exchange(): return lax.ppermute(value, 'dp', pairs)  72.9 us
    ppermute x36, starting transfers between devices, exchange(): return lax.ppermute(value, 'dp', pairs)  56.4 us
    pallas_call x20, Pallas kernels, call(): pl.pallas_call(kernel, out_shape=outs, in_specs=[SMEM] * scalars + [VMEM]...  24.7 us
    ppermute x19, waiting for transfers between devices, swap_cores(): return lax.ppermute(value, 'tensor', [(0, 1), (1, 0)])  4.37 us
    ppermute x19, starting transfers between devices, swap_cores(): return lax.ppermute(value, 'tensor', [(0, 1), (1, 0)])  4.04 us
  transfers between devices with their start and end apart: 55, of which 20 were waited for; matrix products, arithmetic and copies ran while one was open for 4% of the time, Pallas kernels for 11%

profile of v5, /device:TPU:0, one launch (start us, length us, event | category | flops | bytes accessed | tf_op | source)
XLA Modules:
  0.0 175.2 jit_solution(259673904137150894)
XLA Ops:
  0.7 0.7 convert_bitcast_fusion
  1.4 0.9 fusion.4
  2.3 3.1 %collective-permute-start = (bf16[48,1152]{1,0:T(8,128)(2,1)S(1)}, bf16[48,1152]{1,0:T(8,128)(2,1)S(1)}, u32[]{:S(2)}, u32[]{:S(2)}) collective-permute-start(bf16[48,1152]{1,0:T(8,128)(2,1)S(1)} %pad_maximum_fusion.3.refs_0_), channel_id=1, source_target_pairs={{0,8},{2,10},{4,12},{6,14},{8,0},{10,2},{12,4},{14,6},{16,24},{18,... | collective-permute-start | bytes 331784 | tf_op jit(solution)/shard_map/ppermute | solution.py:444
  5.4 2.6 %collective-permute-start.1 = (bf16[48,1152]{1,0:T(8,128)(2,1)S(1)}, bf16[48,1152]{1,0:T(8,128)(2,1)S(1)}, u32[]{:S(2)}, u32[]{:S(2)}) collective-permute-start(bf16[48,1152]{1,0:T(8,128)(2,1)S(1)} %pad_maximum_fusion.3.refs_0_), channel_id=1, source_target_pairs={{0,16},{2,18},{4,20},{6,22},{8,24},{10,26},{12,28},{14,30},{16,0},... | collective-permute-start | bytes 331784 | tf_op jit(solution)/shard_map/ppermute | solution.py:444
  8.0 1.1 fusion.7
  9.2 1.8 %collective-permute-start.13 = (bf16[48,512]{1,0:T(8,128)(2,1)S(1)}, bf16[48,512]{1,0:T(8,128)(2,1)S(1)}, u32[]{:S(2)}, u32[]{:S(2)}) collective-permute-start(bf16[48,512]{1,0:T(8,128)(2,1)S(1)} %bitcast.35), channel_id=1, source_target_pairs={{0,4},{2,6},{4,0},{6,2},{8,12},{10,14},{12,8},{14,10},{16,20},{18,... | collective-permute-start | bytes 147464 | tf_op jit(solution)/shard_map/ppermute | solution.py:444
  11.0 1.5 collective-permute-start.12
  12.5 0.9 fusion.6
  13.3 1.7 collective-permute-start.14
  15.0 1.7 collective-permute-done.1.refs_2_
  16.8 1.6 collective-permute-start.4
  18.4 1.5 collective-permute-start.3
  20.2 1.8 %collective-permute-start.18 = (bf16[48,1664]{1,0:T(8,128)(2,1)S(1)}, bf16[48,1664]{1,0:T(8,128)(2,1)S(1)}, u32[]{:S(2)}, u32[]{:S(2)}) collective-permute-start(bf16[48,1664]{1,0:T(8,128)(2,1)S(1)} %concatenate.18.refs_0_), channel_id=1, source_target_pairs={{0,8},{2,10},{4,12},{6,14},{8,0},{10,2},{12,4},{14,6},{16,24},{18,... | collective-permute-start | bytes 479240 | tf_op jit(solution)/shard_map/ppermute | solution.py:444
  22.0 1.2 collective-permute-start.19
  23.2 1.4 collective-permute-start.20
  24.7 5.2 %collective-permute-done.18.refs_1_ = bf16[48,1664]{1,0:T(8,128)(2,1)S(1)} collective-permute-done((bf16[48,1664]{1,0:T(8,128)(2,1)S(1)}, bf16[48,1664]{1,0:T(8,128)(2,1)S(1)}, u32[]{:S(2)}, u32[]{:S(2)}) %collective-permute-start.18) | collective-permute-done | bytes 159776 | tf_op jit(solution)/shard_map/ppermute | solution.py:444
  29.8 5.2 %collective-permute-done.19.refs_2_ = bf16[48,1664]{1,0:T(8,128)(2,1)S(1)} collective-permute-done((bf16[48,1664]{1,0:T(8,128)(2,1)S(1)}, bf16[48,1664]{1,0:T(8,128)(2,1)S(1)}, u32[]{:S(2)}, u32[]{:S(2)}) %collective-permute-start.19) | collective-permute-done | bytes 159776 | tf_op jit(solution)/shard_map/ppermute | solution.py:444
  35.1 1.2 collective-permute-done.20.refs_3_
  36.3 2.2 %collective-permute-start.17 = (bf16[4,48,512]{2,1,0:T(8,128)(2,1)S(1)}, bf16[4,48,512]{2,1,0:T(8,128)(2,1)S(1)}, u32[]{:S(2)}, u32[]{:S(2)}) collective-permute-start(bf16[4,48,512]{2,1,0:T(8,128)(2,1)S(1)} %shard_map.172.refs_5_), channel_id=1, source_target_pairs={{0,24},{2,26},{4,28},{6,30},{8,16},{10,18},{12,20},{14,22},{16,8},... | collective-permute-start | bytes 589832 | tf_op jit(solution)/shard_map/ppermute | solution.py:444
  39.2 0.6 dynamic_slice.7
  40.0 11.7 %collective-permute-done.16.refs_7_ = bf16[4,48,512]{2,1,0:T(8,128)(2,1)S(1)} collective-permute-done((bf16[4,48,512]{2,1,0:T(8,128)(2,1)S(1)}, bf16[4,48,512]{2,1,0:T(8,128)(2,1)S(1)}, u32[]{:S(2)}, u32[]{:S(2)}) %collective-permute-start.16) | collective-permute-done | bytes 196640 | tf_op jit(solution)/shard_map/ppermute | solution.py:444
  53.2 0.7 and_convert_fusion.refs_14_.refs_9_
  54.1 1.6 collective-permute-start.5
  55.7 1.5 collective-permute-start.6
  57.2 0.6 and_convert_fusion.1
  57.9 0.7 fusion.1.refs_4_
  58.6 9.9 %collective-permute-done.5.refs_5_ = bf16[2,48,1152]{2,1,0:T(8,128)(2,1)S(1)} collective-permute-done((bf16[2,48,1152]{2,1,0:T(8,128)(2,1)S(1)}, bf16[2,48,1152]{2,1,0:T(8,128)(2,1)S(1)}, u32[]{:S(2)}, u32[]{:S(2)}) %collective-permute-start.5) | collective-permute-done | bytes 221216 | tf_op jit(solution)/shard_map/ppermute | solution.py:444
  70.1 1.2 collective-permute-done.10.refs_10_
  71.8 1.6 collective-permute-start.24
  73.9 0.5 fusion.5
  74.7 6.2 %collective-permute-done.23.refs_12_ = bf16[2,48,1664]{2,1,0:T(8,128)(2,1)S(1)} collective-permute-done((bf16[2,48,1664]{2,1,0:T(8,128)(2,1)S(1)}, bf16[2,48,1664]{2,1,0:T(8,128)(2,1)S(1)}, u32[]{:S(2)}, u32[]{:S(2)}) %collective-permute-start.23) | collective-permute-done | bytes 319520 | tf_op jit(solution)/shard_map/ppermute | solution.py:444
  81.5 4.4 %shard_map.171 = (bf16[768,2304]{1,0:T(8,128)(2,1)S(1)}, bf16[256,2304]{1,0:T(8,128)(2,1)S(1)}, bf16[256,768]{1,0:T(8,128)(2,1)S(1)}, bf16[256,384]{1,0:T(8,128)...) custom-call(s32[1]{0:T(128)} %bitcast.refs_0_.me_ref, bf16[256,768]{1,0:T(8,128)(2,1)S(1)} %copy-done.1, ...), custom_call_target="tpu_custom_call" | custom-call | flops 905969664 | bytes 10030084 | tf_op jit(solution)/shard_map/pallas_call | solution.py:392
  86.0 5.2 %shard_map.174 = (bf16[256,768]{1,0:T(8,128)(2,1)}, f32[256,768]{1,0:T(8,128)S(1)}, f32[8,768]{1,0:T(8,128)S(1)}, bf16[768,768]{1,0:T(8,128)(2,1)S(1)}, bf16[768...) custom-call(s32[1]{0:T(128)} %bitcast.refs_0_.me_ref, ...), custom_call_target="tpu_custom_call" | custom-call | flops 1811939328 | bytes 17196036 | tf_op jit(solution)/shard_map/pallas_call | solution.py:392
  91.5 1.5 shard_map.175
  93.0 7.7 %shard_map.176 = (f32[256,768]{1,0:T(8,128)}, bf16[272,1920]{1,0:T(8,128)(2,1)S(1)}, bf16[256,1152]{1,0:T(8,128)(2,1)S(1)}) custom-call(bf16[256,768]{1,0:T(8,128)(2,1)S(1)} %copy-done.1, f32[256,768]{1,0:T(8,128)S(1)} %get-tuple-element.71.refs_1_, bf16[768,768]{1,0:T(8,128)(2,1)S(1)} %get-tuple-element.72.refs_2_, ...), custom_call_target="tpu_custom_call" | custom-call | flops 1509949440 | bytes 10681344 | tf_op jit(solution)/shard_map/pallas_call | solution.py:392
  101.8 2.8 %collective-permute-done.44.refs_8_ = bf16[256,768]{1,0:T(8,128)(2,1)S(1)} collective-permute-done((bf16[256,768]{1,0:T(8,128)(2,1)S(1)}, bf16[256,768]{1,0:T(8,128)(2,1)S(1)}, u32[]{:S(2)}, u32[]{:S(2)}) %collective-permute-start.44) | collective-permute-done | bytes 393248 | tf_op jit(solution)/shard_map/ppermute | solution.py:440
  104.9 2.6 %shard_map.182 = (bf16[8,48,768]{2,1,0:T(8,128)(2,1)S(1)}, bf16[8,48,768]{2,1,0:T(8,128)(2,1)S(1)}, bf16[8,48,640]{2,1,0:T(8,128)(2,1)S(1)}, bf16[8,48,640]{2,1,...) custom-call(s32[1]{0:T(128)} %bitcast.refs_0_.me_ref, ...), custom_call_target="tpu_custom_call" | custom-call | flops 1711276032 | bytes 9093124 | tf_op jit(solution)/shard_map/pallas_call | solution.py:392
  107.5 1.6 collective-permute-start.50
  109.1 1.4 collective-permute-start.49
  110.5 1.4 shard_map.177
  111.9 0.6 collective-permute-start.35
  113.1 5.6 %collective-permute-start.45 = (bf16[8,48,768]{2,1,0:T(8,128)(2,1)S(1)}, bf16[8,48,768]{2,1,0:T(8,128)(2,1)S(1)}, u32[]{:S(2)}, u32[]{:S(2)}) collective-permute-start(bf16[8,48,768]{2,1,0:T(8,128)(2,1)S(1)} %get-tuple-element.99), channel_id=1, source_target_pairs={{0,8},{2,10},{4,12},{6,14},{8,0},{10,2},{12,4},{14,6},{16,24},{18,... | collective-permute-start | bytes 1769480 | tf_op jit(solution)/shard_map/ppermute | solution.py:444
  118.7 4.5 %collective-permute-done.49.refs_1_ = bf16[8,48,640]{2,1,0:T(8,128)(2,1)S(1)} collective-permute-done((bf16[8,48,640]{2,1,0:T(8,128)(2,1)S(1)}, bf16[8,48,640]{2,1,0:T(8,128)(2,1)S(1)}, u32[]{:S(2)}, u32[]{:S(2)}) %collective-permute-start.49) | collective-permute-done | bytes 491552 | tf_op jit(solution)/shard_map/ppermute | solution.py:444
  123.2 0.6 collective-permute-done.50.refs_3_
  124.0 1.5 collective-permute-start.52
  125.5 1.5 collective-permute-start.51
  127.0 6.7 %collective-permute-done.35.refs_1_ = bf16[8,48,640]{2,1,0:T(8,128)(2,1)S(1)} collective-permute-done((bf16[8,48,640]{2,1,0:T(8,128)(2,1)S(1)}, bf16[8,48,640]{2,1,0:T(8,128)(2,1)S(1)}, u32[]{:S(2)}, u32[]{:S(2)}) %collective-permute-start.35) | collective-permute-done | bytes 491552 | tf_op jit(solution)/shard_map/ppermute | solution.py:444
  133.7 0.6 collective-permute-done.36.refs_3_
  134.5 1.6 collective-permute-start.37
  136.1 1.4 collective-permute-start.38
  137.7 6.5 %collective-permute-start.46 = (bf16[4,48,768]{2,1,0:T(8,128)(2,1)S(1)}, bf16[4,48,768]{2,1,0:T(8,128)(2,1)S(1)}, u32[]{:S(2)}, u32[]{:S(2)}) collective-permute-start(bf16[4,48,768]{2,1,0:T(8,128)(2,1)S(1)} %get-tuple-element.101), channel_id=1, source_target_pairs={{0,16},{2,18},{4,20},{6,22},{8,24},{10,26},{12,28},{14,30},{16,0},... | collective-permute-start | bytes 884744 | tf_op jit(solution)/shard_map/ppermute | solution.py:444
  144.3 1.0 collective-permute-start.53
  145.4 4.4 %collective-permute-start.39 = (bf16[2,48,1280]{2,1,0:T(8,128)(2,1)S(1)}, bf16[2,48,1280]{2,1,0:T(8,128)(2,1)S(1)}, u32[]{:S(2)}, u32[]{:S(2)}) collective-permute-start(bf16[2,48,1280]{2,1,0:T(8,128)(2,1)S(1)} %get-tuple-element.89), channel_id=1, source_target_pairs={{0,8},{2,10},{4,12},{6,14},{8,0},{10,2},{12,4},{14,6},{16,24},{18,... | collective-permute-start | bytes 737288 | tf_op jit(solution)/shard_map/ppermute | solution.py:444
  149.8 5.9 %collective-permute-done.46.refs_1_ = bf16[4,48,768]{2,1,0:T(8,128)(2,1)S(1)} collective-permute-done((bf16[4,48,768]{2,1,0:T(8,128)(2,1)S(1)}, bf16[4,48,768]{2,1,0:T(8,128)(2,1)S(1)}, u32[]{:S(2)}, u32[]{:S(2)}) %collective-permute-start.46) | collective-permute-done | bytes 294944 | tf_op jit(solution)/shard_map/ppermute | solution.py:444
  155.7 0.8 collective-permute-start.47
  156.5 2.2 %collective-permute-done.53.refs_1_ = bf16[2,48,1408]{2,1,0:T(8,128)(2,1)S(1)} collective-permute-done((bf16[2,48,1408]{2,1,0:T(8,128)(2,1)S(1)}, bf16[2,48,1408]{2,1,0:T(8,128)(2,1)S(1)}, u32[]{:S(2)}, u32[]{:S(2)}) %collective-permute-start.53) | collective-permute-done | bytes 270368 | tf_op jit(solution)/shard_map/ppermute | solution.py:444
  158.9 4.7 %collective-permute-done.39.refs_1_ = bf16[2,48,1280]{2,1,0:T(8,128)(2,1)S(1)} collective-permute-done((bf16[2,48,1280]{2,1,0:T(8,128)(2,1)S(1)}, bf16[2,48,1280]{2,1,0:T(8,128)(2,1)S(1)}, u32[]{:S(2)}, u32[]{:S(2)}) %collective-permute-start.39) | collective-permute-done | bytes 245792 | tf_op jit(solution)/shard_map/ppermute | solution.py:444
  163.8 1.1 collective-permute-start.48
  165.0 6.3 %collective-permute-done.40.came = bf16[1,48,1280]{2,1,0:T(8,128)(2,1)S(1)} collective-permute-done((bf16[1,48,1280]{2,1,0:T(8,128)(2,1)S(1)}, bf16[1,48,1280]{2,1,0:T(8,128)(2,1)S(1)}, u32[]{:S(2)}, u32[]{:S(2)}) %collective-permute-start.40) | collective-permute-done | bytes 122912 | tf_op jit(solution)/shard_map/ppermute | solution.py:444
  171.3 0.8 shard_map.181
  172.1 0.7 slice_bitcast_fusion
  172.8 0.6 slice_bitcast_fusion.1
  173.4 0.7 slice_reduce_fusion
  174.4 0.8 pad_maximum_fusion
  (117 shorter events, 9.4 us)
Async XLA Ops:
  0.6 39.1 %copy-start = (s32[2,256]{1,0:T(2,128)S(1)}, s32[2,256]{1,0:T(2,128)}, u32[]{:S(2)}) copy-start(s32[2,256]{1,0:T(2,128)} %param.19) | copy-start | bytes 6148
  0.6 19.3 %copy-start.5 = (bf16[48]{0:T(256)(128)(2,1)S(1)}, bf16[48]{0:T(256)(128)(2,1)}, u32[]{:S(2)}) copy-start(bf16[48]{0:T(256)(128)(2,1)} %param.15) | copy-start | bytes 292
  0.7 19.4 %copy-start.4 = (bf16[384,48]{0,1:T(8,128)(2,1)S(1)}, bf16[384,48]{0,1:T(8,128)(2,1)}, u32[]{:S(2)}) copy-start(bf16[384,48]{0,1:T(8,128)(2,1)} %param.14) | copy-start | bytes 110596
  0.7 19.4 %copy-start.3 = (bf16[576,48]{0,1:T(8,128)(2,1)S(1)}, bf16[576,48]{0,1:T(8,128)(2,1)}, u32[]{:S(2)}) copy-start(bf16[576,48]{0,1:T(8,128)(2,1)} %param.17) | copy-start | bytes 165892
  2.3 36.9 %copy-start.6 = (s32[2]{0:T(128)S(1)}, s32[2]{0:T(128)}, u32[]{:S(2)}) copy-start(s32[2]{0:T(128)} %param.20) | copy-start | bytes 28
  2.3 12.7 %collective-permute-start = (bf16[48,1152]{1,0:T(8,128)(2,1)S(1)}, bf16[48,1152]{1,0:T(8,128)(2,1)S(1)}, u32[]{:S(2)}, u32[]{:S(2)}) collective-permute-start(bf16[48,1152]{1,0:T(8,128)(2,1)S(1)} %pad_maximum_fusion.3.refs_0_), channel_id=1, source_target_pairs={{0,8},{2,10},{4,12},{6,14},{8,0},{10,2},{12,4},{14,6},{16,24},{18,... | collective-permute-start | bytes 331784 | tf_op jit(solution)/shard_map/ppermute | solution.py:444
  5.4 11.3 %collective-permute-start.1 = (bf16[48,1152]{1,0:T(8,128)(2,1)S(1)}, bf16[48,1152]{1,0:T(8,128)(2,1)S(1)}, u32[]{:S(2)}, u32[]{:S(2)}) collective-permute-start(bf16[48,1152]{1,0:T(8,128)(2,1)S(1)} %pad_maximum_fusion.3.refs_0_), channel_id=1, source_target_pairs={{0,16},{2,18},{4,20},{6,22},{8,24},{10,26},{12,28},{14,30},{16,0},... | collective-permute-start | bytes 331784 | tf_op jit(solution)/shard_map/ppermute | solution.py:444
  8.0 8.8 %collective-permute-start.2 = (bf16[48,1152]{1,0:T(8,128)(2,1)S(1)}, bf16[48,1152]{1,0:T(8,128)(2,1)S(1)}, u32[]{:S(2)}, u32[]{:S(2)}) collective-permute-start(bf16[48,1152]{1,0:T(8,128)(2,1)S(1)} %pad_maximum_fusion.3.refs_0_), channel_id=1, source_target_pairs={{0,24},{2,26},{4,28},{6,30},{8,16},{10,18},{12,20},{14,22},{16,8},... | collective-permute-start | bytes 331784 | tf_op jit(solution)/shard_map/ppermute | solution.py:444
  9.2 4.2 %collective-permute-start.13 = (bf16[48,512]{1,0:T(8,128)(2,1)S(1)}, bf16[48,512]{1,0:T(8,128)(2,1)S(1)}, u32[]{:S(2)}, u32[]{:S(2)}) collective-permute-start(bf16[48,512]{1,0:T(8,128)(2,1)S(1)} %bitcast.35), channel_id=1, source_target_pairs={{0,4},{2,6},{4,0},{6,2},{8,12},{10,14},{12,8},{14,10},{16,20},{18,... | collective-permute-start | bytes 147464 | tf_op jit(solution)/shard_map/ppermute | solution.py:444
  11.0 11.0 %collective-permute-start.12 = (bf16[48,512]{1,0:T(8,128)(2,1)S(1)}, bf16[48,512]{1,0:T(8,128)(2,1)S(1)}, u32[]{:S(2)}, u32[]{:S(2)}) collective-permute-start(bf16[48,512]{1,0:T(8,128)(2,1)S(1)} %bitcast.36), channel_id=1, source_target_pairs={{0,2},{2,0},{4,6},{6,4},{8,10},{10,8},{12,14},{14,12},{16,18},{18,... | collective-permute-start | bytes 147464 | tf_op jit(solution)/shard_map/ppermute | solution.py:444
  13.3 9.9 %collective-permute-start.14 = (bf16[48,512]{1,0:T(8,128)(2,1)S(1)}, bf16[48,512]{1,0:T(8,128)(2,1)S(1)}, u32[]{:S(2)}, u32[]{:S(2)}) collective-permute-start(bf16[48,512]{1,0:T(8,128)(2,1)S(1)} %collective-permute-done.13.refs_2_), channel_id=1, source_target_pairs={{0,2},{2,0},{4,6},{6,4},{8,10},{10,8},{12,14},{14,12},{16,18},{18,... | collective-permute-start | bytes 147464 | tf_op jit(solution)/shard_map/ppermute | solution.py:444
  16.8 35.9 %collective-permute-start.4 = (bf16[4,48,1152]{2,1,0:T(8,128)(2,1)S(1)}, bf16[4,48,1152]{2,1,0:T(8,128)(2,1)S(1)}, u32[]{:S(2)}, u32[]{:S(2)}) collective-permute-start(bf16[4,48,1152]{2,1,0:T(8,128)(2,1)S(1)} %shard_map.170.refs_2_), channel_id=1, source_target_pairs={{0,4},{2,6},{4,0},{6,2},{8,12},{10,14},{12,8},{14,10},{16,20},{18,... | collective-permute-start | bytes 1327112 | tf_op jit(solution)/shard_map/ppermute | solution.py:444
  18.4 34.2 %collective-permute-start.3 = (bf16[4,48,1152]{2,1,0:T(8,128)(2,1)S(1)}, bf16[4,48,1152]{2,1,0:T(8,128)(2,1)S(1)}, u32[]{:S(2)}, u32[]{:S(2)}) collective-permute-start(bf16[4,48,1152]{2,1,0:T(8,128)(2,1)S(1)} %shard_map.170.refs_2_), channel_id=1, source_target_pairs={{0,2},{2,0},{4,6},{6,4},{8,10},{10,8},{12,14},{14,12},{16,18},{18,... | collective-permute-start | bytes 1327112 | tf_op jit(solution)/shard_map/ppermute | solution.py:444
  20.2 9.6 %collective-permute-start.18 = (bf16[48,1664]{1,0:T(8,128)(2,1)S(1)}, bf16[48,1664]{1,0:T(8,128)(2,1)S(1)}, u32[]{:S(2)}, u32[]{:S(2)}) collective-permute-start(bf16[48,1664]{1,0:T(8,128)(2,1)S(1)} %concatenate.18.refs_0_), channel_id=1, source_target_pairs={{0,8},{2,10},{4,12},{6,14},{8,0},{10,2},{12,4},{14,6},{16,24},{18,... | collective-permute-start | bytes 479240 | tf_op jit(solution)/shard_map/ppermute | solution.py:444
  22.0 13.1 %collective-permute-start.19 = (bf16[48,1664]{1,0:T(8,128)(2,1)S(1)}, bf16[48,1664]{1,0:T(8,128)(2,1)S(1)}, u32[]{:S(2)}, u32[]{:S(2)}) collective-permute-start(bf16[48,1664]{1,0:T(8,128)(2,1)S(1)} %concatenate.18.refs_0_), channel_id=1, source_target_pairs={{0,16},{2,18},{4,20},{6,22},{8,24},{10,26},{12,28},{14,30},{16,0},... | collective-permute-start | bytes 479240 | tf_op jit(solution)/shard_map/ppermute | solution.py:444
  23.2 13.0 %collective-permute-start.20 = (bf16[48,1664]{1,0:T(8,128)(2,1)S(1)}, bf16[48,1664]{1,0:T(8,128)(2,1)S(1)}, u32[]{:S(2)}, u32[]{:S(2)}) collective-permute-start(bf16[48,1664]{1,0:T(8,128)(2,1)S(1)} %concatenate.18.refs_0_), channel_id=1, source_target_pairs={{0,24},{2,26},{4,28},{6,30},{8,16},{10,18},{12,20},{14,22},{16,8},... | collective-permute-start | bytes 479240 | tf_op jit(solution)/shard_map/ppermute | solution.py:444
  29.8 10.1 %collective-permute-start.15 = (bf16[4,48,512]{2,1,0:T(8,128)(2,1)S(1)}, bf16[4,48,512]{2,1,0:T(8,128)(2,1)S(1)}, u32[]{:S(2)}, u32[]{:S(2)}) collective-permute-start(bf16[4,48,512]{2,1,0:T(8,128)(2,1)S(1)} %shard_map.172.refs_5_), channel_id=1, source_target_pairs={{0,8},{2,10},{4,12},{6,14},{8,0},{10,2},{12,4},{14,6},{16,24},{18,... | collective-permute-start | bytes 589832 | tf_op jit(solution)/shard_map/ppermute | solution.py:444
  35.1 16.7 %collective-permute-start.16 = (bf16[4,48,512]{2,1,0:T(8,128)(2,1)S(1)}, bf16[4,48,512]{2,1,0:T(8,128)(2,1)S(1)}, u32[]{:S(2)}, u32[]{:S(2)}) collective-permute-start(bf16[4,48,512]{2,1,0:T(8,128)(2,1)S(1)} %shard_map.172.refs_5_), channel_id=1, source_target_pairs={{0,16},{2,18},{4,20},{6,22},{8,24},{10,26},{12,28},{14,30},{16,0},... | collective-permute-start | bytes 589832 | tf_op jit(solution)/shard_map/ppermute | solution.py:444
  36.3 16.0 %collective-permute-start.17 = (bf16[4,48,512]{2,1,0:T(8,128)(2,1)S(1)}, bf16[4,48,512]{2,1,0:T(8,128)(2,1)S(1)}, u32[]{:S(2)}, u32[]{:S(2)}) collective-permute-start(bf16[4,48,512]{2,1,0:T(8,128)(2,1)S(1)} %shard_map.172.refs_5_), channel_id=1, source_target_pairs={{0,24},{2,26},{4,28},{6,30},{8,16},{10,18},{12,20},{14,22},{16,8},... | collective-permute-start | bytes 589832 | tf_op jit(solution)/shard_map/ppermute | solution.py:444
  40.0 13.9 %collective-permute-start.25 = (bf16[4,48,512]{2,1,0:T(8,128)(2,1)S(1)}, bf16[4,48,512]{2,1,0:T(8,128)(2,1)S(1)}, u32[]{:S(2)}, u32[]{:S(2)}) collective-permute-start(bf16[4,48,512]{2,1,0:T(8,128)(2,1)S(1)} %shard_map.172.refs_5_), channel_id=1, source_target_pairs={{0,1},{1,0},{2,3},{3,2},{4,5},{5,4},{6,7},{7,6},{8,9},{9,8},{10,11... | collective-permute-start | bytes 589832 | tf_op jit(solution)/shard_map/ppermute | solution.py:440
  51.7 17.6 %collective-permute-start.22 = (bf16[4,48,1664]{2,1,0:T(8,128)(2,1)S(1)}, bf16[4,48,1664]{2,1,0:T(8,128)(2,1)S(1)}, u32[]{:S(2)}, u32[]{:S(2)}) collective-permute-start(bf16[4,48,1664]{2,1,0:T(8,128)(2,1)S(1)} %shard_map.173.refs_9_), channel_id=1, source_target_pairs={{0,4},{2,6},{4,0},{6,2},{8,12},{10,14},{12,8},{14,10},{16,20},{18,... | collective-permute-start | bytes 1916936 | tf_op jit(solution)/shard_map/ppermute | solution.py:444
  52.2 17.1 %collective-permute-start.21 = (bf16[4,48,1664]{2,1,0:T(8,128)(2,1)S(1)}, bf16[4,48,1664]{2,1,0:T(8,128)(2,1)S(1)}, u32[]{:S(2)}, u32[]{:S(2)}) collective-permute-start(bf16[4,48,1664]{2,1,0:T(8,128)(2,1)S(1)} %shard_map.173.refs_9_), channel_id=1, source_target_pairs={{0,2},{2,0},{4,6},{6,4},{8,10},{10,8},{12,14},{14,12},{16,18},{18,... | collective-permute-start | bytes 1916936 | tf_op jit(solution)/shard_map/ppermute | solution.py:444
  52.7 1.4 collective-permute-start.26
  52.7 3.0 %collective-permute-start.27 = (bf16[4,48,512]{2,1,0:T(8,128)(2,1)S(1)}, bf16[4,48,512]{2,1,0:T(8,128)(2,1)S(1)}, u32[]{:S(2)}, u32[]{:S(2)}) collective-permute-start(bf16[4,48,512]{2,1,0:T(8,128)(2,1)S(1)} %collective-permute-done.16.refs_7_), channel_id=1, source_target_pairs={{0,1},{1,0},{2,3},{3,2},{4,5},{5,4},{6,7},{7,6},{8,9},{9,8},{10,11... | collective-permute-start | bytes 589832 | tf_op jit(solution)/shard_map/ppermute | solution.py:440
  53.9 27.5 %copy-start.2 = (bf16[256,768]{1,0:T(8,128)(2,1)S(1)}, bf16[256,768]{1,0:T(8,128)(2,1)}, u32[]{:S(2)}) copy-start(bf16[256,768]{1,0:T(8,128)(2,1)} %param.18) | copy-start | bytes 1179652
  53.9 4.6 %collective-permute-start.28 = (bf16[4,48,512]{2,1,0:T(8,128)(2,1)S(1)}, bf16[4,48,512]{2,1,0:T(8,128)(2,1)S(1)}, u32[]{:S(2)}, u32[]{:S(2)}) collective-permute-start(bf16[4,48,512]{2,1,0:T(8,128)(2,1)S(1)} %collective-permute-done.17.refs_8_), channel_id=1, source_target_pairs={{0,1},{1,0},{2,3},{3,2},{4,5},{5,4},{6,7},{7,6},{8,9},{9,8},{10,11... | collective-permute-start | bytes 589832 | tf_op jit(solution)/shard_map/ppermute | solution.py:440
  54.1 14.4 %collective-permute-start.5 = (bf16[2,48,1152]{2,1,0:T(8,128)(2,1)S(1)}, bf16[2,48,1152]{2,1,0:T(8,128)(2,1)S(1)}, u32[]{:S(2)}, u32[]{:S(2)}) collective-permute-start(bf16[2,48,1152]{2,1,0:T(8,128)(2,1)S(1)} %slice.64), channel_id=1, source_target_pairs={{0,2},{2,0},{4,6},{6,4},{8,10},{10,8},{12,14},{14,12},{16,18},{18,... | collective-permute-start | bytes 663560 | tf_op jit(solution)/shard_map/ppermute | solution.py:444
  55.7 12.9 %collective-permute-start.6 = (bf16[2,48,1152]{2,1,0:T(8,128)(2,1)S(1)}, bf16[2,48,1152]{2,1,0:T(8,128)(2,1)S(1)}, u32[]{:S(2)}, u32[]{:S(2)}) collective-permute-start(bf16[2,48,1152]{2,1,0:T(8,128)(2,1)S(1)} %slice.65), channel_id=1, source_target_pairs={{0,4},{2,6},{4,0},{6,2},{8,12},{10,14},{12,8},{14,10},{16,20},{18,... | collective-permute-start | bytes 663560 | tf_op jit(solution)/shard_map/ppermute | solution.py:444
  58.6 11.4 %collective-permute-start.7 = (bf16[4,48,1152]{2,1,0:T(8,128)(2,1)S(1)}, bf16[4,48,1152]{2,1,0:T(8,128)(2,1)S(1)}, u32[]{:S(2)}, u32[]{:S(2)}) collective-permute-start(bf16[4,48,1152]{2,1,0:T(8,128)(2,1)S(1)} %shard_map.170.refs_2_), channel_id=1, source_target_pairs={{0,1},{1,0},{2,3},{3,2},{4,5},{5,4},{6,7},{7,6},{8,9},{9,8},{10,11... | collective-permute-start | bytes 1327112 | tf_op jit(solution)/shard_map/ppermute | solution.py:440
  68.6 4.8 %collective-permute-start.8 = (bf16[4,48,1152]{2,1,0:T(8,128)(2,1)S(1)}, bf16[4,48,1152]{2,1,0:T(8,128)(2,1)S(1)}, u32[]{:S(2)}, u32[]{:S(2)}) collective-permute-start(bf16[4,48,1152]{2,1,0:T(8,128)(2,1)S(1)} %collective-permute-done.3.refs_3_), channel_id=1, source_target_pairs={{0,1},{1,0},{2,3},{3,2},{4,5},{5,4},{6,7},{7,6},{8,9},{9,8},{10,11... | collective-permute-start | bytes 1327112 | tf_op jit(solution)/shard_map/ppermute | solution.py:440
  68.6 4.8 %collective-permute-start.9 = (bf16[4,48,1152]{2,1,0:T(8,128)(2,1)S(1)}, bf16[4,48,1152]{2,1,0:T(8,128)(2,1)S(1)}, u32[]{:S(2)}, u32[]{:S(2)}) collective-permute-start(bf16[4,48,1152]{2,1,0:T(8,128)(2,1)S(1)} %collective-permute-done.4.refs_4_), channel_id=1, source_target_pairs={{0,1},{1,0},{2,3},{3,2},{4,5},{5,4},{6,7},{7,6},{8,9},{9,8},{10,11... | collective-permute-start | bytes 1327112 | tf_op jit(solution)/shard_map/ppermute | solution.py:440
  69.3 2.0 %collective-permute-start.10 = (bf16[2,48,1152]{2,1,0:T(8,128)(2,1)S(1)}, bf16[2,48,1152]{2,1,0:T(8,128)(2,1)S(1)}, u32[]{:S(2)}, u32[]{:S(2)}) collective-permute-start(bf16[2,48,1152]{2,1,0:T(8,128)(2,1)S(1)} %collective-permute-done.5.refs_5_), channel_id=1, source_target_pairs={{0,1},{1,0},{2,3},{3,2},{4,5},{5,4},{6,7},{7,6},{8,9},{9,8},{10,11... | collective-permute-start | bytes 663560 | tf_op jit(solution)/shard_map/ppermute | solution.py:440
  69.4 2.4 %collective-permute-start.11 = (bf16[2,48,1152]{2,1,0:T(8,128)(2,1)S(1)}, bf16[2,48,1152]{2,1,0:T(8,128)(2,1)S(1)}, u32[]{:S(2)}, u32[]{:S(2)}) collective-permute-start(bf16[2,48,1152]{2,1,0:T(8,128)(2,1)S(1)} %collective-permute-done.6.refs_6_), channel_id=1, source_target_pairs={{0,1},{1,0},{2,3},{3,2},{4,5},{5,4},{6,7},{7,6},{8,9},{9,8},{10,11... | collective-permute-start | bytes 663560 | tf_op jit(solution)/shard_map/ppermute | solution.py:440
  69.9 11.6 %copy-start.1 = (bf16[256,768]{1,0:T(8,128)(2,1)S(1)}, bf16[256,768]{1,0:T(8,128)(2,1)}, u32[]{:S(2)}) copy-start(bf16[256,768]{1,0:T(8,128)(2,1)} %refs_0_.1) | copy-start | bytes 1179652
  69.9 16.0 %collective-permute-start.29 = (bf16[4,48,1664]{2,1,0:T(8,128)(2,1)S(1)}, bf16[4,48,1664]{2,1,0:T(8,128)(2,1)S(1)}, u32[]{:S(2)}, u32[]{:S(2)}) collective-permute-start(bf16[4,48,1664]{2,1,0:T(8,128)(2,1)S(1)} %shard_map.173.refs_9_), channel_id=1, source_target_pairs={{0,1},{1,0},{2,3},{3,2},{4,5},{5,4},{6,7},{7,6},{8,9},{9,8},{10,11... | collective-permute-start | bytes 1916936 | tf_op jit(solution)/shard_map/ppermute | solution.py:440
  71.3 9.6 %collective-permute-start.23 = (bf16[2,48,1664]{2,1,0:T(8,128)(2,1)S(1)}, bf16[2,48,1664]{2,1,0:T(8,128)(2,1)S(1)}, u32[]{:S(2)}, u32[]{:S(2)}) collective-permute-start(bf16[2,48,1664]{2,1,0:T(8,128)(2,1)S(1)} %slice.66), channel_id=1, source_target_pairs={{0,2},{2,0},{4,6},{6,4},{8,10},{10,8},{12,14},{14,12},{16,18},{18,... | collective-permute-start | bytes 958472 | tf_op jit(solution)/shard_map/ppermute | solution.py:444
  71.8 9.4 %collective-permute-start.24 = (bf16[2,48,1664]{2,1,0:T(8,128)(2,1)S(1)}, bf16[2,48,1664]{2,1,0:T(8,128)(2,1)S(1)}, u32[]{:S(2)}, u32[]{:S(2)}) collective-permute-start(bf16[2,48,1664]{2,1,0:T(8,128)(2,1)S(1)} %slice.67), channel_id=1, source_target_pairs={{0,4},{2,6},{4,0},{6,2},{8,12},{10,14},{12,8},{14,10},{16,20},{18,... | collective-permute-start | bytes 958472 | tf_op jit(solution)/shard_map/ppermute | solution.py:444
  73.4 12.6 %collective-permute-start.30 = (bf16[4,48,1664]{2,1,0:T(8,128)(2,1)S(1)}, bf16[4,48,1664]{2,1,0:T(8,128)(2,1)S(1)}, u32[]{:S(2)}, u32[]{:S(2)}) collective-permute-start(bf16[4,48,1664]{2,1,0:T(8,128)(2,1)S(1)} %collective-permute-done.21.refs_10_), channel_id=1, source_target_pairs={{0,1},{1,0},{2,3},{3,2},{4,5},{5,4},{6,7},{7,6},{8,9},{9,8},{10,11... | collective-permute-start | bytes 1916936 | tf_op jit(solution)/shard_map/ppermute | solution.py:440
  73.4 12.6 %collective-permute-start.31 = (bf16[4,48,1664]{2,1,0:T(8,128)(2,1)S(1)}, bf16[4,48,1664]{2,1,0:T(8,128)(2,1)S(1)}, u32[]{:S(2)}, u32[]{:S(2)}) collective-permute-start(bf16[4,48,1664]{2,1,0:T(8,128)(2,1)S(1)} %collective-permute-done.22.refs_11_), channel_id=1, source_target_pairs={{0,1},{1,0},{2,3},{3,2},{4,5},{5,4},{6,7},{7,6},{8,9},{9,8},{10,11... | collective-permute-start | bytes 1916936 | tf_op jit(solution)/shard_map/ppermute | solution.py:440
  80.9 5.1 %collective-permute-start.32 = (bf16[2,48,1664]{2,1,0:T(8,128)(2,1)S(1)}, bf16[2,48,1664]{2,1,0:T(8,128)(2,1)S(1)}, u32[]{:S(2)}, u32[]{:S(2)}) collective-permute-start(bf16[2,48,1664]{2,1,0:T(8,128)(2,1)S(1)} %collective-permute-done.23.refs_12_), channel_id=1, source_target_pairs={{0,1},{1,0},{2,3},{3,2},{4,5},{5,4},{6,7},{7,6},{8,9},{9,8},{10,11... | collective-permute-start | bytes 958472 | tf_op jit(solution)/shard_map/ppermute | solution.py:440
  81.2 4.8 %collective-permute-start.33 = (bf16[2,48,1664]{2,1,0:T(8,128)(2,1)S(1)}, bf16[2,48,1664]{2,1,0:T(8,128)(2,1)S(1)}, u32[]{:S(2)}, u32[]{:S(2)}) collective-permute-start(bf16[2,48,1664]{2,1,0:T(8,128)(2,1)S(1)} %collective-permute-done.24.refs_13_), channel_id=1, source_target_pairs={{0,1},{1,0},{2,3},{3,2},{4,5},{5,4},{6,7},{7,6},{8,9},{9,8},{10,11... | collective-permute-start | bytes 958472 | tf_op jit(solution)/shard_map/ppermute | solution.py:440
  91.2 13.6 %collective-permute-start.41 = (bf16[256,2560]{1,0:T(8,128)(2,1)S(1)}, bf16[256,2560]{1,0:T(8,128)(2,1)S(1)}, u32[]{:S(2)}, u32[]{:S(2)}) collective-permute-start(bf16[256,2560]{1,0:T(8,128)(2,1)S(1)} %get-tuple-element.94.refs_0_), channel_id=1, source_target_pairs={{0,1},{1,0},{2,3},{3,2},{4,5},{5,4},{6,7},{7,6},{8,9},{9,8},{10,11... | collective-permute-start | bytes 3932168 | tf_op jit(solution)/shard_map/ppermute | solution.py:440
  100.8 9.7 %collective-permute-start.34 = (bf16[272,1920]{1,0:T(8,128)(2,1)S(1)}, bf16[272,1920]{1,0:T(8,128)(2,1)S(1)}, u32[]{:S(2)}, u32[]{:S(2)}) collective-permute-start(bf16[272,1920]{1,0:T(8,128)(2,1)S(1)} %get-tuple-element.78.refs_0_), channel_id=1, source_target_pairs={{0,1},{1,0},{2,3},{3,2},{4,5},{5,4},{6,7},{7,6},{8,9},{9,8},{10,11... | collective-permute-start | bytes 3133448 | tf_op jit(solution)/shard_map/ppermute | solution.py:440
  101.0 3.9 %collective-permute-start.42 = (bf16[272,768]{1,0:T(8,128)(2,1)S(1)}, bf16[272,768]{1,0:T(8,128)(2,1)S(1)}, u32[]{:S(2)}, u32[]{:S(2)}) collective-permute-start(bf16[272,768]{1,0:T(8,128)(2,1)S(1)} %get-tuple-element.96.refs_3_), channel_id=1, source_target_pairs={{0,1},{1,0},{2,3},{3,2},{4,5},{5,4},{6,7},{7,6},{8,9},{9,8},{10,11... | collective-permute-start | bytes 1253384 | tf_op jit(solution)/shard_map/ppermute | solution.py:440
  101.3 3.3 %collective-permute-start.44 = (bf16[256,768]{1,0:T(8,128)(2,1)S(1)}, bf16[256,768]{1,0:T(8,128)(2,1)S(1)}, u32[]{:S(2)}, u32[]{:S(2)}) collective-permute-start(bf16[256,768]{1,0:T(8,128)(2,1)S(1)} %multiply_convert_fusion.refs_3_.gm_ref.refs_7_), channel_id=1, source_target_pairs={{0,1},{1,0},{2,3},{3,2},{4,5},{5,4},{6,7},{7,6},{8,9},{9,8},{10,11... | collective-permute-start | bytes 1179656 | tf_op jit(solution)/shard_map/ppermute | solution.py:440
  101.5 3.4 %collective-permute-start.43 = (bf16[256,384]{1,0:T(8,128)(2,1)S(1)}, bf16[256,384]{1,0:T(8,128)(2,1)S(1)}, u32[]{:S(2)}, u32[]{:S(2)}) collective-permute-start(bf16[256,384]{1,0:T(8,128)(2,1)S(1)} %get-tuple-element.97), channel_id=1, source_target_pairs={{0,1},{1,0},{2,3},{3,2},{4,5},{5,4},{6,7},{7,6},{8,9},{9,8},{10,11... | collective-permute-start | bytes 589832 | tf_op jit(solution)/shard_map/ppermute | solution.py:440
  107.5 16.3 %collective-permute-start.50 = (bf16[8,48,768]{2,1,0:T(8,128)(2,1)S(1)}, bf16[8,48,768]{2,1,0:T(8,128)(2,1)S(1)}, u32[]{:S(2)}, u32[]{:S(2)}) collective-permute-start(bf16[8,48,768]{2,1,0:T(8,128)(2,1)S(1)} %get-tuple-element.109), channel_id=1, source_target_pairs={{0,4},{2,6},{4,0},{6,2},{8,12},{10,14},{12,8},{14,10},{16,20},{18,... | collective-permute-start | bytes 1769480 | tf_op jit(solution)/shard_map/ppermute | solution.py:444
  109.1 14.1 %collective-permute-start.49 = (bf16[8,48,640]{2,1,0:T(8,128)(2,1)S(1)}, bf16[8,48,640]{2,1,0:T(8,128)(2,1)S(1)}, u32[]{:S(2)}, u32[]{:S(2)}) collective-permute-start(bf16[8,48,640]{2,1,0:T(8,128)(2,1)S(1)} %get-tuple-element.107), channel_id=1, source_target_pairs={{0,2},{2,0},{4,6},{6,4},{8,10},{10,8},{12,14},{14,12},{16,18},{18,... | collective-permute-start | bytes 1474568 | tf_op jit(solution)/shard_map/ppermute | solution.py:444
  111.9 21.8 %collective-permute-start.35 = (bf16[8,48,640]{2,1,0:T(8,128)(2,1)S(1)}, bf16[8,48,640]{2,1,0:T(8,128)(2,1)S(1)}, u32[]{:S(2)}, u32[]{:S(2)}) collective-permute-start(bf16[8,48,640]{2,1,0:T(8,128)(2,1)S(1)} %get-tuple-element.81), channel_id=1, source_target_pairs={{0,2},{2,0},{4,6},{6,4},{8,10},{10,8},{12,14},{14,12},{16,18},{18,... | collective-permute-start | bytes 1474568 | tf_op jit(solution)/shard_map/ppermute | solution.py:444
  112.6 21.7 %collective-permute-start.36 = (bf16[8,48,640]{2,1,0:T(8,128)(2,1)S(1)}, bf16[8,48,640]{2,1,0:T(8,128)(2,1)S(1)}, u32[]{:S(2)}, u32[]{:S(2)}) collective-permute-start(bf16[8,48,640]{2,1,0:T(8,128)(2,1)S(1)} %get-tuple-element.83), channel_id=1, source_target_pairs={{0,4},{2,6},{4,0},{6,2},{8,12},{10,14},{12,8},{14,10},{16,20},{18,... | collective-permute-start | bytes 1474568 | tf_op jit(solution)/shard_map/ppermute | solution.py:444
  113.1 24.4 %collective-permute-start.45 = (bf16[8,48,768]{2,1,0:T(8,128)(2,1)S(1)}, bf16[8,48,768]{2,1,0:T(8,128)(2,1)S(1)}, u32[]{:S(2)}, u32[]{:S(2)}) collective-permute-start(bf16[8,48,768]{2,1,0:T(8,128)(2,1)S(1)} %get-tuple-element.99), channel_id=1, source_target_pairs={{0,8},{2,10},{4,12},{6,14},{8,0},{10,2},{12,4},{14,6},{16,24},{18,... | collective-permute-start | bytes 1769480 | tf_op jit(solution)/shard_map/ppermute | solution.py:444
  124.0 20.2 %collective-permute-start.52 = (bf16[4,48,768]{2,1,0:T(8,128)(2,1)S(1)}, bf16[4,48,768]{2,1,0:T(8,128)(2,1)S(1)}, u32[]{:S(2)}, u32[]{:S(2)}) collective-permute-start(bf16[4,48,768]{2,1,0:T(8,128)(2,1)S(1)} %get-tuple-element.113), channel_id=1, source_target_pairs={{0,2},{2,0},{4,6},{6,4},{8,10},{10,8},{12,14},{14,12},{16,18},{18,... | collective-permute-start | bytes 884744 | tf_op jit(solution)/shard_map/ppermute | solution.py:444
  125.5 18.7 %collective-permute-start.51 = (bf16[4,48,640]{2,1,0:T(8,128)(2,1)S(1)}, bf16[4,48,640]{2,1,0:T(8,128)(2,1)S(1)}, u32[]{:S(2)}, u32[]{:S(2)}) collective-permute-start(bf16[4,48,640]{2,1,0:T(8,128)(2,1)S(1)} %get-tuple-element.111), channel_id=1, source_target_pairs={{0,4},{2,6},{4,0},{6,2},{8,12},{10,14},{12,8},{14,10},{16,20},{18,... | collective-permute-start | bytes 737288 | tf_op jit(solution)/shard_map/ppermute | solution.py:444
  134.5 10.8 %collective-permute-start.37 = (bf16[4,48,640]{2,1,0:T(8,128)(2,1)S(1)}, bf16[4,48,640]{2,1,0:T(8,128)(2,1)S(1)}, u32[]{:S(2)}, u32[]{:S(2)}) collective-permute-start(bf16[4,48,640]{2,1,0:T(8,128)(2,1)S(1)} %get-tuple-element.85), channel_id=1, source_target_pairs={{0,4},{2,6},{4,0},{6,2},{8,12},{10,14},{12,8},{14,10},{16,20},{18,... | collective-permute-start | bytes 737288 | tf_op jit(solution)/shard_map/ppermute | solution.py:444
  136.1 9.2 %collective-permute-start.38 = (bf16[4,48,640]{2,1,0:T(8,128)(2,1)S(1)}, bf16[4,48,640]{2,1,0:T(8,128)(2,1)S(1)}, u32[]{:S(2)}, u32[]{:S(2)}) collective-permute-start(bf16[4,48,640]{2,1,0:T(8,128)(2,1)S(1)} %get-tuple-element.87), channel_id=1, source_target_pairs={{0,2},{2,0},{4,6},{6,4},{8,10},{10,8},{12,14},{14,12},{16,18},{18,... | collective-permute-start | bytes 737288 | tf_op jit(solution)/shard_map/ppermute | solution.py:444
  137.7 18.0 %collective-permute-start.46 = (bf16[4,48,768]{2,1,0:T(8,128)(2,1)S(1)}, bf16[4,48,768]{2,1,0:T(8,128)(2,1)S(1)}, u32[]{:S(2)}, u32[]{:S(2)}) collective-permute-start(bf16[4,48,768]{2,1,0:T(8,128)(2,1)S(1)} %get-tuple-element.101), channel_id=1, source_target_pairs={{0,16},{2,18},{4,20},{6,22},{8,24},{10,26},{12,28},{14,30},{16,0},... | collective-permute-start | bytes 884744 | tf_op jit(solution)/shard_map/ppermute | solution.py:444
  144.3 14.4 %collective-permute-start.53 = (bf16[2,48,1408]{2,1,0:T(8,128)(2,1)S(1)}, bf16[2,48,1408]{2,1,0:T(8,128)(2,1)S(1)}, u32[]{:S(2)}, u32[]{:S(2)}) collective-permute-start(bf16[2,48,1408]{2,1,0:T(8,128)(2,1)S(1)} %get-tuple-element.115), channel_id=1, source_target_pairs={{0,8},{2,10},{4,12},{6,14},{8,0},{10,2},{12,4},{14,6},{16,24},{18,... | collective-permute-start | bytes 811016 | tf_op jit(solution)/shard_map/ppermute | solution.py:444
  145.4 18.2 %collective-permute-start.39 = (bf16[2,48,1280]{2,1,0:T(8,128)(2,1)S(1)}, bf16[2,48,1280]{2,1,0:T(8,128)(2,1)S(1)}, u32[]{:S(2)}, u32[]{:S(2)}) collective-permute-start(bf16[2,48,1280]{2,1,0:T(8,128)(2,1)S(1)} %get-tuple-element.89), channel_id=1, source_target_pairs={{0,8},{2,10},{4,12},{6,14},{8,0},{10,2},{12,4},{14,6},{16,24},{18,... | collective-permute-start | bytes 737288 | tf_op jit(solution)/shard_map/ppermute | solution.py:444
  155.7 8.0 %collective-permute-start.47 = (bf16[2,48,768]{2,1,0:T(8,128)(2,1)S(1)}, bf16[2,48,768]{2,1,0:T(8,128)(2,1)S(1)}, u32[]{:S(2)}, u32[]{:S(2)}) collective-permute-start(bf16[2,48,768]{2,1,0:T(8,128)(2,1)S(1)} %get-tuple-element.103), channel_id=1, source_target_pairs={{0,2},{2,0},{4,6},{6,4},{8,10},{10,8},{12,14},{14,12},{16,18},{18,... | collective-permute-start | bytes 442376 | tf_op jit(solution)/shard_map/ppermute | solution.py:444
  158.8 13.2 %collective-permute-start.54 = (bf16[1,48,1408]{2,1,0:T(8,128)(2,1)S(1)}, bf16[1,48,1408]{2,1,0:T(8,128)(2,1)S(1)}, u32[]{:S(2)}, u32[]{:S(2)}) collective-permute-start(bf16[1,48,1408]{2,1,0:T(8,128)(2,1)S(1)} %get-tuple-element.117), channel_id=1, source_target_pairs={{0,16},{2,18},{4,20},{6,22},{8,24},{10,26},{12,28},{14,30},{16,0},... | collective-permute-start | bytes 405512 | tf_op jit(solution)/shard_map/ppermute | solution.py:444
  163.7 7.6 %collective-permute-start.40 = (bf16[1,48,1280]{2,1,0:T(8,128)(2,1)S(1)}, bf16[1,48,1280]{2,1,0:T(8,128)(2,1)S(1)}, u32[]{:S(2)}, u32[]{:S(2)}) collective-permute-start(bf16[1,48,1280]{2,1,0:T(8,128)(2,1)S(1)} %get-tuple-element.91), channel_id=1, source_target_pairs={{0,16},{2,18},{4,20},{6,22},{8,24},{10,26},{12,28},{14,30},{16,0},... | collective-permute-start | bytes 368648 | tf_op jit(solution)/shard_map/ppermute | solution.py:444
  163.8 8.2 %collective-permute-start.48 = (bf16[1,48,768]{2,1,0:T(8,128)(2,1)S(1)}, bf16[1,48,768]{2,1,0:T(8,128)(2,1)S(1)}, u32[]{:S(2)}, u32[]{:S(2)}) collective-permute-start(bf16[1,48,768]{2,1,0:T(8,128)(2,1)S(1)} %get-tuple-element.105), channel_id=1, source_target_pairs={{0,4},{2,6},{4,0},{6,2},{8,12},{10,14},{12,8},{14,10},{16,20},{18,... | collective-permute-start | bytes 221192 | tf_op jit(solution)/shard_map/ppermute | solution.py:444
